TPU v7x, 256 devices: a whole 4x4x8 slice. The times are simulated.
256 devices in a mesh: layer: 8 (over z_lo, core), row: 32 (over x, y, z_hi).
Axes of the slice: x: 4, y: 4, z: 8 (z_hi: 2, z_lo: 4; z = z_hi * 4 + z_lo), core: 2. Of those that a mesh axis runs over, the one named last changes fastest.
Arguments:
- residual: float32 [2, 2, 64, 2048, 192], P(None, None, 'layer', 'row'), may hold values from -6 to 6
- wavenumber: float32 [64, 2048, 192], P('layer', 'row'), may hold values from 0.25 to 1.5
- inverse: bfloat16 [2, 8, 6144, 6144], P(None, 'layer', 'row'), may hold values from -3 to 3
Outputs:
- preconditioned: float32 [2, 2, 64, 2048, 192], P(None, None, 'layer', 'row')
All inputs are finite; a program needn't handle non-finite values.
Results may differ from a plain program's by a relative error of at most 0.003.
Values may be sent and summed in bfloat16 or wider, within the bound.
No kernel may reach another device: no remote copies, remote signals or barrier semaphores. Data moves between devices by JAX's collectives and lax.ppermute only.
A program may use at most 64 MiB of HBM per device.

v0:
```python
import jax
import jax.numpy as jnp
from jax import lax
from jax.sharding import PartitionSpec as P

QY = 16
PX = 4
SWEEPS = 4


damping = 0.8
absorb = 0.5
coupling = 0.45


def padded_2(array, sides, width):
    edges = {}
    for axis, dim in sides:
        size, length = (lax.axis_size(axis), array.shape[dim])
        up = [(i, (i + 1) % size) for i in range(size - 1)]
        last = lax.slice_in_dim(array, length - width, length, axis=dim)
        first = lax.slice_in_dim(array, 0, width, axis=dim)
        edges[dim] = (
            lax.ppermute(last, axis, up),
            lax.ppermute(first, axis, [(b, a) for a, b in up]),
        )
    done = []
    for _, dim in sides:
        low, high = edges[dim]
        around = [(width, width) if d in done else (0, 0) for d in range(array.ndim)]
        array = jnp.concatenate([jnp.pad(low, around), array, jnp.pad(high, around)], axis=dim)
        done.append(dim)
    return array


def from_behind(block, axis, distance):
    devices = range(lax.axis_size(axis))
    route = [(i - distance, i) for i in devices if i - distance in devices]
    return lax.ppermute(block, axis, route)


def sent_to_all(array, axis):
    length = lax.axis_size(axis)
    return lax.all_to_all(
        jnp.broadcast_to(array[None], (length, *array.shape)), axis, 0, 0, tiled=True
    )


def laid_out(parts, dim):
    shape = list(parts.shape[1:])
    shape[dim] *= parts.shape[0]
    return jnp.moveaxis(parts, 0, dim).reshape(shape)


def gathered_copies(array, axis, dim):
    parts = sent_to_all(array, axis)
    return laid_out(parts, dim)


def diagonal_parts(wavenumber):
    real_part = 6.0 - wavenumber
    imag_part = -absorb * wavenumber
    modulus = real_part * real_part + imag_part * imag_part
    return (real_part, imag_part, real_part / modulus, -imag_part / modulus)


def first_sweep(source, reciprocal_re, reciprocal_im):
    update_re = reciprocal_re * source[:, 0] - reciprocal_im * source[:, 1]
    update_im = reciprocal_re * source[:, 1] + reciprocal_im * source[:, 0]
    return damping * jnp.stack([update_re, update_im], axis=1)


def relax(extended, source, diagonal_re, diagonal_im, reciprocal_re, reciprocal_im):
    centre = extended[:, :, 1:-1, 1:-1, :]
    beside = extended[:, :, 2:, 1:-1, :] + extended[:, :, :-2, 1:-1, :]
    beside = beside + extended[:, :, 1:-1, 2:, :] + extended[:, :, 1:-1, :-2, :]
    padded = jnp.pad(centre, ((0, 0), (0, 0), (0, 0), (0, 0), (1, 1)))
    beside = beside + padded[..., 2:] + padded[..., :-2]
    applied_re = diagonal_re * centre[:, 0] - diagonal_im * centre[:, 1] - beside[:, 0]
    applied_im = diagonal_re * centre[:, 1] + diagonal_im * centre[:, 0] - beside[:, 1]
    remain_re = source[:, 0] - applied_re
    remain_im = source[:, 1] - applied_im
    update_re = reciprocal_re * remain_re - reciprocal_im * remain_im
    update_im = reciprocal_re * remain_im + reciprocal_im * remain_re
    return centre + damping * jnp.stack([update_re, update_im], axis=1)


def on_device(residual, wavenumber, inverse):
    shot_count = residual.shape[0]
    slab_depth = residual.shape[2]
    height = residual.shape[3]
    across = residual.shape[4]
    diagonal_re, diagonal_im, reciprocal_re, reciprocal_im = diagonal_parts(wavenumber)
    iterate = first_sweep(residual, reciprocal_re, reciprocal_im)
    for counter in range(SWEEPS - 1):
        extended = padded_2(iterate.astype(jnp.bfloat16), (("layer", 2), ("row", 3)), 1).astype(
            iterate.dtype
        )
        iterate = relax(extended, residual, diagonal_re, diagonal_im, reciprocal_re, reciprocal_im)
    blocks = residual.reshape(shot_count, 2, slab_depth, height // QY, QY, across // PX, PX).mean(
        axis=(2, 4, 6)
    )
    coarse_rhs = blocks.reshape(shot_count, 2, -1).transpose(1, 0, 2)
    matrix_re = inverse[0, 0]
    matrix_im = inverse[1, 0]
    layers = lax.axis_size("layer")

    def fold_into(shard_piece):
        product_re = jnp.einsum(
            "rc,ksc->ksr", matrix_re, shard_piece, preferred_element_type=jnp.float32
        )
        product_im = jnp.einsum(
            "rc,ksc->ksr", matrix_im, shard_piece, preferred_element_type=jnp.float32
        )
        return jnp.stack([product_re[0] - product_im[1], product_re[1] + product_im[0]])

    def advance_all(counter, solved):
        incoming = from_behind(solved, "layer", 1)
        vector = (coarse_rhs + coupling * incoming).astype(jnp.bfloat16)
        return fold_into(gathered_copies(vector, "row", 2))

    coarse = lax.fori_loop(0, layers, advance_all, jnp.zeros_like(coarse_rhs))
    lifted = coarse.transpose(1, 0, 2).reshape(shot_count, 2, 1, height // QY, 1, across // PX, 1)
    lifted = jnp.broadcast_to(
        lifted, (shot_count, 2, slab_depth, height // QY, QY, across // PX, PX)
    )
    lifted = lifted.reshape(shot_count, 2, slab_depth, height, across)
    return iterate + lifted


def solution(mesh):
    return jax.shard_map(
        on_device,
        mesh=mesh,
        in_specs=(
            P(None, None, "layer", "row", None),
            P("layer", "row", None),
            P(None, "layer", "row", None),
        ),
        out_specs=P(None, None, "layer", "row", None),
        check_vma=False,
    )
```

profile of v0, /device:TPU:32, one launch (start us, length us, event | category | flops | bytes accessed | tf_op | source)
XLA Modules:
  0.0 305.8 jit_solution(17134527748194606609)
XLA Ops:
  5.2 9.4 %collective-permute-start.1 = (bf16[2,2,8,1,192]{4,3,2,1,0:T(2,128)(2,1)}, bf16[2,2,8,1,192]{4,3,2,1,0:T(2,128)(2,1)}, u32[]{:S(2)}, u32[]{:S(2)}) collective-permute-start(bf16[2,2,8,1,192]{4,3,2,1,0:T(2,128)(2,1)} %get-tuple-element.78), channel_id=1, source_target_pairs={{0,1},{1,2},{2,3},{3,4},{4,5},{5,6},{6,7},{7,8},{8,9},{9,10},{10,1... | collective-permute-start | bytes 36872 | tf_op jit(solution)/shard_map/ppermute | solution.py:24
  35.9 8.8 %collective-permute-start.5 = (bf16[2,2,8,1,192]{4,3,2,1,0:T(2,128)(2,1)}, bf16[2,2,8,1,192]{4,3,2,1,0:T(2,128)(2,1)S(1)}, u32[]{:S(2)}, u32[]{:S(2)}) collective-permute-start(bf16[2,2,8,1,192]{4,3,2,1,0:T(2,128)(2,1)} %get-tuple-element.74), channel_id=1, source_target_pairs={{0,1},{1,2},{2,3},{3,4},{4,5},{5,6},{6,7},{7,8},{8,9},{9,10},{10,1... | collective-permute-start | bytes 36872 | tf_op jit(solution)/shard_map/ppermute | solution.py:24
  44.7 2.9 collective-permute-start.7
  50.5 4.0 %collective-permute-done.6 = bf16[2,2,1,64,192]{4,3,2,1,0:T(8,128)(2,1)} collective-permute-done((bf16[2,2,1,64,192]{4,3,2,1,0:T(8,128)(2,1)}, bf16[2,2,1,64,192]{4,3,2,1,0:T(8,128)(2,1)}, u32[]{:S(2)}, u32[]{:S(2)}) %collective-permute-start.6) | collective-permute-done | bytes 98336 | tf_op jit(solution)/shard_map/ppermute | solution.py:24
  62.6 9.3 %collective-permute-start.9 = (bf16[2,2,8,1,192]{4,3,2,1,0:T(2,128)(2,1)}, bf16[2,2,8,1,192]{4,3,2,1,0:T(2,128)(2,1)}, u32[]{:S(2)}, u32[]{:S(2)}) collective-permute-start(bf16[2,2,8,1,192]{4,3,2,1,0:T(2,128)(2,1)} %get-tuple-element.70), channel_id=1, source_target_pairs={{0,1},{1,2},{2,3},{3,4},{4,5},{5,6},{6,7},{7,8},{8,9},{9,10},{10,1... | collective-permute-start | bytes 36872 | tf_op jit(solution)/shard_map/ppermute | solution.py:24
  73.8 2.6 collective-permute-start.10
  76.4 217.6 %while.10 = (s32[]{:T(128)}, f32[2,2,192]{2,1,0:T(2,128)S(1)}, f32[2,2,192]{2,1,0:T(2,128)S(1)}, bf16[192,6144]{1,0:T(8,128)(2,1)}, bf16[192,6144]{1,0:T(8,128)(2,1)}, /*index=5*/s32[]{:T(128)}) while((s32[]{:T(128)}, f32[2,2,192]{2,1,0:T(2,128)S(1)}, f32[2,2,192]{2,1,0:T(2,128)S(1)}, bf16[192,6144]{1,0:T(8,128)(2,1)}, ...), condition=%wide.region_3.4_spmd, body=%wide.region_2.3_spmd.sunk | while | flops 18878208 | bytes 14723241 | solution.py:122
  76.4 2.6 collective-permute-start
  82.0 19.1 %all-to-all-start = ((bf16[32,2,2,192]{3,2,1,0:T(2,128)(2,1)}), bf16[32,2,2,192]{3,2,1,0:T(2,128)(2,1)S(1)}, u32[]{:S(2)}, u32[]{:S(2)}) async-start(bf16[32,2,2,192]{3,2,1,0:T(2,128)(2,1)} %broadcast_in_dim.19), calls=%async_computation | async-start | bytes 131072 | tf_op jit(solution)/shard_map/while/body/eval_jaxpr/all_to_all | solution.py:44
  101.2 12.3 %all-to-all-done = bf16[32,2,2,192]{3,2,1,0:T(2,128)(2,1)S(1)} async-done(((bf16[32,2,2,192]{3,2,1,0:T(2,128)(2,1)}), bf16[32,2,2,192]{3,2,1,0:T(2,128)(2,1)S(1)}, u32[]{:S(2)}, u32[]{:S(2)}) %all-to-all-start) | async-done | bytes 49184 | tf_op jit(solution)/shard_map/while/body/eval_jaxpr/all_to_all | solution.py:44
  118.9 3.0 collective-permute-done
  122.6 3.9 %all-to-all-start = ((bf16[32,2,2,192]{3,2,1,0:T(2,128)(2,1)}), bf16[32,2,2,192]{3,2,1,0:T(2,128)(2,1)S(1)}, u32[]{:S(2)}, u32[]{:S(2)}) async-start(bf16[32,2,2,192]{3,2,1,0:T(2,128)(2,1)} %broadcast_in_dim.19), calls=%async_computation | async-start | bytes 131072 | tf_op jit(solution)/shard_map/while/body/eval_jaxpr/all_to_all | solution.py:44
  126.5 12.3 %all-to-all-done = bf16[32,2,2,192]{3,2,1,0:T(2,128)(2,1)S(1)} async-done(((bf16[32,2,2,192]{3,2,1,0:T(2,128)(2,1)}), bf16[32,2,2,192]{3,2,1,0:T(2,128)(2,1)S(1)}, u32[]{:S(2)}, u32[]{:S(2)}) %all-to-all-start) | async-done | bytes 49184 | tf_op jit(solution)/shard_map/while/body/eval_jaxpr/all_to_all | solution.py:44
  138.9 2.6 fusion.63
  144.2 3.0 collective-permute-done
  147.9 3.9 %all-to-all-start = ((bf16[32,2,2,192]{3,2,1,0:T(2,128)(2,1)}), bf16[32,2,2,192]{3,2,1,0:T(2,128)(2,1)S(1)}, u32[]{:S(2)}, u32[]{:S(2)}) async-start(bf16[32,2,2,192]{3,2,1,0:T(2,128)(2,1)} %broadcast_in_dim.19), calls=%async_computation | async-start | bytes 131072 | tf_op jit(solution)/shard_map/while/body/eval_jaxpr/all_to_all | solution.py:44
  151.7 12.3 %all-to-all-done = bf16[32,2,2,192]{3,2,1,0:T(2,128)(2,1)S(1)} async-done(((bf16[32,2,2,192]{3,2,1,0:T(2,128)(2,1)}), bf16[32,2,2,192]{3,2,1,0:T(2,128)(2,1)S(1)}, u32[]{:S(2)}, u32[]{:S(2)}) %all-to-all-start) | async-done | bytes 49184 | tf_op jit(solution)/shard_map/while/body/eval_jaxpr/all_to_all | solution.py:44
  169.5 3.0 collective-permute-done
  173.2 3.9 %all-to-all-start = ((bf16[32,2,2,192]{3,2,1,0:T(2,128)(2,1)}), bf16[32,2,2,192]{3,2,1,0:T(2,128)(2,1)S(1)}, u32[]{:S(2)}, u32[]{:S(2)}) async-start(bf16[32,2,2,192]{3,2,1,0:T(2,128)(2,1)} %broadcast_in_dim.19), calls=%async_computation | async-start | bytes 131072 | tf_op jit(solution)/shard_map/while/body/eval_jaxpr/all_to_all | solution.py:44
  177.0 12.3 %all-to-all-done = bf16[32,2,2,192]{3,2,1,0:T(2,128)(2,1)S(1)} async-done(((bf16[32,2,2,192]{3,2,1,0:T(2,128)(2,1)}), bf16[32,2,2,192]{3,2,1,0:T(2,128)(2,1)S(1)}, u32[]{:S(2)}, u32[]{:S(2)}) %all-to-all-start) | async-done | bytes 49184 | tf_op jit(solution)/shard_map/while/body/eval_jaxpr/all_to_all | solution.py:44
  194.8 3.0 collective-permute-done
  198.5 3.9 %all-to-all-start = ((bf16[32,2,2,192]{3,2,1,0:T(2,128)(2,1)}), bf16[32,2,2,192]{3,2,1,0:T(2,128)(2,1)S(1)}, u32[]{:S(2)}, u32[]{:S(2)}) async-start(bf16[32,2,2,192]{3,2,1,0:T(2,128)(2,1)} %broadcast_in_dim.19), calls=%async_computation | async-start | bytes 131072 | tf_op jit(solution)/shard_map/while/body/eval_jaxpr/all_to_all | solution.py:44
  202.3 12.3 %all-to-all-done = bf16[32,2,2,192]{3,2,1,0:T(2,128)(2,1)S(1)} async-done(((bf16[32,2,2,192]{3,2,1,0:T(2,128)(2,1)}), bf16[32,2,2,192]{3,2,1,0:T(2,128)(2,1)S(1)}, u32[]{:S(2)}, u32[]{:S(2)}) %all-to-all-start) | async-done | bytes 49184 | tf_op jit(solution)/shard_map/while/body/eval_jaxpr/all_to_all | solution.py:44
  220.1 3.0 collective-permute-done
  223.7 3.9 %all-to-all-start = ((bf16[32,2,2,192]{3,2,1,0:T(2,128)(2,1)}), bf16[32,2,2,192]{3,2,1,0:T(2,128)(2,1)S(1)}, u32[]{:S(2)}, u32[]{:S(2)}) async-start(bf16[32,2,2,192]{3,2,1,0:T(2,128)(2,1)} %broadcast_in_dim.19), calls=%async_computation | async-start | bytes 131072 | tf_op jit(solution)/shard_map/while/body/eval_jaxpr/all_to_all | solution.py:44
  227.6 12.3 %all-to-all-done = bf16[32,2,2,192]{3,2,1,0:T(2,128)(2,1)S(1)} async-done(((bf16[32,2,2,192]{3,2,1,0:T(2,128)(2,1)}), bf16[32,2,2,192]{3,2,1,0:T(2,128)(2,1)S(1)}, u32[]{:S(2)}, u32[]{:S(2)}) %all-to-all-start) | async-done | bytes 49184 | tf_op jit(solution)/shard_map/while/body/eval_jaxpr/all_to_all | solution.py:44
  245.4 3.0 collective-permute-done
  249.0 3.9 %all-to-all-start = ((bf16[32,2,2,192]{3,2,1,0:T(2,128)(2,1)}), bf16[32,2,2,192]{3,2,1,0:T(2,128)(2,1)S(1)}, u32[]{:S(2)}, u32[]{:S(2)}) async-start(bf16[32,2,2,192]{3,2,1,0:T(2,128)(2,1)} %broadcast_in_dim.19), calls=%async_computation | async-start | bytes 131072 | tf_op jit(solution)/shard_map/while/body/eval_jaxpr/all_to_all | solution.py:44
  252.9 12.3 %all-to-all-done = bf16[32,2,2,192]{3,2,1,0:T(2,128)(2,1)S(1)} async-done(((bf16[32,2,2,192]{3,2,1,0:T(2,128)(2,1)}), bf16[32,2,2,192]{3,2,1,0:T(2,128)(2,1)S(1)}, u32[]{:S(2)}, u32[]{:S(2)}) %all-to-all-start) | async-done | bytes 49184 | tf_op jit(solution)/shard_map/while/body/eval_jaxpr/all_to_all | solution.py:44
  270.6 3.0 collective-permute-done
  274.3 3.9 %all-to-all-start = ((bf16[32,2,2,192]{3,2,1,0:T(2,128)(2,1)}), bf16[32,2,2,192]{3,2,1,0:T(2,128)(2,1)S(1)}, u32[]{:S(2)}, u32[]{:S(2)}) async-start(bf16[32,2,2,192]{3,2,1,0:T(2,128)(2,1)} %broadcast_in_dim.19), calls=%async_computation | async-start | bytes 131072 | tf_op jit(solution)/shard_map/while/body/eval_jaxpr/all_to_all | solution.py:44
  278.2 12.3 %all-to-all-done = bf16[32,2,2,192]{3,2,1,0:T(2,128)(2,1)S(1)} async-done(((bf16[32,2,2,192]{3,2,1,0:T(2,128)(2,1)}), bf16[32,2,2,192]{3,2,1,0:T(2,128)(2,1)S(1)}, u32[]{:S(2)}, u32[]{:S(2)}) %all-to-all-start) | async-done | bytes 49184 | tf_op jit(solution)/shard_map/while/body/eval_jaxpr/all_to_all | solution.py:44
  (174 shorter events, 97.3 us)
Async XLA Ops:
  2.4 17.3 %slice-start = ((s8[4718592]{0:T(1024)(128)(4,1)}), s8[4194304]{0:T(1024)(128)(4,1)S(1)}, s32[]{:S(2)}) async-start(s8[4718592]{0:T(1024)(128)(4,1)} %bitcast.36), calls=%async_computation.1 | async-start | bytes 8388608
  2.4 17.3 %slice-start.1 = ((s8[4718592]{0:T(1024)(128)(4,1)}), s8[524288]{0:T(1024)(128)(4,1)S(1)}, s32[]{:S(2)}) async-start(s8[4718592]{0:T(1024)(128)(4,1)} %bitcast.36), calls=%async_computation.2 | async-start | bytes 1048576
  3.1 11.5 %copy-start.9 = (bf16[2,2,8,64,192]{4,3,2,1,0:T(8,128)(2,1)}, bf16[2,2,8,64,192]{4,3,2,1,0:T(8,128)(2,1)S(1)}, u32[]{:S(2)}) copy-start(bf16[2,2,8,64,192]{4,3,2,1,0:T(8,128)(2,1)S(1)} %fusion.16) | copy-start | bytes 2359300
  3.7 24.1 %collective-permute-start.4 = (bf16[2,2,8,1,192]{4,3,2,1,0:T(2,128)(2,1)}, bf16[2,2,8,1,192]{4,3,2,1,0:T(2,128)(2,1)}, u32[]{:S(2)}, u32[]{:S(2)}) collective-permute-start(bf16[2,2,8,1,192]{4,3,2,1,0:T(2,128)(2,1)} %get-tuple-element.79), channel_id=1, source_target_pairs={{1,0},{2,1},{3,2},{4,3},{5,4},{6,5},{7,6},{8,7},{9,8},{10,9},{11,1... | collective-permute-start | bytes 36872 | tf_op jit(solution)/shard_map/ppermute | solution.py:25
  5.2 22.6 %collective-permute-start.1 = (bf16[2,2,8,1,192]{4,3,2,1,0:T(2,128)(2,1)}, bf16[2,2,8,1,192]{4,3,2,1,0:T(2,128)(2,1)}, u32[]{:S(2)}, u32[]{:S(2)}) collective-permute-start(bf16[2,2,8,1,192]{4,3,2,1,0:T(2,128)(2,1)} %get-tuple-element.78), channel_id=1, source_target_pairs={{0,1},{1,2},{2,3},{3,4},{4,5},{5,6},{6,7},{7,8},{8,9},{9,10},{10,1... | collective-permute-start | bytes 36872 | tf_op jit(solution)/shard_map/ppermute | solution.py:24
  15.3 12.5 %collective-permute-start.3 = (bf16[2,2,1,64,192]{4,3,2,1,0:T(8,128)(2,1)}, bf16[2,2,1,64,192]{4,3,2,1,0:T(8,128)(2,1)}, u32[]{:S(2)}, u32[]{:S(2)}) collective-permute-start(bf16[2,2,1,64,192]{4,3,2,1,0:T(8,128)(2,1)} %get-tuple-element.77), channel_id=1, source_target_pairs={{32,0},{64,32},{96,64},{128,96},{160,128},{192,160},{224,192},{33,... | collective-permute-start | bytes 294920 | tf_op jit(solution)/shard_map/ppermute | solution.py:25
  17.4 10.5 %collective-permute-start.2 = (bf16[2,2,1,64,192]{4,3,2,1,0:T(8,128)(2,1)}, bf16[2,2,1,64,192]{4,3,2,1,0:T(8,128)(2,1)}, u32[]{:S(2)}, u32[]{:S(2)}) collective-permute-start(bf16[2,2,1,64,192]{4,3,2,1,0:T(8,128)(2,1)} %get-tuple-element.76), channel_id=1, source_target_pairs={{0,32},{32,64},{64,96},{96,128},{128,160},{160,192},{192,224},{1,3... | collective-permute-start | bytes 294920 | tf_op jit(solution)/shard_map/ppermute | solution.py:24
  34.6 15.1 %collective-permute-start.8 = (bf16[2,2,8,1,192]{4,3,2,1,0:T(2,128)(2,1)}, bf16[2,2,8,1,192]{4,3,2,1,0:T(2,128)(2,1)S(1)}, u32[]{:S(2)}, u32[]{:S(2)}) collective-permute-start(bf16[2,2,8,1,192]{4,3,2,1,0:T(2,128)(2,1)} %get-tuple-element.75), channel_id=1, source_target_pairs={{1,0},{2,1},{3,2},{4,3},{5,4},{6,5},{7,6},{8,7},{9,8},{10,9},{11,1... | collective-permute-start | bytes 36872 | tf_op jit(solution)/shard_map/ppermute | solution.py:25
  35.9 13.8 %collective-permute-start.5 = (bf16[2,2,8,1,192]{4,3,2,1,0:T(2,128)(2,1)}, bf16[2,2,8,1,192]{4,3,2,1,0:T(2,128)(2,1)S(1)}, u32[]{:S(2)}, u32[]{:S(2)}) collective-permute-start(bf16[2,2,8,1,192]{4,3,2,1,0:T(2,128)(2,1)} %get-tuple-element.74), channel_id=1, source_target_pairs={{0,1},{1,2},{2,3},{3,4},{4,5},{5,6},{6,7},{7,8},{8,9},{9,10},{10,1... | collective-permute-start | bytes 36872 | tf_op jit(solution)/shard_map/ppermute | solution.py:24
  44.7 5.8 %collective-permute-start.7 = (bf16[2,2,1,64,192]{4,3,2,1,0:T(8,128)(2,1)}, bf16[2,2,1,64,192]{4,3,2,1,0:T(8,128)(2,1)S(1)}, u32[]{:S(2)}, u32[]{:S(2)}) collective-permute-start(bf16[2,2,1,64,192]{4,3,2,1,0:T(8,128)(2,1)} %get-tuple-element.73), channel_id=1, source_target_pairs={{32,0},{64,32},{96,64},{128,96},{160,128},{192,160},{224,192},{33,... | collective-permute-start | bytes 294920 | tf_op jit(solution)/shard_map/ppermute | solution.py:25
  47.6 7.0 %collective-permute-start.6 = (bf16[2,2,1,64,192]{4,3,2,1,0:T(8,128)(2,1)}, bf16[2,2,1,64,192]{4,3,2,1,0:T(8,128)(2,1)}, u32[]{:S(2)}, u32[]{:S(2)}) collective-permute-start(bf16[2,2,1,64,192]{4,3,2,1,0:T(8,128)(2,1)} %get-tuple-element.72), channel_id=1, source_target_pairs={{0,32},{32,64},{64,96},{96,128},{128,160},{160,192},{192,224},{1,3... | collective-permute-start | bytes 294920 | tf_op jit(solution)/shard_map/ppermute | solution.py:24
  61.3 237.3 %collective-permute-start.12 = (bf16[2,2,8,1,192]{4,3,2,1,0:T(2,128)(2,1)}, bf16[2,2,8,1,192]{4,3,2,1,0:T(2,128)(2,1)}, u32[]{:S(2)}, u32[]{:S(2)}) collective-permute-start(bf16[2,2,8,1,192]{4,3,2,1,0:T(2,128)(2,1)} %get-tuple-element.71), channel_id=1, source_target_pairs={{1,0},{2,1},{3,2},{4,3},{5,4},{6,5},{7,6},{8,7},{9,8},{10,9},{11,1... | collective-permute-start | bytes 36872 | tf_op jit(solution)/shard_map/ppermute | solution.py:25
  62.6 236.0 %collective-permute-start.9 = (bf16[2,2,8,1,192]{4,3,2,1,0:T(2,128)(2,1)}, bf16[2,2,8,1,192]{4,3,2,1,0:T(2,128)(2,1)}, u32[]{:S(2)}, u32[]{:S(2)}) collective-permute-start(bf16[2,2,8,1,192]{4,3,2,1,0:T(2,128)(2,1)} %get-tuple-element.70), channel_id=1, source_target_pairs={{0,1},{1,2},{2,3},{3,4},{4,5},{5,6},{6,7},{7,8},{8,9},{9,10},{10,1... | collective-permute-start | bytes 36872 | tf_op jit(solution)/shard_map/ppermute | solution.py:24
  71.9 226.7 %collective-permute-start.11 = (bf16[2,2,1,64,192]{4,3,2,1,0:T(8,128)(2,1)}, bf16[2,2,1,64,192]{4,3,2,1,0:T(8,128)(2,1)}, u32[]{:S(2)}, u32[]{:S(2)}) collective-permute-start(bf16[2,2,1,64,192]{4,3,2,1,0:T(8,128)(2,1)} %get-tuple-element.69), channel_id=1, source_target_pairs={{32,0},{64,32},{96,64},{128,96},{160,128},{192,160},{224,192},{33,... | collective-permute-start | bytes 294920 | tf_op jit(solution)/shard_map/ppermute | solution.py:25
  73.8 224.8 %collective-permute-start.10 = (bf16[2,2,1,64,192]{4,3,2,1,0:T(8,128)(2,1)}, bf16[2,2,1,64,192]{4,3,2,1,0:T(8,128)(2,1)}, u32[]{:S(2)}, u32[]{:S(2)}) collective-permute-start(bf16[2,2,1,64,192]{4,3,2,1,0:T(8,128)(2,1)} %get-tuple-element.68), channel_id=1, source_target_pairs={{0,32},{32,64},{64,96},{96,128},{128,160},{160,192},{192,224},{1,3... | collective-permute-start | bytes 294920 | tf_op jit(solution)/shard_map/ppermute | solution.py:24
  76.4 4.9 %collective-permute-start = (f32[2,2,192]{2,1,0:T(2,128)S(1)}, f32[2,2,192]{2,1,0:T(2,128)S(1)}, u32[]{:S(2)}, u32[]{:S(2)}) collective-permute-start(f32[2,2,192]{2,1,0:T(2,128)S(1)} %get-tuple-element.126), channel_id=1, source_target_pairs={{0,32},{32,64},{64,96},{96,128},{128,160},{160,192},{192,224},{1,3... | collective-permute-start | bytes 9224 | tf_op jit(solution)/shard_map/while/body/eval_jaxpr/ppermute | solution.py:39
  82.0 31.4 %all-to-all-start = ((bf16[32,2,2,192]{3,2,1,0:T(2,128)(2,1)}), bf16[32,2,2,192]{3,2,1,0:T(2,128)(2,1)S(1)}, u32[]{:S(2)}, u32[]{:S(2)}) async-start(bf16[32,2,2,192]{3,2,1,0:T(2,128)(2,1)} %broadcast_in_dim.19), calls=%async_computation | async-start | bytes 131072 | tf_op jit(solution)/shard_map/while/body/eval_jaxpr/all_to_all | solution.py:44
  117.0 4.9 %collective-permute-start = (f32[2,2,192]{2,1,0:T(2,128)S(1)}, f32[2,2,192]{2,1,0:T(2,128)S(1)}, u32[]{:S(2)}, u32[]{:S(2)}) collective-permute-start(f32[2,2,192]{2,1,0:T(2,128)S(1)} %get-tuple-element.126), channel_id=1, source_target_pairs={{0,32},{32,64},{64,96},{96,128},{128,160},{160,192},{192,224},{1,3... | collective-permute-start | bytes 9224 | tf_op jit(solution)/shard_map/while/body/eval_jaxpr/ppermute | solution.py:39
  122.6 16.1 %all-to-all-start = ((bf16[32,2,2,192]{3,2,1,0:T(2,128)(2,1)}), bf16[32,2,2,192]{3,2,1,0:T(2,128)(2,1)S(1)}, u32[]{:S(2)}, u32[]{:S(2)}) async-start(bf16[32,2,2,192]{3,2,1,0:T(2,128)(2,1)} %broadcast_in_dim.19), calls=%async_computation | async-start | bytes 131072 | tf_op jit(solution)/shard_map/while/body/eval_jaxpr/all_to_all | solution.py:44
  138.9 2.6 copy-start.10
  142.3 4.9 %collective-permute-start = (f32[2,2,192]{2,1,0:T(2,128)S(1)}, f32[2,2,192]{2,1,0:T(2,128)S(1)}, u32[]{:S(2)}, u32[]{:S(2)}) collective-permute-start(f32[2,2,192]{2,1,0:T(2,128)S(1)} %get-tuple-element.126), channel_id=1, source_target_pairs={{0,32},{32,64},{64,96},{96,128},{128,160},{160,192},{192,224},{1,3... | collective-permute-start | bytes 9224 | tf_op jit(solution)/shard_map/while/body/eval_jaxpr/ppermute | solution.py:39
  147.9 16.1 %all-to-all-start = ((bf16[32,2,2,192]{3,2,1,0:T(2,128)(2,1)}), bf16[32,2,2,192]{3,2,1,0:T(2,128)(2,1)S(1)}, u32[]{:S(2)}, u32[]{:S(2)}) async-start(bf16[32,2,2,192]{3,2,1,0:T(2,128)(2,1)} %broadcast_in_dim.19), calls=%async_computation | async-start | bytes 131072 | tf_op jit(solution)/shard_map/while/body/eval_jaxpr/all_to_all | solution.py:44
  167.6 4.9 %collective-permute-start = (f32[2,2,192]{2,1,0:T(2,128)S(1)}, f32[2,2,192]{2,1,0:T(2,128)S(1)}, u32[]{:S(2)}, u32[]{:S(2)}) collective-permute-start(f32[2,2,192]{2,1,0:T(2,128)S(1)} %get-tuple-element.126), channel_id=1, source_target_pairs={{0,32},{32,64},{64,96},{96,128},{128,160},{160,192},{192,224},{1,3... | collective-permute-start | bytes 9224 | tf_op jit(solution)/shard_map/while/body/eval_jaxpr/ppermute | solution.py:39
  173.2 16.1 %all-to-all-start = ((bf16[32,2,2,192]{3,2,1,0:T(2,128)(2,1)}), bf16[32,2,2,192]{3,2,1,0:T(2,128)(2,1)S(1)}, u32[]{:S(2)}, u32[]{:S(2)}) async-start(bf16[32,2,2,192]{3,2,1,0:T(2,128)(2,1)} %broadcast_in_dim.19), calls=%async_computation | async-start | bytes 131072 | tf_op jit(solution)/shard_map/while/body/eval_jaxpr/all_to_all | solution.py:44
  192.9 4.9 %collective-permute-start = (f32[2,2,192]{2,1,0:T(2,128)S(1)}, f32[2,2,192]{2,1,0:T(2,128)S(1)}, u32[]{:S(2)}, u32[]{:S(2)}) collective-permute-start(f32[2,2,192]{2,1,0:T(2,128)S(1)} %get-tuple-element.126), channel_id=1, source_target_pairs={{0,32},{32,64},{64,96},{96,128},{128,160},{160,192},{192,224},{1,3... | collective-permute-start | bytes 9224 | tf_op jit(solution)/shard_map/while/body/eval_jaxpr/ppermute | solution.py:39
  198.5 16.1 %all-to-all-start = ((bf16[32,2,2,192]{3,2,1,0:T(2,128)(2,1)}), bf16[32,2,2,192]{3,2,1,0:T(2,128)(2,1)S(1)}, u32[]{:S(2)}, u32[]{:S(2)}) async-start(bf16[32,2,2,192]{3,2,1,0:T(2,128)(2,1)} %broadcast_in_dim.19), calls=%async_computation | async-start | bytes 131072 | tf_op jit(solution)/shard_map/while/body/eval_jaxpr/all_to_all | solution.py:44
  218.1 4.9 %collective-permute-start = (f32[2,2,192]{2,1,0:T(2,128)S(1)}, f32[2,2,192]{2,1,0:T(2,128)S(1)}, u32[]{:S(2)}, u32[]{:S(2)}) collective-permute-start(f32[2,2,192]{2,1,0:T(2,128)S(1)} %get-tuple-element.126), channel_id=1, source_target_pairs={{0,32},{32,64},{64,96},{96,128},{128,160},{160,192},{192,224},{1,3... | collective-permute-start | bytes 9224 | tf_op jit(solution)/shard_map/while/body/eval_jaxpr/ppermute | solution.py:39
  223.7 16.1 %all-to-all-start = ((bf16[32,2,2,192]{3,2,1,0:T(2,128)(2,1)}), bf16[32,2,2,192]{3,2,1,0:T(2,128)(2,1)S(1)}, u32[]{:S(2)}, u32[]{:S(2)}) async-start(bf16[32,2,2,192]{3,2,1,0:T(2,128)(2,1)} %broadcast_in_dim.19), calls=%async_computation | async-start | bytes 131072 | tf_op jit(solution)/shard_map/while/body/eval_jaxpr/all_to_all | solution.py:44
  243.4 4.9 %collective-permute-start = (f32[2,2,192]{2,1,0:T(2,128)S(1)}, f32[2,2,192]{2,1,0:T(2,128)S(1)}, u32[]{:S(2)}, u32[]{:S(2)}) collective-permute-start(f32[2,2,192]{2,1,0:T(2,128)S(1)} %get-tuple-element.126), channel_id=1, source_target_pairs={{0,32},{32,64},{64,96},{96,128},{128,160},{160,192},{192,224},{1,3... | collective-permute-start | bytes 9224 | tf_op jit(solution)/shard_map/while/body/eval_jaxpr/ppermute | solution.py:39
  249.0 16.1 %all-to-all-start = ((bf16[32,2,2,192]{3,2,1,0:T(2,128)(2,1)}), bf16[32,2,2,192]{3,2,1,0:T(2,128)(2,1)S(1)}, u32[]{:S(2)}, u32[]{:S(2)}) async-start(bf16[32,2,2,192]{3,2,1,0:T(2,128)(2,1)} %broadcast_in_dim.19), calls=%async_computation | async-start | bytes 131072 | tf_op jit(solution)/shard_map/while/body/eval_jaxpr/all_to_all | solution.py:44
  268.7 4.9 %collective-permute-start = (f32[2,2,192]{2,1,0:T(2,128)S(1)}, f32[2,2,192]{2,1,0:T(2,128)S(1)}, u32[]{:S(2)}, u32[]{:S(2)}) collective-permute-start(f32[2,2,192]{2,1,0:T(2,128)S(1)} %get-tuple-element.126), channel_id=1, source_target_pairs={{0,32},{32,64},{64,96},{96,128},{128,160},{160,192},{192,224},{1,3... | collective-permute-start | bytes 9224 | tf_op jit(solution)/shard_map/while/body/eval_jaxpr/ppermute | solution.py:39
  274.3 16.1 %all-to-all-start = ((bf16[32,2,2,192]{3,2,1,0:T(2,128)(2,1)}), bf16[32,2,2,192]{3,2,1,0:T(2,128)(2,1)S(1)}, u32[]{:S(2)}, u32[]{:S(2)}) async-start(bf16[32,2,2,192]{3,2,1,0:T(2,128)(2,1)} %broadcast_in_dim.19), calls=%async_computation | async-start | bytes 131072 | tf_op jit(solution)/shard_map/while/body/eval_jaxpr/all_to_all | solution.py:44
  (17 other events, 30.7 us)
where the time goes:
time: 307 us; the launch traced here: 306 us
  waiting for transfers between devices  126 us (41%)
  starting transfers between devices  107 us (35%)
  matrix products  26.7 us (9%)
  local copies, waits for them, and re-layouts  23 us (7%)
  other arithmetic  21.4 us (7%)
    all_to_all x8, waiting for transfers between devices, sent_to_all(): lax.all_to_all(jnp.broadcast_to(array[None], (length, *array.shape)), axi...  98.2 us
    all_to_all x8, starting transfers between devices, sent_to_all(): lax.all_to_all(jnp.broadcast_to(array[None], (length, *array.shape)), axi...  46.1 us
    ppermute x6, starting transfers between devices, padded_2(): lax.ppermute(last, axis, up)  34.3 us
    ppermute x8, waiting for transfers between devices, from_behind(): return lax.ppermute(block, axis, route)  23.3 us
    dot_general x8, matrix products, fold_into(): jnp.einsum('rc,ksc->ksr', matrix_im, shard_piece, preferred_element_type=...  20.5 us
    ppermute x8, starting transfers between devices, from_behind(): return lax.ppermute(block, axis, route)  16 us
    ppermute x6, starting transfers between devices, padded_2(): lax.ppermute(first, axis, [(b, a) for a, b in up])  10.8 us
    dot_general x8, matrix products, fold_into(): jnp.einsum('rc,ksc->ksr', matrix_re, shard_piece, preferred_element_type=...  6.21 us
  transfers between devices with their start and end apart: 28, of which 18 were waited for; matrix products, arithmetic and copies ran while one was open for 15% of the time, Pallas kernels for 0%

commit v1 on v0

v1 whole, which is shorter than its diff:
```python
import functools

import jax
import jax.numpy as jnp
from jax import lax
from jax.experimental import pallas as pl
from jax.experimental.pallas import tpu as pltpu
from jax.sharding import PartitionSpec as P

QY = 16
PX = 4
SWEEPS = 4
HALO = SWEEPS - 1
ROWS = 8
LANES = 256

damping = 0.8
absorb = 0.5
coupling = 0.45

VMEM = pltpu.VMEM
f32 = jnp.float32
bf16 = jnp.bfloat16


def limit(mebibytes):
    return pltpu.CompilerParams(vmem_limit_bytes=mebibytes << 20)


def membership(fine, coarse):
    row = lax.broadcasted_iota(jnp.int32, (fine, coarse), 0)
    col = lax.broadcasted_iota(jnp.int32, (fine, coarse), 1)
    return jnp.where((row >= col * PX) & (row < col * PX + PX), 1.0, 0.0).astype(bf16)


def exact_dot(values, selection, contract):
    first = values.astype(bf16)
    rest = values - first.astype(f32)
    second = rest.astype(bf16)
    third = (rest - second.astype(f32)).astype(bf16)
    total = None
    for piece in (third, second, first):
        part = lax.dot_general(piece, selection, (((1,), (contract,)), ((), ())), preferred_element_type=f32)
        total = part if total is None else total + part
    return total


def restrict_kernel(residual, rhs, spread):
    shots, _, depth, height, width = residual.shape
    strips, across = height // QY, width // PX
    sums = []
    for strip in range(strips):
        for part in range(2):
            for shot in range(shots):
                total = residual[shot, part, 0, strip * QY : (strip + 1) * QY, :]
                for plane in range(1, depth):
                    total = total + residual[shot, part, plane, strip * QY : (strip + 1) * QY, :]
                sums.append(jnp.sum(total, axis=0, keepdims=True))
    means = exact_dot(jnp.concatenate(sums, axis=0), membership(width, across), 0) * (1.0 / (depth * QY * PX))
    lines = 2 * shots
    for strip in range(strips):
        rhs[:, strip * across : (strip + 1) * across] = means[strip * lines : (strip + 1) * lines, :]
    vector = rhs[...].astype(bf16)
    for device in range(spread.shape[0]):
        spread[device] = vector


def restrict(residual, devices):
    shots, _, _, height, width = residual.shape
    cells = (height // QY) * (width // PX)
    return pl.pallas_call(
        restrict_kernel,
        out_shape=(
            jax.ShapeDtypeStruct((2 * shots, cells), f32),
            jax.ShapeDtypeStruct((devices, 2 * shots, cells), bf16),
        ),
        compiler_params=limit(8),
        name="restrict",
    )(residual)


def layer_kernel(step, here, matrix, gathered, next_rhs, kept_before, kept, spread, held, vector, arrived):
    devices, lines, cells = gathered.shape
    shots = lines // 2
    pieces = arrived.shape[0]
    across = matrix.shape[2] // pieces
    columns = [slice(piece * across, (piece + 1) * across) for piece in range(pieces)]
    copies = [
        pltpu.make_async_copy(matrix.at[:, :, columns[piece]], held.at[:, :, columns[piece]], arrived.at[piece])
        for piece in range(pieces)
    ]
    for copy in copies:
        copy.start()
    for device in range(devices):
        vector[:, device * cells : (device + 1) * cells] = gathered[device]
    by_re = by_im = None
    for piece in range(pieces):
        part = vector[:, columns[piece]]
        copies[piece].wait()
        products = [
            lax.dot_general(part, held[side, :, columns[piece]], (((1,), (1,)), ((), ())), preferred_element_type=f32)
            for side in range(2)
        ]
        by_re = products[0] if by_re is None else by_re + products[0]
        by_im = products[1] if by_im is None else by_im + products[1]
    solved = jnp.concatenate([by_re[:shots] - by_im[shots:], by_re[shots:] + by_im[:shots]], axis=0)
    kept[...] = jnp.where(here[0] == step, solved, kept_before[...])
    out = (next_rhs[...] + coupling * solved).astype(bf16)
    for device in range(devices):
        spread[device] = out


def solve_layer(step, here, matrix, gathered, next_rhs, kept):
    devices, lines, cells = gathered.shape
    pieces = 6
    return pl.pallas_call(
        functools.partial(layer_kernel, step),
        out_shape=(
            jax.ShapeDtypeStruct((lines, cells), f32),
            jax.ShapeDtypeStruct((devices, lines, cells), bf16),
        ),
        in_specs=[pl.BlockSpec(memory_space=pltpu.SMEM), pl.BlockSpec(memory_space=pltpu.HBM)]
        + [pl.BlockSpec(memory_space=VMEM)] * 3,
        scratch_shapes=[
            pltpu.VMEM(matrix.shape, bf16),
            pltpu.VMEM((lines, devices * cells), bf16),
            pltpu.SemaphoreType.DMA((pieces,)),
        ],
        compiler_params=limit(8),
        cost_estimate=pl.CostEstimate(flops=4 * matrix.size, bytes_accessed=2 * matrix.size, transcendentals=0),
        name="solve_layer",
    )(here, matrix, gathered, next_rhs, kept)


def smooth_kernel(inside, residual, wavenumber, row_low, row_high, deep_low, deep_high, smoothed, gain, source, first, second):
    shots, _, depth, height, width = residual.shape
    top = ROWS
    start = top + ROWS
    total = height + 2 * ROWS
    planes = depth + 2 * HALO
    rest = LANES - width
    sides = (
        (0, HALO, deep_low, inside[0]),
        (HALO + depth, HALO, deep_high, inside[1]),
    )

    def gains(values, factor):
        real_part = 6.0 - values
        imag_part = -absorb * values
        scale = damping * factor / (real_part * real_part + imag_part * imag_part)
        return real_part * scale, -imag_part * scale

    def put_gain(plane, row, values, factor):
        real_part, imag_part = gains(values, factor)
        rows = values.shape[0]
        gain[0, plane, pl.ds(row, rows), 0:width] = real_part
        gain[1, plane, pl.ds(row, rows), 0:width] = imag_part

    blank = jnp.zeros((total, rest), f32)

    def clear(plane, _):
        for part in range(2):
            gain[part, plane, top : top + total, width:LANES] = blank
            source[part, plane, top : top + total, width:LANES] = blank
        return _

    lax.fori_loop(0, planes, clear, 0)

    def own_gain(plane, _):
        for row in range(0, height, 16):
            put_gain(HALO + plane, start + row, wavenumber[plane, row : row + 16, :], 1.0)
        put_gain(HALO + plane, top, row_low[2 * shots, plane].astype(f32), inside[2])
        put_gain(HALO + plane, start + height, row_high[2 * shots, plane].astype(f32), inside[3])
        return _

    lax.fori_loop(0, depth, own_gain, 0)
    for base, count, ghost, factor in sides:
        for plane in range(count):
            for row in range(0, total, 16):
                values = ghost[2 * shots, plane, row : row + 16, :].astype(f32)
                put_gain(base + plane, top + row, values, factor)
    for base, count, _, _ in sides:
        for plane in range(count):
            for part in range(2):
                low = gain[part, base + plane, top:start, :]
                gain[part, base + plane, top:start, :] = low * inside[2]
                high = gain[part, base + plane, start + height : start + height + ROWS, :]
                gain[part, base + plane, start + height : start + height + ROWS, :] = high * inside[3]

    def sweep(old, new, plane, row, rows, store):
        here = pl.ds(row, rows)
        terms = []
        for part in range(2):
            centre = old[part, plane, here, :]
            beside = old[part, plane - 1, here, :] + old[part, plane + 1, here, :]
            beside = beside + old[part, plane, pl.ds(row - 1, rows), :] + old[part, plane, pl.ds(row + 1, rows), :]
            beside = beside + pltpu.roll(centre, 1, 1) + pltpu.roll(centre, LANES - 1, 1)
            terms.append((centre, source[part, plane, here, :] + beside))
        (centre_re, sum_re), (centre_im, sum_im) = terms
        gain_re, gain_im = gain[0, plane, here, :], gain[1, plane, here, :]
        store(0, (1.0 - damping) * centre_re + (gain_re * sum_re - gain_im * sum_im))
        store(1, (1.0 - damping) * centre_im + (gain_re * sum_im + gain_im * sum_re))

    for shot in range(shots):

        def own_source(plane, _):
            for part in range(2):
                source[part, HALO + plane, start : start + height, 0:width] = residual[shot, part, plane]
                source[part, HALO + plane, top:start, 0:width] = row_low[2 * shot + part, plane].astype(f32)
                source[part, HALO + plane, start + height : start + height + ROWS, 0:width] = row_high[
                    2 * shot + part, plane
                ].astype(f32)
            return _

        lax.fori_loop(0, depth, own_source, 0)
        for base, count, ghost, _ in sides:
            for plane in range(count):
                for part in range(2):
                    source[part, base + plane, top : top + total, 0:width] = ghost[2 * shot + part, plane].astype(f32)

        def begin(plane, _):
            for row in range(top, top + total, 16):
                here = pl.ds(row, 16)
                gain_re, gain_im = gain[0, plane, here, :], gain[1, plane, here, :]
                source_re, source_im = source[0, plane, here, :], source[1, plane, here, :]
                first[0, plane, here, :] = gain_re * source_re - gain_im * source_im
                first[1, plane, here, :] = gain_re * source_im + gain_im * source_re
            return _

        lax.fori_loop(0, planes, begin, 0)
        old, new = first, second
        for counter in range(1, SWEEPS):
            last = counter == SWEEPS - 1

            def one_plane(plane, _, old=old, new=new, last=last, shot=shot):
                low, high = (start, start + height) if last else (top, top + total)
                for row in range(low, high, 16):

                    def store(part, value, row=row):
                        if last:
                            smoothed[shot, part, plane - HALO, row - start : row - start + 16, :] = value[:, :width]
                        else:
                            new[part, plane, pl.ds(row, 16), :] = value

                    sweep(old, new, plane, row, 16, store)
                return _

            lax.fori_loop(counter, planes - counter, one_plane, 0)
            old, new = new, old


def smooth(inside, residual, wavenumber, row_low, row_high, deep_low, deep_high):
    shots, _, depth, height, width = residual.shape
    scratch = pltpu.VMEM((2, depth + 2 * HALO, height + 4 * ROWS, LANES), f32)
    return pl.pallas_call(
        smooth_kernel,
        out_shape=jax.ShapeDtypeStruct(residual.shape, f32),
        in_specs=[pl.BlockSpec(memory_space=pltpu.SMEM)] + [pl.BlockSpec(memory_space=VMEM)] * 6,
        scratch_shapes=[scratch] * 4,
        cost_estimate=pl.CostEstimate(flops=300 * residual.size, bytes_accessed=12 * residual.size, transcendentals=0),
        compiler_params=limit(28),
        name="smooth",
    )(inside, residual, wavenumber, row_low, row_high, deep_low, deep_high)


def lift_kernel(smoothed, coarse, out):
    shots, _, depth, height, width = smoothed.shape
    strips, across = height // QY, width // PX
    pick = membership(width, across)
    lines = [coarse[:, strip * across : (strip + 1) * across] for strip in range(strips)]
    wide = exact_dot(jnp.concatenate(lines, axis=0), pick, 1)
    for part in range(2):
        for shot in range(shots):
            for strip in range(strips):
                at = strip * 2 * shots + part * shots + shot
                value = jnp.broadcast_to(wide[at : at + 1, :], (QY, width))
                rows = slice(strip * QY, (strip + 1) * QY)
                for plane in range(depth):
                    out[shot, part, plane, rows, :] = smoothed[shot, part, plane, rows, :] + value


def lift(smoothed, coarse):
    return pl.pallas_call(
        lift_kernel,
        out_shape=jax.ShapeDtypeStruct(smoothed.shape, f32),
        compiler_params=limit(8),
        name="lift",
    )(smoothed, coarse)


def both_ways(low_block, high_block, axis):
    size = lax.axis_size(axis)
    up = [(i, i + 1) for i in range(size - 1)]
    return lax.ppermute(high_block, axis, up), lax.ppermute(low_block, axis, [(b, a) for a, b in up])


def on_device(residual, wavenumber, inverse):
    shots, _, depth, height, width = residual.shape
    layers, devices = lax.axis_size("layer"), lax.axis_size("row")
    layer, row = lax.axis_index("layer"), lax.axis_index("row")
    here = jnp.reshape(layer, (1,)).astype(jnp.int32)
    inside = jnp.stack([layer > 0, layer < layers - 1, row > 0, row < devices - 1]).astype(f32)

    with jax.named_scope("restrict"):
        rhs, spread = restrict(residual, devices)
    matrix = pltpu.with_memory_space_constraint(inverse[:, 0], pltpu.HBM)

    with jax.named_scope("halo"):
        fields = jnp.concatenate([residual.reshape(2 * shots, depth, height, width), wavenumber[None]]).astype(bf16)
        row_low, row_high = both_ways(fields[:, :, :ROWS], fields[:, :, height - ROWS :], "row")

        def with_rows(planes):
            return jnp.concatenate([row_low[:, planes], fields[:, planes], row_high[:, planes]], axis=2)

        deep_low, deep_high = both_ways(
            with_rows(slice(0, HALO)), with_rows(slice(depth - HALO, depth)), "layer"
        )
        next_rhs = lax.ppermute(rhs, "layer", [(i + 1, i) for i in range(layers - 1)])
    with jax.named_scope("smooth"):
        smoothed = smooth(inside, residual, wavenumber, row_low, row_high, deep_low, deep_high)

    kept = rhs
    for step in range(layers):
        with jax.named_scope(f"chain_{step}"):
            gathered = lax.all_to_all(spread, "row", 0, 0, tiled=True)
            if step:
                gathered = lax.ppermute(gathered, "layer", hop(step - 1, layers))
            kept, spread = solve_layer(step, here, matrix, gathered, next_rhs, kept)
    with jax.named_scope("lift"):
        return lift(smoothed, kept)


def hop(source, layers):
    if source % 2 == 0:
        return [(i, i ^ 1) for i in range(layers)]
    pairs = [(i, i + 1) for i in range(1, layers - 1, 2)]
    return pairs + [(b, a) for a, b in pairs] + [(0, 0), (layers - 1, layers - 1)]


def solution(mesh):
    return jax.shard_map(
        on_device,
        mesh=mesh,
        in_specs=(
            P(None, None, "layer", "row", None),
            P("layer", "row", None),
            P(None, "layer", "row", None),
        ),
        out_specs=P(None, None, "layer", "row", None),
        check_vma=False,
    )
```

time: 307 us -> 218 us (0.71)
  waiting for transfers between devices: 126 us -> 62.1 us
  starting transfers between devices: 107 us -> 53.8 us
  blocking collectives: 0 us -> 51.2 us
  Pallas kernels: 0 us -> 41.1 us
  matrix products: 26.7 us -> 0 us
  local copies, waits for them, and re-layouts: 23 us -> 2.53 us
  other arithmetic: 21.4 us -> 5.32 us
    all_to_all x0 -> x3, blocking collectives: none -> 51.2 us  [on_device(): gathered = lax.all_to_all(spread, 'row', 0, 0, tiled=True)]
    all_to_all x8 -> x5, waiting for transfers between devices: 98.2 us -> 48.3 us  [on_device(): gathered = lax.all_to_all(spread, 'row', 0, 0, tiled=True)]
    ppermute x20 -> x12, starting transfers between devices: 61.1 us -> 16.2 us  [the longest x7 5.92 us: on_device(): gathered = lax.ppermute(gathered, 'layer', hop(step - 1, layers))]
    pallas_call x0 -> x11, Pallas kernels: none -> 41.1 us  [the longest x8 25.7 us: solve_layer(): pl.pallas_call(functools.partial(layer_kernel, step), out_shape=(jax.Shap...]
    dot_general x16 -> x0, matrix products: 26.7 us -> none  [the longest x8 20.5 us: fold_into(): jnp.einsum('rc,ksc->ksr', matrix_im, shard_piece, preferred_element_type=...]
    ppermute x20 -> x12, waiting for transfers between devices: 28.2 us -> 13.8 us  [the longest x7 12.5 us: on_device(): gathered = lax.ppermute(gathered, 'layer', hop(step - 1, layers))]
    broadcast_in_dim x14 -> x0, local copies, waits for them, and re-layouts: 9.94 us -> none  [the longest x8 5.35 us: sent_to_all(): jnp.broadcast_to(array[None], (length, *array.shape))]
    all_to_all x8 -> x5, starting transfers between devices: 46.1 us -> 37.6 us  [on_device(): gathered = lax.all_to_all(spread, 'row', 0, 0, tiled=True)]
  transfers between devices with their start and end apart: 28 -> 17, of which waited for: 18 -> 11; matrix products, arithmetic and copies ran while one was open for 15% -> 2% of each run, Pallas kernels for 0% -> 10%
where the time goes in v1:
time: 218 us; the launch traced here: 216 us
  waiting for transfers between devices  62.1 us (28%)
  starting transfers between devices  53.8 us (25%)
  blocking collectives  51.2 us (23%)
  Pallas kernels  41.1 us (19%)
  other arithmetic  5.32 us (2%)
  local copies, waits for them, and re-layouts  2.53 us (1%)
    all_to_all x3, blocking collectives, on_device(): gathered = lax.all_to_all(spread, 'row', 0, 0, tiled=True)  51.2 us
    all_to_all x5, waiting for transfers between devices, on_device(): gathered = lax.all_to_all(spread, 'row', 0, 0, tiled=True)  48.3 us
    all_to_all x5, starting transfers between devices, on_device(): gathered = lax.all_to_all(spread, 'row', 0, 0, tiled=True)  37.6 us
    pallas_call x8, Pallas kernels, solve_layer(): pl.pallas_call(functools.partial(layer_kernel, step), out_shape=(jax.Shap...  25.7 us
    pallas_call x1, Pallas kernels, smooth(): pl.pallas_call(smooth_kernel, out_shape=jax.ShapeDtypeStruct(residual.sha...  12.6 us
    ppermute x7, waiting for transfers between devices, on_device(): gathered = lax.ppermute(gathered, 'layer', hop(step - 1, layers))  12.5 us
    ppermute x7, starting transfers between devices, on_device(): gathered = lax.ppermute(gathered, 'layer', hop(step - 1, layers))  5.92 us
    ppermute x2, starting transfers between devices, both_ways(): lax.ppermute(high_block, axis, up)  5.06 us
  transfers between devices with their start and end apart: 17, of which 11 were waited for; matrix products, arithmetic and copies ran while one was open for 2% of the time, Pallas kernels for 10%

profile of v1, /device:TPU:32, one launch (start us, length us, event | category | flops | bytes accessed | tf_op | source)
XLA Modules:
  0.0 216.3 jit_solution(12466544741341171029)
XLA Ops:
  2.6 13.0 %all-to-all-start = ((bf16[32,4,192]{2,1,0:T(4,128)(2,1)}), bf16[32,4,192]{2,1,0:T(4,128)(2,1)S(1)}, u32[]{:S(2)}, u32[]{:S(2)}) async-start(bf16[32,4,192]{2,1,0:T(4,128)(2,1)} %get-tuple-element.22), calls=%async_computation | async-start | bytes 131072 | tf_op jit(solution)/shard_map/chain_0/all_to_all | solution.py:325
  15.7 2.1 collective-permute-start.4
  19.1 8.9 %all-to-all-done.gathered = bf16[32,4,192]{2,1,0:T(4,128)(2,1)S(1)} async-done(((bf16[32,4,192]{2,1,0:T(4,128)(2,1)}), bf16[32,4,192]{2,1,0:T(4,128)(2,1)S(1)}, u32[]{:S(2)}, u32[]{:S(2)}) %all-to-all-start) | async-done | bytes 49184 | tf_op jit(solution)/shard_map/chain_0/all_to_all | solution.py:325
  27.9 2.8 %solve_layer.8 = (f32[4,192]{1,0:T(4,128)S(1)}, bf16[32,4,192]{2,1,0:T(4,128)(2,1)S(1)}) custom-call(s32[1]{0:T(128)} %bitcast.6.here, bf16[2,192,6144]{2,1,0:T(8,128)(2,1)} %bitcast.9, bf16[32,4,192]{2,1,0:T(4,128)(2,1)S(1)} %all-to-all-done.gathered, f32[4,192]{1,0:T(4,128)S(1)} %collective-permute-done.4.next_rhs, f32[4,192]{1,0:T(4,128)S(1)} %get-tuple-element.23.kept_before), custom_call_target="tpu_custom_call" | custom-call | flops 9437184 | bytes 4718592 | tf_op jit(solution)/shard_map/chain_0/solve_layer/pallas_call | solution.py:116
  30.7 15.8 %all_to_all.40 = bf16[32,4,192]{2,1,0:T(4,128)(2,1)S(1)} all-to-all(bf16[32,4,192]{2,1,0:T(4,128)(2,1)S(1)} %get-tuple-element.24), channel_id=1, replica_groups=mesh['layer'=8,'row'=32] {'row'}, dimensions={0} | all-to-all | bytes 98304 | tf_op jit(solution)/shard_map/chain_1/all_to_all | solution.py:325
  47.8 3.0 %solve_layer.9 = (f32[4,192]{1,0:T(4,128)S(1)}, bf16[32,4,192]{2,1,0:T(4,128)(2,1)S(1)}) custom-call(s32[1]{0:T(128)} %bitcast.6.here, bf16[2,192,6144]{2,1,0:T(8,128)(2,1)} %bitcast.10, bf16[32,4,192]{2,1,0:T(4,128)(2,1)S(1)} %collective-permute-done.5.gathered, f32[4,192]{1,0:T(4,128)S(1)} %collective-permute-done.4.next_rhs, ...), custom_call_target="tpu_custom_call" | custom-call | flops 9437184 | bytes 4718592 | tf_op jit(solution)/shard_map/chain_1/solve_layer/pallas_call | solution.py:116
  50.8 16.0 %all_to_all.41 = bf16[32,4,192]{2,1,0:T(4,128)(2,1)S(1)} all-to-all(bf16[32,4,192]{2,1,0:T(4,128)(2,1)S(1)} %get-tuple-element.26), channel_id=1, replica_groups=mesh['layer'=8,'row'=32] {'row'}, dimensions={0} | all-to-all | bytes 98304 | tf_op jit(solution)/shard_map/chain_2/all_to_all | solution.py:325
  66.7 1.9 collective-permute-start.6
  69.8 2.5 %collective-permute-done.6.gathered = bf16[32,4,192]{2,1,0:T(4,128)(2,1)S(1)} collective-permute-done((bf16[32,4,192]{2,1,0:T(4,128)(2,1)S(1)}, bf16[32,4,192]{2,1,0:T(4,128)(2,1)S(1)}, u32[]{:S(2)}, u32[]{:S(2)}) %collective-permute-start.6) | collective-permute-done | bytes 49184 | tf_op jit(solution)/shard_map/chain_2/ppermute | solution.py:327
  72.3 3.4 %solve_layer.10 = (f32[4,192]{1,0:T(4,128)S(1)}, bf16[32,4,192]{2,1,0:T(4,128)(2,1)}) custom-call(s32[1]{0:T(128)} %bitcast.6.here, bf16[2,192,6144]{2,1,0:T(8,128)(2,1)} %bitcast.11, bf16[32,4,192]{2,1,0:T(4,128)(2,1)S(1)} %collective-permute-done.6.gathered, f32[4,192]{1,0:T(4,128)S(1)} %collective-permute-done.4.next_rhs, ...), custom_call_target="tpu_custom_call" | custom-call | flops 9437184 | bytes 4718592 | tf_op jit(solution)/shard_map/chain_2/solve_layer/pallas_call | solution.py:116
  75.7 4.6 %all-to-all-start.3 = ((bf16[32,4,192]{2,1,0:T(4,128)(2,1)}), bf16[32,4,192]{2,1,0:T(4,128)(2,1)}, u32[]{:S(2)}, u32[]{:S(2)}) async-start(bf16[32,4,192]{2,1,0:T(4,128)(2,1)} %get-tuple-element.28), calls=%async_computation.3 | async-start | bytes 131072 | tf_op jit(solution)/shard_map/chain_3/all_to_all | solution.py:325
  83.3 9.4 %all-to-all-done.3 = bf16[32,4,192]{2,1,0:T(4,128)(2,1)} async-done(((bf16[32,4,192]{2,1,0:T(4,128)(2,1)}), bf16[32,4,192]{2,1,0:T(4,128)(2,1)}, u32[]{:S(2)}, u32[]{:S(2)}) %all-to-all-start.3) | async-done | bytes 49184 | tf_op jit(solution)/shard_map/chain_3/all_to_all | solution.py:325
  92.7 2.7 %collective-permute-start = (bf16[5,8,8,192]{3,2,1,0:T(8,128)(2,1)S(1)}, bf16[5,8,8,192]{3,2,1,0:T(8,128)(2,1)S(1)}, u32[]{:S(2)}, u32[]{:S(2)}) collective-permute-start(bf16[5,8,8,192]{3,2,1,0:T(8,128)(2,1)S(1)} %get-tuple-element.42), channel_id=1, source_target_pairs={{0,1},{1,2},{2,3},{3,4},{4,5},{5,6},{6,7},{7,8},{8,9},{9,10},{10,1... | collective-permute-start | bytes 368648 | tf_op jit(solution)/shard_map/halo/ppermute | solution.py:294
  95.3 3.4 %solve_layer.11 = (f32[4,192]{1,0:T(4,128)S(1)}, bf16[32,4,192]{2,1,0:T(4,128)(2,1)}) custom-call(s32[1]{0:T(128)} %bitcast.6.here, bf16[2,192,6144]{2,1,0:T(8,128)(2,1)} %bitcast.12, bf16[32,4,192]{2,1,0:T(4,128)(2,1)S(1)} %collective-permute-done.7.gathered, f32[4,192]{1,0:T(4,128)S(1)} %collective-permute-done.4.next_rhs, ...), custom_call_target="tpu_custom_call" | custom-call | flops 9437184 | bytes 4718592 | tf_op jit(solution)/shard_map/chain_3/solve_layer/pallas_call | solution.py:116
  98.8 11.5 %all-to-all-start.4 = ((bf16[32,4,192]{2,1,0:T(4,128)(2,1)}), bf16[32,4,192]{2,1,0:T(4,128)(2,1)}, u32[]{:S(2)}, u32[]{:S(2)}) async-start(bf16[32,4,192]{2,1,0:T(4,128)(2,1)} %get-tuple-element.30), calls=%async_computation.4 | async-start | bytes 131072 | tf_op jit(solution)/shard_map/chain_4/all_to_all | solution.py:325
  110.3 12.3 %all-to-all-done.4 = bf16[32,4,192]{2,1,0:T(4,128)(2,1)} async-done(((bf16[32,4,192]{2,1,0:T(4,128)(2,1)}), bf16[32,4,192]{2,1,0:T(4,128)(2,1)}, u32[]{:S(2)}, u32[]{:S(2)}) %all-to-all-start.4) | async-done | bytes 49184 | tf_op jit(solution)/shard_map/chain_4/all_to_all | solution.py:325
  122.6 1.9 collective-permute-start.8
  124.5 3.8 %collective-permute-done.8.gathered = bf16[32,4,192]{2,1,0:T(4,128)(2,1)S(1)} collective-permute-done((bf16[32,4,192]{2,1,0:T(4,128)(2,1)}, bf16[32,4,192]{2,1,0:T(4,128)(2,1)S(1)}, u32[]{:S(2)}, u32[]{:S(2)}) %collective-permute-start.8) | collective-permute-done | bytes 49184 | tf_op jit(solution)/shard_map/chain_4/ppermute | solution.py:327
  128.4 3.4 %solve_layer.12 = (f32[4,192]{1,0:T(4,128)S(1)}, bf16[32,4,192]{2,1,0:T(4,128)(2,1)}) custom-call(s32[1]{0:T(128)} %bitcast.6.here, bf16[2,192,6144]{2,1,0:T(8,128)(2,1)} %bitcast.13, bf16[32,4,192]{2,1,0:T(4,128)(2,1)S(1)} %collective-permute-done.8.gathered, f32[4,192]{1,0:T(4,128)S(1)} %collective-permute-done.4.next_rhs, ...), custom_call_target="tpu_custom_call" | custom-call | flops 9437184 | bytes 4718592 | tf_op jit(solution)/shard_map/chain_4/solve_layer/pallas_call | solution.py:116
  131.8 4.6 %all-to-all-start.5 = ((bf16[32,4,192]{2,1,0:T(4,128)(2,1)}), bf16[32,4,192]{2,1,0:T(4,128)(2,1)}, u32[]{:S(2)}, u32[]{:S(2)}) async-start(bf16[32,4,192]{2,1,0:T(4,128)(2,1)} %get-tuple-element.32), calls=%async_computation.5 | async-start | bytes 131072 | tf_op jit(solution)/shard_map/chain_5/all_to_all | solution.py:325
  136.4 2.4 %fusion.1 = (bf16[5,3,80,192]{3,2,1,0:T(8,128)(2,1)}, bf16[5,3,80,192]{3,2,1,0:T(8,128)(2,1)}) fusion(bf16[1,8,64,192]{3,2,1,0:T(8,128)(2,1)S(1)} %convert_bitcast_fusion, bf16[4,8,64,192]{3,2,1,0:T(8,128)(2,1)} %bitcast.18, bf16[5,3,8,192]{3,2,1,0:T(8,128)(2,1)S(1)} %get-tuple-element.45, bf16[5,3,8,192]{3,2,1,0:T(8,128)(2,1)S(1)} %get-tuple-element.43, ...), kind=kLoop, calls=%fused_computation.2 | loop fusion | flops 3686400 | bytes 2088960 | tf_op jit(solution)/shard_map/halo/concatenate | solution.py:313
  140.7 2.4 %collective-permute-start.2 = (bf16[5,3,80,192]{3,2,1,0:T(8,128)(2,1)}, bf16[5,3,80,192]{3,2,1,0:T(8,128)(2,1)}, u32[]{:S(2)}, u32[]{:S(2)}) collective-permute-start(bf16[5,3,80,192]{3,2,1,0:T(8,128)(2,1)} %get-tuple-element.40), channel_id=1, source_target_pairs={{0,32},{32,64},{64,96},{96,128},{128,160},{160,192},{192,224},{1,3... | collective-permute-start | bytes 1382408 | tf_op jit(solution)/shard_map/halo/ppermute | solution.py:294
  143.1 5.5 %all-to-all-done.5 = bf16[32,4,192]{2,1,0:T(4,128)(2,1)} async-done(((bf16[32,4,192]{2,1,0:T(4,128)(2,1)}), bf16[32,4,192]{2,1,0:T(4,128)(2,1)}, u32[]{:S(2)}, u32[]{:S(2)}) %all-to-all-start.5) | async-done | bytes 49184 | tf_op jit(solution)/shard_map/chain_5/all_to_all | solution.py:325
  150.1 2.8 %solve_layer.13 = (f32[4,192]{1,0:T(4,128)S(1)}, bf16[32,4,192]{2,1,0:T(4,128)(2,1)S(1)}) custom-call(s32[1]{0:T(128)} %bitcast.6.here, bf16[2,192,6144]{2,1,0:T(8,128)(2,1)} %bitcast.14, bf16[32,4,192]{2,1,0:T(4,128)(2,1)S(1)} %collective-permute-done.9.gathered, f32[4,192]{1,0:T(4,128)S(1)} %collective-permute-done.4.next_rhs, ...), custom_call_target="tpu_custom_call" | custom-call | flops 9437184 | bytes 4718592 | tf_op jit(solution)/shard_map/chain_5/solve_layer/pallas_call | solution.py:116
  152.9 19.4 %all_to_all.42 = bf16[32,4,192]{2,1,0:T(4,128)(2,1)S(1)} all-to-all(bf16[32,4,192]{2,1,0:T(4,128)(2,1)S(1)} %get-tuple-element.34), channel_id=1, replica_groups=mesh['layer'=8,'row'=32] {'row'}, dimensions={0} | all-to-all | bytes 98304 | tf_op jit(solution)/shard_map/chain_6/all_to_all | solution.py:325
  172.3 2.1 collective-permute-start.10
  174.4 3.5 %collective-permute-done.10.gathered = bf16[32,4,192]{2,1,0:T(4,128)(2,1)S(1)} collective-permute-done((bf16[32,4,192]{2,1,0:T(4,128)(2,1)S(1)}, bf16[32,4,192]{2,1,0:T(4,128)(2,1)S(1)}, u32[]{:S(2)}, u32[]{:S(2)}) %collective-permute-start.10) | collective-permute-done | bytes 49184 | tf_op jit(solution)/shard_map/chain_6/ppermute | solution.py:327
  177.9 3.4 %solve_layer.14 = (f32[4,192]{1,0:T(4,128)S(1)}, bf16[32,4,192]{2,1,0:T(4,128)(2,1)}) custom-call(s32[1]{0:T(128)} %bitcast.6.here, bf16[2,192,6144]{2,1,0:T(8,128)(2,1)} %bitcast.15, bf16[32,4,192]{2,1,0:T(4,128)(2,1)S(1)} %collective-permute-done.10.gathered, f32[4,192]{1,0:T(4,128)S(1)} %collective-permute-done.4.next_rhs, ...), custom_call_target="tpu_custom_call" | custom-call | flops 9437184 | bytes 4718592 | tf_op jit(solution)/shard_map/chain_6/solve_layer/pallas_call | solution.py:116
  181.3 3.9 %all-to-all-start.7 = ((bf16[32,4,192]{2,1,0:T(4,128)(2,1)}), bf16[32,4,192]{2,1,0:T(4,128)(2,1)S(1)}, u32[]{:S(2)}, u32[]{:S(2)}) async-start(bf16[32,4,192]{2,1,0:T(4,128)(2,1)} %get-tuple-element.36), calls=%async_computation.7 | async-start | bytes 131072 | tf_op jit(solution)/shard_map/chain_7/all_to_all | solution.py:325
  185.2 12.3 %all-to-all-done.7 = bf16[32,4,192]{2,1,0:T(4,128)(2,1)S(1)} async-done(((bf16[32,4,192]{2,1,0:T(4,128)(2,1)}), bf16[32,4,192]{2,1,0:T(4,128)(2,1)S(1)}, u32[]{:S(2)}, u32[]{:S(2)}) %all-to-all-start.7) | async-done | bytes 49184 | tf_op jit(solution)/shard_map/chain_7/all_to_all | solution.py:325
  198.5 12.6 %smooth.1.smoothed = f32[2,2,8,64,192]{4,3,2,1,0:T(8,128)S(1)} custom-call(f32[4]{0:T(128)S(1)} %add_convert_fusion.inside, f32[2,2,8,64,192]{4,3,2,1,0:T(8,128)S(1)} %copy-done.1, f32[8,64,192]{2,1,0:T(8,128)S(1)} %copy-done.2, bf16[5,8,8,192]{3,2,1,0:T(8,128)(2,1)S(1)} %copy-done.4, bf16[5,8,8,192]{3,2,1,0:T(8,128)(2,1)S(1)} %collective-permute-done.1.row_high, ...), custom_call_target="tpu_custom_call" | custom-call | flops 117964800 | bytes 4718592 | tf_op jit(solution)/shard_map/smooth/smooth/pallas_call | solution.py:255
  211.1 3.4 %solve_layer.15 = (f32[4,192]{1,0:T(4,128)S(1)}, bf16[32,4,192]{2,1,0:T(4,128)(2,1)}) custom-call(s32[1]{0:T(128)} %bitcast.6.here, bf16[2,192,6144]{2,1,0:T(8,128)(2,1)} %bitcast.16, bf16[32,4,192]{2,1,0:T(4,128)(2,1)S(1)} %collective-permute-done.11.gathered, f32[4,192]{1,0:T(4,128)S(1)} %collective-permute-done.4.next_rhs, ...), custom_call_target="tpu_custom_call" | custom-call | flops 9437184 | bytes 4718592 | tf_op jit(solution)/shard_map/chain_7/solve_layer/pallas_call | solution.py:116
  (33 shorter events, 15.4 us)
Async XLA Ops:
  0.0 1.6 copy-start
  2.6 25.3 %all-to-all-start = ((bf16[32,4,192]{2,1,0:T(4,128)(2,1)}), bf16[32,4,192]{2,1,0:T(4,128)(2,1)S(1)}, u32[]{:S(2)}, u32[]{:S(2)}) async-start(bf16[32,4,192]{2,1,0:T(4,128)(2,1)} %get-tuple-element.22), calls=%async_computation | async-start | bytes 131072 | tf_op jit(solution)/shard_map/chain_0/all_to_all | solution.py:325
  15.7 3.4 %collective-permute-start.4 = (f32[4,192]{1,0:T(4,128)S(1)}, f32[4,192]{1,0:T(4,128)S(1)}, u32[]{:S(2)}, u32[]{:S(2)}) collective-permute-start(f32[4,192]{1,0:T(4,128)S(1)} %get-tuple-element.23.kept_before), channel_id=1, source_target_pairs={{32,0},{64,32},{96,64},{128,96},{160,128},{192,160},{224,192},{33,... | collective-permute-start | bytes 9224 | tf_op jit(solution)/shard_map/halo/ppermute | solution.py:318
  46.5 1.3 collective-permute-start.5
  47.8 20.9 %copy-start.2 = (f32[8,64,192]{2,1,0:T(8,128)S(1)}, f32[8,64,192]{2,1,0:T(8,128)}, u32[]{:S(2)}) copy-start(f32[8,64,192]{2,1,0:T(8,128)} %wavenumber.1) | copy-start | bytes 1179652
  47.8 20.9 %copy-start.1 = (f32[2,2,8,64,192]{4,3,2,1,0:T(8,128)S(1)}, f32[2,2,8,64,192]{4,3,2,1,0:T(8,128)}, u32[]{:S(2)}) copy-start(f32[2,2,8,64,192]{4,3,2,1,0:T(8,128)} %residual.3) | copy-start | bytes 4718596
  66.7 5.6 %collective-permute-start.6 = (bf16[32,4,192]{2,1,0:T(4,128)(2,1)S(1)}, bf16[32,4,192]{2,1,0:T(4,128)(2,1)S(1)}, u32[]{:S(2)}, u32[]{:S(2)}) collective-permute-start(bf16[32,4,192]{2,1,0:T(4,128)(2,1)S(1)} %all_to_all.41), channel_id=1, source_target_pairs={{32,64},{96,128},{160,192},{64,32},{128,96},{192,160},{0,0},{224,2... | collective-permute-start | bytes 147464 | tf_op jit(solution)/shard_map/chain_2/ppermute | solution.py:327
  75.7 16.9 %all-to-all-start.3 = ((bf16[32,4,192]{2,1,0:T(4,128)(2,1)}), bf16[32,4,192]{2,1,0:T(4,128)(2,1)}, u32[]{:S(2)}, u32[]{:S(2)}) async-start(bf16[32,4,192]{2,1,0:T(4,128)(2,1)} %get-tuple-element.28), calls=%async_computation.3 | async-start | bytes 131072 | tf_op jit(solution)/shard_map/chain_3/all_to_all | solution.py:325
  82.0 28.3 %collective-permute-start.1 = (bf16[5,8,8,192]{3,2,1,0:T(8,128)(2,1)}, bf16[5,8,8,192]{3,2,1,0:T(8,128)(2,1)S(1)}, u32[]{:S(2)}, u32[]{:S(2)}) collective-permute-start(bf16[5,8,8,192]{3,2,1,0:T(8,128)(2,1)} %get-tuple-element.41), channel_id=1, source_target_pairs={{1,0},{2,1},{3,2},{4,3},{5,4},{6,5},{7,6},{8,7},{9,8},{10,9},{11,1... | collective-permute-start | bytes 368648 | tf_op jit(solution)/shard_map/halo/ppermute | solution.py:294
  92.7 2.7 %collective-permute-start.7 = (bf16[32,4,192]{2,1,0:T(4,128)(2,1)}, bf16[32,4,192]{2,1,0:T(4,128)(2,1)S(1)}, u32[]{:S(2)}, u32[]{:S(2)}) collective-permute-start(bf16[32,4,192]{2,1,0:T(4,128)(2,1)} %all-to-all-done.3), channel_id=1, source_target_pairs={{0,32},{32,0},{64,96},{96,64},{128,160},{160,128},{192,224},{224,1... | collective-permute-start | bytes 147464 | tf_op jit(solution)/shard_map/chain_3/ppermute | solution.py:327
  92.7 31.9 %collective-permute-start = (bf16[5,8,8,192]{3,2,1,0:T(8,128)(2,1)S(1)}, bf16[5,8,8,192]{3,2,1,0:T(8,128)(2,1)S(1)}, u32[]{:S(2)}, u32[]{:S(2)}) collective-permute-start(bf16[5,8,8,192]{3,2,1,0:T(8,128)(2,1)S(1)} %get-tuple-element.42), channel_id=1, source_target_pairs={{0,1},{1,2},{2,3},{3,4},{4,5},{5,6},{6,7},{7,8},{8,9},{9,10},{10,1... | collective-permute-start | bytes 368648 | tf_op jit(solution)/shard_map/halo/ppermute | solution.py:294
  98.8 23.8 %all-to-all-start.4 = ((bf16[32,4,192]{2,1,0:T(4,128)(2,1)}), bf16[32,4,192]{2,1,0:T(4,128)(2,1)}, u32[]{:S(2)}, u32[]{:S(2)}) async-start(bf16[32,4,192]{2,1,0:T(4,128)(2,1)} %get-tuple-element.30), calls=%async_computation.4 | async-start | bytes 131072 | tf_op jit(solution)/shard_map/chain_4/all_to_all | solution.py:325
  122.6 5.8 %collective-permute-start.8 = (bf16[32,4,192]{2,1,0:T(4,128)(2,1)}, bf16[32,4,192]{2,1,0:T(4,128)(2,1)S(1)}, u32[]{:S(2)}, u32[]{:S(2)}) collective-permute-start(bf16[32,4,192]{2,1,0:T(4,128)(2,1)} %all-to-all-done.4), channel_id=1, source_target_pairs={{32,64},{96,128},{160,192},{64,32},{128,96},{192,160},{0,0},{224,2... | collective-permute-start | bytes 147464 | tf_op jit(solution)/shard_map/chain_4/ppermute | solution.py:327
  124.5 7.3 %copy-start.3 = (bf16[5,8,8,192]{3,2,1,0:T(8,128)(2,1)}, bf16[5,8,8,192]{3,2,1,0:T(8,128)(2,1)S(1)}, u32[]{:S(2)}) copy-start(bf16[5,8,8,192]{3,2,1,0:T(8,128)(2,1)S(1)} %collective-permute-done.row_low) | copy-start | bytes 368644
  131.8 16.8 %all-to-all-start.5 = ((bf16[32,4,192]{2,1,0:T(4,128)(2,1)}), bf16[32,4,192]{2,1,0:T(4,128)(2,1)}, u32[]{:S(2)}, u32[]{:S(2)}) async-start(bf16[32,4,192]{2,1,0:T(4,128)(2,1)} %get-tuple-element.32), calls=%async_computation.5 | async-start | bytes 131072 | tf_op jit(solution)/shard_map/chain_5/all_to_all | solution.py:325
  138.8 58.8 %collective-permute-start.3 = (bf16[5,3,80,192]{3,2,1,0:T(8,128)(2,1)}, bf16[5,3,80,192]{3,2,1,0:T(8,128)(2,1)S(1)}, u32[]{:S(2)}, u32[]{:S(2)}) collective-permute-start(bf16[5,3,80,192]{3,2,1,0:T(8,128)(2,1)} %get-tuple-element.39), channel_id=1, source_target_pairs={{32,0},{64,32},{96,64},{128,96},{160,128},{192,160},{224,192},{33,... | collective-permute-start | bytes 1382408 | tf_op jit(solution)/shard_map/halo/ppermute | solution.py:294
  140.7 56.9 %collective-permute-start.2 = (bf16[5,3,80,192]{3,2,1,0:T(8,128)(2,1)}, bf16[5,3,80,192]{3,2,1,0:T(8,128)(2,1)}, u32[]{:S(2)}, u32[]{:S(2)}) collective-permute-start(bf16[5,3,80,192]{3,2,1,0:T(8,128)(2,1)} %get-tuple-element.40), channel_id=1, source_target_pairs={{0,32},{32,64},{64,96},{96,128},{128,160},{160,192},{192,224},{1,3... | collective-permute-start | bytes 1382408 | tf_op jit(solution)/shard_map/halo/ppermute | solution.py:294
  148.6 1.5 collective-permute-start.9
  172.3 5.6 %collective-permute-start.10 = (bf16[32,4,192]{2,1,0:T(4,128)(2,1)S(1)}, bf16[32,4,192]{2,1,0:T(4,128)(2,1)S(1)}, u32[]{:S(2)}, u32[]{:S(2)}) collective-permute-start(bf16[32,4,192]{2,1,0:T(4,128)(2,1)S(1)} %all_to_all.42), channel_id=1, source_target_pairs={{32,64},{96,128},{160,192},{64,32},{128,96},{192,160},{0,0},{224,2... | collective-permute-start | bytes 147464 | tf_op jit(solution)/shard_map/chain_6/ppermute | solution.py:327
  181.3 16.1 %all-to-all-start.7 = ((bf16[32,4,192]{2,1,0:T(4,128)(2,1)}), bf16[32,4,192]{2,1,0:T(4,128)(2,1)S(1)}, u32[]{:S(2)}, u32[]{:S(2)}) async-start(bf16[32,4,192]{2,1,0:T(4,128)(2,1)} %get-tuple-element.36), calls=%async_computation.7 | async-start | bytes 131072 | tf_op jit(solution)/shard_map/chain_7/all_to_all | solution.py:325
  197.5 13.7 %collective-permute-start.11 = (bf16[32,4,192]{2,1,0:T(4,128)(2,1)S(1)}, bf16[32,4,192]{2,1,0:T(4,128)(2,1)S(1)}, u32[]{:S(2)}, u32[]{:S(2)}) collective-permute-start(bf16[32,4,192]{2,1,0:T(4,128)(2,1)S(1)} %all-to-all-done.7), channel_id=1, source_target_pairs={{0,32},{32,0},{64,96},{96,64},{128,160},{160,128},{192,224},{224,1... | collective-permute-start | bytes 147464 | tf_op jit(solution)/shard_map/chain_7/ppermute | solution.py:327
  197.6 0.9 copy-start.4

commit v2 on v1

--- a/solution.py
+++ b/solution.py
@@ -6,6 +6,7 @@
 from jax.experimental import pallas as pl
 from jax.experimental.pallas import tpu as pltpu
 from jax.sharding import PartitionSpec as P
+
 
 QY = 16
 PX = 4
@@ -79,9 +80,30 @@
     )(residual)
 
 
-def layer_kernel(step, here, matrix, gathered, next_rhs, kept_before, kept, spread, held, vector, arrived):
-    devices, lines, cells = gathered.shape
-    shots = lines // 2
+def ordered(vector, same, other, first_end):
+    columns, _, cells = same.shape
+    for column in range(columns):
+        own, far = same[column], other[column]
+        at = 2 * column * cells
+        vector[:, at : at + cells] = jnp.where(first_end, own, far)
+        vector[:, at + cells : at + 2 * cells] = jnp.where(first_end, far, own)
+
+
+def hand_on(step, place, by_re, by_im, next_rhs, kept_before, kept, spread):
+    shots = by_re.shape[0] // 2
+    solved = jnp.concatenate([by_re[:shots] - by_im[shots:], by_re[shots:] + by_im[:shots]], axis=0)
+    kept[...] = jnp.where(place[0] == step, solved, kept_before[...])
+    out = (next_rhs[...] + coupling * solved).astype(bf16)
+    for column in range(spread.shape[0]):
+        spread[column] = out
+
+
+def times(part, rows):
+    return lax.dot_general(part, rows, (((1,), (1,)), ((), ())), preferred_element_type=f32)
+
+
+def first_kernel(place, matrix, gathered, next_rhs, kept_before, kept, spread, held, vector, arrived):
+    devices, _, cells = gathered.shape
     pieces = arrived.shape[0]
     across = matrix.shape[2] // pieces
     columns = [slice(piece * across, (piece + 1) * across) for piece in range(pieces)]
@@ -93,43 +115,56 @@
         copy.start()
     for device in range(devices):
         vector[:, device * cells : (device + 1) * cells] = gathered[device]
-    by_re = by_im = None
+    by = [None, None]
     for piece in range(pieces):
         part = vector[:, columns[piece]]
         copies[piece].wait()
-        products = [
-            lax.dot_general(part, held[side, :, columns[piece]], (((1,), (1,)), ((), ())), preferred_element_type=f32)
-            for side in range(2)
-        ]
-        by_re = products[0] if by_re is None else by_re + products[0]
-        by_im = products[1] if by_im is None else by_im + products[1]
-    solved = jnp.concatenate([by_re[:shots] - by_im[shots:], by_re[shots:] + by_im[:shots]], axis=0)
-    kept[...] = jnp.where(here[0] == step, solved, kept_before[...])
-    out = (next_rhs[...] + coupling * solved).astype(bf16)
-    for device in range(devices):
-        spread[device] = out
-
-
-def solve_layer(step, here, matrix, gathered, next_rhs, kept):
+        for side in range(2):
+            product = times(part, held[side, :, columns[piece]])
+            by[side] = product if by[side] is None else by[side] + product
+    hand_on(0, place, by[0], by[1], next_rhs, kept_before, kept, spread)
+
+
+def solve_first(place, matrix, gathered, next_rhs, kept):
     devices, lines, cells = gathered.shape
     pieces = 6
+    return pl.pallas_call(
+        first_kernel,
+        out_shape=(
+            jax.ShapeDtypeStruct((lines, cells), f32),
+            jax.ShapeDtypeStruct((devices // 2, lines, cells), bf16),
+            pltpu.VMEM(matrix.shape, bf16),
+        ),
+        in_specs=[pl.BlockSpec(memory_space=pltpu.SMEM), pl.BlockSpec(memory_space=pltpu.HBM)]
+        + [pl.BlockSpec(memory_space=VMEM)] * 3,
+        out_specs=[pl.BlockSpec(memory_space=VMEM)] * 3,
+        scratch_shapes=[pltpu.VMEM((lines, devices * cells), bf16), pltpu.SemaphoreType.DMA((pieces,))],
+        compiler_params=limit(3),
+        cost_estimate=pl.CostEstimate(flops=4 * matrix.size, bytes_accessed=2 * matrix.size, transcendentals=0),
+        name="solve_first",
+    )(place, matrix, gathered, next_rhs, kept)
+
+
+def layer_kernel(step, place, matrix, same, other, next_rhs, kept_before, kept, spread, vector):
+    ordered(vector, same, other, place[1] == 0)
+    full = vector[...]
+    hand_on(step, place, times(full, matrix[0]), times(full, matrix[1]), next_rhs, kept_before, kept, spread)
+
+
+def solve_layer(step, place, matrix, same, other, next_rhs, kept):
+    columns, lines, cells = same.shape
     return pl.pallas_call(
         functools.partial(layer_kernel, step),
         out_shape=(
             jax.ShapeDtypeStruct((lines, cells), f32),
-            jax.ShapeDtypeStruct((devices, lines, cells), bf16),
+            jax.ShapeDtypeStruct((columns, lines, cells), bf16),
         ),
-        in_specs=[pl.BlockSpec(memory_space=pltpu.SMEM), pl.BlockSpec(memory_space=pltpu.HBM)]
-        + [pl.BlockSpec(memory_space=VMEM)] * 3,
-        scratch_shapes=[
-            pltpu.VMEM(matrix.shape, bf16),
-            pltpu.VMEM((lines, devices * cells), bf16),
-            pltpu.SemaphoreType.DMA((pieces,)),
-        ],
-        compiler_params=limit(8),
+        in_specs=[pl.BlockSpec(memory_space=pltpu.SMEM)] + [pl.BlockSpec(memory_space=VMEM)] * 5,
+        scratch_shapes=[pltpu.VMEM((lines, 2 * columns * cells), bf16)],
+        compiler_params=limit(3),
         cost_estimate=pl.CostEstimate(flops=4 * matrix.size, bytes_accessed=2 * matrix.size, transcendentals=0),
         name="solve_layer",
-    )(here, matrix, gathered, next_rhs, kept)
+    )(place, matrix, same, other, next_rhs, kept)
 
 
 def smooth_kernel(inside, residual, wavenumber, row_low, row_high, deep_low, deep_high, smoothed, gain, source, first, second):
@@ -169,25 +204,23 @@
     def own_gain(plane, _):
         for row in range(0, height, 16):
             put_gain(HALO + plane, start + row, wavenumber[plane, row : row + 16, :], 1.0)
-        put_gain(HALO + plane, top, row_low[2 * shots, plane].astype(f32), inside[2])
-        put_gain(HALO + plane, start + height, row_high[2 * shots, plane].astype(f32), inside[3])
         return _
 
     lax.fori_loop(0, depth, own_gain, 0)
     for base, count, ghost, factor in sides:
         for plane in range(count):
-            for row in range(0, total, 16):
-                values = ghost[2 * shots, plane, row : row + 16, :].astype(f32)
-                put_gain(base + plane, top + row, values, factor)
-    for base, count, _, _ in sides:
-        for plane in range(count):
-            for part in range(2):
-                low = gain[part, base + plane, top:start, :]
-                gain[part, base + plane, top:start, :] = low * inside[2]
-                high = gain[part, base + plane, start + height : start + height + ROWS, :]
-                gain[part, base + plane, start + height : start + height + ROWS, :] = high * inside[3]
-
-    def sweep(old, new, plane, row, rows, store):
+            for row in range(0, height, 16):
+                put_gain(base + plane, start + row, ghost[2 * shots, plane, row : row + 16, :].astype(f32), factor)
+    for base, count, factor in ((0, HALO, inside[0]), (HALO, depth, 1.0), (HALO + depth, HALO, inside[1])):
+
+        def row_gain(plane, _, factor=factor):
+            put_gain(plane, top, row_low[2 * shots, plane].astype(f32), factor * inside[2])
+            put_gain(plane, start + height, row_high[2 * shots, plane].astype(f32), factor * inside[3])
+            return _
+
+        lax.fori_loop(base, base + count, row_gain, 0)
+
+    def sweep(old, plane, row, rows, store):
         here = pl.ds(row, rows)
         terms = []
         for part in range(2):
@@ -206,17 +239,22 @@
         def own_source(plane, _):
             for part in range(2):
                 source[part, HALO + plane, start : start + height, 0:width] = residual[shot, part, plane]
-                source[part, HALO + plane, top:start, 0:width] = row_low[2 * shot + part, plane].astype(f32)
-                source[part, HALO + plane, start + height : start + height + ROWS, 0:width] = row_high[
+            return _
+
+        def row_source(plane, _):
+            for part in range(2):
+                source[part, plane, top:start, 0:width] = row_low[2 * shot + part, plane].astype(f32)
+                source[part, plane, start + height : start + height + ROWS, 0:width] = row_high[
                     2 * shot + part, plane
                 ].astype(f32)
             return _
 
         lax.fori_loop(0, depth, own_source, 0)
+        lax.fori_loop(0, planes, row_source, 0)
         for base, count, ghost, _ in sides:
             for plane in range(count):
                 for part in range(2):
-                    source[part, base + plane, top : top + total, 0:width] = ghost[2 * shot + part, plane].astype(f32)
+                    source[part, base + plane, start : start + height, 0:width] = ghost[2 * shot + part, plane].astype(f32)
 
         def begin(plane, _):
             for row in range(top, top + total, 16):
@@ -242,7 +280,7 @@
                         else:
                             new[part, plane, pl.ds(row, 16), :] = value
 
-                    sweep(old, new, plane, row, 16, store)
+                    sweep(old, plane, row, 16, store)
                 return _
 
             lax.fori_loop(counter, planes - counter, one_plane, 0)
@@ -288,58 +326,84 @@
     )(smoothed, coarse)
 
 
+def pack_planes_kernel(residual, wavenumber, first, last):
+    shots, _, depth, height, width = residual.shape
+    for out, base in ((first, 0), (last, depth - HALO)):
+        for plane in range(HALO):
+            for shot in range(shots):
+                for part in range(2):
+                    out[2 * shot + part, plane] = residual[shot, part, base + plane].astype(bf16)
+            out[2 * shots, plane] = wavenumber[base + plane].astype(bf16)
+
+
+def pack_planes(residual, wavenumber):
+    shots, _, _, height, width = residual.shape
+    shape = jax.ShapeDtypeStruct((2 * shots + 1, HALO, height, width), bf16)
+    return pl.pallas_call(
+        pack_planes_kernel, out_shape=(shape, shape), compiler_params=limit(10), name="pack_planes"
+    )(residual, wavenumber)
+
+
+def pack_rows_kernel(residual, wavenumber, below, above, first, last):
+    shots, _, depth, height, width = residual.shape
+    for out, base in ((first, 0), (last, height - ROWS)):
+        rows = slice(base, base + ROWS)
+        for field in range(2 * shots + 1):
+            for plane in range(HALO):
+                out[field, plane] = below[field, plane, rows, :]
+                out[field, HALO + depth + plane] = above[field, plane, rows, :]
+            for plane in range(depth):
+                own = wavenumber[plane, rows, :] if field == 2 * shots else residual[field // 2, field % 2, plane, rows, :]
+                out[field, HALO + plane] = own.astype(bf16)
+
+
+def pack_rows(residual, wavenumber, below, above):
+    shots, _, depth, _, width = residual.shape
+    shape = jax.ShapeDtypeStruct((2 * shots + 1, depth + 2 * HALO, ROWS, width), bf16)
+    return pl.pallas_call(
+        pack_rows_kernel, out_shape=(shape, shape), compiler_params=limit(10), name="pack_rows"
+    )(residual, wavenumber, below, above)
+
+
 def both_ways(low_block, high_block, axis):
     size = lax.axis_size(axis)
     up = [(i, i + 1) for i in range(size - 1)]
     return lax.ppermute(high_block, axis, up), lax.ppermute(low_block, axis, [(b, a) for a, b in up])
 
 
-def on_device(residual, wavenumber, inverse):
-    shots, _, depth, height, width = residual.shape
+def every_layer(residual, wavenumber, inverse):
     layers, devices = lax.axis_size("layer"), lax.axis_size("row")
     layer, row = lax.axis_index("layer"), lax.axis_index("row")
-    here = jnp.reshape(layer, (1,)).astype(jnp.int32)
+    place = jnp.stack([layer, row & 1]).astype(jnp.int32)
     inside = jnp.stack([layer > 0, layer < layers - 1, row > 0, row < devices - 1]).astype(f32)
 
-    with jax.named_scope("restrict"):
-        rhs, spread = restrict(residual, devices)
+    rhs, spread = restrict(residual, devices)
+    next_rhs = lax.ppermute(rhs, "layer", [(i + 1, i) for i in range(layers - 1)])
     matrix = pltpu.with_memory_space_constraint(inverse[:, 0], pltpu.HBM)
-
-    with jax.named_scope("halo"):
-        fields = jnp.concatenate([residual.reshape(2 * shots, depth, height, width), wavenumber[None]]).astype(bf16)
-        row_low, row_high = both_ways(fields[:, :, :ROWS], fields[:, :, height - ROWS :], "row")
-
-        def with_rows(planes):
-            return jnp.concatenate([row_low[:, planes], fields[:, planes], row_high[:, planes]], axis=2)
-
-        deep_low, deep_high = both_ways(
-            with_rows(slice(0, HALO)), with_rows(slice(depth - HALO, depth)), "layer"
-        )
-        next_rhs = lax.ppermute(rhs, "layer", [(i + 1, i) for i in range(layers - 1)])
-    with jax.named_scope("smooth"):
-        smoothed = smooth(inside, residual, wavenumber, row_low, row_high, deep_low, deep_high)
-
-    kept = rhs
-    for step in range(layers):
-        with jax.named_scope(f"chain_{step}"):
-            gathered = lax.all_to_all(spread, "row", 0, 0, tiled=True)
-            if step:
-                gathered = lax.ppermute(gathered, "layer", hop(step - 1, layers))
-            kept, spread = solve_layer(step, here, matrix, gathered, next_rhs, kept)
-    with jax.named_scope("lift"):
-        return lift(smoothed, kept)
-
-
-def hop(source, layers):
-    if source % 2 == 0:
-        return [(i, i ^ 1) for i in range(layers)]
-    pairs = [(i, i + 1) for i in range(1, layers - 1, 2)]
-    return pairs + [(b, a) for a, b in pairs] + [(0, 0), (layers - 1, layers - 1)]
+    gathered = lax.all_to_all(spread, "row", 0, 0, tiled=True)
+    kept, spread, matrix = solve_first(place, matrix, gathered, next_rhs, rhs)
+
+    ends = [[2 * column + end for column in range(devices // 2)] for end in range(2)]
+    for step in range(1, layers):
+        half = lax.all_to_all(spread, "row", 0, 0, axis_index_groups=ends, tiled=True)
+        ways = [
+            [((step - 1) * devices + i, step * devices + (i ^ flip)) for i in range(devices)] for flip in range(2)
+        ]
+        other = lax.ppermute(half, ("layer", "row"), ways[1])
+        same = lax.ppermute(half, ("layer", "row"), ways[0])
+        kept, spread = solve_layer(step, place, matrix, same, other, next_rhs, kept)
+
+    first, last = pack_planes(residual, wavenumber)
+    below, above = both_ways(first, last, "layer")
+    first, last = pack_rows(residual, wavenumber, below, above)
+    row_low, row_high = both_ways(first, last, "row")
+    smoothed = smooth(inside, residual, wavenumber, row_low, row_high, below, above)
+    return lift(smoothed, kept)
 
 
 def solution(mesh):
     return jax.shard_map(
-        on_device,
+        every_layer,
         mesh=mesh,
         in_specs=(
             P(None, None, "layer", "row", None),

time: 218 us -> 204 us (0.936)
  the two profiles are of different devices: /device:TPU:32 before, /device:TPU:97 now
where the time goes in v2:
time: 204 us; the launch traced here: 203 us
  waiting for transfers between devices  62.4 us (31%)
  blocking collectives  56.2 us (28%)
  starting transfers between devices  39.9 us (20%)
  Pallas kernels  36.9 us (18%)
  local copies, waits for them, and re-layouts  7.31 us (4%)
    all_to_all x5, blocking collectives, every_layer(): lax.all_to_all(spread, 'row', 0, 0, axis_index_groups=ends, tiled=True)  56.2 us
    ppermute x7, waiting for transfers between devices, every_layer(): same = lax.ppermute(half, ('layer', 'row'), ways[0])  39.5 us
    pallas_call x7, Pallas kernels, solve_layer(): pl.pallas_call(functools.partial(layer_kernel, step), out_shape=(jax.Shap...  15.2 us
    pallas_call x1, Pallas kernels, smooth(): pl.pallas_call(smooth_kernel, out_shape=jax.ShapeDtypeStruct(residual.sha...  12.7 us
    all_to_all x1, waiting for transfers between devices, every_layer(): gathered = lax.all_to_all(spread, 'row', 0, 0, tiled=True)  11.2 us
    all_to_all x1, starting transfers between devices, every_layer(): gathered = lax.all_to_all(spread, 'row', 0, 0, tiled=True)  11 us
    all_to_all x2, waiting for transfers between devices, every_layer(): lax.all_to_all(spread, 'row', 0, 0, axis_index_groups=ends, tiled=True)  7.51 us
    unnamed x14, local copies, waits for them, and re-layouts  7.31 us
  transfers between devices with their start and end apart: 22, of which 5 were waited for; matrix products, arithmetic and copies ran while one was open for 0% of the time, Pallas kernels for 11%

profile of v2, /device:TPU:97, one launch (start us, length us, event | category | flops | bytes accessed | tf_op | source)
XLA Modules:
  0.0 203.3 jit_solution(15007094250995288887)
XLA Ops:
  0.0 1.6 copy-done.3
  5.0 4.0 %collective-permute-start.1 = (bf16[5,3,64,192]{3,2,1,0:T(8,128)(2,1)}, bf16[5,3,64,192]{3,2,1,0:T(8,128)(2,1)}, u32[]{:S(2)}, u32[]{:S(2)}) collective-permute-start(bf16[5,3,64,192]{3,2,1,0:T(8,128)(2,1)} %get-tuple-element.28), channel_id=1, source_target_pairs={{32,0},{64,32},{96,64},{128,96},{160,128},{192,160},{224,192},{33,... | collective-permute-start | bytes 1105928 | tf_op jit(solution)/shard_map/ppermute | solution.py:371
  10.0 2.8 %collective-permute-start.4 = (f32[4,192]{1,0:T(4,128)S(1)}, f32[4,192]{1,0:T(4,128)S(1)}, u32[]{:S(2)}, u32[]{:S(2)}) collective-permute-start(f32[4,192]{1,0:T(4,128)S(1)} %get-tuple-element.32.kept_before), channel_id=1, source_target_pairs={{32,0},{64,32},{96,64},{128,96},{160,128},{192,160},{224,192},{33,... | collective-permute-start | bytes 9224 | tf_op jit(solution)/shard_map/ppermute | solution.py:381
  12.8 11.0 %all-to-all-start = ((bf16[32,4,192]{2,1,0:T(4,128)(2,1)}), bf16[32,4,192]{2,1,0:T(4,128)(2,1)S(1)}, u32[]{:S(2)}, u32[]{:S(2)}) async-start(bf16[32,4,192]{2,1,0:T(4,128)(2,1)} %get-tuple-element.31), calls=%async_computation | async-start | bytes 131072 | tf_op jit(solution)/shard_map/all_to_all | solution.py:383
  23.9 11.2 %all-to-all-done.gathered = bf16[32,4,192]{2,1,0:T(4,128)(2,1)S(1)} async-done(((bf16[32,4,192]{2,1,0:T(4,128)(2,1)}), bf16[32,4,192]{2,1,0:T(4,128)(2,1)S(1)}, u32[]{:S(2)}, u32[]{:S(2)}) %all-to-all-start) | async-done | bytes 49184 | tf_op jit(solution)/shard_map/all_to_all | solution.py:383
  35.2 3.3 %solve_first.1 = (f32[4,192]{1,0:T(4,128)S(1)}, bf16[16,4,192]{2,1,0:T(4,128)(2,1)S(1)}, bf16[2,192,6144]{2,1,0:T(8,128)(2,1)S(1)}) custom-call(s32[2]{0:T(128)S(1)} %pad_add_fusion.place, bf16[2,192,6144]{2,1,0:T(8,128)(2,1)} %bitcast.7, bf16[32,4,192]{2,1,0:T(4,128)(2,1)S(1)} %all-to-all-done.gathered, f32[4,192]{1,0:T(4,128)S(1)} %collective-permute-done.4.next_rhs, ...), custom_call_target="tpu_custom_call" | custom-call | flops 9437184 | bytes 4718592 | tf_op jit(solution)/shard_map/solve_first/pallas_call | solution.py:131
  38.5 9.6 %all_to_all.40 = bf16[16,4,192]{2,1,0:T(4,128)(2,1)S(1)} all-to-all(bf16[16,4,192]{2,1,0:T(4,128)(2,1)S(1)} %get-tuple-element.34), channel_id=1, replica_groups={{0,2,4,6,8,10,12,14,16,18,20,22,24,26,28,30},{1,3,5,7,9,11,13,15,17,19,..., dimensions={0} | all-to-all | bytes 49152 | tf_op jit(solution)/shard_map/all_to_all | solution.py:388
  49.4 1.9 solve_layer.7
  51.4 9.6 %all_to_all.41 = bf16[16,4,192]{2,1,0:T(4,128)(2,1)S(1)} all-to-all(bf16[16,4,192]{2,1,0:T(4,128)(2,1)S(1)} %get-tuple-element.36), channel_id=1, replica_groups={{0,2,4,6,8,10,12,14,16,18,20,22,24,26,28,30},{1,3,5,7,9,11,13,15,17,19,..., dimensions={0} | all-to-all | bytes 49152 | tf_op jit(solution)/shard_map/all_to_all | solution.py:388
  62.3 1.9 solve_layer.8
  64.2 9.3 %all_to_all.42 = bf16[16,4,192]{2,1,0:T(4,128)(2,1)S(1)} all-to-all(bf16[16,4,192]{2,1,0:T(4,128)(2,1)S(1)} %get-tuple-element.38), channel_id=1, replica_groups={{0,2,4,6,8,10,12,14,16,18,20,22,24,26,28,30},{1,3,5,7,9,11,13,15,17,19,..., dimensions={0} | all-to-all | bytes 49152 | tf_op jit(solution)/shard_map/all_to_all | solution.py:388
  74.8 1.9 solve_layer.9
  76.7 9.3 %all_to_all.43 = bf16[16,4,192]{2,1,0:T(4,128)(2,1)S(1)} all-to-all(bf16[16,4,192]{2,1,0:T(4,128)(2,1)S(1)} %get-tuple-element.40), channel_id=1, replica_groups={{0,2,4,6,8,10,12,14,16,18,20,22,24,26,28,30},{1,3,5,7,9,11,13,15,17,19,..., dimensions={0} | all-to-all | bytes 49152 | tf_op jit(solution)/shard_map/all_to_all | solution.py:388
  87.4 2.5 %solve_layer.10 = (f32[4,192]{1,0:T(4,128)S(1)}, bf16[16,4,192]{2,1,0:T(4,128)(2,1)}) custom-call(s32[2]{0:T(128)S(1)} %pad_add_fusion.place, bf16[2,192,6144]{2,1,0:T(8,128)(2,1)S(1)} %get-tuple-element.33.matrix, bf16[16,4,192]{2,1,0:T(4,128)(2,1)S(1)} %collective-permute-done.11.same, bf16[16,4,192]{2,1,0:T(4,128)(2,1)S(1)} %collective-permute-done.12.other, ...), custom_call_target="tpu_custom_call" | custom-call | flops 9437184 | bytes 4718592 | tf_op jit(solution)/shard_map/solve_layer/pallas_call | solution.py:156
  89.9 3.5 %all-to-all-start.5 = ((bf16[16,4,192]{2,1,0:T(4,128)(2,1)}), bf16[16,4,192]{2,1,0:T(4,128)(2,1)S(1)}, u32[]{:S(2)}, u32[]{:S(2)}) async-start(bf16[16,4,192]{2,1,0:T(4,128)(2,1)} %get-tuple-element.42), calls=%async_computation.5 | async-start | bytes 65536 | tf_op jit(solution)/shard_map/all_to_all | solution.py:388
  93.5 1.9 pack_rows.1
  95.3 2.1 %collective-permute-start.2 = (bf16[5,14,8,192]{3,2,1,0:T(8,128)(2,1)}, bf16[5,14,8,192]{3,2,1,0:T(8,128)(2,1)S(1)}, u32[]{:S(2)}, u32[]{:S(2)}) collective-permute-start(bf16[5,14,8,192]{3,2,1,0:T(8,128)(2,1)} %get-tuple-element.29), channel_id=1, source_target_pairs={{0,1},{1,2},{2,3},{3,4},{4,5},{5,6},{6,7},{7,8},{8,9},{9,10},{10,1... | collective-permute-start | bytes 645128 | tf_op jit(solution)/shard_map/ppermute | solution.py:371
  97.4 1.3 collective-permute-start.3
  101.2 2.3 %copy-done.1 = bf16[2,192,6144]{2,1,0:T(8,128)(2,1)S(1)} copy-done((bf16[2,192,6144]{2,1,0:T(8,128)(2,1)S(1)}, bf16[2,192,6144]{2,1,0:T(8,128)(2,1)}, u32[]{:S(2)}) %copy-start.1) | copy-done | bytes 4718616
  103.5 1.9 solve_layer.11
  105.4 18.5 %all_to_all.44 = bf16[16,4,192]{2,1,0:T(4,128)(2,1)S(1)} all-to-all(bf16[16,4,192]{2,1,0:T(4,128)(2,1)S(1)} %get-tuple-element.44), channel_id=1, replica_groups={{0,2,4,6,8,10,12,14,16,18,20,22,24,26,28,30},{1,3,5,7,9,11,13,15,17,19,..., dimensions={0} | all-to-all | bytes 49152 | tf_op jit(solution)/shard_map/all_to_all | solution.py:388
  125.3 2.5 %solve_layer.12 = (f32[4,192]{1,0:T(4,128)S(1)}, bf16[16,4,192]{2,1,0:T(4,128)(2,1)}) custom-call(s32[2]{0:T(128)S(1)} %pad_add_fusion.place, bf16[2,192,6144]{2,1,0:T(8,128)(2,1)S(1)} %copy-done.1, bf16[16,4,192]{2,1,0:T(4,128)(2,1)S(1)} %collective-permute-done.15.same, bf16[16,4,192]{2,1,0:T(4,128)(2,1)S(1)} %collective-permute-done.16.other, ...), custom_call_target="tpu_custom_call" | custom-call | flops 9437184 | bytes 4718592 | tf_op jit(solution)/shard_map/solve_layer/pallas_call | solution.py:156
  127.8 3.5 %all-to-all-start.7 = ((bf16[16,4,192]{2,1,0:T(4,128)(2,1)}), bf16[16,4,192]{2,1,0:T(4,128)(2,1)S(1)}, u32[]{:S(2)}, u32[]{:S(2)}) async-start(bf16[16,4,192]{2,1,0:T(4,128)(2,1)} %get-tuple-element.46), calls=%async_computation.7 | async-start | bytes 65536 | tf_op jit(solution)/shard_map/all_to_all | solution.py:388
  131.3 6.4 %all-to-all-done.7 = bf16[16,4,192]{2,1,0:T(4,128)(2,1)S(1)} async-done(((bf16[16,4,192]{2,1,0:T(4,128)(2,1)}), bf16[16,4,192]{2,1,0:T(4,128)(2,1)S(1)}, u32[]{:S(2)}, u32[]{:S(2)}) %all-to-all-start.7) | async-done | bytes 24608 | tf_op jit(solution)/shard_map/all_to_all | solution.py:388
  137.7 1.3 collective-permute-start.17
  139.0 1.3 collective-permute-start.18
  140.4 39.5 %collective-permute-done.17.same = bf16[16,4,192]{2,1,0:T(4,128)(2,1)S(1)} collective-permute-done((bf16[16,4,192]{2,1,0:T(4,128)(2,1)S(1)}, bf16[16,4,192]{2,1,0:T(4,128)(2,1)S(1)}, u32[]{:S(2)}, u32[]{:S(2)}) %collective-permute-start.17) | collective-permute-done | bytes 24608 | tf_op jit(solution)/shard_map/ppermute | solution.py:393
  179.8 4.2 %collective-permute-done.18.other = bf16[16,4,192]{2,1,0:T(4,128)(2,1)S(1)} collective-permute-done((bf16[16,4,192]{2,1,0:T(4,128)(2,1)S(1)}, bf16[16,4,192]{2,1,0:T(4,128)(2,1)S(1)}, u32[]{:S(2)}, u32[]{:S(2)}) %collective-permute-start.18) | collective-permute-done | bytes 24608 | tf_op jit(solution)/shard_map/ppermute | solution.py:392
  184.0 2.3 %copy-done.2 = bf16[2,192,6144]{2,1,0:T(8,128)(2,1)S(1)} copy-done((bf16[2,192,6144]{2,1,0:T(8,128)(2,1)S(1)}, bf16[2,192,6144]{2,1,0:T(8,128)(2,1)}, u32[]{:S(2)}) %copy-start.2) | copy-done | bytes 4718616
  186.3 2.5 %solve_layer.13 = (f32[4,192]{1,0:T(4,128)S(1)}, bf16[16,4,192]{2,1,0:T(4,128)(2,1)}) custom-call(s32[2]{0:T(128)S(1)} %pad_add_fusion.place, bf16[2,192,6144]{2,1,0:T(8,128)(2,1)S(1)} %copy-done.2, bf16[16,4,192]{2,1,0:T(4,128)(2,1)S(1)} %collective-permute-done.17.same, bf16[16,4,192]{2,1,0:T(4,128)(2,1)S(1)} %collective-permute-done.18.other, ...), custom_call_target="tpu_custom_call" | custom-call | flops 9437184 | bytes 4718592 | tf_op jit(solution)/shard_map/solve_layer/pallas_call | solution.py:156
  188.9 12.7 %smooth.1.smoothed = f32[2,2,8,64,192]{4,3,2,1,0:T(8,128)S(1)} custom-call(f32[4]{0:T(128)S(1)} %add_convert_fusion.inside, f32[2,2,8,64,192]{4,3,2,1,0:T(8,128)S(1)} %copy-done.4, f32[8,64,192]{2,1,0:T(8,128)S(1)} %copy-done.6, bf16[5,14,8,192]{3,2,1,0:T(8,128)(2,1)S(1)} %collective-permute-done.2.row_low, ...), custom_call_target="tpu_custom_call" | custom-call | flops 117964800 | bytes 4718592 | tf_op jit(solution)/shard_map/smooth/pallas_call | solution.py:293
  201.5 1.7 lift.1
  (46 shorter events, 13.6 us)
Async XLA Ops:
  0.0 1.6 copy-start.3
  1.6 1.0 copy-start.5
  2.6 6.4 %copy-start.4 = (f32[2,2,8,64,192]{4,3,2,1,0:T(8,128)S(1)}, f32[2,2,8,64,192]{4,3,2,1,0:T(8,128)}, u32[]{:S(2)}) copy-start(f32[2,2,8,64,192]{4,3,2,1,0:T(8,128)} %residual.7) | copy-start | bytes 4718596
  3.7 89.8 %collective-permute-start = (bf16[5,3,64,192]{3,2,1,0:T(8,128)(2,1)}, bf16[5,3,64,192]{3,2,1,0:T(8,128)(2,1)S(1)}, u32[]{:S(2)}, u32[]{:S(2)}) collective-permute-start(bf16[5,3,64,192]{3,2,1,0:T(8,128)(2,1)} %get-tuple-element.27), channel_id=1, source_target_pairs={{0,32},{32,64},{64,96},{96,128},{128,160},{160,192},{192,224},{1,3... | collective-permute-start | bytes 1105928 | tf_op jit(solution)/shard_map/ppermute | solution.py:371
  5.0 88.5 %collective-permute-start.1 = (bf16[5,3,64,192]{3,2,1,0:T(8,128)(2,1)}, bf16[5,3,64,192]{3,2,1,0:T(8,128)(2,1)}, u32[]{:S(2)}, u32[]{:S(2)}) collective-permute-start(bf16[5,3,64,192]{3,2,1,0:T(8,128)(2,1)} %get-tuple-element.28), channel_id=1, source_target_pairs={{32,0},{64,32},{96,64},{128,96},{160,128},{192,160},{224,192},{33,... | collective-permute-start | bytes 1105928 | tf_op jit(solution)/shard_map/ppermute | solution.py:371
  10.0 13.9 %collective-permute-start.4 = (f32[4,192]{1,0:T(4,128)S(1)}, f32[4,192]{1,0:T(4,128)S(1)}, u32[]{:S(2)}, u32[]{:S(2)}) collective-permute-start(f32[4,192]{1,0:T(4,128)S(1)} %get-tuple-element.32.kept_before), channel_id=1, source_target_pairs={{32,0},{64,32},{96,64},{128,96},{160,128},{192,160},{224,192},{33,... | collective-permute-start | bytes 9224 | tf_op jit(solution)/shard_map/ppermute | solution.py:381
  12.8 22.3 %all-to-all-start = ((bf16[32,4,192]{2,1,0:T(4,128)(2,1)}), bf16[32,4,192]{2,1,0:T(4,128)(2,1)S(1)}, u32[]{:S(2)}, u32[]{:S(2)}) async-start(bf16[32,4,192]{2,1,0:T(4,128)(2,1)} %get-tuple-element.31), calls=%async_computation | async-start | bytes 131072 | tf_op jit(solution)/shard_map/all_to_all | solution.py:383
  38.5 48.9 %copy-start = (bf16[2,192,6144]{2,1,0:T(8,128)(2,1)}, bf16[2,192,6144]{2,1,0:T(8,128)(2,1)S(1)}, u32[]{:S(2)}) copy-start(bf16[2,192,6144]{2,1,0:T(8,128)(2,1)S(1)} %get-tuple-element.33.matrix) | copy-start | bytes 14155780
  48.1 1.3 collective-permute-start.5
  48.7 0.7 collective-permute-start.6
  60.9 1.3 collective-permute-start.7
  61.6 0.7 collective-permute-start.8
  73.5 1.3 collective-permute-start.10
  74.1 0.7 collective-permute-start.9
  86.0 1.3 collective-permute-start.11
  86.7 0.7 collective-permute-start.12
  87.4 6.1 %copy-start.6 = (f32[8,64,192]{2,1,0:T(8,128)S(1)}, f32[8,64,192]{2,1,0:T(8,128)}, u32[]{:S(2)}) copy-start(f32[8,64,192]{2,1,0:T(8,128)} %wavenumber.5) | copy-start | bytes 1179652
  89.9 9.9 %all-to-all-start.5 = ((bf16[16,4,192]{2,1,0:T(4,128)(2,1)}), bf16[16,4,192]{2,1,0:T(4,128)(2,1)S(1)}, u32[]{:S(2)}, u32[]{:S(2)}) async-start(bf16[16,4,192]{2,1,0:T(4,128)(2,1)} %get-tuple-element.42), calls=%async_computation.5 | async-start | bytes 65536 | tf_op jit(solution)/shard_map/all_to_all | solution.py:388
  95.3 93.5 %collective-permute-start.2 = (bf16[5,14,8,192]{3,2,1,0:T(8,128)(2,1)}, bf16[5,14,8,192]{3,2,1,0:T(8,128)(2,1)S(1)}, u32[]{:S(2)}, u32[]{:S(2)}) collective-permute-start(bf16[5,14,8,192]{3,2,1,0:T(8,128)(2,1)} %get-tuple-element.29), channel_id=1, source_target_pairs={{0,1},{1,2},{2,3},{3,4},{4,5},{5,6},{6,7},{7,8},{8,9},{9,10},{10,1... | collective-permute-start | bytes 645128 | tf_op jit(solution)/shard_map/ppermute | solution.py:371
  97.4 91.4 %collective-permute-start.3 = (bf16[5,14,8,192]{3,2,1,0:T(8,128)(2,1)}, bf16[5,14,8,192]{3,2,1,0:T(8,128)(2,1)}, u32[]{:S(2)}, u32[]{:S(2)}) collective-permute-start(bf16[5,14,8,192]{3,2,1,0:T(8,128)(2,1)} %get-tuple-element.30), channel_id=1, source_target_pairs={{1,0},{2,1},{3,2},{4,3},{5,4},{6,5},{7,6},{8,7},{9,8},{10,9},{11,1... | collective-permute-start | bytes 645128 | tf_op jit(solution)/shard_map/ppermute | solution.py:371
  99.8 1.3 collective-permute-start.13
  100.5 0.7 collective-permute-start.14
  101.2 2.3 %copy-start.1 = (bf16[2,192,6144]{2,1,0:T(8,128)(2,1)S(1)}, bf16[2,192,6144]{2,1,0:T(8,128)(2,1)}, u32[]{:S(2)}) copy-start(bf16[2,192,6144]{2,1,0:T(8,128)(2,1)} %copy-done) | copy-start | bytes 14155780
  123.9 1.3 collective-permute-start.15
  124.6 0.7 collective-permute-start.16
  127.8 9.9 %all-to-all-start.7 = ((bf16[16,4,192]{2,1,0:T(4,128)(2,1)}), bf16[16,4,192]{2,1,0:T(4,128)(2,1)S(1)}, u32[]{:S(2)}, u32[]{:S(2)}) async-start(bf16[16,4,192]{2,1,0:T(4,128)(2,1)} %get-tuple-element.46), calls=%async_computation.7 | async-start | bytes 65536 | tf_op jit(solution)/shard_map/all_to_all | solution.py:388
  137.7 42.1 %collective-permute-start.17 = (bf16[16,4,192]{2,1,0:T(4,128)(2,1)S(1)}, bf16[16,4,192]{2,1,0:T(4,128)(2,1)S(1)}, u32[]{:S(2)}, u32[]{:S(2)}) collective-permute-start(bf16[16,4,192]{2,1,0:T(4,128)(2,1)S(1)} %all-to-all-done.7), channel_id=1, source_target_pairs={{192,224},{193,225},{194,226},{195,227},{196,228},{197,229},{198,2... | collective-permute-start | bytes 73736 | tf_op jit(solution)/shard_map/ppermute | solution.py:393
  139.0 45.0 %collective-permute-start.18 = (bf16[16,4,192]{2,1,0:T(4,128)(2,1)S(1)}, bf16[16,4,192]{2,1,0:T(4,128)(2,1)S(1)}, u32[]{:S(2)}, u32[]{:S(2)}) collective-permute-start(bf16[16,4,192]{2,1,0:T(4,128)(2,1)S(1)} %all-to-all-done.7), channel_id=1, source_target_pairs={{192,225},{193,224},{194,227},{195,226},{196,229},{197,228},{198,2... | collective-permute-start | bytes 73736 | tf_op jit(solution)/shard_map/ppermute | solution.py:392
  184.0 2.3 %copy-start.2 = (bf16[2,192,6144]{2,1,0:T(8,128)(2,1)S(1)}, bf16[2,192,6144]{2,1,0:T(8,128)(2,1)}, u32[]{:S(2)}) copy-start(bf16[2,192,6144]{2,1,0:T(8,128)(2,1)} %copy-done) | copy-start | bytes 14155780

commit v3 on v2

--- a/solution.py
+++ b/solution.py
@@ -80,6 +80,26 @@
     )(residual)
 
 
+def hold_kernel(step, place, matrix, held, arrived):
+    @pl.when(place[0] == step)
+    def _():
+        copy = pltpu.make_async_copy(matrix, held, arrived)
+        copy.start()
+        copy.wait()
+
+
+def hold(step, place, matrix):
+    return pl.pallas_call(
+        functools.partial(hold_kernel, step),
+        out_shape=pltpu.VMEM(matrix.shape, matrix.dtype),
+        in_specs=[pl.BlockSpec(memory_space=pltpu.SMEM), pl.BlockSpec(memory_space=pltpu.HBM)],
+        out_specs=pl.BlockSpec(memory_space=VMEM),
+        scratch_shapes=[pltpu.SemaphoreType.DMA],
+        compiler_params=limit(1),
+        name="hold",
+    )(place, matrix)
+
+
 def ordered(vector, same, other, first_end):
     columns, _, cells = same.shape
     for column in range(columns):
@@ -89,10 +109,10 @@
         vector[:, at + cells : at + 2 * cells] = jnp.where(first_end, far, own)
 
 
-def hand_on(step, place, by_re, by_im, next_rhs, kept_before, kept, spread):
+def hand_on(by_re, by_im, next_rhs, kept, spread):
     shots = by_re.shape[0] // 2
     solved = jnp.concatenate([by_re[:shots] - by_im[shots:], by_re[shots:] + by_im[:shots]], axis=0)
-    kept[...] = jnp.where(place[0] == step, solved, kept_before[...])
+    kept[...] = solved
     out = (next_rhs[...] + coupling * solved).astype(bf16)
     for column in range(spread.shape[0]):
         spread[column] = out
@@ -102,7 +122,7 @@
     return lax.dot_general(part, rows, (((1,), (1,)), ((), ())), preferred_element_type=f32)
 
 
-def first_kernel(place, matrix, gathered, next_rhs, kept_before, kept, spread, held, vector, arrived):
+def first_kernel(matrix, gathered, next_rhs, kept, spread, held, vector, arrived):
     devices, _, cells = gathered.shape
     pieces = arrived.shape[0]
     across = matrix.shape[2] // pieces
@@ -122,10 +142,10 @@
         for side in range(2):
             product = times(part, held[side, :, columns[piece]])
             by[side] = product if by[side] is None else by[side] + product
-    hand_on(0, place, by[0], by[1], next_rhs, kept_before, kept, spread)
-
-
-def solve_first(place, matrix, gathered, next_rhs, kept):
+    hand_on(by[0], by[1], next_rhs, kept, spread)
+
+
+def solve_first(matrix, gathered, next_rhs):
     devices, lines, cells = gathered.shape
     pieces = 6
     return pl.pallas_call(
@@ -133,22 +153,29 @@
         out_shape=(
             jax.ShapeDtypeStruct((lines, cells), f32),
             jax.ShapeDtypeStruct((devices // 2, lines, cells), bf16),
+        ),
+        in_specs=[pl.BlockSpec(memory_space=pltpu.HBM)] + [pl.BlockSpec(memory_space=VMEM)] * 2,
+        scratch_shapes=[
             pltpu.VMEM(matrix.shape, bf16),
-        ),
-        in_specs=[pl.BlockSpec(memory_space=pltpu.SMEM), pl.BlockSpec(memory_space=pltpu.HBM)]
-        + [pl.BlockSpec(memory_space=VMEM)] * 3,
-        out_specs=[pl.BlockSpec(memory_space=VMEM)] * 3,
-        scratch_shapes=[pltpu.VMEM((lines, devices * cells), bf16), pltpu.SemaphoreType.DMA((pieces,))],
-        compiler_params=limit(3),
+            pltpu.VMEM((lines, devices * cells), bf16),
+            pltpu.SemaphoreType.DMA((pieces,)),
+        ],
+        compiler_params=limit(8),
         cost_estimate=pl.CostEstimate(flops=4 * matrix.size, bytes_accessed=2 * matrix.size, transcendentals=0),
         name="solve_first",
-    )(place, matrix, gathered, next_rhs, kept)
+    )(matrix, gathered, next_rhs)
 
 
 def layer_kernel(step, place, matrix, same, other, next_rhs, kept_before, kept, spread, vector):
-    ordered(vector, same, other, place[1] == 0)
-    full = vector[...]
-    hand_on(step, place, times(full, matrix[0]), times(full, matrix[1]), next_rhs, kept_before, kept, spread)
+    @pl.when(place[0] == step)
+    def _():
+        ordered(vector, same, other, place[1] == 0)
+        full = vector[...]
+        hand_on(times(full, matrix[0]), times(full, matrix[1]), next_rhs, kept, spread)
+
+    @pl.when(place[0] != step)
+    def _():
+        kept[...] = kept_before[...]
 
 
 def solve_layer(step, place, matrix, same, other, next_rhs, kept):
@@ -381,17 +408,23 @@
     next_rhs = lax.ppermute(rhs, "layer", [(i + 1, i) for i in range(layers - 1)])
     matrix = pltpu.with_memory_space_constraint(inverse[:, 0], pltpu.HBM)
     gathered = lax.all_to_all(spread, "row", 0, 0, tiled=True)
-    kept, spread, matrix = solve_first(place, matrix, gathered, next_rhs, rhs)
+    kept, spread = solve_first(matrix, gathered, next_rhs)
 
     ends = [[2 * column + end for column in range(devices // 2)] for end in range(2)]
     for step in range(1, layers):
-        half = lax.all_to_all(spread, "row", 0, 0, axis_index_groups=ends, tiled=True)
+        half = lax.cond(
+            layer == step - 1,
+            lambda blocks: lax.all_to_all(blocks, "row", 0, 0, axis_index_groups=ends, tiled=True),
+            lambda blocks: blocks,
+            spread,
+        )
         ways = [
             [((step - 1) * devices + i, step * devices + (i ^ flip)) for i in range(devices)] for flip in range(2)
         ]
         other = lax.ppermute(half, ("layer", "row"), ways[1])
         same = lax.ppermute(half, ("layer", "row"), ways[0])
-        kept, spread = solve_layer(step, place, matrix, same, other, next_rhs, kept)
+        held = hold(step, place, matrix)
+        kept, spread = solve_layer(step, place, held, same, other, next_rhs, kept)
 
     first, last = pack_planes(residual, wavenumber)
     below, above = both_ways(first, last, "layer")

time: 204 us -> 205 us (level)
  the two profiles are of different devices: /device:TPU:97 before, /device:TPU:225 now
where the time goes in v3:
time: 205 us; the launch traced here: 204 us
  waiting for transfers between devices  98.6 us (48%)
  starting transfers between devices  40.3 us (20%)
  Pallas kernels  33.2 us (16%)
  local copies, waits for them, and re-layouts  31.4 us (15%)
    ppermute x7, waiting for transfers between devices, every_layer(): same = lax.ppermute(half, ('layer', 'row'), ways[0])  88.8 us
    unnamed x34, local copies, waits for them, and re-layouts  31.4 us
    pallas_call x1, Pallas kernels, smooth(): pl.pallas_call(smooth_kernel, out_shape=jax.ShapeDtypeStruct(residual.sha...  12.7 us
    all_to_all x1, starting transfers between devices, every_layer(): gathered = lax.all_to_all(spread, 'row', 0, 0, tiled=True)  11.9 us
    ppermute x2, starting transfers between devices, both_ways(): lax.ppermute(high_block, axis, up)  8 us
    ppermute x7, waiting for transfers between devices, every_layer(): other = lax.ppermute(half, ('layer', 'row'), ways[1])  6.66 us
    ppermute x2, starting transfers between devices, both_ways(): lax.ppermute(low_block, axis, [(b, a) for a, b in up])  6.49 us
    pallas_call x7, Pallas kernels, hold(): pl.pallas_call(functools.partial(hold_kernel, step), out_shape=pltpu.VMEM...  6.23 us
  transfers between devices with their start and end apart: 20, of which 4 were waited for; matrix products, arithmetic and copies ran while one was open for 0% of the time, Pallas kernels for 9%

profile of v3, /device:TPU:225, one launch (start us, length us, event | category | flops | bytes accessed | tf_op | source)
XLA Modules:
  0.0 204.2 jit_solution(4485445364710858547)
XLA Ops:
  0.0 1.6 copy-done
  2.6 1.0 pack_planes.1
  3.7 1.3 collective-permute-start
  5.0 4.0 %collective-permute-start.1 = (bf16[5,3,64,192]{3,2,1,0:T(8,128)(2,1)}, bf16[5,3,64,192]{3,2,1,0:T(8,128)(2,1)}, u32[]{:S(2)}, u32[]{:S(2)}) collective-permute-start(bf16[5,3,64,192]{3,2,1,0:T(8,128)(2,1)} %get-tuple-element.62), channel_id=1, source_target_pairs={{32,0},{64,32},{96,64},{128,96},{160,128},{192,160},{224,192},{33,... | collective-permute-start | bytes 1105928 | tf_op jit(solution)/shard_map/ppermute | solution.py:398
  9.0 1.6 copy-done.1
  11.6 11.9 %all-to-all-start.7 = ((bf16[32,4,192]{2,1,0:T(4,128)(2,1)}), bf16[32,4,192]{2,1,0:T(4,128)(2,1)S(1)}, u32[]{:S(2)}, u32[]{:S(2)}) async-start(bf16[32,4,192]{2,1,0:T(4,128)(2,1)} %get-tuple-element.65), calls=%async_computation.7 | async-start | bytes 131072 | tf_op jit(solution)/shard_map/all_to_all | solution.py:410
  23.5 3.4 %collective-permute-start.4 = (f32[4,192]{1,0:T(4,128)S(1)}, f32[4,192]{1,0:T(4,128)S(1)}, u32[]{:S(2)}, u32[]{:S(2)}) collective-permute-start(f32[4,192]{1,0:T(4,128)S(1)} %get-tuple-element.66), channel_id=1, source_target_pairs={{32,0},{64,32},{96,64},{128,96},{160,128},{192,160},{224,192},{33,... | collective-permute-start | bytes 9224 | tf_op jit(solution)/shard_map/ppermute | solution.py:408
  27.7 2.3 %all-to-all-done.7.gathered = bf16[32,4,192]{2,1,0:T(4,128)(2,1)S(1)} async-done(((bf16[32,4,192]{2,1,0:T(4,128)(2,1)}), bf16[32,4,192]{2,1,0:T(4,128)(2,1)S(1)}, u32[]{:S(2)}, u32[]{:S(2)}) %all-to-all-start.7) | async-done | bytes 49184 | tf_op jit(solution)/shard_map/all_to_all | solution.py:410
  30.0 2.8 %solve_first.1 = (f32[4,192]{1,0:T(4,128)S(1)}, bf16[16,4,192]{2,1,0:T(4,128)(2,1)S(1)}) custom-call(bf16[2,192,6144]{2,1,0:T(8,128)(2,1)} %bitcast.7, bf16[32,4,192]{2,1,0:T(4,128)(2,1)S(1)} %all-to-all-done.7.gathered, f32[4,192]{1,0:T(4,128)S(1)} %collective-permute-done.4.next_rhs), custom_call_target="tpu_custom_call" | custom-call | flops 9437184 | bytes 4718592 | tf_op jit(solution)/shard_map/solve_first/pallas_call | solution.py:151
  34.9 2.2 %copy-done.13 = bf16[2,192,6144]{2,1,0:T(8,128)(2,1)} copy-done((bf16[2,192,6144]{2,1,0:T(8,128)(2,1)}, bf16[2,192,6144]{2,1,0:T(8,128)(2,1)S(1)}, u32[]{:S(2)}) %copy-start.13) | copy-done | bytes 4718616
  37.0 2.3 %copy-done.14 = bf16[2,192,6144]{2,1,0:T(8,128)(2,1)S(1)} copy-done((bf16[2,192,6144]{2,1,0:T(8,128)(2,1)S(1)}, bf16[2,192,6144]{2,1,0:T(8,128)(2,1)}, u32[]{:S(2)}) %copy-start.14) | copy-done | bytes 4718616
  41.9 2.2 %copy-done.5 = bf16[2,192,6144]{2,1,0:T(8,128)(2,1)} copy-done((bf16[2,192,6144]{2,1,0:T(8,128)(2,1)}, bf16[2,192,6144]{2,1,0:T(8,128)(2,1)S(1)}, u32[]{:S(2)}) %copy-start.5) | copy-done | bytes 4718616
  44.1 2.5 %copy-done.6 = bf16[2,192,6144]{2,1,0:T(8,128)(2,1)S(1)} copy-done((bf16[2,192,6144]{2,1,0:T(8,128)(2,1)S(1)}, bf16[2,192,6144]{2,1,0:T(8,128)(2,1)}, u32[]{:S(2)}) %copy-start.6) | copy-done | bytes 4718616
  48.5 1.9 pack_rows.1
  50.4 6.7 %collective-permute-start.2 = (bf16[5,14,8,192]{3,2,1,0:T(8,128)(2,1)}, bf16[5,14,8,192]{3,2,1,0:T(8,128)(2,1)S(1)}, u32[]{:S(2)}, u32[]{:S(2)}) collective-permute-start(bf16[5,14,8,192]{3,2,1,0:T(8,128)(2,1)} %get-tuple-element.63), channel_id=1, source_target_pairs={{0,1},{1,2},{2,3},{3,4},{4,5},{5,6},{6,7},{7,8},{8,9},{9,10},{10,1... | collective-permute-start | bytes 645128 | tf_op jit(solution)/shard_map/ppermute | solution.py:398
  57.1 2.5 %collective-permute-start.3 = (bf16[5,14,8,192]{3,2,1,0:T(8,128)(2,1)}, bf16[5,14,8,192]{3,2,1,0:T(8,128)(2,1)}, u32[]{:S(2)}, u32[]{:S(2)}) collective-permute-start(bf16[5,14,8,192]{3,2,1,0:T(8,128)(2,1)} %get-tuple-element.64), channel_id=1, source_target_pairs={{1,0},{2,1},{3,2},{4,3},{5,4},{6,5},{7,6},{8,7},{9,8},{10,9},{11,1... | collective-permute-start | bytes 645128 | tf_op jit(solution)/shard_map/ppermute | solution.py:398
  60.2 2.2 %copy-done.7 = bf16[2,192,6144]{2,1,0:T(8,128)(2,1)} copy-done((bf16[2,192,6144]{2,1,0:T(8,128)(2,1)}, bf16[2,192,6144]{2,1,0:T(8,128)(2,1)S(1)}, u32[]{:S(2)}) %copy-start.7) | copy-done | bytes 4718616
  62.3 2.3 %copy-done.8 = bf16[2,192,6144]{2,1,0:T(8,128)(2,1)S(1)} copy-done((bf16[2,192,6144]{2,1,0:T(8,128)(2,1)S(1)}, bf16[2,192,6144]{2,1,0:T(8,128)(2,1)}, u32[]{:S(2)}) %copy-start.8) | copy-done | bytes 4718616
  67.2 2.2 %copy-done.9 = bf16[2,192,6144]{2,1,0:T(8,128)(2,1)} copy-done((bf16[2,192,6144]{2,1,0:T(8,128)(2,1)}, bf16[2,192,6144]{2,1,0:T(8,128)(2,1)S(1)}, u32[]{:S(2)}) %copy-start.9) | copy-done | bytes 4718616
  69.3 2.3 %copy-done.10 = bf16[2,192,6144]{2,1,0:T(8,128)(2,1)S(1)} copy-done((bf16[2,192,6144]{2,1,0:T(8,128)(2,1)S(1)}, bf16[2,192,6144]{2,1,0:T(8,128)(2,1)}, u32[]{:S(2)}) %copy-start.10) | copy-done | bytes 4718616
  74.2 2.2 %copy-done.11 = bf16[2,192,6144]{2,1,0:T(8,128)(2,1)} copy-done((bf16[2,192,6144]{2,1,0:T(8,128)(2,1)}, bf16[2,192,6144]{2,1,0:T(8,128)(2,1)S(1)}, u32[]{:S(2)}) %copy-start.11) | copy-done | bytes 4718616
  76.3 2.3 %copy-done.12 = bf16[2,192,6144]{2,1,0:T(8,128)(2,1)S(1)} copy-done((bf16[2,192,6144]{2,1,0:T(8,128)(2,1)S(1)}, bf16[2,192,6144]{2,1,0:T(8,128)(2,1)}, u32[]{:S(2)}) %copy-start.12) | copy-done | bytes 4718616
  81.2 2.2 %copy-done.3 = bf16[2,192,6144]{2,1,0:T(8,128)(2,1)} copy-done((bf16[2,192,6144]{2,1,0:T(8,128)(2,1)}, bf16[2,192,6144]{2,1,0:T(8,128)(2,1)S(1)}, u32[]{:S(2)}) %copy-start.3) | copy-done | bytes 4718616
  83.3 2.3 %copy-done.4 = bf16[2,192,6144]{2,1,0:T(8,128)(2,1)S(1)} copy-done((bf16[2,192,6144]{2,1,0:T(8,128)(2,1)S(1)}, bf16[2,192,6144]{2,1,0:T(8,128)(2,1)}, u32[]{:S(2)}) %copy-start.4) | copy-done | bytes 4718616
  86.3 1.3 collective-permute-start.17
  87.6 1.3 collective-permute-start.18
  88.9 2.9 %hold.7.matrix = bf16[2,192,6144]{2,1,0:T(8,128)(2,1)S(1)} custom-call(s32[2]{0:T(128)S(1)} %pad_add_fusion.place, bf16[2,192,6144]{2,1,0:T(8,128)(2,1)} %bitcast.14), custom_call_target="tpu_custom_call" | custom-call | tf_op jit(solution)/shard_map/hold/pallas_call | solution.py:92
  91.8 88.8 %collective-permute-done.17.same = bf16[16,4,192]{2,1,0:T(4,128)(2,1)S(1)} collective-permute-done((bf16[16,4,192]{2,1,0:T(4,128)(2,1)S(1)}, bf16[16,4,192]{2,1,0:T(4,128)(2,1)S(1)}, u32[]{:S(2)}, u32[]{:S(2)}) %collective-permute-start.17) | collective-permute-done | bytes 24608 | tf_op jit(solution)/shard_map/ppermute | solution.py:425
  180.6 6.6 %collective-permute-done.18.other = bf16[16,4,192]{2,1,0:T(4,128)(2,1)S(1)} collective-permute-done((bf16[16,4,192]{2,1,0:T(4,128)(2,1)S(1)}, bf16[16,4,192]{2,1,0:T(4,128)(2,1)S(1)}, u32[]{:S(2)}, u32[]{:S(2)}) %collective-permute-start.18) | collective-permute-done | bytes 24608 | tf_op jit(solution)/shard_map/ppermute | solution.py:424
  187.3 2.5 %solve_layer.13 = (f32[4,192]{1,0:T(4,128)S(1)}, bf16[16,4,192]{2,1,0:T(4,128)(2,1)}) custom-call(s32[2]{0:T(128)S(1)} %pad_add_fusion.place, bf16[2,192,6144]{2,1,0:T(8,128)(2,1)S(1)} %hold.7.matrix, bf16[16,4,192]{2,1,0:T(4,128)(2,1)S(1)} %collective-permute-done.17.same, bf16[16,4,192]{2,1,0:T(4,128)(2,1)S(1)} %collective-permute-done.18.other, ...), custom_call_target="tpu_custom_call" | custom-call | flops 9437184 | bytes 4718592 | tf_op jit(solution)/shard_map/solve_layer/pallas_call | solution.py:183
  189.8 12.7 %smooth.1.smoothed = f32[2,2,8,64,192]{4,3,2,1,0:T(8,128)S(1)} custom-call(f32[4]{0:T(128)S(1)} %add_convert_fusion.inside, f32[2,2,8,64,192]{4,3,2,1,0:T(8,128)S(1)} %copy-done.2, f32[8,64,192]{2,1,0:T(8,128)S(1)} %copy-done.16, bf16[5,14,8,192]{3,2,1,0:T(8,128)(2,1)S(1)} %collective-permute-done.2.row_low, ...), custom_call_target="tpu_custom_call" | custom-call | flops 117964800 | bytes 4718592 | tf_op jit(solution)/shard_map/smooth/pallas_call | solution.py:320
  202.5 1.7 lift.1
  (71 shorter events, 17.8 us)
Async XLA Ops:
  3.7 44.8 %collective-permute-start = (bf16[5,3,64,192]{3,2,1,0:T(8,128)(2,1)}, bf16[5,3,64,192]{3,2,1,0:T(8,128)(2,1)S(1)}, u32[]{:S(2)}, u32[]{:S(2)}) collective-permute-start(bf16[5,3,64,192]{3,2,1,0:T(8,128)(2,1)} %get-tuple-element.61), channel_id=1, source_target_pairs={{0,32},{32,64},{64,96},{96,128},{128,160},{160,192},{192,224},{1,3... | collective-permute-start | bytes 1105928 | tf_op jit(solution)/shard_map/ppermute | solution.py:398
  5.0 43.5 %collective-permute-start.1 = (bf16[5,3,64,192]{3,2,1,0:T(8,128)(2,1)}, bf16[5,3,64,192]{3,2,1,0:T(8,128)(2,1)}, u32[]{:S(2)}, u32[]{:S(2)}) collective-permute-start(bf16[5,3,64,192]{3,2,1,0:T(8,128)(2,1)} %get-tuple-element.62), channel_id=1, source_target_pairs={{32,0},{64,32},{96,64},{128,96},{160,128},{192,160},{224,192},{33,... | collective-permute-start | bytes 1105928 | tf_op jit(solution)/shard_map/ppermute | solution.py:398
  11.6 18.5 %all-to-all-start.7 = ((bf16[32,4,192]{2,1,0:T(4,128)(2,1)}), bf16[32,4,192]{2,1,0:T(4,128)(2,1)S(1)}, u32[]{:S(2)}, u32[]{:S(2)}) async-start(bf16[32,4,192]{2,1,0:T(4,128)(2,1)} %get-tuple-element.65), calls=%async_computation.7 | async-start | bytes 131072 | tf_op jit(solution)/shard_map/all_to_all | solution.py:410
  23.5 4.2 %collective-permute-start.4 = (f32[4,192]{1,0:T(4,128)S(1)}, f32[4,192]{1,0:T(4,128)S(1)}, u32[]{:S(2)}, u32[]{:S(2)}) collective-permute-start(f32[4,192]{1,0:T(4,128)S(1)} %get-tuple-element.66), channel_id=1, source_target_pairs={{32,0},{64,32},{96,64},{128,96},{160,128},{192,160},{224,192},{33,... | collective-permute-start | bytes 9224 | tf_op jit(solution)/shard_map/ppermute | solution.py:408
  32.9 4.2 %collective-permute-start.5 = (bf16[16,4,192]{2,1,0:T(4,128)(2,1)S(1)}, bf16[16,4,192]{2,1,0:T(4,128)(2,1)S(1)}, u32[]{:S(2)}, u32[]{:S(2)}) collective-permute-start(bf16[16,4,192]{2,1,0:T(4,128)(2,1)S(1)} %get-tuple-element.82), channel_id=1, source_target_pairs={{0,32},{1,33},{2,34},{3,35},{4,36},{5,37},{6,38},{7,39},{8,40},{9,... | collective-permute-start | bytes 73736 | tf_op jit(solution)/shard_map/ppermute | solution.py:425
  33.5 3.5 %collective-permute-start.6 = (bf16[16,4,192]{2,1,0:T(4,128)(2,1)S(1)}, bf16[16,4,192]{2,1,0:T(4,128)(2,1)S(1)}, u32[]{:S(2)}, u32[]{:S(2)}) collective-permute-start(bf16[16,4,192]{2,1,0:T(4,128)(2,1)S(1)} %get-tuple-element.82), channel_id=1, source_target_pairs={{0,33},{1,32},{2,35},{3,34},{4,37},{5,36},{6,39},{7,38},{8,41},{9,... | collective-permute-start | bytes 73736 | tf_op jit(solution)/shard_map/ppermute | solution.py:424
  34.9 2.2 %copy-start.13 = (bf16[2,192,6144]{2,1,0:T(8,128)(2,1)}, bf16[2,192,6144]{2,1,0:T(8,128)(2,1)S(1)}, u32[]{:S(2)}) copy-start(bf16[2,192,6144]{2,1,0:T(8,128)(2,1)S(1)} %hold.13.matrix) | copy-start | bytes 14155780
  37.0 2.3 %copy-start.14 = (bf16[2,192,6144]{2,1,0:T(8,128)(2,1)S(1)}, bf16[2,192,6144]{2,1,0:T(8,128)(2,1)}, u32[]{:S(2)}) copy-start(bf16[2,192,6144]{2,1,0:T(8,128)(2,1)} %copy-done.13) | copy-start | bytes 14155780
  39.9 4.1 %collective-permute-start.7 = (bf16[16,4,192]{2,1,0:T(4,128)(2,1)S(1)}, bf16[16,4,192]{2,1,0:T(4,128)(2,1)S(1)}, u32[]{:S(2)}, u32[]{:S(2)}) collective-permute-start(bf16[16,4,192]{2,1,0:T(4,128)(2,1)S(1)} %get-tuple-element.83), channel_id=1, source_target_pairs={{32,64},{33,65},{34,66},{35,67},{36,68},{37,69},{38,70},{39,71},{4... | collective-permute-start | bytes 73736 | tf_op jit(solution)/shard_map/ppermute | solution.py:425
  40.6 3.4 %collective-permute-start.8 = (bf16[16,4,192]{2,1,0:T(4,128)(2,1)S(1)}, bf16[16,4,192]{2,1,0:T(4,128)(2,1)S(1)}, u32[]{:S(2)}, u32[]{:S(2)}) collective-permute-start(bf16[16,4,192]{2,1,0:T(4,128)(2,1)S(1)} %get-tuple-element.83), channel_id=1, source_target_pairs={{32,65},{33,64},{34,67},{35,66},{36,69},{37,68},{38,71},{39,70},{4... | collective-permute-start | bytes 73736 | tf_op jit(solution)/shard_map/ppermute | solution.py:424
  41.3 7.2 %copy-start.16 = (f32[8,64,192]{2,1,0:T(8,128)S(1)}, f32[8,64,192]{2,1,0:T(8,128)}, u32[]{:S(2)}) copy-start(f32[8,64,192]{2,1,0:T(8,128)} %wavenumber.5) | copy-start | bytes 1179652
  41.9 2.2 %copy-start.5 = (bf16[2,192,6144]{2,1,0:T(8,128)(2,1)}, bf16[2,192,6144]{2,1,0:T(8,128)(2,1)S(1)}, u32[]{:S(2)}) copy-start(bf16[2,192,6144]{2,1,0:T(8,128)(2,1)S(1)} %hold.12.matrix) | copy-start | bytes 14155780
  44.0 4.5 %copy-start.2 = (f32[2,2,8,64,192]{4,3,2,1,0:T(8,128)S(1)}, f32[2,2,8,64,192]{4,3,2,1,0:T(8,128)}, u32[]{:S(2)}) copy-start(f32[2,2,8,64,192]{4,3,2,1,0:T(8,128)} %residual.7) | copy-start | bytes 4718596
  44.0 2.5 %copy-start.6 = (bf16[2,192,6144]{2,1,0:T(8,128)(2,1)S(1)}, bf16[2,192,6144]{2,1,0:T(8,128)(2,1)}, u32[]{:S(2)}) copy-start(bf16[2,192,6144]{2,1,0:T(8,128)(2,1)} %copy-done.5) | copy-start | bytes 14155780
  47.1 15.2 %collective-permute-start.10 = (bf16[16,4,192]{2,1,0:T(4,128)(2,1)S(1)}, bf16[16,4,192]{2,1,0:T(4,128)(2,1)S(1)}, u32[]{:S(2)}, u32[]{:S(2)}) collective-permute-start(bf16[16,4,192]{2,1,0:T(4,128)(2,1)S(1)} %get-tuple-element.84), channel_id=1, source_target_pairs={{64,97},{65,96},{66,99},{67,98},{68,101},{69,100},{70,103},{71,102... | collective-permute-start | bytes 73736 | tf_op jit(solution)/shard_map/ppermute | solution.py:424
  47.8 14.5 %collective-permute-start.9 = (bf16[16,4,192]{2,1,0:T(4,128)(2,1)S(1)}, bf16[16,4,192]{2,1,0:T(4,128)(2,1)S(1)}, u32[]{:S(2)}, u32[]{:S(2)}) collective-permute-start(bf16[16,4,192]{2,1,0:T(4,128)(2,1)S(1)} %get-tuple-element.84), channel_id=1, source_target_pairs={{64,96},{65,97},{66,98},{67,99},{68,100},{69,101},{70,102},{71,103... | collective-permute-start | bytes 73736 | tf_op jit(solution)/shard_map/ppermute | solution.py:425
  50.4 139.4 %collective-permute-start.2 = (bf16[5,14,8,192]{3,2,1,0:T(8,128)(2,1)}, bf16[5,14,8,192]{3,2,1,0:T(8,128)(2,1)S(1)}, u32[]{:S(2)}, u32[]{:S(2)}) collective-permute-start(bf16[5,14,8,192]{3,2,1,0:T(8,128)(2,1)} %get-tuple-element.63), channel_id=1, source_target_pairs={{0,1},{1,2},{2,3},{3,4},{4,5},{5,6},{6,7},{7,8},{8,9},{9,10},{10,1... | collective-permute-start | bytes 645128 | tf_op jit(solution)/shard_map/ppermute | solution.py:398
  57.1 132.7 %collective-permute-start.3 = (bf16[5,14,8,192]{3,2,1,0:T(8,128)(2,1)}, bf16[5,14,8,192]{3,2,1,0:T(8,128)(2,1)}, u32[]{:S(2)}, u32[]{:S(2)}) collective-permute-start(bf16[5,14,8,192]{3,2,1,0:T(8,128)(2,1)} %get-tuple-element.64), channel_id=1, source_target_pairs={{1,0},{2,1},{3,2},{4,3},{5,4},{6,5},{7,6},{8,7},{9,8},{10,9},{11,1... | collective-permute-start | bytes 645128 | tf_op jit(solution)/shard_map/ppermute | solution.py:398
  60.2 2.2 %copy-start.7 = (bf16[2,192,6144]{2,1,0:T(8,128)(2,1)}, bf16[2,192,6144]{2,1,0:T(8,128)(2,1)S(1)}, u32[]{:S(2)}) copy-start(bf16[2,192,6144]{2,1,0:T(8,128)(2,1)S(1)} %hold.11.matrix) | copy-start | bytes 14155780
  62.3 2.3 %copy-start.8 = (bf16[2,192,6144]{2,1,0:T(8,128)(2,1)S(1)}, bf16[2,192,6144]{2,1,0:T(8,128)(2,1)}, u32[]{:S(2)}) copy-start(bf16[2,192,6144]{2,1,0:T(8,128)(2,1)} %copy-done.7) | copy-start | bytes 14155780
  65.2 4.1 %collective-permute-start.11 = (bf16[16,4,192]{2,1,0:T(4,128)(2,1)S(1)}, bf16[16,4,192]{2,1,0:T(4,128)(2,1)S(1)}, u32[]{:S(2)}, u32[]{:S(2)}) collective-permute-start(bf16[16,4,192]{2,1,0:T(4,128)(2,1)S(1)} %get-tuple-element.85), channel_id=1, source_target_pairs={{96,128},{97,129},{98,130},{99,131},{100,132},{101,133},{102,134},... | collective-permute-start | bytes 73736 | tf_op jit(solution)/shard_map/ppermute | solution.py:425
  65.9 3.4 %collective-permute-start.12 = (bf16[16,4,192]{2,1,0:T(4,128)(2,1)S(1)}, bf16[16,4,192]{2,1,0:T(4,128)(2,1)S(1)}, u32[]{:S(2)}, u32[]{:S(2)}) collective-permute-start(bf16[16,4,192]{2,1,0:T(4,128)(2,1)S(1)} %get-tuple-element.85), channel_id=1, source_target_pairs={{96,129},{97,128},{98,131},{99,130},{100,133},{101,132},{102,135},... | collective-permute-start | bytes 73736 | tf_op jit(solution)/shard_map/ppermute | solution.py:424
  69.3 2.3 %copy-start.10 = (bf16[2,192,6144]{2,1,0:T(8,128)(2,1)S(1)}, bf16[2,192,6144]{2,1,0:T(8,128)(2,1)}, u32[]{:S(2)}) copy-start(bf16[2,192,6144]{2,1,0:T(8,128)(2,1)} %copy-done.9) | copy-start | bytes 14155780
  72.3 4.1 %collective-permute-start.13 = (bf16[16,4,192]{2,1,0:T(4,128)(2,1)S(1)}, bf16[16,4,192]{2,1,0:T(4,128)(2,1)S(1)}, u32[]{:S(2)}, u32[]{:S(2)}) collective-permute-start(bf16[16,4,192]{2,1,0:T(4,128)(2,1)S(1)} %get-tuple-element.86), channel_id=1, source_target_pairs={{128,160},{129,161},{130,162},{131,163},{132,164},{133,165},{134,1... | collective-permute-start | bytes 73736 | tf_op jit(solution)/shard_map/ppermute | solution.py:425
  72.9 3.4 %collective-permute-start.14 = (bf16[16,4,192]{2,1,0:T(4,128)(2,1)S(1)}, bf16[16,4,192]{2,1,0:T(4,128)(2,1)S(1)}, u32[]{:S(2)}, u32[]{:S(2)}) collective-permute-start(bf16[16,4,192]{2,1,0:T(4,128)(2,1)S(1)} %get-tuple-element.86), channel_id=1, source_target_pairs={{128,161},{129,160},{130,163},{131,162},{132,165},{133,164},{134,1... | collective-permute-start | bytes 73736 | tf_op jit(solution)/shard_map/ppermute | solution.py:424
  76.3 2.3 %copy-start.12 = (bf16[2,192,6144]{2,1,0:T(8,128)(2,1)S(1)}, bf16[2,192,6144]{2,1,0:T(8,128)(2,1)}, u32[]{:S(2)}) copy-start(bf16[2,192,6144]{2,1,0:T(8,128)(2,1)} %copy-done.11) | copy-start | bytes 14155780
  79.3 4.1 %collective-permute-start.15 = (bf16[16,4,192]{2,1,0:T(4,128)(2,1)S(1)}, bf16[16,4,192]{2,1,0:T(4,128)(2,1)S(1)}, u32[]{:S(2)}, u32[]{:S(2)}) collective-permute-start(bf16[16,4,192]{2,1,0:T(4,128)(2,1)S(1)} %get-tuple-element.87), channel_id=1, source_target_pairs={{160,192},{161,193},{162,194},{163,195},{164,196},{165,197},{166,1... | collective-permute-start | bytes 73736 | tf_op jit(solution)/shard_map/ppermute | solution.py:425
  79.9 3.4 %collective-permute-start.16 = (bf16[16,4,192]{2,1,0:T(4,128)(2,1)S(1)}, bf16[16,4,192]{2,1,0:T(4,128)(2,1)S(1)}, u32[]{:S(2)}, u32[]{:S(2)}) collective-permute-start(bf16[16,4,192]{2,1,0:T(4,128)(2,1)S(1)} %get-tuple-element.87), channel_id=1, source_target_pairs={{160,193},{161,192},{162,195},{163,194},{164,197},{165,196},{166,1... | collective-permute-start | bytes 73736 | tf_op jit(solution)/shard_map/ppermute | solution.py:424
  81.2 2.2 %copy-start.3 = (bf16[2,192,6144]{2,1,0:T(8,128)(2,1)}, bf16[2,192,6144]{2,1,0:T(8,128)(2,1)S(1)}, u32[]{:S(2)}) copy-start(bf16[2,192,6144]{2,1,0:T(8,128)(2,1)S(1)} %hold.8.matrix) | copy-start | bytes 14155780
  83.3 2.3 %copy-start.4 = (bf16[2,192,6144]{2,1,0:T(8,128)(2,1)S(1)}, bf16[2,192,6144]{2,1,0:T(8,128)(2,1)}, u32[]{:S(2)}) copy-start(bf16[2,192,6144]{2,1,0:T(8,128)(2,1)} %copy-done.3) | copy-start | bytes 14155780
  86.3 94.4 %collective-permute-start.17 = (bf16[16,4,192]{2,1,0:T(4,128)(2,1)S(1)}, bf16[16,4,192]{2,1,0:T(4,128)(2,1)S(1)}, u32[]{:S(2)}, u32[]{:S(2)}) collective-permute-start(bf16[16,4,192]{2,1,0:T(4,128)(2,1)S(1)} %get-tuple-element.88), channel_id=1, source_target_pairs={{192,224},{193,225},{194,226},{195,227},{196,228},{197,229},{198,2... | collective-permute-start | bytes 73736 | tf_op jit(solution)/shard_map/ppermute | solution.py:425
  87.6 99.7 %collective-permute-start.18 = (bf16[16,4,192]{2,1,0:T(4,128)(2,1)S(1)}, bf16[16,4,192]{2,1,0:T(4,128)(2,1)S(1)}, u32[]{:S(2)}, u32[]{:S(2)}) collective-permute-start(bf16[16,4,192]{2,1,0:T(4,128)(2,1)S(1)} %get-tuple-element.88), channel_id=1, source_target_pairs={{192,225},{193,224},{194,227},{195,226},{196,229},{197,228},{198,2... | collective-permute-start | bytes 73736 | tf_op jit(solution)/shard_map/ppermute | solution.py:424
  (5 other events, 8.6 us)

commit v4 on v3

--- a/solution.py
+++ b/solution.py
@@ -80,24 +80,22 @@
     )(residual)
 
 
-def hold_kernel(step, place, matrix, held, arrived):
-    @pl.when(place[0] == step)
-    def _():
-        copy = pltpu.make_async_copy(matrix, held, arrived)
-        copy.start()
-        copy.wait()
-
-
-def hold(step, place, matrix):
-    return pl.pallas_call(
-        functools.partial(hold_kernel, step),
+def hold_kernel(matrix, held, arrived):
+    copy = pltpu.make_async_copy(matrix, held, arrived)
+    copy.start()
+    copy.wait()
+
+
+def hold(matrix):
+    return pl.pallas_call(
+        hold_kernel,
         out_shape=pltpu.VMEM(matrix.shape, matrix.dtype),
-        in_specs=[pl.BlockSpec(memory_space=pltpu.SMEM), pl.BlockSpec(memory_space=pltpu.HBM)],
+        in_specs=[pl.BlockSpec(memory_space=pltpu.HBM)],
         out_specs=pl.BlockSpec(memory_space=VMEM),
         scratch_shapes=[pltpu.SemaphoreType.DMA],
         compiler_params=limit(1),
         name="hold",
-    )(place, matrix)
+    )(matrix)
 
 
 def ordered(vector, same, other, first_end):
@@ -109,10 +107,12 @@
         vector[:, at + cells : at + 2 * cells] = jnp.where(first_end, far, own)
 
 
-def hand_on(by_re, by_im, next_rhs, kept, spread):
+def combined(by_re, by_im):
     shots = by_re.shape[0] // 2
-    solved = jnp.concatenate([by_re[:shots] - by_im[shots:], by_re[shots:] + by_im[:shots]], axis=0)
-    kept[...] = solved
+    return jnp.concatenate([by_re[:shots] - by_im[shots:], by_re[shots:] + by_im[:shots]], axis=0)
+
+
+def hand_on(solved, next_rhs, spread):
     out = (next_rhs[...] + coupling * solved).astype(bf16)
     for column in range(spread.shape[0]):
         spread[column] = out
@@ -142,7 +142,9 @@
         for side in range(2):
             product = times(part, held[side, :, columns[piece]])
             by[side] = product if by[side] is None else by[side] + product
-    hand_on(by[0], by[1], next_rhs, kept, spread)
+    solved = combined(by[0], by[1])
+    kept[...] = solved
+    hand_on(solved, next_rhs, spread)
 
 
 def solve_first(matrix, gathered, next_rhs):
@@ -166,19 +168,15 @@
     )(matrix, gathered, next_rhs)
 
 
-def layer_kernel(step, place, matrix, same, other, next_rhs, kept_before, kept, spread, vector):
-    @pl.when(place[0] == step)
-    def _():
-        ordered(vector, same, other, place[1] == 0)
-        full = vector[...]
-        hand_on(times(full, matrix[0]), times(full, matrix[1]), next_rhs, kept, spread)
-
-    @pl.when(place[0] != step)
-    def _():
-        kept[...] = kept_before[...]
-
-
-def solve_layer(step, place, matrix, same, other, next_rhs, kept):
+def layer_kernel(step, matrix, same, other, next_rhs, kept_before, kept, spread, vector):
+    ordered(vector, same, other, lax.axis_index("row") % 2 == 0)
+    full = vector[...]
+    solved = combined(times(full, matrix[0]), times(full, matrix[1]))
+    kept[...] = jnp.where(lax.axis_index("layer") == step, solved, kept_before[...])
+    hand_on(solved, next_rhs, spread)
+
+
+def solve_layer(step, matrix, same, other, next_rhs, kept):
     columns, lines, cells = same.shape
     return pl.pallas_call(
         functools.partial(layer_kernel, step),
@@ -186,12 +184,12 @@
             jax.ShapeDtypeStruct((lines, cells), f32),
             jax.ShapeDtypeStruct((columns, lines, cells), bf16),
         ),
-        in_specs=[pl.BlockSpec(memory_space=pltpu.SMEM)] + [pl.BlockSpec(memory_space=VMEM)] * 5,
+        in_specs=[pl.BlockSpec(memory_space=VMEM)] * 5,
         scratch_shapes=[pltpu.VMEM((lines, 2 * columns * cells), bf16)],
         compiler_params=limit(3),
         cost_estimate=pl.CostEstimate(flops=4 * matrix.size, bytes_accessed=2 * matrix.size, transcendentals=0),
         name="solve_layer",
-    )(place, matrix, same, other, next_rhs, kept)
+    )(matrix, same, other, next_rhs, kept)
 
 
 def smooth_kernel(inside, residual, wavenumber, row_low, row_high, deep_low, deep_high, smoothed, gain, source, first, second):
@@ -328,29 +326,74 @@
     )(inside, residual, wavenumber, row_low, row_high, deep_low, deep_high)
 
 
-def lift_kernel(smoothed, coarse, out):
+def lifted(smoothed, coarse, out, fine, wide, arrived, left, before=None):
     shots, _, depth, height, width = smoothed.shape
     strips, across = height // QY, width // PX
-    pick = membership(width, across)
-    lines = [coarse[:, strip * across : (strip + 1) * across] for strip in range(strips)]
-    wide = exact_dot(jnp.concatenate(lines, axis=0), pick, 1)
-    for part in range(2):
-        for shot in range(shots):
-            for strip in range(strips):
-                at = strip * 2 * shots + part * shots + shot
-                value = jnp.broadcast_to(wide[at : at + 1, :], (QY, width))
+    blocks = [(shot, part) for part in range(2) for shot in range(shots)]
+    comes = [
+        pltpu.make_async_copy(smoothed.at[block], fine.at[at], arrived.at[at]) for at, block in enumerate(blocks)
+    ]
+    goes = [pltpu.make_async_copy(fine.at[at], out.at[block], left.at[at]) for at, block in enumerate(blocks)]
+    for copy in comes:
+        copy.start()
+    if before is not None:
+        before()
+    values = coarse[...]
+    lines = [values[:, strip * across : (strip + 1) * across] for strip in range(strips)]
+    wide[...] = exact_dot(jnp.concatenate(lines, axis=0), membership(width, across), 1)
+    for at in range(len(blocks)):
+        comes[at].wait()
+        for strip in range(strips):
+            line = strip * 2 * shots + at
+            value = jnp.broadcast_to(wide[line : line + 1, :], (QY, width))
+            for plane in range(depth):
                 rows = slice(strip * QY, (strip + 1) * QY)
-                for plane in range(depth):
-                    out[shot, part, plane, rows, :] = smoothed[shot, part, plane, rows, :] + value
-
-
-def lift(smoothed, coarse):
-    return pl.pallas_call(
-        lift_kernel,
-        out_shape=jax.ShapeDtypeStruct(smoothed.shape, f32),
-        compiler_params=limit(8),
+                fine[at, plane, rows, :] = fine[at, plane, rows, :] + value
+        goes[at].start()
+    for copy in goes:
+        copy.wait()
+
+
+def lift_kernel(smoothed, coarse, out, fine, wide, arrived, left):
+    lifted(smoothed, coarse, out, fine, wide, arrived, left)
+
+
+def last_kernel(step, smoothed, kept_before, matrix, same, other, out, fine, wide, arrived, left, vector, coarse):
+    def product():
+        coarse[...] = kept_before[...]
+
+        @pl.when(lax.axis_index("layer") == step)
+        def _():
+            ordered(vector, same, other, lax.axis_index("row") % 2 == 0)
+            full = vector[...]
+            coarse[...] = combined(times(full, matrix[0]), times(full, matrix[1]))
+
+    lifted(smoothed, coarse, out, fine, wide, arrived, left, product)
+
+
+def lift(smoothed, kept, step=None, *operands):
+    shots, _, depth, height, width = smoothed.shape
+    lines, cells = kept.shape
+    scratch = [
+        pltpu.VMEM((2 * shots, depth, height, width), f32),
+        pltpu.VMEM((height // QY * lines, width), f32),
+        pltpu.SemaphoreType.DMA((2 * shots,)),
+        pltpu.SemaphoreType.DMA((2 * shots,)),
+    ]
+    kernel = lift_kernel
+    if operands:
+        columns = operands[1].shape[0]
+        kernel = functools.partial(last_kernel, step)
+        scratch += [pltpu.VMEM((lines, 2 * columns * cells), bf16), pltpu.VMEM((lines, cells), f32)]
+    return pl.pallas_call(
+        kernel,
+        out_shape=pltpu.HBM(smoothed.shape, f32),
+        in_specs=[pl.BlockSpec(memory_space=pltpu.HBM)] + [pl.BlockSpec(memory_space=VMEM)] * (1 + len(operands)),
+        out_specs=pl.BlockSpec(memory_space=pltpu.HBM),
+        scratch_shapes=scratch,
+        compiler_params=limit(5),
         name="lift",
-    )(smoothed, coarse)
+    )(smoothed, kept, *operands)
 
 
 def pack_planes_kernel(residual, wavenumber, first, last):
@@ -401,7 +444,6 @@
 def every_layer(residual, wavenumber, inverse):
     layers, devices = lax.axis_size("layer"), lax.axis_size("row")
     layer, row = lax.axis_index("layer"), lax.axis_index("row")
-    place = jnp.stack([layer, row & 1]).astype(jnp.int32)
     inside = jnp.stack([layer > 0, layer < layers - 1, row > 0, row < devices - 1]).astype(f32)
 
     rhs, spread = restrict(residual, devices)
@@ -411,27 +453,68 @@
     kept, spread = solve_first(matrix, gathered, next_rhs)
 
     ends = [[2 * column + end for column in range(devices // 2)] for end in range(2)]
-    for step in range(1, layers):
-        half = lax.cond(
-            layer == step - 1,
+
+    def gather(step, spread):
+        return lax.cond(
+            layer == step,
             lambda blocks: lax.all_to_all(blocks, "row", 0, 0, axis_index_groups=ends, tiled=True),
             lambda blocks: blocks,
             spread,
         )
-        ways = [
-            [((step - 1) * devices + i, step * devices + (i ^ flip)) for i in range(devices)] for flip in range(2)
-        ]
-        other = lax.ppermute(half, ("layer", "row"), ways[1])
-        same = lax.ppermute(half, ("layer", "row"), ways[0])
-        held = hold(step, place, matrix)
-        kept, spread = solve_layer(step, place, held, same, other, next_rhs, kept)
+
+    def swap(step, half):
+        found = []
+        for flip in (1, 0):
+            way = [
+                (i * devices + j, (i ^ (step - 1) ^ step) * devices + (j ^ flip))
+                for i in range(layers)
+                for j in range(devices)
+            ]
+            found.append(lax.ppermute(half, ("layer", "row"), way))
+        return found
+
+    def send(step, half):
+        found = []
+        for flip in (1, 0):
+            way = [((step - 1) * devices + j, step * devices + (j ^ flip)) for j in range(devices)]
+            found.append(lax.ppermute(half, ("layer", "row"), way))
+        return found
+
+    def solve(step, other, same, kept):
+        held = hold(matrix)
+        return solve_layer(step, held, same, other, next_rhs, kept)
+
+    middle = layers // 2
+    for step in range(1, layers - 1):
+        half = gather(step - 1, spread)
+        if step == middle:
+            kept, spread = solve(step, *send(step, half), kept)
+            continue
+        kept, spread = lax.cond(
+            (layer == step - 1) | (layer == step),
+            lambda half, kept, step=step: tuple(solve(step, *swap(step, half), kept)),
+            lambda half, kept: (kept, half),
+            half,
+            kept,
+        )
 
     first, last = pack_planes(residual, wavenumber)
     below, above = both_ways(first, last, "layer")
     first, last = pack_rows(residual, wavenumber, below, above)
     row_low, row_high = both_ways(first, last, "row")
     smoothed = smooth(inside, residual, wavenumber, row_low, row_high, below, above)
-    return lift(smoothed, kept)
+
+    step = layers - 1
+    half = gather(step - 1, spread)
+
+    def finish(half, smoothed, kept):
+        other, same = swap(step, half)
+        held = hold(matrix)
+        return lift(smoothed, kept, step, held, same, other)
+
+    return lax.cond(
+        layer >= step - 1, finish, lambda half, smoothed, kept: lift(smoothed, kept), half, smoothed, kept
+    )
 
 
 def solution(mesh):

time: 205 us -> 190 us (0.927)
  the two profiles are of different devices: /device:TPU:225 before, /device:TPU:96 now
where the time goes in v4:
time: 190 us; the launch traced here: 189 us
  starting transfers between devices  118 us (62%)
  Pallas kernels  29.3 us (15%)
  waiting for transfers between devices  22.1 us (12%)
  blocking collectives  10.7 us (6%)
  local copies, waits for them, and re-layouts  8.2 us (4%)
    ppermute x4, starting transfers between devices, swap(): found.append(lax.ppermute(half, ('layer', 'row'), way))  86 us
    all_to_all x1, starting transfers between devices, every_layer(): gathered = lax.all_to_all(spread, 'row', 0, 0, tiled=True)  13.8 us
    pallas_call x1, Pallas kernels, smooth(): pl.pallas_call(smooth_kernel, out_shape=jax.ShapeDtypeStruct(residual.sha...  12.8 us
    all_to_all x1, blocking collectives, gather(): lax.all_to_all(blocks, 'row', 0, 0, axis_index_groups=ends, tiled=True)  10.7 us
    all_to_all x1, waiting for transfers between devices, every_layer(): gathered = lax.all_to_all(spread, 'row', 0, 0, tiled=True)  8.96 us
    ppermute x2, starting transfers between devices, both_ways(): lax.ppermute(high_block, axis, up)  8.89 us
    unnamed x16, local copies, waits for them, and re-layouts  8.19 us
    pallas_call x3, Pallas kernels, hold(): pl.pallas_call(hold_kernel, out_shape=pltpu.VMEM(matrix.shape, matrix.dty...  7.04 us
  transfers between devices with their start and end apart: 12, of which 6 were waited for; matrix products, arithmetic and copies ran while one was open for 0% of the time, Pallas kernels for 7%

profile of v4, /device:TPU:96, one launch (start us, length us, event | category | flops | bytes accessed | tf_op | source)
XLA Modules:
  0.0 189.1 jit_solution(10999266056200887955)
XLA Ops:
  0.0 1.6 copy-done
  1.6 1.0 copy-done.4
  2.7 2.1 %collective-permute-start.12 = (bf16[5,3,64,192]{3,2,1,0:T(8,128)(2,1)S(1)}, bf16[5,3,64,192]{3,2,1,0:T(8,128)(2,1)S(1)}, u32[]{:S(2)}, u32[]{:S(2)}) collective-permute-start(bf16[5,3,64,192]{3,2,1,0:T(8,128)(2,1)S(1)} %get-tuple-element.186), channel_id=1, source_target_pairs={{0,32},{32,64},{64,96},{96,128},{128,160},{160,192},{192,224},{1,3... | collective-permute-start | bytes 1105928 | tf_op jit(solution)/shard_map/ppermute | solution.py:441
  4.8 3.6 %collective-permute-start.13 = (bf16[5,3,64,192]{3,2,1,0:T(8,128)(2,1)S(1)}, bf16[5,3,64,192]{3,2,1,0:T(8,128)(2,1)S(1)}, u32[]{:S(2)}, u32[]{:S(2)}) collective-permute-start(bf16[5,3,64,192]{3,2,1,0:T(8,128)(2,1)S(1)} %get-tuple-element.187), channel_id=1, source_target_pairs={{32,0},{64,32},{96,64},{128,96},{160,128},{192,160},{224,192},{33,... | collective-permute-start | bytes 1105928 | tf_op jit(solution)/shard_map/ppermute | solution.py:441
  8.4 4.6 %collective-permute-done.12.below.deep_low = bf16[5,3,64,192]{3,2,1,0:T(8,128)(2,1)S(1)} collective-permute-done((bf16[5,3,64,192]{3,2,1,0:T(8,128)(2,1)S(1)}, bf16[5,3,64,192]{3,2,1,0:T(8,128)(2,1)S(1)}, u32[]{:S(2)}, u32[]{:S(2)}) %collective-permute-start.12) | collective-permute-done | bytes 368672 | tf_op jit(solution)/shard_map/ppermute | solution.py:441
  13.0 1.8 collective-permute-done.13.above.deep_high
  14.8 1.0 pack_rows.1
  15.8 6.8 %collective-permute-start.14 = (bf16[5,14,8,192]{3,2,1,0:T(8,128)(2,1)}, bf16[5,14,8,192]{3,2,1,0:T(8,128)(2,1)S(1)}, u32[]{:S(2)}, u32[]{:S(2)}) collective-permute-start(bf16[5,14,8,192]{3,2,1,0:T(8,128)(2,1)} %get-tuple-element.188), channel_id=1, source_target_pairs={{0,1},{1,2},{2,3},{3,4},{4,5},{5,6},{6,7},{7,8},{8,9},{9,10},{10,1... | collective-permute-start | bytes 645128 | tf_op jit(solution)/shard_map/ppermute | solution.py:441
  22.6 1.3 collective-permute-start.15
  23.9 1.0 restrict.1
  24.9 13.8 %all-to-all-start.7 = ((bf16[32,4,192]{2,1,0:T(4,128)(2,1)}), bf16[32,4,192]{2,1,0:T(4,128)(2,1)S(1)}, u32[]{:S(2)}, u32[]{:S(2)}) async-start(bf16[32,4,192]{2,1,0:T(4,128)(2,1)} %get-tuple-element.190), calls=%async_computation.7 | async-start | bytes 131072 | tf_op jit(solution)/shard_map/all_to_all | solution.py:452
  38.8 3.0 %collective-permute-start.16 = (f32[4,192]{1,0:T(4,128)S(1)}, f32[4,192]{1,0:T(4,128)S(1)}, u32[]{:S(2)}, u32[]{:S(2)}) collective-permute-start(f32[4,192]{1,0:T(4,128)S(1)} %get-tuple-element.191), channel_id=1, source_target_pairs={{32,0},{64,32},{96,64},{128,96},{160,128},{192,160},{224,192},{33,... | collective-permute-start | bytes 9224 | tf_op jit(solution)/shard_map/ppermute | solution.py:450
  41.8 3.8 %collective-permute-done.16.next_rhs = f32[4,192]{1,0:T(4,128)S(1)} collective-permute-done((f32[4,192]{1,0:T(4,128)S(1)}, f32[4,192]{1,0:T(4,128)S(1)}, u32[]{:S(2)}, u32[]{:S(2)}) %collective-permute-start.16) | collective-permute-done | bytes 3104 | tf_op jit(solution)/shard_map/ppermute | solution.py:450
  45.6 9.0 %all-to-all-done.7.gathered = bf16[32,4,192]{2,1,0:T(4,128)(2,1)S(1)} async-done(((bf16[32,4,192]{2,1,0:T(4,128)(2,1)}), bf16[32,4,192]{2,1,0:T(4,128)(2,1)S(1)}, u32[]{:S(2)}, u32[]{:S(2)}) %all-to-all-start.7) | async-done | bytes 49184 | tf_op jit(solution)/shard_map/all_to_all | solution.py:452
  54.6 2.8 %solve_first.1 = (f32[4,192]{1,0:T(4,128)S(1)}, bf16[16,4,192]{2,1,0:T(4,128)(2,1)S(1)}) custom-call(bf16[2,192,6144]{2,1,0:T(8,128)(2,1)} %bitcast.5, bf16[32,4,192]{2,1,0:T(4,128)(2,1)S(1)} %all-to-all-done.7.gathered, f32[4,192]{1,0:T(4,128)S(1)} %collective-permute-done.16.next_rhs), custom_call_target="tpu_custom_call" | custom-call | flops 9437184 | bytes 4718592 | tf_op jit(solution)/shard_map/solve_first/pallas_call | solution.py:153
  58.9 2.3 %hold.13.matrix = bf16[2,192,6144]{2,1,0:T(8,128)(2,1)S(1)} custom-call(bf16[2,192,6144]{2,1,0:T(8,128)(2,1)} %bitcast.9), custom_call_target="tpu_custom_call" | custom-call | tf_op jit(solution)/shard_map/hold/pallas_call | solution.py:90
  61.3 2.2 %copy-done.2 = bf16[2,192,6144]{2,1,0:T(8,128)(2,1)} copy-done((bf16[2,192,6144]{2,1,0:T(8,128)(2,1)}, bf16[2,192,6144]{2,1,0:T(8,128)(2,1)S(1)}, u32[]{:S(2)}) %copy-start.2) | copy-done | bytes 4718616
  63.5 2.3 %copy-done.3 = bf16[2,192,6144]{2,1,0:T(8,128)(2,1)S(1)} copy-done((bf16[2,192,6144]{2,1,0:T(8,128)(2,1)S(1)}, bf16[2,192,6144]{2,1,0:T(8,128)(2,1)}, u32[]{:S(2)}) %copy-start.3) | copy-done | bytes 4718616
  65.8 1.4 solve_layer.11
  67.4 87.7 %conditional.23 = ((f32[4,192]{1,0:T(4,128)S(1)}, bf16[16,4,192]{2,1,0:T(4,128)(2,1)S(1)})) conditional(s32[]{:T(128)} %convert_element_type.44, (f32[4,192]{1,0:T(4,128)S(1)}, bf16[16,4,192]{2,1,0:T(4,128)(2,1)S(1)}) %tuple.111, (bf16[2,192,6144]{2,1,0:T(8,128)(2,1)}, bf16[16,4,192]{2,1,0:T(4,128)(2,1)S(1)}, f32[4,192]{1,0:T(4,128)S(1)}, ...), branch_computations={%region_20.0_spmd, %region_21.0_spmd} | conditional | flops 9437184 | bytes 4921432 | solution.py:493
  67.4 83.0 %collective-permute-start.9 = (bf16[16,4,192]{2,1,0:T(4,128)(2,1)S(1)}, bf16[16,4,192]{2,1,0:T(4,128)(2,1)S(1)}, u32[]{:S(2)}, u32[]{:S(2)}) collective-permute-start(bf16[16,4,192]{2,1,0:T(4,128)(2,1)S(1)} %get-tuple-element.157), channel_id=1, source_target_pairs={{0,97},{1,96},{2,99},{3,98},{4,101},{5,100},{6,103},{7,102},{8,105... | collective-permute-start | bytes 73736 | tf_op jit(solution)/shard_map/cond/branch_1_fun/ppermute | solution.py:473
  150.5 2.3 %hold.11.matrix = bf16[2,192,6144]{2,1,0:T(8,128)(2,1)S(1)} custom-call(bf16[2,192,6144]{2,1,0:T(8,128)(2,1)} %get-tuple-element.156.matrix), custom_call_target="tpu_custom_call" | custom-call | tf_op jit(solution)/shard_map/cond/branch_1_fun/hold/pallas_call | solution.py:90
  153.8 1.4 solve_layer.10
  155.2 10.8 %conditional.24 = (bf16[16,4,192]{2,1,0:T(4,128)(2,1)S(1)}) conditional(s32[]{:T(128)} %convert_element_type.55, bf16[16,4,192]{2,1,0:T(4,128)(2,1)S(1)} %get-tuple-element.205, bf16[16,4,192]{2,1,0:T(4,128)(2,1)S(1)} %get-tuple-element.205), branch_computations={%region_22.0_spmd, %region_23.0_spmd} | conditional | bytes 98312 | solution.py:458
  155.2 10.7 %all_to_all.39 = bf16[16,4,192]{2,1,0:T(4,128)(2,1)S(1)} all-to-all(bf16[16,4,192]{2,1,0:T(4,128)(2,1)S(1)} %copy.58), channel_id=1, replica_groups={{0,2,4,6,8,10,12,14,16,18,20,22,24,26,28,30},{1,3,5,7,9,11,13,15,17,19,..., dimensions={0} | all-to-all | bytes 49152 | tf_op jit(solution)/shard_map/cond/branch_1_fun/all_to_all | solution.py:460
  166.0 1.0 copy-done.7
  167.0 12.8 %smooth.1 = f32[2,2,8,64,192]{4,3,2,1,0:T(8,128)S(1)} custom-call(f32[4]{0:T(128)S(1)} %add_convert_fusion.inside, f32[2,2,8,64,192]{4,3,2,1,0:T(8,128)S(1)} %copy-done.1, f32[8,64,192]{2,1,0:T(8,128)S(1)} %copy-done.5, bf16[5,14,8,192]{3,2,1,0:T(8,128)(2,1)S(1)} %collective-permute-done.14.row_low, ...), custom_call_target="tpu_custom_call" | custom-call | flops 117964800 | bytes 4718592 | tf_op jit(solution)/shard_map/smooth/pallas_call | solution.py:318
  179.7 9.2 %conditional.25 = (f32[2,2,8,64,192]{4,3,2,1,0:T(8,128)}) conditional(s32[]{:T(128)} %convert_element_type.42, (f32[2,2,8,64,192]{4,3,2,1,0:T(8,128)S(1)}, f32[4,192]{1,0:T(4,128)S(1)}) %tuple.113, (bf16[2,192,6144]{2,1,0:T(8,128)(2,1)}, bf16[16,4,192]{2,1,0:T(4,128)(2,1)S(1)}, f32[2,2,8,64,192]{4,3,2,1,0:T(8,128)S(1)}, ...), branch_computations={%region_24.0_spmd, %region_25.0_spmd} | conditional | bytes 196696 | solution.py:515
  179.9 2.9 %collective-permute-start.10 = (bf16[16,4,192]{2,1,0:T(4,128)(2,1)S(1)}, bf16[16,4,192]{2,1,0:T(4,128)(2,1)S(1)}, u32[]{:S(2)}, u32[]{:S(2)}) collective-permute-start(bf16[16,4,192]{2,1,0:T(4,128)(2,1)S(1)} %get-tuple-element.165), channel_id=1, source_target_pairs={{0,32},{1,33},{2,34},{3,35},{4,36},{5,37},{6,38},{7,39},{8,40},{9,... | collective-permute-start | bytes 73736 | tf_op jit(solution)/shard_map/cond/branch_1_fun/ppermute | solution.py:473
  182.7 2.3 %hold.12.matrix = bf16[2,192,6144]{2,1,0:T(8,128)(2,1)S(1)} custom-call(bf16[2,192,6144]{2,1,0:T(8,128)(2,1)} %get-tuple-element.164.matrix), custom_call_target="tpu_custom_call" | custom-call | tf_op jit(solution)/shard_map/cond/branch_1_fun/hold/pallas_call | solution.py:90
  185.1 2.0 %collective-permute-done.11.other = bf16[16,4,192]{2,1,0:T(4,128)(2,1)S(1)} collective-permute-done((bf16[16,4,192]{2,1,0:T(4,128)(2,1)S(1)}, bf16[16,4,192]{2,1,0:T(4,128)(2,1)S(1)}, u32[]{:S(2)}, u32[]{:S(2)}) %collective-permute-start.11) | collective-permute-done | bytes 24608 | tf_op jit(solution)/shard_map/cond/branch_1_fun/ppermute | solution.py:473
  187.1 1.8 lift.3
  (36 shorter events, 2.9 us)
Async XLA Ops:
  0.0 1.6 copy-start
  1.6 1.0 copy-start.4
  2.6 21.3 %copy-start.1 = (f32[2,2,8,64,192]{4,3,2,1,0:T(8,128)S(1)}, f32[2,2,8,64,192]{4,3,2,1,0:T(8,128)}, u32[]{:S(2)}) copy-start(f32[2,2,8,64,192]{4,3,2,1,0:T(8,128)} %residual.7) | copy-start | bytes 4718596
  2.7 10.3 %collective-permute-start.12 = (bf16[5,3,64,192]{3,2,1,0:T(8,128)(2,1)S(1)}, bf16[5,3,64,192]{3,2,1,0:T(8,128)(2,1)S(1)}, u32[]{:S(2)}, u32[]{:S(2)}) collective-permute-start(bf16[5,3,64,192]{3,2,1,0:T(8,128)(2,1)S(1)} %get-tuple-element.186), channel_id=1, source_target_pairs={{0,32},{32,64},{64,96},{96,128},{128,160},{160,192},{192,224},{1,3... | collective-permute-start | bytes 1105928 | tf_op jit(solution)/shard_map/ppermute | solution.py:441
  4.8 10.0 %collective-permute-start.13 = (bf16[5,3,64,192]{3,2,1,0:T(8,128)(2,1)S(1)}, bf16[5,3,64,192]{3,2,1,0:T(8,128)(2,1)S(1)}, u32[]{:S(2)}, u32[]{:S(2)}) collective-permute-start(bf16[5,3,64,192]{3,2,1,0:T(8,128)(2,1)S(1)} %get-tuple-element.187), channel_id=1, source_target_pairs={{32,0},{64,32},{96,64},{128,96},{160,128},{192,160},{224,192},{33,... | collective-permute-start | bytes 1105928 | tf_op jit(solution)/shard_map/ppermute | solution.py:441
  14.8 1.0 copy-start.6
  15.8 150.2 %collective-permute-start.14 = (bf16[5,14,8,192]{3,2,1,0:T(8,128)(2,1)}, bf16[5,14,8,192]{3,2,1,0:T(8,128)(2,1)S(1)}, u32[]{:S(2)}, u32[]{:S(2)}) collective-permute-start(bf16[5,14,8,192]{3,2,1,0:T(8,128)(2,1)} %get-tuple-element.188), channel_id=1, source_target_pairs={{0,1},{1,2},{2,3},{3,4},{4,5},{5,6},{6,7},{7,8},{8,9},{9,10},{10,1... | collective-permute-start | bytes 645128 | tf_op jit(solution)/shard_map/ppermute | solution.py:441
  22.6 143.3 %collective-permute-start.15 = (bf16[5,14,8,192]{3,2,1,0:T(8,128)(2,1)}, bf16[5,14,8,192]{3,2,1,0:T(8,128)(2,1)}, u32[]{:S(2)}, u32[]{:S(2)}) collective-permute-start(bf16[5,14,8,192]{3,2,1,0:T(8,128)(2,1)} %get-tuple-element.189), channel_id=1, source_target_pairs={{1,0},{2,1},{3,2},{4,3},{5,4},{6,5},{7,6},{8,7},{9,8},{10,9},{11,1... | collective-permute-start | bytes 645128 | tf_op jit(solution)/shard_map/ppermute | solution.py:441
  24.9 29.6 %all-to-all-start.7 = ((bf16[32,4,192]{2,1,0:T(4,128)(2,1)}), bf16[32,4,192]{2,1,0:T(4,128)(2,1)S(1)}, u32[]{:S(2)}, u32[]{:S(2)}) async-start(bf16[32,4,192]{2,1,0:T(4,128)(2,1)} %get-tuple-element.190), calls=%async_computation.7 | async-start | bytes 131072 | tf_op jit(solution)/shard_map/all_to_all | solution.py:452
  38.8 6.8 %collective-permute-start.16 = (f32[4,192]{1,0:T(4,128)S(1)}, f32[4,192]{1,0:T(4,128)S(1)}, u32[]{:S(2)}, u32[]{:S(2)}) collective-permute-start(f32[4,192]{1,0:T(4,128)S(1)} %get-tuple-element.191), channel_id=1, source_target_pairs={{32,0},{64,32},{96,64},{128,96},{160,128},{192,160},{224,192},{33,... | collective-permute-start | bytes 9224 | tf_op jit(solution)/shard_map/ppermute | solution.py:450
  57.5 6.0 %collective-permute-start.18 = (bf16[16,4,192]{2,1,0:T(4,128)(2,1)S(1)}, bf16[16,4,192]{2,1,0:T(4,128)(2,1)S(1)}, u32[]{:S(2)}, u32[]{:S(2)}) collective-permute-start(bf16[16,4,192]{2,1,0:T(4,128)(2,1)S(1)} %get-tuple-element.235), channel_id=1, source_target_pairs={{96,129},{97,128},{98,131},{99,130},{100,133},{101,132},{102,135},... | collective-permute-start | bytes 73736 | tf_op jit(solution)/shard_map/ppermute | solution.py:480
  58.2 5.3 %collective-permute-start.17 = (bf16[16,4,192]{2,1,0:T(4,128)(2,1)S(1)}, bf16[16,4,192]{2,1,0:T(4,128)(2,1)S(1)}, u32[]{:S(2)}, u32[]{:S(2)}) collective-permute-start(bf16[16,4,192]{2,1,0:T(4,128)(2,1)S(1)} %get-tuple-element.235), channel_id=1, source_target_pairs={{96,128},{97,129},{98,130},{99,131},{100,132},{101,133},{102,134},... | collective-permute-start | bytes 73736 | tf_op jit(solution)/shard_map/ppermute | solution.py:480
  61.3 2.2 %copy-start.2 = (bf16[2,192,6144]{2,1,0:T(8,128)(2,1)}, bf16[2,192,6144]{2,1,0:T(8,128)(2,1)S(1)}, u32[]{:S(2)}) copy-start(bf16[2,192,6144]{2,1,0:T(8,128)(2,1)S(1)} %hold.13.matrix) | copy-start | bytes 14155780
  63.5 2.3 %copy-start.3 = (bf16[2,192,6144]{2,1,0:T(8,128)(2,1)S(1)}, bf16[2,192,6144]{2,1,0:T(8,128)(2,1)}, u32[]{:S(2)}) copy-start(bf16[2,192,6144]{2,1,0:T(8,128)(2,1)} %copy-done.2) | copy-start | bytes 14155780
  67.4 98.5 %copy-start.5 = (f32[8,64,192]{2,1,0:T(8,128)S(1)}, f32[8,64,192]{2,1,0:T(8,128)}, u32[]{:S(2)}) copy-start(f32[8,64,192]{2,1,0:T(8,128)} %wavenumber.5) | copy-start | bytes 1179652
  67.4 85.4 %collective-permute-start.9 = (bf16[16,4,192]{2,1,0:T(4,128)(2,1)S(1)}, bf16[16,4,192]{2,1,0:T(4,128)(2,1)S(1)}, u32[]{:S(2)}, u32[]{:S(2)}) collective-permute-start(bf16[16,4,192]{2,1,0:T(4,128)(2,1)S(1)} %get-tuple-element.157), channel_id=1, source_target_pairs={{0,97},{1,96},{2,99},{3,98},{4,101},{5,100},{6,103},{7,102},{8,105... | collective-permute-start | bytes 73736 | tf_op jit(solution)/shard_map/cond/branch_1_fun/ppermute | solution.py:473
  150.5 3.3 %collective-permute-start.8 = (bf16[16,4,192]{2,1,0:T(4,128)(2,1)S(1)}, bf16[16,4,192]{2,1,0:T(4,128)(2,1)S(1)}, u32[]{:S(2)}, u32[]{:S(2)}) collective-permute-start(bf16[16,4,192]{2,1,0:T(4,128)(2,1)S(1)} %get-tuple-element.157), channel_id=1, source_target_pairs={{0,96},{1,97},{2,98},{3,99},{4,100},{5,101},{6,102},{7,103},{8,104... | collective-permute-start | bytes 73736 | tf_op jit(solution)/shard_map/cond/branch_1_fun/ppermute | solution.py:473
  166.0 1.0 copy-start.7
  179.8 7.3 %collective-permute-start.11 = (bf16[16,4,192]{2,1,0:T(4,128)(2,1)S(1)}, bf16[16,4,192]{2,1,0:T(4,128)(2,1)S(1)}, u32[]{:S(2)}, u32[]{:S(2)}) collective-permute-start(bf16[16,4,192]{2,1,0:T(4,128)(2,1)S(1)} %get-tuple-element.165), channel_id=1, source_target_pairs={{0,33},{1,32},{2,35},{3,34},{4,37},{5,36},{6,39},{7,38},{8,41},{9,... | collective-permute-start | bytes 73736 | tf_op jit(solution)/shard_map/cond/branch_1_fun/ppermute | solution.py:473
  179.9 7.2 %collective-permute-start.10 = (bf16[16,4,192]{2,1,0:T(4,128)(2,1)S(1)}, bf16[16,4,192]{2,1,0:T(4,128)(2,1)S(1)}, u32[]{:S(2)}, u32[]{:S(2)}) collective-permute-start(bf16[16,4,192]{2,1,0:T(4,128)(2,1)S(1)} %get-tuple-element.165), channel_id=1, source_target_pairs={{0,32},{1,33},{2,34},{3,35},{4,36},{5,37},{6,38},{7,39},{8,40},{9,... | collective-permute-start | bytes 73736 | tf_op jit(solution)/shard_map/cond/branch_1_fun/ppermute | solution.py:473

commit v5 on v4

--- a/solution.py
+++ b/solution.py
@@ -80,15 +80,17 @@
     )(residual)
 
 
-def hold_kernel(matrix, held, arrived):
-    copy = pltpu.make_async_copy(matrix, held, arrived)
-    copy.start()
-    copy.wait()
-
-
-def hold(matrix):
-    return pl.pallas_call(
-        hold_kernel,
+def hold_kernel(step, matrix, held, arrived):
+    @pl.when(lax.axis_index("layer") == step)
+    def _():
+        copy = pltpu.make_async_copy(matrix, held, arrived)
+        copy.start()
+        copy.wait()
+
+
+def hold(step, matrix):
+    return pl.pallas_call(
+        functools.partial(hold_kernel, step),
         out_shape=pltpu.VMEM(matrix.shape, matrix.dtype),
         in_specs=[pl.BlockSpec(memory_space=pltpu.HBM)],
         out_specs=pl.BlockSpec(memory_space=VMEM),
@@ -326,49 +328,39 @@
     )(inside, residual, wavenumber, row_low, row_high, deep_low, deep_high)
 
 
-def lifted(smoothed, coarse, out, fine, wide, arrived, left, before=None):
+def lifted(smoothed, values, out, fine, wide, left):
     shots, _, depth, height, width = smoothed.shape
     strips, across = height // QY, width // PX
     blocks = [(shot, part) for part in range(2) for shot in range(shots)]
-    comes = [
-        pltpu.make_async_copy(smoothed.at[block], fine.at[at], arrived.at[at]) for at, block in enumerate(blocks)
-    ]
     goes = [pltpu.make_async_copy(fine.at[at], out.at[block], left.at[at]) for at, block in enumerate(blocks)]
-    for copy in comes:
-        copy.start()
-    if before is not None:
-        before()
-    values = coarse[...]
     lines = [values[:, strip * across : (strip + 1) * across] for strip in range(strips)]
     wide[...] = exact_dot(jnp.concatenate(lines, axis=0), membership(width, across), 1)
-    for at in range(len(blocks)):
-        comes[at].wait()
+    for at, (shot, part) in enumerate(blocks):
         for strip in range(strips):
             line = strip * 2 * shots + at
             value = jnp.broadcast_to(wide[line : line + 1, :], (QY, width))
             for plane in range(depth):
                 rows = slice(strip * QY, (strip + 1) * QY)
-                fine[at, plane, rows, :] = fine[at, plane, rows, :] + value
+                fine[at, plane, rows, :] = smoothed[shot, part, plane, rows, :] + value
         goes[at].start()
     for copy in goes:
         copy.wait()
 
 
-def lift_kernel(smoothed, coarse, out, fine, wide, arrived, left):
-    lifted(smoothed, coarse, out, fine, wide, arrived, left)
-
-
-def last_kernel(step, smoothed, kept_before, matrix, same, other, out, fine, wide, arrived, left, vector, coarse):
-    def product():
-        coarse[...] = kept_before[...]
-
-        @pl.when(lax.axis_index("layer") == step)
-        def _():
-            ordered(vector, same, other, lax.axis_index("row") % 2 == 0)
-            full = vector[...]
-            coarse[...] = combined(times(full, matrix[0]), times(full, matrix[1]))
-
-    lifted(smoothed, coarse, out, fine, wide, arrived, left, product)
+def lift_kernel(smoothed, coarse, out, fine, wide, left):
+    lifted(smoothed, coarse[...], out, fine, wide, left)
+
+
+def last_kernel(step, smoothed, kept_before, matrix, same, other, out, fine, wide, left, vector, coarse):
+    coarse[...] = kept_before[...]
+
+    @pl.when(lax.axis_index("layer") == step)
+    def _():
+        ordered(vector, same, other, lax.axis_index("row") % 2 == 0)
+        full = vector[...]
+        coarse[...] = combined(times(full, matrix[0]), times(full, matrix[1]))
+
+    lifted(smoothed, coarse[...], out, fine, wide, left)
 
 
 def lift(smoothed, kept, step=None, *operands):
@@ -378,7 +370,6 @@
         pltpu.VMEM((2 * shots, depth, height, width), f32),
         pltpu.VMEM((height // QY * lines, width), f32),
         pltpu.SemaphoreType.DMA((2 * shots,)),
-        pltpu.SemaphoreType.DMA((2 * shots,)),
     ]
     kernel = lift_kernel
     if operands:
@@ -388,10 +379,10 @@
     return pl.pallas_call(
         kernel,
         out_shape=pltpu.HBM(smoothed.shape, f32),
-        in_specs=[pl.BlockSpec(memory_space=pltpu.HBM)] + [pl.BlockSpec(memory_space=VMEM)] * (1 + len(operands)),
+        in_specs=[pl.BlockSpec(memory_space=VMEM)] * (2 + len(operands)),
         out_specs=pl.BlockSpec(memory_space=pltpu.HBM),
         scratch_shapes=scratch,
-        compiler_params=limit(5),
+        compiler_params=limit(6),
         name="lift",
     )(smoothed, kept, *operands)
 
@@ -481,7 +472,7 @@
         return found
 
     def solve(step, other, same, kept):
-        held = hold(matrix)
+        held = hold(step, matrix)
         return solve_layer(step, held, same, other, next_rhs, kept)
 
     middle = layers // 2
@@ -509,7 +500,7 @@
 
     def finish(half, smoothed, kept):
         other, same = swap(step, half)
-        held = hold(matrix)
+        held = hold(step, matrix)
         return lift(smoothed, kept, step, held, same, other)
 
     return lax.cond(

time: 190 us -> 190 us (level)
  Pallas kernels: 29.3 us -> 24.5 us
  waiting for transfers between devices: 22.1 us -> 24.4 us
  starting transfers between devices: 118 us -> 120 us
    pallas_call x3, Pallas kernels: 7.04 us -> 2.36 us  [hold(): pl.pallas_call(functools.partial(hold_kernel, step), out_shape=pltpu.VMEM...]
    ppermute x4, starting transfers between devices: 86 us -> 88.3 us  [swap(): found.append(lax.ppermute(half, ('layer', 'row'), way))]
    ppermute x4, waiting for transfers between devices: 3 us -> 5.33 us  [swap(): found.append(lax.ppermute(half, ('layer', 'row'), way))]
  transfers between devices with their start and end apart: 12 -> 12, of which waited for: 6 -> 6; matrix products, arithmetic and copies ran while one was open for 0% -> 0% of each run, Pallas kernels for 7% -> 5%
where the time goes in v5:
time: 190 us; the launch traced here: 189 us
  starting transfers between devices  120 us (63%)
  Pallas kernels  24.5 us (13%)
  waiting for transfers between devices  24.4 us (13%)
  blocking collectives  10.7 us (6%)
  local copies, waits for them, and re-layouts  8.2 us (4%)
    ppermute x4, starting transfers between devices, swap(): found.append(lax.ppermute(half, ('layer', 'row'), way))  88.3 us
    all_to_all x1, starting transfers between devices, every_layer(): gathered = lax.all_to_all(spread, 'row', 0, 0, tiled=True)  13.8 us
    pallas_call x1, Pallas kernels, smooth(): pl.pallas_call(smooth_kernel, out_shape=jax.ShapeDtypeStruct(residual.sha...  12.8 us
    all_to_all x1, blocking collectives, gather(): lax.all_to_all(blocks, 'row', 0, 0, axis_index_groups=ends, tiled=True)  10.7 us
    all_to_all x1, waiting for transfers between devices, every_layer(): gathered = lax.all_to_all(spread, 'row', 0, 0, tiled=True)  8.96 us
    ppermute x2, starting transfers between devices, both_ways(): lax.ppermute(high_block, axis, up)  8.89 us
    unnamed x16, local copies, waits for them, and re-layouts  8.19 us
    ppermute x4, waiting for transfers between devices, swap(): found.append(lax.ppermute(half, ('layer', 'row'), way))  5.33 us
  transfers between devices with their start and end apart: 12, of which 6 were waited for; matrix products, arithmetic and copies ran while one was open for 0% of the time, Pallas kernels for 5%

profile of v5, /device:TPU:96, one launch (start us, length us, event | category | flops | bytes accessed | tf_op | source)
XLA Modules:
  0.0 189.0 jit_solution(11789212542408470018)
XLA Ops:
  0.0 1.6 copy-done
  1.6 1.0 copy-done.4
  2.7 2.1 %collective-permute-start.12 = (bf16[5,3,64,192]{3,2,1,0:T(8,128)(2,1)S(1)}, bf16[5,3,64,192]{3,2,1,0:T(8,128)(2,1)S(1)}, u32[]{:S(2)}, u32[]{:S(2)}) collective-permute-start(bf16[5,3,64,192]{3,2,1,0:T(8,128)(2,1)S(1)} %get-tuple-element.186), channel_id=1, source_target_pairs={{0,32},{32,64},{64,96},{96,128},{128,160},{160,192},{192,224},{1,3... | collective-permute-start | bytes 1105928 | tf_op jit(solution)/shard_map/ppermute | solution.py:432
  4.8 3.6 %collective-permute-start.13 = (bf16[5,3,64,192]{3,2,1,0:T(8,128)(2,1)S(1)}, bf16[5,3,64,192]{3,2,1,0:T(8,128)(2,1)S(1)}, u32[]{:S(2)}, u32[]{:S(2)}) collective-permute-start(bf16[5,3,64,192]{3,2,1,0:T(8,128)(2,1)S(1)} %get-tuple-element.187), channel_id=1, source_target_pairs={{32,0},{64,32},{96,64},{128,96},{160,128},{192,160},{224,192},{33,... | collective-permute-start | bytes 1105928 | tf_op jit(solution)/shard_map/ppermute | solution.py:432
  8.4 4.6 %collective-permute-done.12.below.deep_low = bf16[5,3,64,192]{3,2,1,0:T(8,128)(2,1)S(1)} collective-permute-done((bf16[5,3,64,192]{3,2,1,0:T(8,128)(2,1)S(1)}, bf16[5,3,64,192]{3,2,1,0:T(8,128)(2,1)S(1)}, u32[]{:S(2)}, u32[]{:S(2)}) %collective-permute-start.12) | collective-permute-done | bytes 368672 | tf_op jit(solution)/shard_map/ppermute | solution.py:432
  13.0 1.8 collective-permute-done.13.above.deep_high
  14.8 1.0 pack_rows.1
  15.8 6.8 %collective-permute-start.14 = (bf16[5,14,8,192]{3,2,1,0:T(8,128)(2,1)}, bf16[5,14,8,192]{3,2,1,0:T(8,128)(2,1)S(1)}, u32[]{:S(2)}, u32[]{:S(2)}) collective-permute-start(bf16[5,14,8,192]{3,2,1,0:T(8,128)(2,1)} %get-tuple-element.188), channel_id=1, source_target_pairs={{0,1},{1,2},{2,3},{3,4},{4,5},{5,6},{6,7},{7,8},{8,9},{9,10},{10,1... | collective-permute-start | bytes 645128 | tf_op jit(solution)/shard_map/ppermute | solution.py:432
  22.6 1.3 collective-permute-start.15
  23.9 1.0 restrict.1
  24.9 13.8 %all-to-all-start.7 = ((bf16[32,4,192]{2,1,0:T(4,128)(2,1)}), bf16[32,4,192]{2,1,0:T(4,128)(2,1)S(1)}, u32[]{:S(2)}, u32[]{:S(2)}) async-start(bf16[32,4,192]{2,1,0:T(4,128)(2,1)} %get-tuple-element.190), calls=%async_computation.7 | async-start | bytes 131072 | tf_op jit(solution)/shard_map/all_to_all | solution.py:443
  38.8 3.0 %collective-permute-start.16 = (f32[4,192]{1,0:T(4,128)S(1)}, f32[4,192]{1,0:T(4,128)S(1)}, u32[]{:S(2)}, u32[]{:S(2)}) collective-permute-start(f32[4,192]{1,0:T(4,128)S(1)} %get-tuple-element.191), channel_id=1, source_target_pairs={{32,0},{64,32},{96,64},{128,96},{160,128},{192,160},{224,192},{33,... | collective-permute-start | bytes 9224 | tf_op jit(solution)/shard_map/ppermute | solution.py:441
  41.8 3.8 %collective-permute-done.16.next_rhs = f32[4,192]{1,0:T(4,128)S(1)} collective-permute-done((f32[4,192]{1,0:T(4,128)S(1)}, f32[4,192]{1,0:T(4,128)S(1)}, u32[]{:S(2)}, u32[]{:S(2)}) %collective-permute-start.16) | collective-permute-done | bytes 3104 | tf_op jit(solution)/shard_map/ppermute | solution.py:441
  45.6 9.0 %all-to-all-done.7.gathered = bf16[32,4,192]{2,1,0:T(4,128)(2,1)S(1)} async-done(((bf16[32,4,192]{2,1,0:T(4,128)(2,1)}), bf16[32,4,192]{2,1,0:T(4,128)(2,1)S(1)}, u32[]{:S(2)}, u32[]{:S(2)}) %all-to-all-start.7) | async-done | bytes 49184 | tf_op jit(solution)/shard_map/all_to_all | solution.py:443
  54.6 2.8 %solve_first.1 = (f32[4,192]{1,0:T(4,128)S(1)}, bf16[16,4,192]{2,1,0:T(4,128)(2,1)S(1)}) custom-call(bf16[2,192,6144]{2,1,0:T(8,128)(2,1)} %bitcast.5, bf16[32,4,192]{2,1,0:T(4,128)(2,1)S(1)} %all-to-all-done.7.gathered, f32[4,192]{1,0:T(4,128)S(1)} %collective-permute-done.16.next_rhs), custom_call_target="tpu_custom_call" | custom-call | flops 9437184 | bytes 4718592 | tf_op jit(solution)/shard_map/solve_first/pallas_call | solution.py:155
  57.5 0.7 collective-permute-start.18
  58.9 2.2 %copy-done.2 = bf16[2,192,6144]{2,1,0:T(8,128)(2,1)} copy-done((bf16[2,192,6144]{2,1,0:T(8,128)(2,1)}, bf16[2,192,6144]{2,1,0:T(8,128)(2,1)S(1)}, u32[]{:S(2)}) %copy-start.2) | copy-done | bytes 4718616
  61.1 2.3 %copy-done.3 = bf16[2,192,6144]{2,1,0:T(8,128)(2,1)S(1)} copy-done((bf16[2,192,6144]{2,1,0:T(8,128)(2,1)S(1)}, bf16[2,192,6144]{2,1,0:T(8,128)(2,1)}, u32[]{:S(2)}) %copy-start.3) | copy-done | bytes 4718616
  63.5 1.4 solve_layer.11
  65.1 90.1 %conditional.23 = ((f32[4,192]{1,0:T(4,128)S(1)}, bf16[16,4,192]{2,1,0:T(4,128)(2,1)S(1)})) conditional(s32[]{:T(128)} %convert_element_type.44, (f32[4,192]{1,0:T(4,128)S(1)}, bf16[16,4,192]{2,1,0:T(4,128)(2,1)S(1)}) %tuple.111, (bf16[2,192,6144]{2,1,0:T(8,128)(2,1)}, bf16[16,4,192]{2,1,0:T(4,128)(2,1)S(1)}, f32[4,192]{1,0:T(4,128)S(1)}, ...), branch_computations={%region_20.0_spmd, %region_21.0_spmd} | conditional | flops 9437184 | bytes 4921432 | solution.py:484
  65.1 85.3 %collective-permute-start.9 = (bf16[16,4,192]{2,1,0:T(4,128)(2,1)S(1)}, bf16[16,4,192]{2,1,0:T(4,128)(2,1)S(1)}, u32[]{:S(2)}, u32[]{:S(2)}) collective-permute-start(bf16[16,4,192]{2,1,0:T(4,128)(2,1)S(1)} %get-tuple-element.157), channel_id=1, source_target_pairs={{0,97},{1,96},{2,99},{3,98},{4,101},{5,100},{6,103},{7,102},{8,105... | collective-permute-start | bytes 73736 | tf_op jit(solution)/shard_map/cond/branch_1_fun/ppermute | solution.py:464
  150.5 2.3 %hold.11.matrix = bf16[2,192,6144]{2,1,0:T(8,128)(2,1)S(1)} custom-call(bf16[2,192,6144]{2,1,0:T(8,128)(2,1)} %get-tuple-element.156.matrix), custom_call_target="tpu_custom_call" | custom-call | tf_op jit(solution)/shard_map/cond/branch_1_fun/hold/pallas_call | solution.py:92
  152.8 1.0 collective-permute-done.8.same
  153.8 1.4 solve_layer.10
  155.2 10.8 %conditional.24 = (bf16[16,4,192]{2,1,0:T(4,128)(2,1)S(1)}) conditional(s32[]{:T(128)} %convert_element_type.55, bf16[16,4,192]{2,1,0:T(4,128)(2,1)S(1)} %get-tuple-element.205, bf16[16,4,192]{2,1,0:T(4,128)(2,1)S(1)} %get-tuple-element.205), branch_computations={%region_22.0_spmd, %region_23.0_spmd} | conditional | bytes 98312 | solution.py:449
  155.2 10.7 %all_to_all.39 = bf16[16,4,192]{2,1,0:T(4,128)(2,1)S(1)} all-to-all(bf16[16,4,192]{2,1,0:T(4,128)(2,1)S(1)} %copy.58), channel_id=1, replica_groups={{0,2,4,6,8,10,12,14,16,18,20,22,24,26,28,30},{1,3,5,7,9,11,13,15,17,19,..., dimensions={0} | all-to-all | bytes 49152 | tf_op jit(solution)/shard_map/cond/branch_1_fun/all_to_all | solution.py:451
  166.0 1.0 copy-done.7
  167.0 12.8 %smooth.1 = f32[2,2,8,64,192]{4,3,2,1,0:T(8,128)S(1)} custom-call(f32[4]{0:T(128)S(1)} %add_convert_fusion.inside, f32[2,2,8,64,192]{4,3,2,1,0:T(8,128)S(1)} %copy-done.1, f32[8,64,192]{2,1,0:T(8,128)S(1)} %copy-done.5, bf16[5,14,8,192]{3,2,1,0:T(8,128)(2,1)S(1)} %collective-permute-done.14.row_low, ...), custom_call_target="tpu_custom_call" | custom-call | flops 117964800 | bytes 4718592 | tf_op jit(solution)/shard_map/smooth/pallas_call | solution.py:320
  179.7 9.1 %conditional.25 = (f32[2,2,8,64,192]{4,3,2,1,0:T(8,128)}) conditional(s32[]{:T(128)} %convert_element_type.42, (f32[2,2,8,64,192]{4,3,2,1,0:T(8,128)S(1)}, f32[4,192]{1,0:T(4,128)S(1)}) %tuple.113, (bf16[2,192,6144]{2,1,0:T(8,128)(2,1)}, bf16[16,4,192]{2,1,0:T(4,128)(2,1)S(1)}, f32[2,2,8,64,192]{4,3,2,1,0:T(8,128)S(1)}, ...), branch_computations={%region_24.0_spmd, %region_25.0_spmd} | conditional | bytes 196696 | solution.py:506
  179.9 2.9 %collective-permute-start.10 = (bf16[16,4,192]{2,1,0:T(4,128)(2,1)S(1)}, bf16[16,4,192]{2,1,0:T(4,128)(2,1)S(1)}, u32[]{:S(2)}, u32[]{:S(2)}) collective-permute-start(bf16[16,4,192]{2,1,0:T(4,128)(2,1)S(1)} %get-tuple-element.165), channel_id=1, source_target_pairs={{0,32},{1,33},{2,34},{3,35},{4,36},{5,37},{6,38},{7,39},{8,40},{9,... | collective-permute-start | bytes 73736 | tf_op jit(solution)/shard_map/cond/branch_1_fun/ppermute | solution.py:464
  182.7 4.4 %collective-permute-done.11.other = bf16[16,4,192]{2,1,0:T(4,128)(2,1)S(1)} collective-permute-done((bf16[16,4,192]{2,1,0:T(4,128)(2,1)S(1)}, bf16[16,4,192]{2,1,0:T(4,128)(2,1)S(1)}, u32[]{:S(2)}, u32[]{:S(2)}) %collective-permute-start.11) | collective-permute-done | bytes 24608 | tf_op jit(solution)/shard_map/cond/branch_1_fun/ppermute | solution.py:464
  187.1 1.7 lift.3
  (36 shorter events, 1.3 us)
Async XLA Ops:
  0.0 1.6 copy-start
  1.6 1.0 copy-start.4
  2.6 21.3 %copy-start.1 = (f32[2,2,8,64,192]{4,3,2,1,0:T(8,128)S(1)}, f32[2,2,8,64,192]{4,3,2,1,0:T(8,128)}, u32[]{:S(2)}) copy-start(f32[2,2,8,64,192]{4,3,2,1,0:T(8,128)} %residual.7) | copy-start | bytes 4718596
  2.7 10.3 %collective-permute-start.12 = (bf16[5,3,64,192]{3,2,1,0:T(8,128)(2,1)S(1)}, bf16[5,3,64,192]{3,2,1,0:T(8,128)(2,1)S(1)}, u32[]{:S(2)}, u32[]{:S(2)}) collective-permute-start(bf16[5,3,64,192]{3,2,1,0:T(8,128)(2,1)S(1)} %get-tuple-element.186), channel_id=1, source_target_pairs={{0,32},{32,64},{64,96},{96,128},{128,160},{160,192},{192,224},{1,3... | collective-permute-start | bytes 1105928 | tf_op jit(solution)/shard_map/ppermute | solution.py:432
  4.8 10.0 %collective-permute-start.13 = (bf16[5,3,64,192]{3,2,1,0:T(8,128)(2,1)S(1)}, bf16[5,3,64,192]{3,2,1,0:T(8,128)(2,1)S(1)}, u32[]{:S(2)}, u32[]{:S(2)}) collective-permute-start(bf16[5,3,64,192]{3,2,1,0:T(8,128)(2,1)S(1)} %get-tuple-element.187), channel_id=1, source_target_pairs={{32,0},{64,32},{96,64},{128,96},{160,128},{192,160},{224,192},{33,... | collective-permute-start | bytes 1105928 | tf_op jit(solution)/shard_map/ppermute | solution.py:432
  14.8 1.0 copy-start.6
  15.8 150.2 %collective-permute-start.14 = (bf16[5,14,8,192]{3,2,1,0:T(8,128)(2,1)}, bf16[5,14,8,192]{3,2,1,0:T(8,128)(2,1)S(1)}, u32[]{:S(2)}, u32[]{:S(2)}) collective-permute-start(bf16[5,14,8,192]{3,2,1,0:T(8,128)(2,1)} %get-tuple-element.188), channel_id=1, source_target_pairs={{0,1},{1,2},{2,3},{3,4},{4,5},{5,6},{6,7},{7,8},{8,9},{9,10},{10,1... | collective-permute-start | bytes 645128 | tf_op jit(solution)/shard_map/ppermute | solution.py:432
  22.6 143.3 %collective-permute-start.15 = (bf16[5,14,8,192]{3,2,1,0:T(8,128)(2,1)}, bf16[5,14,8,192]{3,2,1,0:T(8,128)(2,1)}, u32[]{:S(2)}, u32[]{:S(2)}) collective-permute-start(bf16[5,14,8,192]{3,2,1,0:T(8,128)(2,1)} %get-tuple-element.189), channel_id=1, source_target_pairs={{1,0},{2,1},{3,2},{4,3},{5,4},{6,5},{7,6},{8,7},{9,8},{10,9},{11,1... | collective-permute-start | bytes 645128 | tf_op jit(solution)/shard_map/ppermute | solution.py:432
  24.9 29.6 %all-to-all-start.7 = ((bf16[32,4,192]{2,1,0:T(4,128)(2,1)}), bf16[32,4,192]{2,1,0:T(4,128)(2,1)S(1)}, u32[]{:S(2)}, u32[]{:S(2)}) async-start(bf16[32,4,192]{2,1,0:T(4,128)(2,1)} %get-tuple-element.190), calls=%async_computation.7 | async-start | bytes 131072 | tf_op jit(solution)/shard_map/all_to_all | solution.py:443
  38.8 6.8 %collective-permute-start.16 = (f32[4,192]{1,0:T(4,128)S(1)}, f32[4,192]{1,0:T(4,128)S(1)}, u32[]{:S(2)}, u32[]{:S(2)}) collective-permute-start(f32[4,192]{1,0:T(4,128)S(1)} %get-tuple-element.191), channel_id=1, source_target_pairs={{32,0},{64,32},{96,64},{128,96},{160,128},{192,160},{224,192},{33,... | collective-permute-start | bytes 9224 | tf_op jit(solution)/shard_map/ppermute | solution.py:441
  57.5 3.6 %collective-permute-start.18 = (bf16[16,4,192]{2,1,0:T(4,128)(2,1)S(1)}, bf16[16,4,192]{2,1,0:T(4,128)(2,1)S(1)}, u32[]{:S(2)}, u32[]{:S(2)}) collective-permute-start(bf16[16,4,192]{2,1,0:T(4,128)(2,1)S(1)} %get-tuple-element.235), channel_id=1, source_target_pairs={{96,129},{97,128},{98,131},{99,130},{100,133},{101,132},{102,135},... | collective-permute-start | bytes 73736 | tf_op jit(solution)/shard_map/ppermute | solution.py:471
  58.2 3.0 %collective-permute-start.17 = (bf16[16,4,192]{2,1,0:T(4,128)(2,1)S(1)}, bf16[16,4,192]{2,1,0:T(4,128)(2,1)S(1)}, u32[]{:S(2)}, u32[]{:S(2)}) collective-permute-start(bf16[16,4,192]{2,1,0:T(4,128)(2,1)S(1)} %get-tuple-element.235), channel_id=1, source_target_pairs={{96,128},{97,129},{98,130},{99,131},{100,132},{101,133},{102,134},... | collective-permute-start | bytes 73736 | tf_op jit(solution)/shard_map/ppermute | solution.py:471
  58.9 2.2 %copy-start.2 = (bf16[2,192,6144]{2,1,0:T(8,128)(2,1)}, bf16[2,192,6144]{2,1,0:T(8,128)(2,1)S(1)}, u32[]{:S(2)}) copy-start(bf16[2,192,6144]{2,1,0:T(8,128)(2,1)S(1)} %hold.13.matrix) | copy-start | bytes 14155780
  61.1 2.3 %copy-start.3 = (bf16[2,192,6144]{2,1,0:T(8,128)(2,1)S(1)}, bf16[2,192,6144]{2,1,0:T(8,128)(2,1)}, u32[]{:S(2)}) copy-start(bf16[2,192,6144]{2,1,0:T(8,128)(2,1)} %copy-done.2) | copy-start | bytes 14155780
  65.1 100.9 %copy-start.5 = (f32[8,64,192]{2,1,0:T(8,128)S(1)}, f32[8,64,192]{2,1,0:T(8,128)}, u32[]{:S(2)}) copy-start(f32[8,64,192]{2,1,0:T(8,128)} %wavenumber.5) | copy-start | bytes 1179652
  65.1 87.7 %collective-permute-start.9 = (bf16[16,4,192]{2,1,0:T(4,128)(2,1)S(1)}, bf16[16,4,192]{2,1,0:T(4,128)(2,1)S(1)}, u32[]{:S(2)}, u32[]{:S(2)}) collective-permute-start(bf16[16,4,192]{2,1,0:T(4,128)(2,1)S(1)} %get-tuple-element.157), channel_id=1, source_target_pairs={{0,97},{1,96},{2,99},{3,98},{4,101},{5,100},{6,103},{7,102},{8,105... | collective-permute-start | bytes 73736 | tf_op jit(solution)/shard_map/cond/branch_1_fun/ppermute | solution.py:464
  150.5 3.3 %collective-permute-start.8 = (bf16[16,4,192]{2,1,0:T(4,128)(2,1)S(1)}, bf16[16,4,192]{2,1,0:T(4,128)(2,1)S(1)}, u32[]{:S(2)}, u32[]{:S(2)}) collective-permute-start(bf16[16,4,192]{2,1,0:T(4,128)(2,1)S(1)} %get-tuple-element.157), channel_id=1, source_target_pairs={{0,96},{1,97},{2,98},{3,99},{4,100},{5,101},{6,102},{7,103},{8,104... | collective-permute-start | bytes 73736 | tf_op jit(solution)/shard_map/cond/branch_1_fun/ppermute | solution.py:464
  166.0 1.0 copy-start.7
  179.8 7.3 %collective-permute-start.11 = (bf16[16,4,192]{2,1,0:T(4,128)(2,1)S(1)}, bf16[16,4,192]{2,1,0:T(4,128)(2,1)S(1)}, u32[]{:S(2)}, u32[]{:S(2)}) collective-permute-start(bf16[16,4,192]{2,1,0:T(4,128)(2,1)S(1)} %get-tuple-element.165), channel_id=1, source_target_pairs={{0,33},{1,32},{2,35},{3,34},{4,37},{5,36},{6,39},{7,38},{8,41},{9,... | collective-permute-start | bytes 73736 | tf_op jit(solution)/shard_map/cond/branch_1_fun/ppermute | solution.py:464
  179.9 7.2 %collective-permute-start.10 = (bf16[16,4,192]{2,1,0:T(4,128)(2,1)S(1)}, bf16[16,4,192]{2,1,0:T(4,128)(2,1)S(1)}, u32[]{:S(2)}, u32[]{:S(2)}) collective-permute-start(bf16[16,4,192]{2,1,0:T(4,128)(2,1)S(1)} %get-tuple-element.165), channel_id=1, source_target_pairs={{0,32},{1,33},{2,34},{3,35},{4,36},{5,37},{6,38},{7,39},{8,40},{9,... | collective-permute-start | bytes 73736 | tf_op jit(solution)/shard_map/cond/branch_1_fun/ppermute | solution.py:464

commit v6 on v5

--- a/solution.py
+++ b/solution.py
@@ -100,8 +100,20 @@
     )(matrix)
 
 
-def ordered(vector, same, other, first_end):
+def ordered(vector, both):
+    columns, lines, cells = both.shape
+    half = lines // 2
+    first_end = lax.axis_index("row") % 2 == 0
+    for column in range(columns):
+        own, far = both[column, :half], both[column, half:]
+        at = 2 * column * cells
+        vector[:, at : at + cells] = jnp.where(first_end, own, far)
+        vector[:, at + cells : at + 2 * cells] = jnp.where(first_end, far, own)
+
+
+def ordered_two(vector, same, other):
     columns, _, cells = same.shape
+    first_end = lax.axis_index("row") % 2 == 0
     for column in range(columns):
         own, far = same[column], other[column]
         at = 2 * column * cells
@@ -124,7 +136,7 @@
     return lax.dot_general(part, rows, (((1,), (1,)), ((), ())), preferred_element_type=f32)
 
 
-def first_kernel(matrix, gathered, next_rhs, kept, spread, held, vector, arrived):
+def first_kernel(matrix, gathered, solved, held, vector, arrived):
     devices, _, cells = gathered.shape
     pieces = arrived.shape[0]
     across = matrix.shape[2] // pieces
@@ -144,21 +156,16 @@
         for side in range(2):
             product = times(part, held[side, :, columns[piece]])
             by[side] = product if by[side] is None else by[side] + product
-    solved = combined(by[0], by[1])
-    kept[...] = solved
-    hand_on(solved, next_rhs, spread)
-
-
-def solve_first(matrix, gathered, next_rhs):
+    solved[...] = combined(by[0], by[1])
+
+
+def solve_first(matrix, gathered):
     devices, lines, cells = gathered.shape
     pieces = 6
     return pl.pallas_call(
         first_kernel,
-        out_shape=(
-            jax.ShapeDtypeStruct((lines, cells), f32),
-            jax.ShapeDtypeStruct((devices // 2, lines, cells), bf16),
-        ),
-        in_specs=[pl.BlockSpec(memory_space=pltpu.HBM)] + [pl.BlockSpec(memory_space=VMEM)] * 2,
+        out_shape=jax.ShapeDtypeStruct((lines, cells), f32),
+        in_specs=[pl.BlockSpec(memory_space=pltpu.HBM), pl.BlockSpec(memory_space=VMEM)],
         scratch_shapes=[
             pltpu.VMEM(matrix.shape, bf16),
             pltpu.VMEM((lines, devices * cells), bf16),
@@ -167,31 +174,70 @@
         compiler_params=limit(8),
         cost_estimate=pl.CostEstimate(flops=4 * matrix.size, bytes_accessed=2 * matrix.size, transcendentals=0),
         name="solve_first",
-    )(matrix, gathered, next_rhs)
-
-
-def layer_kernel(step, matrix, same, other, next_rhs, kept_before, kept, spread, vector):
-    ordered(vector, same, other, lax.axis_index("row") % 2 == 0)
+    )(matrix, gathered)
+
+
+def meet_kernel(near, far, rhs, far_rhs, spread):
+    lines = rhs.shape[0]
+    own = (rhs[...] + coupling * near[...]).astype(bf16)
+    partner = (far_rhs[...] + coupling * far[...]).astype(bf16)
+    for column in range(spread.shape[0]):
+        spread[column, :lines] = own
+        spread[column, lines:] = partner
+
+
+def meet(near, far, rhs, far_rhs, columns):
+    lines, cells = rhs.shape
+    return pl.pallas_call(
+        meet_kernel,
+        out_shape=jax.ShapeDtypeStruct((columns, 2 * lines, cells), bf16),
+        compiler_params=limit(2),
+        name="meet",
+    )(near, far, rhs, far_rhs)
+
+
+def odd_kernel(step, matrix, both, next_rhs, kept_before, kept, spread, vector):
+    ordered(vector, both)
     full = vector[...]
     solved = combined(times(full, matrix[0]), times(full, matrix[1]))
     kept[...] = jnp.where(lax.axis_index("layer") == step, solved, kept_before[...])
     hand_on(solved, next_rhs, spread)
 
 
-def solve_layer(step, matrix, same, other, next_rhs, kept):
+def solve_odd(step, matrix, both, next_rhs, kept):
+    columns, lines, cells = both.shape
+    return pl.pallas_call(
+        functools.partial(odd_kernel, step),
+        out_shape=(
+            jax.ShapeDtypeStruct((lines // 2, cells), f32),
+            jax.ShapeDtypeStruct((columns, lines // 2, cells), bf16),
+        ),
+        in_specs=[pl.BlockSpec(memory_space=VMEM)] * 4,
+        scratch_shapes=[pltpu.VMEM((lines // 2, 2 * columns * cells), bf16)],
+        compiler_params=limit(3),
+        cost_estimate=pl.CostEstimate(flops=4 * matrix.size, bytes_accessed=2 * matrix.size, transcendentals=0),
+        name="solve_odd",
+    )(matrix, both, next_rhs, kept)
+
+
+def even_kernel(step, matrix, same, other, kept_before, kept, vector):
+    ordered_two(vector, same, other)
+    full = vector[...]
+    solved = combined(times(full, matrix[0]), times(full, matrix[1]))
+    kept[...] = jnp.where(lax.axis_index("layer") == step, solved, kept_before[...])
+
+
+def solve_even(step, matrix, same, other, kept):
     columns, lines, cells = same.shape
     return pl.pallas_call(
-        functools.partial(layer_kernel, step),
-        out_shape=(
-            jax.ShapeDtypeStruct((lines, cells), f32),
-            jax.ShapeDtypeStruct((columns, lines, cells), bf16),
-        ),
-        in_specs=[pl.BlockSpec(memory_space=VMEM)] * 5,
+        functools.partial(even_kernel, step),
+        out_shape=jax.ShapeDtypeStruct((lines, cells), f32),
+        in_specs=[pl.BlockSpec(memory_space=VMEM)] * 4,
         scratch_shapes=[pltpu.VMEM((lines, 2 * columns * cells), bf16)],
         compiler_params=limit(3),
         cost_estimate=pl.CostEstimate(flops=4 * matrix.size, bytes_accessed=2 * matrix.size, transcendentals=0),
-        name="solve_layer",
-    )(matrix, same, other, next_rhs, kept)
+        name="solve_even",
+    )(matrix, same, other, kept)
 
 
 def smooth_kernel(inside, residual, wavenumber, row_low, row_high, deep_low, deep_high, smoothed, gain, source, first, second):
@@ -351,12 +397,12 @@
     lifted(smoothed, coarse[...], out, fine, wide, left)
 
 
-def last_kernel(step, smoothed, kept_before, matrix, same, other, out, fine, wide, left, vector, coarse):
+def last_kernel(step, smoothed, kept_before, matrix, both, out, fine, wide, left, vector, coarse):
     coarse[...] = kept_before[...]
 
     @pl.when(lax.axis_index("layer") == step)
     def _():
-        ordered(vector, same, other, lax.axis_index("row") % 2 == 0)
+        ordered(vector, both)
         full = vector[...]
         coarse[...] = combined(times(full, matrix[0]), times(full, matrix[1]))
 
@@ -426,9 +472,8 @@
     )(residual, wavenumber, below, above)
 
 
-def both_ways(low_block, high_block, axis):
-    size = lax.axis_size(axis)
-    up = [(i, i + 1) for i in range(size - 1)]
+def both_ways(low_block, high_block, axis, lowest=0):
+    up = [(i, i + 1) for i in range(lowest, lax.axis_size(axis) - 1)]
     return lax.ppermute(high_block, axis, up), lax.ppermute(low_block, axis, [(b, a) for a, b in up])
 
 
@@ -436,24 +481,38 @@
     layers, devices = lax.axis_size("layer"), lax.axis_size("row")
     layer, row = lax.axis_index("layer"), lax.axis_index("row")
     inside = jnp.stack([layer > 0, layer < layers - 1, row > 0, row < devices - 1]).astype(f32)
+    matrix = pltpu.with_memory_space_constraint(inverse[:, 0], pltpu.HBM)
+    columns = devices // 2
 
     rhs, spread = restrict(residual, devices)
-    next_rhs = lax.ppermute(rhs, "layer", [(i + 1, i) for i in range(layers - 1)])
-    matrix = pltpu.with_memory_space_constraint(inverse[:, 0], pltpu.HBM)
-    gathered = lax.all_to_all(spread, "row", 0, 0, tiled=True)
-    kept, spread = solve_first(matrix, gathered, next_rhs)
-
-    ends = [[2 * column + end for column in range(devices // 2)] for end in range(2)]
-
-    def gather(step, spread):
-        return lax.cond(
-            layer == step,
-            lambda blocks: lax.all_to_all(blocks, "row", 0, 0, axis_index_groups=ends, tiled=True),
-            lambda blocks: blocks,
-            spread,
-        )
-
-    def swap(step, half):
+
+    def early(residual, wavenumber, rhs):
+        first, last = pack_planes(residual, wavenumber)
+        below, above = both_ways(first, last, "layer", 1)
+        next_rhs = lax.ppermute(rhs, "layer", [(i + 1, i) for i in range(1, layers - 1, 2)])
+        ways = [(i, i ^ 1) for i in range(devices)]
+        return below, above, next_rhs, lax.ppermute(rhs, "row", ways)
+
+    def nothing(residual, wavenumber, rhs):
+        planes = jnp.zeros((2 * residual.shape[0] + 1, HALO, *residual.shape[3:]), bf16)
+        return planes, planes, rhs, rhs
+
+    below, above, next_rhs, far_rhs = lax.cond(layer > 0, early, nothing, residual, wavenumber, rhs)
+
+    gathered = lax.cond(
+        layer == 0,
+        lambda blocks: lax.all_to_all(blocks, "row", 0, 0, tiled=True),
+        lambda blocks: blocks,
+        spread,
+    )
+    kept = solve_first(matrix, gathered)
+
+    ends = [[2 * column + end for column in range(columns)] for end in range(2)]
+
+    def gather(blocks):
+        return lax.all_to_all(blocks, "row", 0, 0, axis_index_groups=ends, tiled=True)
+
+    def swap(step, block):
         found = []
         for flip in (1, 0):
             way = [
@@ -461,51 +520,67 @@
                 for i in range(layers)
                 for j in range(devices)
             ]
-            found.append(lax.ppermute(half, ("layer", "row"), way))
+            found.append(lax.ppermute(block, ("layer", "row"), way))
         return found
 
-    def send(step, half):
+    def send(step, block):
         found = []
         for flip in (1, 0):
             way = [((step - 1) * devices + j, step * devices + (j ^ flip)) for j in range(devices)]
-            found.append(lax.ppermute(half, ("layer", "row"), way))
+            found.append(lax.ppermute(block, ("layer", "row"), way))
         return found
 
-    def solve(step, other, same, kept):
-        held = hold(step, matrix)
-        return solve_layer(step, held, same, other, next_rhs, kept)
+    def held(step):
+        return hold(step, matrix)
+
+    def to_odd(step, kept):
+        far, near = swap(step, kept)
+        return gather(meet(near, far, rhs, far_rhs, columns))
+
+    def odd_step(step, kept):
+        own = held(step)
+        return tuple(solve_odd(step, own, to_odd(step, kept), next_rhs, kept))
 
     middle = layers // 2
     for step in range(1, layers - 1):
-        half = gather(step - 1, spread)
+        takes_part = (layer == step - 1) | (layer == step)
+        if step % 2:
+            kept, spread = lax.cond(
+                takes_part,
+                lambda kept, spread, step=step: odd_step(step, kept),
+                lambda kept, spread: (kept, spread),
+                kept,
+                spread[:columns] if step == 1 else spread,
+            )
+            continue
+        half = lax.cond(layer == step - 1, gather, lambda blocks: blocks, spread)
         if step == middle:
-            kept, spread = solve(step, *send(step, half), kept)
+            other, same = send(step, half)
+            kept = solve_even(step, held(step), same, other, kept)
             continue
-        kept, spread = lax.cond(
-            (layer == step - 1) | (layer == step),
-            lambda half, kept, step=step: tuple(solve(step, *swap(step, half), kept)),
-            lambda half, kept: (kept, half),
-            half,
-            kept,
-        )
+
+        def even_step(half, kept, step=step):
+            own = held(step)
+            other, same = swap(step, half)
+            return solve_even(step, own, same, other, kept)
+
+        kept = lax.cond(takes_part, even_step, lambda half, kept: kept, half, kept)
 
     first, last = pack_planes(residual, wavenumber)
-    below, above = both_ways(first, last, "layer")
+    below = jnp.where(layer == 1, lax.ppermute(last, "layer", [(0, 1)]), below)
+    above = jnp.where(layer == 0, lax.ppermute(first, "layer", [(1, 0)]), above)
     first, last = pack_rows(residual, wavenumber, below, above)
     row_low, row_high = both_ways(first, last, "row")
     smoothed = smooth(inside, residual, wavenumber, row_low, row_high, below, above)
 
     step = layers - 1
-    half = gather(step - 1, spread)
-
-    def finish(half, smoothed, kept):
-        other, same = swap(step, half)
-        held = hold(step, matrix)
-        return lift(smoothed, kept, step, held, same, other)
-
-    return lax.cond(
-        layer >= step - 1, finish, lambda half, smoothed, kept: lift(smoothed, kept), half, smoothed, kept
-    )
+
+    def finish(smoothed, kept):
+        own = held(step)
+        both = to_odd(step, kept)
+        return lift(smoothed, kept, step, own, both)
+
+    return lax.cond(layer >= step - 1, finish, lambda smoothed, kept: lift(smoothed, kept), smoothed, kept)
 
 
 def solution(mesh):

time: 190 us -> 232 us (1.22)
  starting transfers between devices: 120 us -> 167 us
  blocking collectives: 10.7 us -> 0 us
  waiting for transfers between devices: 24.4 us -> 15 us
  Pallas kernels: 24.5 us -> 32.7 us
  local copies, waits for them, and re-layouts: 8.2 us -> 12.6 us
    ppermute x7 -> x10, starting transfers between devices: 92.6 us -> 154 us  [the longest x4 143 us: swap(): found.append(lax.ppermute(block, ('layer', 'row'), way))]
    all_to_all x1 -> x0, blocking collectives: 10.7 us -> none  [gather(): lax.all_to_all(blocks, 'row', 0, 0, axis_index_groups=ends, tiled=True)]
    all_to_all x1, starting transfers between devices: 13.8 us -> 3.49 us  [gather(): lax.all_to_all(blocks, 'row', 0, 0, axis_index_groups=ends, tiled=True)]
    cond x2 -> x13, local copies, waits for them, and re-layouts: 0.02 us -> 7.51 us
    ppermute x2, waiting for transfers between devices: 4.57 us -> 0.02 us  [both_ways(): lax.ppermute(high_block, axis, up)]
    unnamed x16 -> x8, local copies, waits for them, and re-layouts: 8.19 us -> 4.49 us
    all_to_all x1, waiting for transfers between devices: 8.96 us -> 5.28 us  [gather(): lax.all_to_all(blocks, 'row', 0, 0, axis_index_groups=ends, tiled=True)]
    ppermute x2, starting transfers between devices: 8.89 us -> 5.27 us  [both_ways(): lax.ppermute(high_block, axis, up)]
  transfers between devices with their start and end apart: 12 -> 15, of which waited for: 6 -> 4; matrix products, arithmetic and copies ran while one was open for 0% -> 2% of each run, Pallas kernels for 5% -> 6%
where the time goes in v6:
time: 232 us; the launch traced here: 231 us
  starting transfers between devices  167 us (72%)
  Pallas kernels  32.7 us (14%)
  waiting for transfers between devices  15 us (6%)
  local copies, waits for them, and re-layouts  12.6 us (5%)
    ppermute x4, starting transfers between devices, swap(): found.append(lax.ppermute(block, ('layer', 'row'), way))  143 us
    pallas_call x1, Pallas kernels, smooth(): pl.pallas_call(smooth_kernel, out_shape=jax.ShapeDtypeStruct(residual.sha...  13.1 us
    cond x13, local copies, waits for them, and re-layouts  7.51 us
    all_to_all x1, waiting for transfers between devices, gather(): lax.all_to_all(blocks, 'row', 0, 0, axis_index_groups=ends, tiled=True)  5.28 us
    ppermute x2, starting transfers between devices, both_ways(): lax.ppermute(high_block, axis, up)  5.27 us
    ppermute x4, waiting for transfers between devices, swap(): found.append(lax.ppermute(block, ('layer', 'row'), way))  4.96 us
    ppermute x2, starting transfers between devices, both_ways(): lax.ppermute(low_block, axis, [(b, a) for a, b in up])  4.94 us
    ppermute x1, waiting for transfers between devices, early(): return (below, above, next_rhs, lax.ppermute(rhs, 'row', ways))  4.73 us
  transfers between devices with their start and end apart: 15, of which 4 were waited for; matrix products, arithmetic and copies ran while one was open for 2% of the time, Pallas kernels for 6%

profile of v6, /device:TPU:96, one launch (start us, length us, event | category | flops | bytes accessed | tf_op | source)
XLA Modules:
  0.0 230.6 jit_solution(9838976750186073740)
XLA Ops:
  0.0 1.9 pack_planes.3
  1.9 1.5 collective-permute-start.17
  3.4 2.0 restrict.1
  5.4 18.3 %conditional.11 = (bf16[5,3,64,192]{3,2,1,0:T(8,128)(2,1)}, bf16[5,3,64,192]{3,2,1,0:T(8,128)(2,1)}, f32[4,192]{1,0:T(4,128)}, f32[4,192]{1,0:T(4,128)}) conditional(s32[]{:T(128)} %convert_element_type.38, f32[4,192]{1,0:T(4,128)S(1)} %get-tuple-element.195, (f32[2,2,8,64,192]{4,3,2,1,0:T(8,128)S(1)}, f32[8,64,192]{2,1,0:T(8,128)}, ...), branch_computations={%region_0.0_spmd, %region_1.0_spmd} | conditional | bytes 2973888 | solution.py:500
  6.5 1.9 collective-permute-start
  8.5 3.6 %collective-permute-start.1 = (bf16[5,3,64,192]{3,2,1,0:T(8,128)(2,1)S(1)}, bf16[5,3,64,192]{3,2,1,0:T(8,128)(2,1)}, u32[]{:S(2)}, u32[]{:S(2)}) collective-permute-start(bf16[5,3,64,192]{3,2,1,0:T(8,128)(2,1)S(1)} %get-tuple-element.132), channel_id=1, source_target_pairs={{64,32},{96,64},{128,96},{160,128},{192,160},{224,192},{65,33},{97... | collective-permute-start | bytes 1105928 | tf_op jit(solution)/shard_map/cond/branch_1_fun/ppermute | solution.py:477
  12.1 4.6 %collective-permute-start.3 = (f32[4,192]{1,0:T(4,128)S(1)}, f32[4,192]{1,0:T(4,128)}, u32[]{:S(2)}, u32[]{:S(2)}) collective-permute-start(f32[4,192]{1,0:T(4,128)S(1)} %get-tuple-element.133), channel_id=1, source_target_pairs={{0,1},{1,0},{2,3},{3,2},{4,5},{5,4},{6,7},{7,6},{8,9},{9,8},{10,11... | collective-permute-start | bytes 9224 | tf_op jit(solution)/shard_map/cond/branch_1_fun/ppermute | solution.py:494
  16.7 2.2 collective-permute-start.2
  18.9 4.7 %collective-permute-done.3 = f32[4,192]{1,0:T(4,128)} collective-permute-done((f32[4,192]{1,0:T(4,128)S(1)}, f32[4,192]{1,0:T(4,128)}, u32[]{:S(2)}, u32[]{:S(2)}) %collective-permute-start.3) | collective-permute-done | bytes 3104 | tf_op jit(solution)/shard_map/cond/branch_1_fun/ppermute | solution.py:494
  26.6 1.7 pack_rows.1
  28.3 3.4 %collective-permute-start.18 = (bf16[5,14,8,192]{3,2,1,0:T(8,128)(2,1)S(1)}, bf16[5,14,8,192]{3,2,1,0:T(8,128)(2,1)S(1)}, u32[]{:S(2)}, u32[]{:S(2)}) collective-permute-start(bf16[5,14,8,192]{3,2,1,0:T(8,128)(2,1)S(1)} %get-tuple-element.199), channel_id=1, source_target_pairs={{0,1},{1,2},{2,3},{3,4},{4,5},{5,6},{6,7},{7,8},{8,9},{9,10},{10,1... | collective-permute-start | bytes 645128 | tf_op jit(solution)/shard_map/ppermute | solution.py:477
  31.7 1.3 collective-permute-start.19
  33.1 3.4 %solve_first.1 = f32[4,192]{1,0:T(4,128)} custom-call(bf16[2,192,6144]{2,1,0:T(8,128)(2,1)} %bitcast.5, bf16[32,4,192]{2,1,0:T(4,128)(2,1)S(1)} %get-tuple-element.245.gathered), custom_call_target="tpu_custom_call" | custom-call | flops 9437184 | bytes 4718592 | tf_op jit(solution)/shard_map/solve_first/pallas_call | solution.py:165
  36.5 2.1 conditional.13
  40.7 2.1 copy-done
  42.9 2.3 %copy-done.1 = bf16[2,192,6144]{2,1,0:T(8,128)(2,1)S(1)} copy-done((bf16[2,192,6144]{2,1,0:T(8,128)(2,1)S(1)}, bf16[2,192,6144]{2,1,0:T(8,128)(2,1)}, u32[]{:S(2)}) %copy-start.1) | copy-done | bytes 4718616
  45.2 2.0 solve_even.5
  47.9 145.8 %conditional.20 = (f32[4,192]{1,0:T(4,128)S(1)}) conditional(s32[]{:T(128)} %convert_element_type.39, f32[4,192]{1,0:T(4,128)S(1)} %get-tuple-element.211, (bf16[2,192,6144]{2,1,0:T(8,128)(2,1)}, bf16[16,4,192]{2,1,0:T(4,128)(2,1)}, f32[4,192]{1,0:T(4,128)}) %tuple.138), branch_computations={%region_18.0_spmd, %region_19.0_spmd} | conditional | flops 9437184 | bytes 4915288 | solution.py:567
  47.9 140.2 %collective-permute-start.13 = (bf16[16,4,192]{2,1,0:T(4,128)(2,1)}, bf16[16,4,192]{2,1,0:T(4,128)(2,1)S(1)}, u32[]{:S(2)}, u32[]{:S(2)}) collective-permute-start(bf16[16,4,192]{2,1,0:T(4,128)(2,1)} %get-tuple-element.165), channel_id=1, source_target_pairs={{0,97},{1,96},{2,99},{3,98},{4,101},{5,100},{6,103},{7,102},{8,105... | collective-permute-start | bytes 73736 | tf_op jit(solution)/shard_map/cond/branch_1_fun/ppermute | solution.py:523
  188.1 2.3 %hold.11.matrix = bf16[2,192,6144]{2,1,0:T(8,128)(2,1)S(1)} custom-call(bf16[2,192,6144]{2,1,0:T(8,128)(2,1)} %get-tuple-element.164.matrix), custom_call_target="tpu_custom_call" | custom-call | tf_op jit(solution)/shard_map/cond/branch_1_fun/hold/pallas_call | solution.py:92
  190.5 1.2 collective-permute-done.12.same
  191.7 2.0 solve_even.4
  193.7 13.1 %smooth.1 = f32[2,2,8,64,192]{4,3,2,1,0:T(8,128)S(1)} custom-call(f32[4]{0:T(128)S(1)} %add_convert_fusion.inside, f32[2,2,8,64,192]{4,3,2,1,0:T(8,128)} %residual.7, f32[8,64,192]{2,1,0:T(8,128)S(1)} %copy-done.13, bf16[5,14,8,192]{3,2,1,0:T(8,128)(2,1)S(1)} %collective-permute-done.18.row_low, ...), custom_call_target="tpu_custom_call" | custom-call | flops 117964800 | bytes 4718592 | tf_op jit(solution)/shard_map/smooth/pallas_call | solution.py:366
  206.9 23.5 %conditional.21 = (f32[2,2,8,64,192]{4,3,2,1,0:T(8,128)}) conditional(s32[]{:T(128)} %convert_element_type.36, (f32[2,2,8,64,192]{4,3,2,1,0:T(8,128)S(1)}, f32[4,192]{1,0:T(4,128)S(1)}) %tuple.108, (bf16[2,192,6144]{2,1,0:T(8,128)(2,1)}, f32[4,192]{1,0:T(4,128)S(1)}, f32[4,192]{1,0:T(4,128)S(1)}, f32[4,192]{1,0:T(4,128)}, ...), branch_computations={%region_20.21_spmd, %region_21.22_spmd} | conditional | bytes 50536680 | solution.py:583
  207.0 3.2 %collective-permute-start.14 = (f32[4,192]{1,0:T(4,128)S(1)}, f32[4,192]{1,0:T(4,128)S(1)}, u32[]{:S(2)}, u32[]{:S(2)}) collective-permute-start(f32[4,192]{1,0:T(4,128)S(1)} %get-tuple-element.170.kept_before), channel_id=1, source_target_pairs={{0,32},{1,33},{2,34},{3,35},{4,36},{5,37},{6,38},{7,39},{8,40},{9,... | collective-permute-start | bytes 9224 | tf_op jit(solution)/shard_map/cond/branch_1_fun/ppermute | solution.py:523
  210.2 3.8 %collective-permute-done.15.far = f32[4,192]{1,0:T(4,128)S(1)} collective-permute-done((f32[4,192]{1,0:T(4,128)S(1)}, f32[4,192]{1,0:T(4,128)S(1)}, u32[]{:S(2)}, u32[]{:S(2)}) %collective-permute-start.15) | collective-permute-done | bytes 3104 | tf_op jit(solution)/shard_map/cond/branch_1_fun/ppermute | solution.py:523
  214.0 1.3 meet.7
  215.3 3.5 %all-to-all-start.7 = ((bf16[16,8,192]{2,1,0:T(8,128)(2,1)}), bf16[16,8,192]{2,1,0:T(8,128)(2,1)S(1)}, u32[]{:S(2)}, u32[]{:S(2)}) async-start(bf16[16,8,192]{2,1,0:T(8,128)(2,1)} %meet.7), calls=%async_computation.7 | async-start | bytes 131072 | tf_op jit(solution)/shard_map/cond/branch_1_fun/all_to_all | solution.py:513
  218.8 2.3 copy-done.8
  221.1 5.3 %all-to-all-done.7.both = bf16[16,8,192]{2,1,0:T(8,128)(2,1)S(1)} async-done(((bf16[16,8,192]{2,1,0:T(8,128)(2,1)}), bf16[16,8,192]{2,1,0:T(8,128)(2,1)S(1)}, u32[]{:S(2)}, u32[]{:S(2)}) %all-to-all-start.7) | async-done | bytes 49184 | tf_op jit(solution)/shard_map/cond/branch_1_fun/all_to_all | solution.py:513
  226.4 2.3 %copy-done.9 = bf16[2,192,6144]{2,1,0:T(8,128)(2,1)S(1)} copy-done((bf16[2,192,6144]{2,1,0:T(8,128)(2,1)S(1)}, bf16[2,192,6144]{2,1,0:T(8,128)(2,1)}, u32[]{:S(2)}) %copy-start.9) | copy-done | bytes 4718616 | tf_op jit(solution)/shard_map/cond
  228.7 1.7 lift.3
  (47 shorter events, 10.6 us)
Async XLA Ops:
  0.0 5.4 %copy-start.10 = (f32[2,2,8,64,192]{4,3,2,1,0:T(8,128)S(1)}, f32[2,2,8,64,192]{4,3,2,1,0:T(8,128)}, u32[]{:S(2)}) copy-start(f32[2,2,8,64,192]{4,3,2,1,0:T(8,128)} %residual.7) | copy-start | bytes 4718596
  1.9 22.4 %collective-permute-start.17 = (bf16[5,3,64,192]{3,2,1,0:T(8,128)(2,1)S(1)}, bf16[5,3,64,192]{3,2,1,0:T(8,128)(2,1)}, u32[]{:S(2)}, u32[]{:S(2)}) collective-permute-start(bf16[5,3,64,192]{3,2,1,0:T(8,128)(2,1)S(1)} %get-tuple-element.197), channel_id=1, source_target_pairs={{32,0},{33,1},{34,2},{35,3},{36,4},{37,5},{38,6},{39,7},{40,8},{41... | collective-permute-start | bytes 1105928 | tf_op jit(solution)/shard_map/ppermute | solution.py:571
  6.5 17.1 %collective-permute-start = (bf16[5,3,64,192]{3,2,1,0:T(8,128)(2,1)S(1)}, bf16[5,3,64,192]{3,2,1,0:T(8,128)(2,1)}, u32[]{:S(2)}, u32[]{:S(2)}) collective-permute-start(bf16[5,3,64,192]{3,2,1,0:T(8,128)(2,1)S(1)} %get-tuple-element.131), channel_id=1, source_target_pairs={{32,64},{64,96},{96,128},{128,160},{160,192},{192,224},{33,65},{65... | collective-permute-start | bytes 1105928 | tf_op jit(solution)/shard_map/cond/branch_1_fun/ppermute | solution.py:477
  8.5 15.2 %collective-permute-start.1 = (bf16[5,3,64,192]{3,2,1,0:T(8,128)(2,1)S(1)}, bf16[5,3,64,192]{3,2,1,0:T(8,128)(2,1)}, u32[]{:S(2)}, u32[]{:S(2)}) collective-permute-start(bf16[5,3,64,192]{3,2,1,0:T(8,128)(2,1)S(1)} %get-tuple-element.132), channel_id=1, source_target_pairs={{64,32},{96,64},{128,96},{160,128},{192,160},{224,192},{65,33},{97... | collective-permute-start | bytes 1105928 | tf_op jit(solution)/shard_map/cond/branch_1_fun/ppermute | solution.py:477
  12.1 11.5 %collective-permute-start.3 = (f32[4,192]{1,0:T(4,128)S(1)}, f32[4,192]{1,0:T(4,128)}, u32[]{:S(2)}, u32[]{:S(2)}) collective-permute-start(f32[4,192]{1,0:T(4,128)S(1)} %get-tuple-element.133), channel_id=1, source_target_pairs={{0,1},{1,0},{2,3},{3,2},{4,5},{5,4},{6,7},{7,6},{8,9},{9,8},{10,11... | collective-permute-start | bytes 9224 | tf_op jit(solution)/shard_map/cond/branch_1_fun/ppermute | solution.py:494
  16.7 6.9 %collective-permute-start.2 = (f32[4,192]{1,0:T(4,128)S(1)}, f32[4,192]{1,0:T(4,128)}, u32[]{:S(2)}, u32[]{:S(2)}) collective-permute-start(f32[4,192]{1,0:T(4,128)S(1)} %get-tuple-element.133), channel_id=1, source_target_pairs={{64,32},{128,96},{192,160},{65,33},{129,97},{193,161},{66,34},{130... | collective-permute-start | bytes 9224 | tf_op jit(solution)/shard_map/cond/branch_1_fun/ppermute | solution.py:492
  23.7 1.8 collective-permute-start.16
  28.3 165.4 %collective-permute-start.18 = (bf16[5,14,8,192]{3,2,1,0:T(8,128)(2,1)S(1)}, bf16[5,14,8,192]{3,2,1,0:T(8,128)(2,1)S(1)}, u32[]{:S(2)}, u32[]{:S(2)}) collective-permute-start(bf16[5,14,8,192]{3,2,1,0:T(8,128)(2,1)S(1)} %get-tuple-element.199), channel_id=1, source_target_pairs={{0,1},{1,2},{2,3},{3,4},{4,5},{5,6},{6,7},{7,8},{8,9},{9,10},{10,1... | collective-permute-start | bytes 645128 | tf_op jit(solution)/shard_map/ppermute | solution.py:477
  31.7 162.0 %collective-permute-start.19 = (bf16[5,14,8,192]{3,2,1,0:T(8,128)(2,1)S(1)}, bf16[5,14,8,192]{3,2,1,0:T(8,128)(2,1)S(1)}, u32[]{:S(2)}, u32[]{:S(2)}) collective-permute-start(bf16[5,14,8,192]{3,2,1,0:T(8,128)(2,1)S(1)} %get-tuple-element.200), channel_id=1, source_target_pairs={{1,0},{2,1},{3,2},{4,3},{5,4},{6,5},{7,6},{8,7},{9,8},{10,9},{11,1... | collective-permute-start | bytes 645128 | tf_op jit(solution)/shard_map/ppermute | solution.py:477
  39.3 3.6 %collective-permute-start.21 = (bf16[16,4,192]{2,1,0:T(4,128)(2,1)S(1)}, bf16[16,4,192]{2,1,0:T(4,128)(2,1)S(1)}, u32[]{:S(2)}, u32[]{:S(2)}) collective-permute-start(bf16[16,4,192]{2,1,0:T(4,128)(2,1)S(1)} %get-tuple-element.248), channel_id=1, source_target_pairs={{96,129},{97,128},{98,131},{99,130},{100,133},{101,132},{102,135},... | collective-permute-start | bytes 73736 | tf_op jit(solution)/shard_map/ppermute | solution.py:530
  40.0 2.9 %collective-permute-start.20 = (bf16[16,4,192]{2,1,0:T(4,128)(2,1)S(1)}, bf16[16,4,192]{2,1,0:T(4,128)(2,1)S(1)}, u32[]{:S(2)}, u32[]{:S(2)}) collective-permute-start(bf16[16,4,192]{2,1,0:T(4,128)(2,1)S(1)} %get-tuple-element.248), channel_id=1, source_target_pairs={{96,128},{97,129},{98,130},{99,131},{100,132},{101,133},{102,134},... | collective-permute-start | bytes 73736 | tf_op jit(solution)/shard_map/ppermute | solution.py:530
  40.7 2.2 copy-start
  42.9 2.3 %copy-start.1 = (bf16[2,192,6144]{2,1,0:T(8,128)(2,1)S(1)}, bf16[2,192,6144]{2,1,0:T(8,128)(2,1)}, u32[]{:S(2)}) copy-start(bf16[2,192,6144]{2,1,0:T(8,128)(2,1)} %copy-done) | copy-start | bytes 14155780
  47.9 145.8 %copy-start.13 = (f32[8,64,192]{2,1,0:T(8,128)S(1)}, f32[8,64,192]{2,1,0:T(8,128)}, u32[]{:S(2)}) copy-start(f32[8,64,192]{2,1,0:T(8,128)} %wavenumber.5) | copy-start | bytes 1179652
  47.9 142.6 %collective-permute-start.13 = (bf16[16,4,192]{2,1,0:T(4,128)(2,1)}, bf16[16,4,192]{2,1,0:T(4,128)(2,1)S(1)}, u32[]{:S(2)}, u32[]{:S(2)}) collective-permute-start(bf16[16,4,192]{2,1,0:T(4,128)(2,1)} %get-tuple-element.165), channel_id=1, source_target_pairs={{0,97},{1,96},{2,99},{3,98},{4,101},{5,100},{6,103},{7,102},{8,105... | collective-permute-start | bytes 73736 | tf_op jit(solution)/shard_map/cond/branch_1_fun/ppermute | solution.py:523
  188.1 3.6 %collective-permute-start.12 = (bf16[16,4,192]{2,1,0:T(4,128)(2,1)}, bf16[16,4,192]{2,1,0:T(4,128)(2,1)S(1)}, u32[]{:S(2)}, u32[]{:S(2)}) collective-permute-start(bf16[16,4,192]{2,1,0:T(4,128)(2,1)} %get-tuple-element.165), channel_id=1, source_target_pairs={{0,96},{1,97},{2,98},{3,99},{4,100},{5,101},{6,102},{7,103},{8,104... | collective-permute-start | bytes 73736 | tf_op jit(solution)/shard_map/cond/branch_1_fun/ppermute | solution.py:523
  206.9 7.0 %copy-start.11 = (f32[2,2,8,64,192]{4,3,2,1,0:T(8,128)}, f32[2,2,8,64,192]{4,3,2,1,0:T(8,128)S(1)}, u32[]{:S(2)}) copy-start(f32[2,2,8,64,192]{4,3,2,1,0:T(8,128)S(1)} %get-tuple-element.169.smoothed) | copy-start | bytes 4718596 | tf_op jit(solution)/shard_map/cond
  206.9 7.0 %collective-permute-start.15 = (f32[4,192]{1,0:T(4,128)S(1)}, f32[4,192]{1,0:T(4,128)S(1)}, u32[]{:S(2)}, u32[]{:S(2)}) collective-permute-start(f32[4,192]{1,0:T(4,128)S(1)} %get-tuple-element.170.kept_before), channel_id=1, source_target_pairs={{0,33},{1,32},{2,35},{3,34},{4,37},{5,36},{6,39},{7,38},{8,41},{9,... | collective-permute-start | bytes 9224 | tf_op jit(solution)/shard_map/cond/branch_1_fun/ppermute | solution.py:523
  207.0 6.9 %collective-permute-start.14 = (f32[4,192]{1,0:T(4,128)S(1)}, f32[4,192]{1,0:T(4,128)S(1)}, u32[]{:S(2)}, u32[]{:S(2)}) collective-permute-start(f32[4,192]{1,0:T(4,128)S(1)} %get-tuple-element.170.kept_before), channel_id=1, source_target_pairs={{0,32},{1,33},{2,34},{3,35},{4,36},{5,37},{6,38},{7,39},{8,40},{9,... | collective-permute-start | bytes 9224 | tf_op jit(solution)/shard_map/cond/branch_1_fun/ppermute | solution.py:523
  215.3 11.1 %all-to-all-start.7 = ((bf16[16,8,192]{2,1,0:T(8,128)(2,1)}), bf16[16,8,192]{2,1,0:T(8,128)(2,1)S(1)}, u32[]{:S(2)}, u32[]{:S(2)}) async-start(bf16[16,8,192]{2,1,0:T(8,128)(2,1)} %meet.7), calls=%async_computation.7 | async-start | bytes 131072 | tf_op jit(solution)/shard_map/cond/branch_1_fun/all_to_all | solution.py:513
  218.8 7.6 %copy-start.12 = (f32[2,2,8,64,192]{4,3,2,1,0:T(8,128)S(1)}, f32[2,2,8,64,192]{4,3,2,1,0:T(8,128)}, u32[]{:S(2)}) copy-start(f32[2,2,8,64,192]{4,3,2,1,0:T(8,128)} %copy-done.11) | copy-start | bytes 4718596 | tf_op jit(solution)/shard_map/cond
  218.8 2.3 copy-start.8
  226.4 2.3 %copy-start.9 = (bf16[2,192,6144]{2,1,0:T(8,128)(2,1)S(1)}, bf16[2,192,6144]{2,1,0:T(8,128)(2,1)}, u32[]{:S(2)}) copy-start(bf16[2,192,6144]{2,1,0:T(8,128)(2,1)} %copy-done.8) | copy-start | bytes 14155780 | tf_op jit(solution)/shard_map/cond

commit v7 on v6

--- a/solution.py
+++ b/solution.py
@@ -26,6 +26,10 @@
 
 def limit(mebibytes):
     return pltpu.CompilerParams(vmem_limit_bytes=mebibytes << 20)
+
+
+def fast(array):
+    return pltpu.with_memory_space_constraint(array, VMEM)
 
 
 def membership(fine, coarse):
@@ -72,9 +76,10 @@
     return pl.pallas_call(
         restrict_kernel,
         out_shape=(
-            jax.ShapeDtypeStruct((2 * shots, cells), f32),
-            jax.ShapeDtypeStruct((devices, 2 * shots, cells), bf16),
+            pltpu.VMEM((2 * shots, cells), f32),
+            pltpu.VMEM((devices, 2 * shots, cells), bf16),
         ),
+        out_specs=[pl.BlockSpec(memory_space=VMEM)] * 2,
         compiler_params=limit(8),
         name="restrict",
     )(residual)
@@ -164,8 +169,9 @@
     pieces = 6
     return pl.pallas_call(
         first_kernel,
-        out_shape=jax.ShapeDtypeStruct((lines, cells), f32),
+        out_shape=pltpu.VMEM((lines, cells), f32),
         in_specs=[pl.BlockSpec(memory_space=pltpu.HBM), pl.BlockSpec(memory_space=VMEM)],
+        out_specs=pl.BlockSpec(memory_space=VMEM),
         scratch_shapes=[
             pltpu.VMEM(matrix.shape, bf16),
             pltpu.VMEM((lines, devices * cells), bf16),
@@ -174,7 +180,7 @@
         compiler_params=limit(8),
         cost_estimate=pl.CostEstimate(flops=4 * matrix.size, bytes_accessed=2 * matrix.size, transcendentals=0),
         name="solve_first",
-    )(matrix, gathered)
+    )(matrix, fast(gathered))
 
 
 def meet_kernel(near, far, rhs, far_rhs, spread):
@@ -190,10 +196,12 @@
     lines, cells = rhs.shape
     return pl.pallas_call(
         meet_kernel,
-        out_shape=jax.ShapeDtypeStruct((columns, 2 * lines, cells), bf16),
+        out_shape=pltpu.VMEM((columns, 2 * lines, cells), bf16),
+        in_specs=[pl.BlockSpec(memory_space=VMEM)] * 4,
+        out_specs=pl.BlockSpec(memory_space=VMEM),
         compiler_params=limit(2),
         name="meet",
-    )(near, far, rhs, far_rhs)
+    )(fast(near), fast(far), fast(rhs), fast(far_rhs))
 
 
 def odd_kernel(step, matrix, both, next_rhs, kept_before, kept, spread, vector):
@@ -209,15 +217,16 @@
     return pl.pallas_call(
         functools.partial(odd_kernel, step),
         out_shape=(
-            jax.ShapeDtypeStruct((lines // 2, cells), f32),
-            jax.ShapeDtypeStruct((columns, lines // 2, cells), bf16),
+            pltpu.VMEM((lines // 2, cells), f32),
+            pltpu.VMEM((columns, lines // 2, cells), bf16),
         ),
         in_specs=[pl.BlockSpec(memory_space=VMEM)] * 4,
+        out_specs=[pl.BlockSpec(memory_space=VMEM)] * 2,
         scratch_shapes=[pltpu.VMEM((lines // 2, 2 * columns * cells), bf16)],
         compiler_params=limit(3),
         cost_estimate=pl.CostEstimate(flops=4 * matrix.size, bytes_accessed=2 * matrix.size, transcendentals=0),
         name="solve_odd",
-    )(matrix, both, next_rhs, kept)
+    )(matrix, fast(both), fast(next_rhs), fast(kept))
 
 
 def even_kernel(step, matrix, same, other, kept_before, kept, vector):
@@ -231,13 +240,14 @@
     columns, lines, cells = same.shape
     return pl.pallas_call(
         functools.partial(even_kernel, step),
-        out_shape=jax.ShapeDtypeStruct((lines, cells), f32),
+        out_shape=pltpu.VMEM((lines, cells), f32),
         in_specs=[pl.BlockSpec(memory_space=VMEM)] * 4,
+        out_specs=pl.BlockSpec(memory_space=VMEM),
         scratch_shapes=[pltpu.VMEM((lines, 2 * columns * cells), bf16)],
         compiler_params=limit(3),
         cost_estimate=pl.CostEstimate(flops=4 * matrix.size, bytes_accessed=2 * matrix.size, transcendentals=0),
         name="solve_even",
-    )(matrix, same, other, kept)
+    )(matrix, fast(same), fast(other), fast(kept))
 
 
 def smooth_kernel(inside, residual, wavenumber, row_low, row_high, deep_low, deep_high, smoothed, gain, source, first, second):
@@ -430,7 +440,7 @@
         scratch_shapes=scratch,
         compiler_params=limit(6),
         name="lift",
-    )(smoothed, kept, *operands)
+    )(smoothed, fast(kept), *operands)
 
 
 def pack_planes_kernel(residual, wavenumber, first, last):
@@ -486,18 +496,12 @@
 
     rhs, spread = restrict(residual, devices)
 
-    def early(residual, wavenumber, rhs):
-        first, last = pack_planes(residual, wavenumber)
-        below, above = both_ways(first, last, "layer", 1)
+    def early(rhs):
         next_rhs = lax.ppermute(rhs, "layer", [(i + 1, i) for i in range(1, layers - 1, 2)])
         ways = [(i, i ^ 1) for i in range(devices)]
-        return below, above, next_rhs, lax.ppermute(rhs, "row", ways)
-
-    def nothing(residual, wavenumber, rhs):
-        planes = jnp.zeros((2 * residual.shape[0] + 1, HALO, *residual.shape[3:]), bf16)
-        return planes, planes, rhs, rhs
-
-    below, above, next_rhs, far_rhs = lax.cond(layer > 0, early, nothing, residual, wavenumber, rhs)
+        return next_rhs, lax.ppermute(rhs, "row", ways)
+
+    next_rhs, far_rhs = lax.cond(layer > 0, early, lambda rhs: (rhs, rhs), rhs)
 
     gathered = lax.cond(
         layer == 0,
@@ -541,7 +545,7 @@
         own = held(step)
         return tuple(solve_odd(step, own, to_odd(step, kept), next_rhs, kept))
 
-    middle = layers // 2
+    open_hops = (2, layers // 2)
     for step in range(1, layers - 1):
         takes_part = (layer == step - 1) | (layer == step)
         if step % 2:
@@ -554,7 +558,7 @@
             )
             continue
         half = lax.cond(layer == step - 1, gather, lambda blocks: blocks, spread)
-        if step == middle:
+        if step in open_hops:
             other, same = send(step, half)
             kept = solve_even(step, held(step), same, other, kept)
             continue
@@ -566,9 +570,16 @@
 
         kept = lax.cond(takes_part, even_step, lambda half, kept: kept, half, kept)
 
+    def planes_of(first, last, pairs):
+        back = [(high, low) for low, high in pairs]
+        return lax.ppermute(last, "layer", pairs), lax.ppermute(first, "layer", back)
+
     first, last = pack_planes(residual, wavenumber)
-    below = jnp.where(layer == 1, lax.ppermute(last, "layer", [(0, 1)]), below)
-    above = jnp.where(layer == 0, lax.ppermute(first, "layer", [(1, 0)]), above)
+    pairs = [(i, i + 1) for i in range(layers - 1) if i != 1]
+    below, above = planes_of(first, last, pairs)
+    late_below, late_above = planes_of(first, last, [(1, 2)])
+    below = jnp.where(layer == 2, late_below, below)
+    above = jnp.where(layer == 1, late_above, above)
     first, last = pack_rows(residual, wavenumber, below, above)
     row_low, row_high = both_ways(first, last, "row")
     smoothed = smooth(inside, residual, wavenumber, row_low, row_high, below, above)

time: 232 us -> 223 us (0.961)
  starting transfers between devices: 167 us -> 150 us
  local copies, waits for them, and re-layouts: 12.6 us -> 20.9 us
  Pallas kernels: 32.7 us -> 28.4 us
  waiting for transfers between devices: 15 us -> 19 us
    ppermute x4, starting transfers between devices: 143 us -> 118 us  [swap(): found.append(lax.ppermute(block, ('layer', 'row'), way))]
    unnamed x8 -> x20, local copies, waits for them, and re-layouts: 4.49 us -> 13.4 us
    ppermute x3 -> x5, starting transfers between devices: 6.73 us -> 15.2 us  [the longest x1 6.64 us: early(): return (next_rhs, lax.ppermute(rhs, 'row', ways))]
    ppermute x3 -> x5, waiting for transfers between devices: 4.73 us -> 8.87 us  [the longest x1 4.77 us: early(): return (next_rhs, lax.ppermute(rhs, 'row', ways))]
    ppermute x2 -> x1, starting transfers between devices: 4.94 us -> 1.29 us  [both_ways(): lax.ppermute(low_block, axis, [(b, a) for a, b in up])]
    ppermute x2 -> x1, starting transfers between devices: 5.27 us -> 6.4 us  [both_ways(): lax.ppermute(high_block, axis, up)]
    pallas_call x5 -> x6, Pallas kernels: 10.6 us -> 9.83 us  [the longest x3 5.34 us: solve_even(): pl.pallas_call(functools.partial(even_kernel, step), out_shape=pltpu.VMEM...]
    cond x13 -> x12, local copies, waits for them, and re-layouts: 7.51 us -> 6.86 us
  transfers between devices with their start and end apart: 15 -> 17, of which waited for: 4 -> 6; matrix products, arithmetic and copies ran while one was open for 2% -> 2% of each run, Pallas kernels for 6% -> 5%
where the time goes in v7:
time: 223 us; the launch traced here: 221 us
  starting transfers between devices  150 us (67%)
  Pallas kernels  28.4 us (13%)
  local copies, waits for them, and re-layouts  20.9 us (9%)
  waiting for transfers between devices  19 us (9%)
  other arithmetic  2.25 us (1%)
    ppermute x4, starting transfers between devices, swap(): found.append(lax.ppermute(block, ('layer', 'row'), way))  118 us
    unnamed x20, local copies, waits for them, and re-layouts  13.4 us
    pallas_call x1, Pallas kernels, smooth(): pl.pallas_call(smooth_kernel, out_shape=jax.ShapeDtypeStruct(residual.sha...  12.7 us
    cond x12, local copies, waits for them, and re-layouts  6.86 us
    ppermute x1, starting transfers between devices, early(): return (next_rhs, lax.ppermute(rhs, 'row', ways))  6.64 us
    ppermute x1, starting transfers between devices, both_ways(): lax.ppermute(high_block, axis, up)  6.4 us
    pallas_call x3, Pallas kernels, solve_even(): pl.pallas_call(functools.partial(even_kernel, step), out_shape=pltpu.VMEM...  5.34 us
    all_to_all x1, waiting for transfers between devices, gather(): lax.all_to_all(blocks, 'row', 0, 0, axis_index_groups=ends, tiled=True)  5.28 us
  transfers between devices with their start and end apart: 17, of which 6 were waited for; matrix products, arithmetic and copies ran while one was open for 2% of the time, Pallas kernels for 5%

profile of v7, /device:TPU:96, one launch (start us, length us, event | category | flops | bytes accessed | tf_op | source)
XLA Modules:
  0.0 221.4 jit_solution(15496384636284790547)
XLA Ops:
  0.0 1.6 copy-done
  3.5 2.0 collective-permute-start.13
  5.6 1.5 collective-permute-start.12
  7.0 3.6 %collective-permute-start.15 = (bf16[5,3,64,192]{3,2,1,0:T(8,128)(2,1)}, bf16[5,3,64,192]{3,2,1,0:T(8,128)(2,1)}, u32[]{:S(2)}, u32[]{:S(2)}) collective-permute-start(bf16[5,3,64,192]{3,2,1,0:T(8,128)(2,1)} %get-tuple-element.168), channel_id=1, source_target_pairs={{32,0},{96,64},{128,96},{160,128},{192,160},{224,192},{33,1},{97,6... | collective-permute-start | bytes 1105928 | tf_op jit(solution)/shard_map/ppermute | solution.py:575
  10.7 1.5 collective-permute-start.14
  12.1 1.8 collective-permute-done.13
  15.0 2.3 %collective-permute-done.15 = bf16[5,3,64,192]{3,2,1,0:T(8,128)(2,1)} collective-permute-done((bf16[5,3,64,192]{3,2,1,0:T(8,128)(2,1)}, bf16[5,3,64,192]{3,2,1,0:T(8,128)(2,1)}, u32[]{:S(2)}, u32[]{:S(2)}) %collective-permute-start.15) | collective-permute-done | bytes 368672 | tf_op jit(solution)/shard_map/ppermute | solution.py:575
  20.1 6.4 %collective-permute-start.16 = (bf16[5,14,8,192]{3,2,1,0:T(8,128)(2,1)}, bf16[5,14,8,192]{3,2,1,0:T(8,128)(2,1)S(1)}, u32[]{:S(2)}, u32[]{:S(2)}) collective-permute-start(bf16[5,14,8,192]{3,2,1,0:T(8,128)(2,1)} %get-tuple-element.169), channel_id=1, source_target_pairs={{0,1},{1,2},{2,3},{3,4},{4,5},{5,6},{6,7},{7,8},{8,9},{9,10},{10,1... | collective-permute-start | bytes 645128 | tf_op jit(solution)/shard_map/ppermute | solution.py:487
  28.3 2.8 %solve_first.1 = f32[4,192]{1,0:T(4,128)S(1)} custom-call(bf16[2,192,6144]{2,1,0:T(8,128)(2,1)} %bitcast.5, bf16[32,4,192]{2,1,0:T(4,128)(2,1)S(1)} %get-tuple-element.209.gathered), custom_call_target="tpu_custom_call" | custom-call | flops 9437184 | bytes 4718592 | tf_op jit(solution)/shard_map/solve_first/pallas_call | solution.py:170
  31.1 15.0 %conditional.11 = (f32[4,192]{1,0:T(4,128)}, f32[4,192]{1,0:T(4,128)}) conditional(s32[]{:T(128)} %convert_element_type.42, f32[4,192]{1,0:T(4,128)S(1)} %get-tuple-element.172, f32[4,192]{1,0:T(4,128)S(1)} %get-tuple-element.172), branch_computations={%region_2.0_spmd, %region_3.0_spmd} | conditional | bytes 24672 | solution.py:504
  31.1 6.6 %collective-permute-start.1 = (f32[4,192]{1,0:T(4,128)S(1)}, f32[4,192]{1,0:T(4,128)}, u32[]{:S(2)}, u32[]{:S(2)}) collective-permute-start(f32[4,192]{1,0:T(4,128)S(1)} %param.3), channel_id=1, source_target_pairs={{0,1},{1,0},{2,3},{3,2},{4,5},{5,4},{6,7},{7,6},{8,9},{9,8},{10,11... | collective-permute-start | bytes 9224 | tf_op jit(solution)/shard_map/cond/branch_1_fun/ppermute | solution.py:502
  37.7 3.5 %collective-permute-start = (f32[4,192]{1,0:T(4,128)S(1)}, f32[4,192]{1,0:T(4,128)}, u32[]{:S(2)}, u32[]{:S(2)}) collective-permute-start(f32[4,192]{1,0:T(4,128)S(1)} %param.3), channel_id=1, source_target_pairs={{64,32},{128,96},{192,160},{65,33},{129,97},{193,161},{66,34},{130... | collective-permute-start | bytes 9224 | tf_op jit(solution)/shard_map/cond/branch_1_fun/ppermute | solution.py:500
  41.3 4.8 %collective-permute-done.1 = f32[4,192]{1,0:T(4,128)} collective-permute-done((f32[4,192]{1,0:T(4,128)S(1)}, f32[4,192]{1,0:T(4,128)}, u32[]{:S(2)}, u32[]{:S(2)}) %collective-permute-start.1) | collective-permute-done | bytes 3104 | tf_op jit(solution)/shard_map/cond/branch_1_fun/ppermute | solution.py:502
  46.1 1.4 conditional.12
  48.8 2.2 copy-done.4
  51.0 2.3 %copy-done.5 = bf16[2,192,6144]{2,1,0:T(8,128)(2,1)S(1)} copy-done((bf16[2,192,6144]{2,1,0:T(8,128)(2,1)S(1)}, bf16[2,192,6144]{2,1,0:T(8,128)(2,1)}, u32[]{:S(2)}) %copy-start.5) | copy-done | bytes 4718616
  56.9 2.2 copy-done.2
  59.1 2.3 %copy-done.3 = bf16[2,192,6144]{2,1,0:T(8,128)(2,1)S(1)} copy-done((bf16[2,192,6144]{2,1,0:T(8,128)(2,1)S(1)}, bf16[2,192,6144]{2,1,0:T(8,128)(2,1)}, u32[]{:S(2)}) %copy-start.3) | copy-done | bytes 4718616
  61.4 2.0 solve_even.5
  64.1 119.9 %conditional.18 = (f32[4,192]{1,0:T(4,128)S(1)}) conditional(s32[]{:T(128)} %convert_element_type.35, f32[4,192]{1,0:T(4,128)S(1)} %get-tuple-element.181, (bf16[2,192,6144]{2,1,0:T(8,128)(2,1)}, bf16[16,4,192]{2,1,0:T(4,128)(2,1)}, f32[4,192]{1,0:T(4,128)}) %tuple.124), branch_computations={%region_16.0_spmd, %region_17.0_spmd} | conditional | flops 9437184 | bytes 4915288 | solution.py:571
  64.1 114.3 %collective-permute-start.9 = (bf16[16,4,192]{2,1,0:T(4,128)(2,1)}, bf16[16,4,192]{2,1,0:T(4,128)(2,1)S(1)}, u32[]{:S(2)}, u32[]{:S(2)}) collective-permute-start(bf16[16,4,192]{2,1,0:T(4,128)(2,1)} %get-tuple-element.141), channel_id=1, source_target_pairs={{0,97},{1,96},{2,99},{3,98},{4,101},{5,100},{6,103},{7,102},{8,105... | collective-permute-start | bytes 73736 | tf_op jit(solution)/shard_map/cond/branch_1_fun/ppermute | solution.py:527
  178.4 2.3 %hold.10.matrix = bf16[2,192,6144]{2,1,0:T(8,128)(2,1)S(1)} custom-call(bf16[2,192,6144]{2,1,0:T(8,128)(2,1)} %get-tuple-element.140.matrix), custom_call_target="tpu_custom_call" | custom-call | tf_op jit(solution)/shard_map/cond/branch_1_fun/hold/pallas_call | solution.py:97
  181.9 2.0 solve_even.3
  185.0 12.7 %smooth.1 = f32[2,2,8,64,192]{4,3,2,1,0:T(8,128)S(1)} custom-call(f32[4]{0:T(128)S(1)} %add_convert_fusion.inside, f32[2,2,8,64,192]{4,3,2,1,0:T(8,128)S(1)} %copy-done.1, f32[8,64,192]{2,1,0:T(8,128)S(1)} %copy-done.15, bf16[5,14,8,192]{3,2,1,0:T(8,128)(2,1)S(1)} %collective-permute-done.16.row_low, ...), custom_call_target="tpu_custom_call" | custom-call | flops 117964800 | bytes 4718592 | tf_op jit(solution)/shard_map/smooth/pallas_call | solution.py:376
  197.7 23.5 %conditional.19 = (f32[2,2,8,64,192]{4,3,2,1,0:T(8,128)}) conditional(s32[]{:T(128)} %convert_element_type.33, (f32[2,2,8,64,192]{4,3,2,1,0:T(8,128)S(1)}, f32[4,192]{1,0:T(4,128)S(1)}) %tuple.96, (bf16[2,192,6144]{2,1,0:T(8,128)(2,1)}, f32[4,192]{1,0:T(4,128)S(1)}, f32[4,192]{1,0:T(4,128)S(1)}, f32[4,192]{1,0:T(4,128)}, ...), branch_computations={%region_18.19_spmd, %region_19.20_spmd} | conditional | bytes 50536680 | solution.py:594
  197.9 3.3 %collective-permute-start.10 = (f32[4,192]{1,0:T(4,128)S(1)}, f32[4,192]{1,0:T(4,128)S(1)}, u32[]{:S(2)}, u32[]{:S(2)}) collective-permute-start(f32[4,192]{1,0:T(4,128)S(1)} %get-tuple-element.146.kept_before), channel_id=1, source_target_pairs={{0,32},{1,33},{2,34},{3,35},{4,36},{5,37},{6,38},{7,39},{8,40},{9,... | collective-permute-start | bytes 9224 | tf_op jit(solution)/shard_map/cond/branch_1_fun/ppermute | solution.py:527
  201.1 3.6 %collective-permute-done.11.far = f32[4,192]{1,0:T(4,128)S(1)} collective-permute-done((f32[4,192]{1,0:T(4,128)S(1)}, f32[4,192]{1,0:T(4,128)S(1)}, u32[]{:S(2)}, u32[]{:S(2)}) %collective-permute-start.11) | collective-permute-done | bytes 3104 | tf_op jit(solution)/shard_map/cond/branch_1_fun/ppermute | solution.py:527
  206.1 3.5 %all-to-all-start.7 = ((bf16[16,8,192]{2,1,0:T(8,128)(2,1)}), bf16[16,8,192]{2,1,0:T(8,128)(2,1)S(1)}, u32[]{:S(2)}, u32[]{:S(2)}) async-start(bf16[16,8,192]{2,1,0:T(8,128)(2,1)} %meet.7), calls=%async_computation.7 | async-start | bytes 131072 | tf_op jit(solution)/shard_map/cond/branch_1_fun/all_to_all | solution.py:517
  209.7 2.3 %copy-done.12 = bf16[2,192,6144]{2,1,0:T(8,128)(2,1)} copy-done((bf16[2,192,6144]{2,1,0:T(8,128)(2,1)}, bf16[2,192,6144]{2,1,0:T(8,128)(2,1)S(1)}, u32[]{:S(2)}) %copy-start.12) | copy-done | bytes 4718616 | tf_op jit(solution)/shard_map/cond
  211.9 5.3 %all-to-all-done.7.both = bf16[16,8,192]{2,1,0:T(8,128)(2,1)S(1)} async-done(((bf16[16,8,192]{2,1,0:T(8,128)(2,1)}), bf16[16,8,192]{2,1,0:T(8,128)(2,1)S(1)}, u32[]{:S(2)}, u32[]{:S(2)}) %all-to-all-start.7) | async-done | bytes 49184 | tf_op jit(solution)/shard_map/cond/branch_1_fun/all_to_all | solution.py:517
  217.2 2.3 %copy-done.13 = bf16[2,192,6144]{2,1,0:T(8,128)(2,1)S(1)} copy-done((bf16[2,192,6144]{2,1,0:T(8,128)(2,1)S(1)}, bf16[2,192,6144]{2,1,0:T(8,128)(2,1)}, u32[]{:S(2)}) %copy-start.13) | copy-done | bytes 4718616 | tf_op jit(solution)/shard_map/cond
  219.6 1.7 lift.3
  (62 shorter events, 19.6 us)
Async XLA Ops:
  0.0 1.6 copy-start
  1.6 1.0 copy-start.14
  2.6 15.8 %copy-start.1 = (f32[2,2,8,64,192]{4,3,2,1,0:T(8,128)S(1)}, f32[2,2,8,64,192]{4,3,2,1,0:T(8,128)}, u32[]{:S(2)}) copy-start(f32[2,2,8,64,192]{4,3,2,1,0:T(8,128)} %residual.7) | copy-start | bytes 4718596
  2.6 15.8 %copy-start.15 = (f32[8,64,192]{2,1,0:T(8,128)S(1)}, f32[8,64,192]{2,1,0:T(8,128)}, u32[]{:S(2)}) copy-start(f32[8,64,192]{2,1,0:T(8,128)} %wavenumber.5) | copy-start | bytes 1179652
  3.5 10.4 %collective-permute-start.13 = (bf16[5,3,64,192]{3,2,1,0:T(8,128)(2,1)S(1)}, bf16[5,3,64,192]{3,2,1,0:T(8,128)(2,1)}, u32[]{:S(2)}, u32[]{:S(2)}) collective-permute-start(bf16[5,3,64,192]{3,2,1,0:T(8,128)(2,1)S(1)} %get-tuple-element.167), channel_id=1, source_target_pairs={{0,32},{64,96},{96,128},{128,160},{160,192},{192,224},{1,33},{65,9... | collective-permute-start | bytes 1105928 | tf_op jit(solution)/shard_map/ppermute | solution.py:575
  5.6 8.3 %collective-permute-start.12 = (bf16[5,3,64,192]{3,2,1,0:T(8,128)(2,1)S(1)}, bf16[5,3,64,192]{3,2,1,0:T(8,128)(2,1)}, u32[]{:S(2)}, u32[]{:S(2)}) collective-permute-start(bf16[5,3,64,192]{3,2,1,0:T(8,128)(2,1)S(1)} %get-tuple-element.167), channel_id=1, source_target_pairs={{32,64},{33,65},{34,66},{35,67},{36,68},{37,69},{38,70},{39,71},{4... | collective-permute-start | bytes 1105928 | tf_op jit(solution)/shard_map/ppermute | solution.py:575
  7.0 10.3 %collective-permute-start.15 = (bf16[5,3,64,192]{3,2,1,0:T(8,128)(2,1)}, bf16[5,3,64,192]{3,2,1,0:T(8,128)(2,1)}, u32[]{:S(2)}, u32[]{:S(2)}) collective-permute-start(bf16[5,3,64,192]{3,2,1,0:T(8,128)(2,1)} %get-tuple-element.168), channel_id=1, source_target_pairs={{32,0},{96,64},{128,96},{160,128},{192,160},{224,192},{33,1},{97,6... | collective-permute-start | bytes 1105928 | tf_op jit(solution)/shard_map/ppermute | solution.py:575
  10.7 6.6 %collective-permute-start.14 = (bf16[5,3,64,192]{3,2,1,0:T(8,128)(2,1)}, bf16[5,3,64,192]{3,2,1,0:T(8,128)(2,1)}, u32[]{:S(2)}, u32[]{:S(2)}) collective-permute-start(bf16[5,3,64,192]{3,2,1,0:T(8,128)(2,1)} %get-tuple-element.168), channel_id=1, source_target_pairs={{64,32},{65,33},{66,34},{67,35},{68,36},{69,37},{70,38},{71,39},{7... | collective-permute-start | bytes 1105928 | tf_op jit(solution)/shard_map/ppermute | solution.py:575
  19.3 0.8 copy-start.16
  20.1 163.9 %collective-permute-start.16 = (bf16[5,14,8,192]{3,2,1,0:T(8,128)(2,1)}, bf16[5,14,8,192]{3,2,1,0:T(8,128)(2,1)S(1)}, u32[]{:S(2)}, u32[]{:S(2)}) collective-permute-start(bf16[5,14,8,192]{3,2,1,0:T(8,128)(2,1)} %get-tuple-element.169), channel_id=1, source_target_pairs={{0,1},{1,2},{2,3},{3,4},{4,5},{5,6},{6,7},{7,8},{8,9},{9,10},{10,1... | collective-permute-start | bytes 645128 | tf_op jit(solution)/shard_map/ppermute | solution.py:487
  26.5 157.5 %collective-permute-start.17 = (bf16[5,14,8,192]{3,2,1,0:T(8,128)(2,1)}, bf16[5,14,8,192]{3,2,1,0:T(8,128)(2,1)}, u32[]{:S(2)}, u32[]{:S(2)}) collective-permute-start(bf16[5,14,8,192]{3,2,1,0:T(8,128)(2,1)} %get-tuple-element.170), channel_id=1, source_target_pairs={{1,0},{2,1},{3,2},{4,3},{5,4},{6,5},{7,6},{8,7},{9,8},{10,9},{11,1... | collective-permute-start | bytes 645128 | tf_op jit(solution)/shard_map/ppermute | solution.py:487
  31.1 15.0 %collective-permute-start.1 = (f32[4,192]{1,0:T(4,128)S(1)}, f32[4,192]{1,0:T(4,128)}, u32[]{:S(2)}, u32[]{:S(2)}) collective-permute-start(f32[4,192]{1,0:T(4,128)S(1)} %param.3), channel_id=1, source_target_pairs={{0,1},{1,0},{2,3},{3,2},{4,5},{5,4},{6,7},{7,6},{8,9},{9,8},{10,11... | collective-permute-start | bytes 9224 | tf_op jit(solution)/shard_map/cond/branch_1_fun/ppermute | solution.py:502
  37.7 8.3 %collective-permute-start = (f32[4,192]{1,0:T(4,128)S(1)}, f32[4,192]{1,0:T(4,128)}, u32[]{:S(2)}, u32[]{:S(2)}) collective-permute-start(f32[4,192]{1,0:T(4,128)S(1)} %param.3), channel_id=1, source_target_pairs={{64,32},{128,96},{192,160},{65,33},{129,97},{193,161},{66,34},{130... | collective-permute-start | bytes 9224 | tf_op jit(solution)/shard_map/cond/branch_1_fun/ppermute | solution.py:500
  47.5 3.5 %collective-permute-start.19 = (bf16[16,4,192]{2,1,0:T(4,128)(2,1)S(1)}, bf16[16,4,192]{2,1,0:T(4,128)(2,1)S(1)}, u32[]{:S(2)}, u32[]{:S(2)}) collective-permute-start(bf16[16,4,192]{2,1,0:T(4,128)(2,1)S(1)} %get-tuple-element.210), channel_id=1, source_target_pairs={{32,65},{33,64},{34,67},{35,66},{36,69},{37,68},{38,71},{39,70},{4... | collective-permute-start | bytes 73736 | tf_op jit(solution)/shard_map/ppermute | solution.py:534
  48.1 2.9 %collective-permute-start.18 = (bf16[16,4,192]{2,1,0:T(4,128)(2,1)S(1)}, bf16[16,4,192]{2,1,0:T(4,128)(2,1)S(1)}, u32[]{:S(2)}, u32[]{:S(2)}) collective-permute-start(bf16[16,4,192]{2,1,0:T(4,128)(2,1)S(1)} %get-tuple-element.210), channel_id=1, source_target_pairs={{32,64},{33,65},{34,66},{35,67},{36,68},{37,69},{38,70},{39,71},{4... | collective-permute-start | bytes 73736 | tf_op jit(solution)/shard_map/ppermute | solution.py:534
  48.8 2.2 copy-start.4
  51.0 2.3 %copy-start.5 = (bf16[2,192,6144]{2,1,0:T(8,128)(2,1)S(1)}, bf16[2,192,6144]{2,1,0:T(8,128)(2,1)}, u32[]{:S(2)}) copy-start(bf16[2,192,6144]{2,1,0:T(8,128)(2,1)} %copy-done.4) | copy-start | bytes 14155780
  55.5 3.6 %collective-permute-start.21 = (bf16[16,4,192]{2,1,0:T(4,128)(2,1)S(1)}, bf16[16,4,192]{2,1,0:T(4,128)(2,1)S(1)}, u32[]{:S(2)}, u32[]{:S(2)}) collective-permute-start(bf16[16,4,192]{2,1,0:T(4,128)(2,1)S(1)} %get-tuple-element.211), channel_id=1, source_target_pairs={{96,129},{97,128},{98,131},{99,130},{100,133},{101,132},{102,135},... | collective-permute-start | bytes 73736 | tf_op jit(solution)/shard_map/ppermute | solution.py:534
  56.1 2.9 %collective-permute-start.20 = (bf16[16,4,192]{2,1,0:T(4,128)(2,1)S(1)}, bf16[16,4,192]{2,1,0:T(4,128)(2,1)S(1)}, u32[]{:S(2)}, u32[]{:S(2)}) collective-permute-start(bf16[16,4,192]{2,1,0:T(4,128)(2,1)S(1)} %get-tuple-element.211), channel_id=1, source_target_pairs={{96,128},{97,129},{98,130},{99,131},{100,132},{101,133},{102,134},... | collective-permute-start | bytes 73736 | tf_op jit(solution)/shard_map/ppermute | solution.py:534
  56.9 2.2 copy-start.2
  59.1 2.3 %copy-start.3 = (bf16[2,192,6144]{2,1,0:T(8,128)(2,1)S(1)}, bf16[2,192,6144]{2,1,0:T(8,128)(2,1)}, u32[]{:S(2)}) copy-start(bf16[2,192,6144]{2,1,0:T(8,128)(2,1)} %copy-done.2) | copy-start | bytes 14155780
  64.1 116.7 %collective-permute-start.9 = (bf16[16,4,192]{2,1,0:T(4,128)(2,1)}, bf16[16,4,192]{2,1,0:T(4,128)(2,1)S(1)}, u32[]{:S(2)}, u32[]{:S(2)}) collective-permute-start(bf16[16,4,192]{2,1,0:T(4,128)(2,1)} %get-tuple-element.141), channel_id=1, source_target_pairs={{0,97},{1,96},{2,99},{3,98},{4,101},{5,100},{6,103},{7,102},{8,105... | collective-permute-start | bytes 73736 | tf_op jit(solution)/shard_map/cond/branch_1_fun/ppermute | solution.py:527
  178.4 3.6 %collective-permute-start.8 = (bf16[16,4,192]{2,1,0:T(4,128)(2,1)}, bf16[16,4,192]{2,1,0:T(4,128)(2,1)S(1)}, u32[]{:S(2)}, u32[]{:S(2)}) collective-permute-start(bf16[16,4,192]{2,1,0:T(4,128)(2,1)} %get-tuple-element.141), channel_id=1, source_target_pairs={{0,96},{1,97},{2,98},{3,99},{4,100},{5,101},{6,102},{7,103},{8,104... | collective-permute-start | bytes 73736 | tf_op jit(solution)/shard_map/cond/branch_1_fun/ppermute | solution.py:527
  184.0 1.0 copy-start.17
  197.8 7.0 %copy-start.18 = (f32[2,2,8,64,192]{4,3,2,1,0:T(8,128)}, f32[2,2,8,64,192]{4,3,2,1,0:T(8,128)S(1)}, u32[]{:S(2)}) copy-start(f32[2,2,8,64,192]{4,3,2,1,0:T(8,128)S(1)} %get-tuple-element.145.smoothed) | copy-start | bytes 4718596 | tf_op jit(solution)/shard_map/cond
  197.8 7.0 %collective-permute-start.11 = (f32[4,192]{1,0:T(4,128)S(1)}, f32[4,192]{1,0:T(4,128)S(1)}, u32[]{:S(2)}, u32[]{:S(2)}) collective-permute-start(f32[4,192]{1,0:T(4,128)S(1)} %get-tuple-element.146.kept_before), channel_id=1, source_target_pairs={{0,33},{1,32},{2,35},{3,34},{4,37},{5,36},{6,39},{7,38},{8,41},{9,... | collective-permute-start | bytes 9224 | tf_op jit(solution)/shard_map/cond/branch_1_fun/ppermute | solution.py:527
  197.9 6.9 %collective-permute-start.10 = (f32[4,192]{1,0:T(4,128)S(1)}, f32[4,192]{1,0:T(4,128)S(1)}, u32[]{:S(2)}, u32[]{:S(2)}) collective-permute-start(f32[4,192]{1,0:T(4,128)S(1)} %get-tuple-element.146.kept_before), channel_id=1, source_target_pairs={{0,32},{1,33},{2,34},{3,35},{4,36},{5,37},{6,38},{7,39},{8,40},{9,... | collective-permute-start | bytes 9224 | tf_op jit(solution)/shard_map/cond/branch_1_fun/ppermute | solution.py:527
  206.1 11.1 %all-to-all-start.7 = ((bf16[16,8,192]{2,1,0:T(8,128)(2,1)}), bf16[16,8,192]{2,1,0:T(8,128)(2,1)S(1)}, u32[]{:S(2)}, u32[]{:S(2)}) async-start(bf16[16,8,192]{2,1,0:T(8,128)(2,1)} %meet.7), calls=%async_computation.7 | async-start | bytes 131072 | tf_op jit(solution)/shard_map/cond/branch_1_fun/all_to_all | solution.py:517
  209.6 7.6 %copy-start.19 = (f32[2,2,8,64,192]{4,3,2,1,0:T(8,128)S(1)}, f32[2,2,8,64,192]{4,3,2,1,0:T(8,128)}, u32[]{:S(2)}) copy-start(f32[2,2,8,64,192]{4,3,2,1,0:T(8,128)} %copy-done.18) | copy-start | bytes 4718596 | tf_op jit(solution)/shard_map/cond
  209.7 2.3 %copy-start.12 = (bf16[2,192,6144]{2,1,0:T(8,128)(2,1)}, bf16[2,192,6144]{2,1,0:T(8,128)(2,1)S(1)}, u32[]{:S(2)}) copy-start(bf16[2,192,6144]{2,1,0:T(8,128)(2,1)S(1)} %hold.11.matrix) | copy-start | bytes 14155780 | tf_op jit(solution)/shard_map/cond
  217.2 2.3 %copy-start.13 = (bf16[2,192,6144]{2,1,0:T(8,128)(2,1)S(1)}, bf16[2,192,6144]{2,1,0:T(8,128)(2,1)}, u32[]{:S(2)}) copy-start(bf16[2,192,6144]{2,1,0:T(8,128)(2,1)} %copy-done.12) | copy-start | bytes 14155780 | tf_op jit(solution)/shard_map/cond

commit v8 on v5

--- a/solution.py
+++ b/solution.py
@@ -440,7 +440,12 @@
     rhs, spread = restrict(residual, devices)
     next_rhs = lax.ppermute(rhs, "layer", [(i + 1, i) for i in range(layers - 1)])
     matrix = pltpu.with_memory_space_constraint(inverse[:, 0], pltpu.HBM)
-    gathered = lax.all_to_all(spread, "row", 0, 0, tiled=True)
+    gathered = lax.cond(
+        layer == 0,
+        lambda blocks: lax.all_to_all(blocks, "row", 0, 0, tiled=True),
+        lambda blocks: blocks,
+        spread,
+    )
     kept, spread = solve_first(matrix, gathered, next_rhs)
 
     ends = [[2 * column + end for column in range(devices // 2)] for end in range(2)]
@@ -475,10 +480,10 @@
         held = hold(step, matrix)
         return solve_layer(step, held, same, other, next_rhs, kept)
 
-    middle = layers // 2
+    open_hops = (2, layers // 2)
     for step in range(1, layers - 1):
         half = gather(step - 1, spread)
-        if step == middle:
+        if step in open_hops:
             kept, spread = solve(step, *send(step, half), kept)
             continue
         kept, spread = lax.cond(
@@ -489,8 +494,16 @@
             kept,
         )
 
+    def planes_of(first, last, pairs):
+        back = [(high, low) for low, high in pairs]
+        return lax.ppermute(last, "layer", pairs), lax.ppermute(first, "layer", back)
+
     first, last = pack_planes(residual, wavenumber)
-    below, above = both_ways(first, last, "layer")
+    pairs = [(i, i + 1) for i in range(layers - 1) if i != 1]
+    below, above = planes_of(first, last, pairs)
+    late_below, late_above = planes_of(first, last, [(1, 2)])
+    below = jnp.where(layer == 2, late_below, below)
+    above = jnp.where(layer == 1, late_above, above)
     first, last = pack_rows(residual, wavenumber, below, above)
     row_low, row_high = both_ways(first, last, "row")
     smoothed = smooth(inside, residual, wavenumber, row_low, row_high, below, above)

time: 190 us -> 196 us (1.032)
  waiting for transfers between devices: 24.4 us -> 10.7 us
  starting transfers between devices: 120 us -> 132 us
  local copies, waits for them, and re-layouts: 8.2 us -> 13.5 us
  other arithmetic: 0.08 us -> 2.25 us
    ppermute x4, starting transfers between devices: 88.3 us -> 109 us  [swap(): found.append(lax.ppermute(half, ('layer', 'row'), way))]
    all_to_all x1 -> x0, starting transfers between devices: 13.8 us -> none  [every_layer(): gathered = lax.all_to_all(spread, 'row', 0, 0, tiled=True)]
    all_to_all x1 -> x0, waiting for transfers between devices: 8.96 us -> none  [every_layer(): gathered = lax.all_to_all(spread, 'row', 0, 0, tiled=True)]
    ppermute x0 -> x4, starting transfers between devices: none -> 8.61 us  [the longest x2 5.11 us: planes_of(): lax.ppermute(first, 'layer', back)]
    unnamed x16 -> x20, local copies, waits for them, and re-layouts: 8.19 us -> 13.5 us
    ppermute x2 -> x1, waiting for transfers between devices: 4.57 us -> 0.01 us  [both_ways(): lax.ppermute(high_block, axis, up)]
    ppermute x0 -> x4, waiting for transfers between devices: none -> 4.08 us  [the longest x2 2.33 us: planes_of(): lax.ppermute(first, 'layer', back)]
    ppermute x2 -> x1, starting transfers between devices: 4.93 us -> 1.29 us  [both_ways(): lax.ppermute(low_block, axis, [(b, a) for a, b in up])]
  transfers between devices with their start and end apart: 12 -> 15, of which waited for: 6 -> 5; matrix products, arithmetic and copies ran while one was open for 0% -> 1% of each run, Pallas kernels for 5% -> 5%
where the time goes in v8:
time: 196 us; the launch traced here: 195 us
  starting transfers between devices  132 us (67%)
  Pallas kernels  25.9 us (13%)
  local copies, waits for them, and re-layouts  13.5 us (7%)
  waiting for transfers between devices  10.7 us (5%)
  blocking collectives  10.7 us (5%)
  other arithmetic  2.25 us (1%)
    ppermute x4, starting transfers between devices, swap(): found.append(lax.ppermute(half, ('layer', 'row'), way))  109 us
    unnamed x20, local copies, waits for them, and re-layouts  13.5 us
    pallas_call x1, Pallas kernels, smooth(): pl.pallas_call(smooth_kernel, out_shape=jax.ShapeDtypeStruct(residual.sha...  12.8 us
    all_to_all x1, blocking collectives, gather(): lax.all_to_all(blocks, 'row', 0, 0, axis_index_groups=ends, tiled=True)  10.7 us
    ppermute x1, starting transfers between devices, both_ways(): lax.ppermute(high_block, axis, up)  6.4 us
    ppermute x4, waiting for transfers between devices, swap(): found.append(lax.ppermute(half, ('layer', 'row'), way))  5.29 us
    ppermute x2, starting transfers between devices, planes_of(): lax.ppermute(first, 'layer', back)  5.11 us
    pallas_call x3, Pallas kernels, solve_layer(): pl.pallas_call(functools.partial(layer_kernel, step), out_shape=(jax.Shap...  4.13 us
  transfers between devices with their start and end apart: 15, of which 5 were waited for; matrix products, arithmetic and copies ran while one was open for 1% of the time, Pallas kernels for 5%

profile of v8, /device:TPU:96, one launch (start us, length us, event | category | flops | bytes accessed | tf_op | source)
XLA Modules:
  0.0 195.4 jit_solution(11740331982233569719)
XLA Ops:
  0.0 1.6 copy-done
  1.6 1.0 copy-done.6
  3.5 2.0 %collective-permute-start.11 = (bf16[5,3,64,192]{3,2,1,0:T(8,128)(2,1)S(1)}, bf16[5,3,64,192]{3,2,1,0:T(8,128)(2,1)}, u32[]{:S(2)}, u32[]{:S(2)}) collective-permute-start(bf16[5,3,64,192]{3,2,1,0:T(8,128)(2,1)S(1)} %get-tuple-element.170), channel_id=1, source_target_pairs={{0,32},{64,96},{96,128},{128,160},{160,192},{192,224},{1,33},{65,9... | collective-permute-start | bytes 1105928 | tf_op jit(solution)/shard_map/ppermute | solution.py:499
  5.6 1.5 collective-permute-start.10
  7.0 3.6 %collective-permute-start.13 = (bf16[5,3,64,192]{3,2,1,0:T(8,128)(2,1)}, bf16[5,3,64,192]{3,2,1,0:T(8,128)(2,1)}, u32[]{:S(2)}, u32[]{:S(2)}) collective-permute-start(bf16[5,3,64,192]{3,2,1,0:T(8,128)(2,1)} %get-tuple-element.171), channel_id=1, source_target_pairs={{32,0},{96,64},{128,96},{160,128},{192,160},{224,192},{33,1},{97,6... | collective-permute-start | bytes 1105928 | tf_op jit(solution)/shard_map/ppermute | solution.py:499
  10.7 1.5 collective-permute-start.12
  12.1 1.7 collective-permute-done.11
  13.9 1.1 broadcast_select_fusion.1.below.deep_low
  15.0 2.3 %collective-permute-done.13 = bf16[5,3,64,192]{3,2,1,0:T(8,128)(2,1)} collective-permute-done((bf16[5,3,64,192]{3,2,1,0:T(8,128)(2,1)}, bf16[5,3,64,192]{3,2,1,0:T(8,128)(2,1)}, u32[]{:S(2)}, u32[]{:S(2)}) %collective-permute-start.13) | collective-permute-done | bytes 368672 | tf_op jit(solution)/shard_map/ppermute | solution.py:499
  17.3 1.1 broadcast_select_fusion.above.deep_high
  20.1 6.4 %collective-permute-start.14 = (bf16[5,14,8,192]{3,2,1,0:T(8,128)(2,1)}, bf16[5,14,8,192]{3,2,1,0:T(8,128)(2,1)S(1)}, u32[]{:S(2)}, u32[]{:S(2)}) collective-permute-start(bf16[5,14,8,192]{3,2,1,0:T(8,128)(2,1)} %get-tuple-element.172), channel_id=1, source_target_pairs={{0,1},{1,2},{2,3},{3,4},{4,5},{5,6},{6,7},{7,8},{8,9},{9,10},{10,1... | collective-permute-start | bytes 645128 | tf_op jit(solution)/shard_map/ppermute | solution.py:432
  26.5 1.3 collective-permute-start.15
  28.2 3.5 %collective-permute-start.16 = (f32[4,192]{1,0:T(4,128)S(1)}, f32[4,192]{1,0:T(4,128)S(1)}, u32[]{:S(2)}, u32[]{:S(2)}) collective-permute-start(f32[4,192]{1,0:T(4,128)S(1)} %get-tuple-element.175), channel_id=1, source_target_pairs={{32,0},{64,32},{96,64},{128,96},{160,128},{192,160},{224,192},{33,... | collective-permute-start | bytes 9224 | tf_op jit(solution)/shard_map/ppermute | solution.py:441
  31.8 1.3 collective-permute-done.16.next_rhs
  33.0 2.8 %solve_first.1 = (f32[4,192]{1,0:T(4,128)S(1)}, bf16[16,4,192]{2,1,0:T(4,128)(2,1)S(1)}) custom-call(bf16[2,192,6144]{2,1,0:T(8,128)(2,1)} %bitcast.5, bf16[32,4,192]{2,1,0:T(4,128)(2,1)S(1)} %get-tuple-element.209.gathered, f32[4,192]{1,0:T(4,128)S(1)} %collective-permute-done.16.next_rhs), custom_call_target="tpu_custom_call" | custom-call | flops 9437184 | bytes 4718592 | tf_op jit(solution)/shard_map/solve_first/pallas_call | solution.py:155
  37.3 2.2 %copy-done.2 = bf16[2,192,6144]{2,1,0:T(8,128)(2,1)} copy-done((bf16[2,192,6144]{2,1,0:T(8,128)(2,1)}, bf16[2,192,6144]{2,1,0:T(8,128)(2,1)S(1)}, u32[]{:S(2)}) %copy-start.2) | copy-done | bytes 4718616
  39.5 2.3 %copy-done.3 = bf16[2,192,6144]{2,1,0:T(8,128)(2,1)S(1)} copy-done((bf16[2,192,6144]{2,1,0:T(8,128)(2,1)S(1)}, bf16[2,192,6144]{2,1,0:T(8,128)(2,1)}, u32[]{:S(2)}) %copy-start.3) | copy-done | bytes 4718616
  41.8 1.4 solve_layer.10
  44.7 2.2 %copy-done.4 = bf16[2,192,6144]{2,1,0:T(8,128)(2,1)} copy-done((bf16[2,192,6144]{2,1,0:T(8,128)(2,1)}, bf16[2,192,6144]{2,1,0:T(8,128)(2,1)S(1)}, u32[]{:S(2)}) %copy-start.4) | copy-done | bytes 4718616
  46.9 2.3 %copy-done.5 = bf16[2,192,6144]{2,1,0:T(8,128)(2,1)S(1)} copy-done((bf16[2,192,6144]{2,1,0:T(8,128)(2,1)S(1)}, bf16[2,192,6144]{2,1,0:T(8,128)(2,1)}, u32[]{:S(2)}) %copy-start.5) | copy-done | bytes 4718616
  49.2 1.4 solve_layer.11
  50.7 111.0 %conditional.23 = ((f32[4,192]{1,0:T(4,128)S(1)}, bf16[16,4,192]{2,1,0:T(4,128)(2,1)S(1)})) conditional(s32[]{:T(128)} %convert_element_type.42, (f32[4,192]{1,0:T(4,128)S(1)}, bf16[16,4,192]{2,1,0:T(4,128)(2,1)S(1)}) %tuple.105, (bf16[2,192,6144]{2,1,0:T(8,128)(2,1)}, bf16[16,4,192]{2,1,0:T(4,128)(2,1)S(1)}, f32[4,192]{1,0:T(4,128)S(1)}, ...), branch_computations={%region_20.0_spmd, %region_21.0_spmd} | conditional | flops 9437184 | bytes 4921432 | solution.py:489
  50.7 106.0 %collective-permute-start.7 = (bf16[16,4,192]{2,1,0:T(4,128)(2,1)S(1)}, bf16[16,4,192]{2,1,0:T(4,128)(2,1)S(1)}, u32[]{:S(2)}, u32[]{:S(2)}) collective-permute-start(bf16[16,4,192]{2,1,0:T(4,128)(2,1)S(1)} %get-tuple-element.141), channel_id=1, source_target_pairs={{0,97},{1,96},{2,99},{3,98},{4,101},{5,100},{6,103},{7,102},{8,105... | collective-permute-start | bytes 73736 | tf_op jit(solution)/shard_map/cond/branch_1_fun/ppermute | solution.py:469
  156.7 2.3 %hold.10.matrix = bf16[2,192,6144]{2,1,0:T(8,128)(2,1)S(1)} custom-call(bf16[2,192,6144]{2,1,0:T(8,128)(2,1)} %get-tuple-element.140.matrix), custom_call_target="tpu_custom_call" | custom-call | tf_op jit(solution)/shard_map/cond/branch_1_fun/hold/pallas_call | solution.py:92
  160.1 1.4 solve_layer.9
  161.6 10.8 %conditional.24 = (bf16[16,4,192]{2,1,0:T(4,128)(2,1)S(1)}) conditional(s32[]{:T(128)} %convert_element_type.52, bf16[16,4,192]{2,1,0:T(4,128)(2,1)S(1)} %get-tuple-element.189, bf16[16,4,192]{2,1,0:T(4,128)(2,1)S(1)} %get-tuple-element.189), branch_computations={%region_22.23_spmd, %region_23.24_spmd} | conditional | bytes 98312 | solution.py:454
  161.7 10.7 %all_to_all.39 = bf16[16,4,192]{2,1,0:T(4,128)(2,1)S(1)} all-to-all(bf16[16,4,192]{2,1,0:T(4,128)(2,1)S(1)} %copy.55), channel_id=1, replica_groups={{0,2,4,6,8,10,12,14,16,18,20,22,24,26,28,30},{1,3,5,7,9,11,13,15,17,19,..., dimensions={0} | all-to-all | bytes 49152 | tf_op jit(solution)/shard_map/cond/branch_1_fun/all_to_all | solution.py:456
  173.4 12.8 %smooth.1 = f32[2,2,8,64,192]{4,3,2,1,0:T(8,128)S(1)} custom-call(f32[4]{0:T(128)S(1)} %add_convert_fusion.inside, f32[2,2,8,64,192]{4,3,2,1,0:T(8,128)S(1)} %copy-done.1, f32[8,64,192]{2,1,0:T(8,128)S(1)} %copy-done.7, bf16[5,14,8,192]{3,2,1,0:T(8,128)(2,1)S(1)} %collective-permute-done.14.row_low, ...), custom_call_target="tpu_custom_call" | custom-call | flops 117964800 | bytes 4718592 | tf_op jit(solution)/shard_map/smooth/pallas_call | solution.py:320
  186.2 9.1 %conditional.25 = (f32[2,2,8,64,192]{4,3,2,1,0:T(8,128)}) conditional(s32[]{:T(128)} %convert_element_type.40, (f32[2,2,8,64,192]{4,3,2,1,0:T(8,128)S(1)}, f32[4,192]{1,0:T(4,128)S(1)}) %tuple.107, (bf16[2,192,6144]{2,1,0:T(8,128)(2,1)}, bf16[16,4,192]{2,1,0:T(4,128)(2,1)S(1)}, f32[2,2,8,64,192]{4,3,2,1,0:T(8,128)S(1)}, ...), branch_computations={%region_24.25_spmd, %region_25.26_spmd} | conditional | bytes 196696 | solution.py:519
  186.3 2.9 %collective-permute-start.8 = (bf16[16,4,192]{2,1,0:T(4,128)(2,1)S(1)}, bf16[16,4,192]{2,1,0:T(4,128)(2,1)S(1)}, u32[]{:S(2)}, u32[]{:S(2)}) collective-permute-start(bf16[16,4,192]{2,1,0:T(4,128)(2,1)S(1)} %get-tuple-element.149), channel_id=1, source_target_pairs={{0,32},{1,33},{2,34},{3,35},{4,36},{5,37},{6,38},{7,39},{8,40},{9,... | collective-permute-start | bytes 73736 | tf_op jit(solution)/shard_map/cond/branch_1_fun/ppermute | solution.py:469
  189.2 4.3 %collective-permute-done.9.other = bf16[16,4,192]{2,1,0:T(4,128)(2,1)S(1)} collective-permute-done((bf16[16,4,192]{2,1,0:T(4,128)(2,1)S(1)}, bf16[16,4,192]{2,1,0:T(4,128)(2,1)S(1)}, u32[]{:S(2)}, u32[]{:S(2)}) %collective-permute-start.9) | collective-permute-done | bytes 24608 | tf_op jit(solution)/shard_map/cond/branch_1_fun/ppermute | solution.py:469
  193.5 1.7 lift.3
  (50 shorter events, 7.9 us)
Async XLA Ops:
  0.0 1.6 copy-start
  1.6 1.0 copy-start.6
  2.6 15.8 %copy-start.1 = (f32[2,2,8,64,192]{4,3,2,1,0:T(8,128)S(1)}, f32[2,2,8,64,192]{4,3,2,1,0:T(8,128)}, u32[]{:S(2)}) copy-start(f32[2,2,8,64,192]{4,3,2,1,0:T(8,128)} %residual.7) | copy-start | bytes 4718596
  2.6 15.8 %copy-start.7 = (f32[8,64,192]{2,1,0:T(8,128)S(1)}, f32[8,64,192]{2,1,0:T(8,128)}, u32[]{:S(2)}) copy-start(f32[8,64,192]{2,1,0:T(8,128)} %wavenumber.5) | copy-start | bytes 1179652
  3.5 10.4 %collective-permute-start.11 = (bf16[5,3,64,192]{3,2,1,0:T(8,128)(2,1)S(1)}, bf16[5,3,64,192]{3,2,1,0:T(8,128)(2,1)}, u32[]{:S(2)}, u32[]{:S(2)}) collective-permute-start(bf16[5,3,64,192]{3,2,1,0:T(8,128)(2,1)S(1)} %get-tuple-element.170), channel_id=1, source_target_pairs={{0,32},{64,96},{96,128},{128,160},{160,192},{192,224},{1,33},{65,9... | collective-permute-start | bytes 1105928 | tf_op jit(solution)/shard_map/ppermute | solution.py:499
  5.6 8.3 %collective-permute-start.10 = (bf16[5,3,64,192]{3,2,1,0:T(8,128)(2,1)S(1)}, bf16[5,3,64,192]{3,2,1,0:T(8,128)(2,1)}, u32[]{:S(2)}, u32[]{:S(2)}) collective-permute-start(bf16[5,3,64,192]{3,2,1,0:T(8,128)(2,1)S(1)} %get-tuple-element.170), channel_id=1, source_target_pairs={{32,64},{33,65},{34,66},{35,67},{36,68},{37,69},{38,70},{39,71},{4... | collective-permute-start | bytes 1105928 | tf_op jit(solution)/shard_map/ppermute | solution.py:499
  7.0 10.3 %collective-permute-start.13 = (bf16[5,3,64,192]{3,2,1,0:T(8,128)(2,1)}, bf16[5,3,64,192]{3,2,1,0:T(8,128)(2,1)}, u32[]{:S(2)}, u32[]{:S(2)}) collective-permute-start(bf16[5,3,64,192]{3,2,1,0:T(8,128)(2,1)} %get-tuple-element.171), channel_id=1, source_target_pairs={{32,0},{96,64},{128,96},{160,128},{192,160},{224,192},{33,1},{97,6... | collective-permute-start | bytes 1105928 | tf_op jit(solution)/shard_map/ppermute | solution.py:499
  10.7 6.6 %collective-permute-start.12 = (bf16[5,3,64,192]{3,2,1,0:T(8,128)(2,1)}, bf16[5,3,64,192]{3,2,1,0:T(8,128)(2,1)}, u32[]{:S(2)}, u32[]{:S(2)}) collective-permute-start(bf16[5,3,64,192]{3,2,1,0:T(8,128)(2,1)} %get-tuple-element.171), channel_id=1, source_target_pairs={{64,32},{65,33},{66,34},{67,35},{68,36},{69,37},{70,38},{71,39},{7... | collective-permute-start | bytes 1105928 | tf_op jit(solution)/shard_map/ppermute | solution.py:499
  19.3 0.8 copy-start.8
  20.1 152.3 %collective-permute-start.14 = (bf16[5,14,8,192]{3,2,1,0:T(8,128)(2,1)}, bf16[5,14,8,192]{3,2,1,0:T(8,128)(2,1)S(1)}, u32[]{:S(2)}, u32[]{:S(2)}) collective-permute-start(bf16[5,14,8,192]{3,2,1,0:T(8,128)(2,1)} %get-tuple-element.172), channel_id=1, source_target_pairs={{0,1},{1,2},{2,3},{3,4},{4,5},{5,6},{6,7},{7,8},{8,9},{9,10},{10,1... | collective-permute-start | bytes 645128 | tf_op jit(solution)/shard_map/ppermute | solution.py:432
  26.5 145.9 %collective-permute-start.15 = (bf16[5,14,8,192]{3,2,1,0:T(8,128)(2,1)}, bf16[5,14,8,192]{3,2,1,0:T(8,128)(2,1)}, u32[]{:S(2)}, u32[]{:S(2)}) collective-permute-start(bf16[5,14,8,192]{3,2,1,0:T(8,128)(2,1)} %get-tuple-element.173), channel_id=1, source_target_pairs={{1,0},{2,1},{3,2},{4,3},{5,4},{6,5},{7,6},{8,7},{9,8},{10,9},{11,1... | collective-permute-start | bytes 645128 | tf_op jit(solution)/shard_map/ppermute | solution.py:432
  28.2 4.8 %collective-permute-start.16 = (f32[4,192]{1,0:T(4,128)S(1)}, f32[4,192]{1,0:T(4,128)S(1)}, u32[]{:S(2)}, u32[]{:S(2)}) collective-permute-start(f32[4,192]{1,0:T(4,128)S(1)} %get-tuple-element.175), channel_id=1, source_target_pairs={{32,0},{64,32},{96,64},{128,96},{160,128},{192,160},{224,192},{33,... | collective-permute-start | bytes 9224 | tf_op jit(solution)/shard_map/ppermute | solution.py:441
  35.9 3.6 %collective-permute-start.18 = (bf16[16,4,192]{2,1,0:T(4,128)(2,1)S(1)}, bf16[16,4,192]{2,1,0:T(4,128)(2,1)S(1)}, u32[]{:S(2)}, u32[]{:S(2)}) collective-permute-start(bf16[16,4,192]{2,1,0:T(4,128)(2,1)S(1)} %get-tuple-element.212), channel_id=1, source_target_pairs={{32,65},{33,64},{34,67},{35,66},{36,69},{37,68},{38,71},{39,70},{4... | collective-permute-start | bytes 73736 | tf_op jit(solution)/shard_map/ppermute | solution.py:476
  36.6 2.9 %collective-permute-start.17 = (bf16[16,4,192]{2,1,0:T(4,128)(2,1)S(1)}, bf16[16,4,192]{2,1,0:T(4,128)(2,1)S(1)}, u32[]{:S(2)}, u32[]{:S(2)}) collective-permute-start(bf16[16,4,192]{2,1,0:T(4,128)(2,1)S(1)} %get-tuple-element.212), channel_id=1, source_target_pairs={{32,64},{33,65},{34,66},{35,67},{36,68},{37,69},{38,70},{39,71},{4... | collective-permute-start | bytes 73736 | tf_op jit(solution)/shard_map/ppermute | solution.py:476
  37.3 2.2 %copy-start.2 = (bf16[2,192,6144]{2,1,0:T(8,128)(2,1)}, bf16[2,192,6144]{2,1,0:T(8,128)(2,1)S(1)}, u32[]{:S(2)}) copy-start(bf16[2,192,6144]{2,1,0:T(8,128)(2,1)S(1)} %hold.13.matrix) | copy-start | bytes 14155780
  39.5 2.3 %copy-start.3 = (bf16[2,192,6144]{2,1,0:T(8,128)(2,1)S(1)}, bf16[2,192,6144]{2,1,0:T(8,128)(2,1)}, u32[]{:S(2)}) copy-start(bf16[2,192,6144]{2,1,0:T(8,128)(2,1)} %copy-done.2) | copy-start | bytes 14155780
  43.2 3.6 %collective-permute-start.20 = (bf16[16,4,192]{2,1,0:T(4,128)(2,1)S(1)}, bf16[16,4,192]{2,1,0:T(4,128)(2,1)S(1)}, u32[]{:S(2)}, u32[]{:S(2)}) collective-permute-start(bf16[16,4,192]{2,1,0:T(4,128)(2,1)S(1)} %get-tuple-element.215), channel_id=1, source_target_pairs={{96,129},{97,128},{98,131},{99,130},{100,133},{101,132},{102,135},... | collective-permute-start | bytes 73736 | tf_op jit(solution)/shard_map/ppermute | solution.py:476
  43.9 3.0 %collective-permute-start.19 = (bf16[16,4,192]{2,1,0:T(4,128)(2,1)S(1)}, bf16[16,4,192]{2,1,0:T(4,128)(2,1)S(1)}, u32[]{:S(2)}, u32[]{:S(2)}) collective-permute-start(bf16[16,4,192]{2,1,0:T(4,128)(2,1)S(1)} %get-tuple-element.215), channel_id=1, source_target_pairs={{96,128},{97,129},{98,130},{99,131},{100,132},{101,133},{102,134},... | collective-permute-start | bytes 73736 | tf_op jit(solution)/shard_map/ppermute | solution.py:476
  44.7 2.2 %copy-start.4 = (bf16[2,192,6144]{2,1,0:T(8,128)(2,1)}, bf16[2,192,6144]{2,1,0:T(8,128)(2,1)S(1)}, u32[]{:S(2)}) copy-start(bf16[2,192,6144]{2,1,0:T(8,128)(2,1)S(1)} %hold.12.matrix) | copy-start | bytes 14155780
  46.9 2.3 %copy-start.5 = (bf16[2,192,6144]{2,1,0:T(8,128)(2,1)S(1)}, bf16[2,192,6144]{2,1,0:T(8,128)(2,1)}, u32[]{:S(2)}) copy-start(bf16[2,192,6144]{2,1,0:T(8,128)(2,1)} %copy-done.4) | copy-start | bytes 14155780
  50.7 108.4 %collective-permute-start.7 = (bf16[16,4,192]{2,1,0:T(4,128)(2,1)S(1)}, bf16[16,4,192]{2,1,0:T(4,128)(2,1)S(1)}, u32[]{:S(2)}, u32[]{:S(2)}) collective-permute-start(bf16[16,4,192]{2,1,0:T(4,128)(2,1)S(1)} %get-tuple-element.141), channel_id=1, source_target_pairs={{0,97},{1,96},{2,99},{3,98},{4,101},{5,100},{6,103},{7,102},{8,105... | collective-permute-start | bytes 73736 | tf_op jit(solution)/shard_map/cond/branch_1_fun/ppermute | solution.py:469
  156.7 3.3 %collective-permute-start.6 = (bf16[16,4,192]{2,1,0:T(4,128)(2,1)S(1)}, bf16[16,4,192]{2,1,0:T(4,128)(2,1)S(1)}, u32[]{:S(2)}, u32[]{:S(2)}) collective-permute-start(bf16[16,4,192]{2,1,0:T(4,128)(2,1)S(1)} %get-tuple-element.141), channel_id=1, source_target_pairs={{0,96},{1,97},{2,98},{3,99},{4,100},{5,101},{6,102},{7,103},{8,104... | collective-permute-start | bytes 73736 | tf_op jit(solution)/shard_map/cond/branch_1_fun/ppermute | solution.py:469
  172.4 1.0 copy-start.9
  186.2 7.3 %collective-permute-start.9 = (bf16[16,4,192]{2,1,0:T(4,128)(2,1)S(1)}, bf16[16,4,192]{2,1,0:T(4,128)(2,1)S(1)}, u32[]{:S(2)}, u32[]{:S(2)}) collective-permute-start(bf16[16,4,192]{2,1,0:T(4,128)(2,1)S(1)} %get-tuple-element.149), channel_id=1, source_target_pairs={{0,33},{1,32},{2,35},{3,34},{4,37},{5,36},{6,39},{7,38},{8,41},{9,... | collective-permute-start | bytes 73736 | tf_op jit(solution)/shard_map/cond/branch_1_fun/ppermute | solution.py:469
  186.3 7.2 %collective-permute-start.8 = (bf16[16,4,192]{2,1,0:T(4,128)(2,1)S(1)}, bf16[16,4,192]{2,1,0:T(4,128)(2,1)S(1)}, u32[]{:S(2)}, u32[]{:S(2)}) collective-permute-start(bf16[16,4,192]{2,1,0:T(4,128)(2,1)S(1)} %get-tuple-element.149), channel_id=1, source_target_pairs={{0,32},{1,33},{2,34},{3,35},{4,36},{5,37},{6,38},{7,39},{8,40},{9,... | collective-permute-start | bytes 73736 | tf_op jit(solution)/shard_map/cond/branch_1_fun/ppermute | solution.py:469

commit v9 on v8

--- a/solution.py
+++ b/solution.py
@@ -13,6 +13,7 @@
 SWEEPS = 4
 HALO = SWEEPS - 1
 ROWS = 8
+SENT = 4
 LANES = 256
 
 damping = 0.8
@@ -241,7 +242,7 @@
     for base, count, factor in ((0, HALO, inside[0]), (HALO, depth, 1.0), (HALO + depth, HALO, inside[1])):
 
         def row_gain(plane, _, factor=factor):
-            put_gain(plane, top, row_low[2 * shots, plane].astype(f32), factor * inside[2])
+            put_gain(plane, start - SENT, row_low[2 * shots, plane].astype(f32), factor * inside[2])
             put_gain(plane, start + height, row_high[2 * shots, plane].astype(f32), factor * inside[3])
             return _
 
@@ -270,8 +271,8 @@
 
         def row_source(plane, _):
             for part in range(2):
-                source[part, plane, top:start, 0:width] = row_low[2 * shot + part, plane].astype(f32)
-                source[part, plane, start + height : start + height + ROWS, 0:width] = row_high[
+                source[part, plane, start - SENT : start, 0:width] = row_low[2 * shot + part, plane].astype(f32)
+                source[part, plane, start + height : start + height + SENT, 0:width] = row_high[
                     2 * shot + part, plane
                 ].astype(f32)
             return _
@@ -407,8 +408,8 @@
 
 def pack_rows_kernel(residual, wavenumber, below, above, first, last):
     shots, _, depth, height, width = residual.shape
-    for out, base in ((first, 0), (last, height - ROWS)):
-        rows = slice(base, base + ROWS)
+    for out, base in ((first, 0), (last, height - SENT)):
+        rows = slice(base, base + SENT)
         for field in range(2 * shots + 1):
             for plane in range(HALO):
                 out[field, plane] = below[field, plane, rows, :]
@@ -420,7 +421,7 @@
 
 def pack_rows(residual, wavenumber, below, above):
     shots, _, depth, _, width = residual.shape
-    shape = jax.ShapeDtypeStruct((2 * shots + 1, depth + 2 * HALO, ROWS, width), bf16)
+    shape = jax.ShapeDtypeStruct((2 * shots + 1, depth + 2 * HALO, SENT, width), bf16)
     return pl.pallas_call(
         pack_rows_kernel, out_shape=(shape, shape), compiler_params=limit(10), name="pack_rows"
     )(residual, wavenumber, below, above)

time: 196 us -> 178 us (0.908)
  starting transfers between devices: 132 us -> 117 us
  waiting for transfers between devices: 10.7 us -> 6.63 us
    ppermute x4, starting transfers between devices: 109 us -> 94.1 us  [swap(): found.append(lax.ppermute(half, ('layer', 'row'), way))]
    ppermute x2, waiting for transfers between devices: 2.33 us -> 0.01 us  [planes_of(): lax.ppermute(first, 'layer', back)]
    unnamed x20 -> x22, local copies, waits for them, and re-layouts: 13.5 us -> 15.1 us
  transfers between devices with their start and end apart: 15 -> 15, of which waited for: 5 -> 3; matrix products, arithmetic and copies ran while one was open for 1% -> 1% of each run, Pallas kernels for 5% -> 6%
where the time goes in v9:
time: 178 us; the launch traced here: 177 us
  starting transfers between devices  117 us (66%)
  Pallas kernels  25.2 us (14%)
  local copies, waits for them, and re-layouts  15.1 us (8%)
  blocking collectives  10.7 us (6%)
  waiting for transfers between devices  6.63 us (4%)
  other arithmetic  2.28 us (1%)
    ppermute x4, starting transfers between devices, swap(): found.append(lax.ppermute(half, ('layer', 'row'), way))  94.1 us
    unnamed x22, local copies, waits for them, and re-layouts  15.1 us
    pallas_call x1, Pallas kernels, smooth(): pl.pallas_call(smooth_kernel, out_shape=jax.ShapeDtypeStruct(residual.sha...  12.1 us
    all_to_all x1, blocking collectives, gather(): lax.all_to_all(blocks, 'row', 0, 0, axis_index_groups=ends, tiled=True)  10.7 us
    ppermute x1, starting transfers between devices, both_ways(): lax.ppermute(high_block, axis, up)  6.39 us
    ppermute x4, waiting for transfers between devices, swap(): found.append(lax.ppermute(half, ('layer', 'row'), way))  5.32 us
    ppermute x2, starting transfers between devices, planes_of(): lax.ppermute(first, 'layer', back)  5.21 us
    pallas_call x3, Pallas kernels, solve_layer(): pl.pallas_call(functools.partial(layer_kernel, step), out_shape=(jax.Shap...  4.14 us
  transfers between devices with their start and end apart: 15, of which 3 were waited for; matrix products, arithmetic and copies ran while one was open for 1% of the time, Pallas kernels for 6%

profile of v9, /device:TPU:96, one launch (start us, length us, event | category | flops | bytes accessed | tf_op | source)
XLA Modules:
  0.0 177.3 jit_solution(18093234204528848848)
XLA Ops:
  0.0 1.6 copy-done
  1.6 1.0 copy-done.7
  3.5 1.9 %collective-permute-start.11 = (bf16[5,3,64,192]{3,2,1,0:T(8,128)(2,1)S(1)}, bf16[5,3,64,192]{3,2,1,0:T(8,128)(2,1)}, u32[]{:S(2)}, u32[]{:S(2)}) collective-permute-start(bf16[5,3,64,192]{3,2,1,0:T(8,128)(2,1)S(1)} %get-tuple-element.170), channel_id=1, source_target_pairs={{0,32},{64,96},{96,128},{128,160},{160,192},{192,224},{1,33},{65,9... | collective-permute-start | bytes 1105928 | tf_op jit(solution)/shard_map/ppermute | solution.py:500
  5.4 1.5 collective-permute-start.10
  6.9 1.6 copy-done.1
  8.9 3.6 %collective-permute-start.16 = (f32[4,192]{1,0:T(4,128)S(1)}, f32[4,192]{1,0:T(4,128)S(1)}, u32[]{:S(2)}, u32[]{:S(2)}) collective-permute-start(f32[4,192]{1,0:T(4,128)S(1)} %get-tuple-element.175), channel_id=1, source_target_pairs={{32,0},{64,32},{96,64},{128,96},{160,128},{192,160},{224,192},{33,... | collective-permute-start | bytes 9224 | tf_op jit(solution)/shard_map/ppermute | solution.py:442
  12.6 1.3 collective-permute-done.16.next_rhs
  13.8 2.8 %solve_first.1 = (f32[4,192]{1,0:T(4,128)S(1)}, bf16[16,4,192]{2,1,0:T(4,128)(2,1)S(1)}) custom-call(bf16[2,192,6144]{2,1,0:T(8,128)(2,1)} %bitcast.5, bf16[32,4,192]{2,1,0:T(4,128)(2,1)S(1)} %get-tuple-element.209.gathered, f32[4,192]{1,0:T(4,128)S(1)} %collective-permute-done.16.next_rhs), custom_call_target="tpu_custom_call" | custom-call | flops 9437184 | bytes 4718592 | tf_op jit(solution)/shard_map/solve_first/pallas_call | solution.py:156
  18.0 3.6 %collective-permute-start.13 = (bf16[5,3,64,192]{3,2,1,0:T(8,128)(2,1)}, bf16[5,3,64,192]{3,2,1,0:T(8,128)(2,1)}, u32[]{:S(2)}, u32[]{:S(2)}) collective-permute-start(bf16[5,3,64,192]{3,2,1,0:T(8,128)(2,1)} %get-tuple-element.171), channel_id=1, source_target_pairs={{32,0},{96,64},{128,96},{160,128},{192,160},{224,192},{33,1},{97,6... | collective-permute-start | bytes 1105928 | tf_op jit(solution)/shard_map/ppermute | solution.py:500
  21.7 2.2 %copy-done.3 = bf16[2,192,6144]{2,1,0:T(8,128)(2,1)} copy-done((bf16[2,192,6144]{2,1,0:T(8,128)(2,1)}, bf16[2,192,6144]{2,1,0:T(8,128)(2,1)S(1)}, u32[]{:S(2)}) %copy-start.3) | copy-done | bytes 4718616
  23.9 2.3 %copy-done.4 = bf16[2,192,6144]{2,1,0:T(8,128)(2,1)S(1)} copy-done((bf16[2,192,6144]{2,1,0:T(8,128)(2,1)S(1)}, bf16[2,192,6144]{2,1,0:T(8,128)(2,1)}, u32[]{:S(2)}) %copy-start.4) | copy-done | bytes 4718616
  26.2 1.4 solve_layer.10
  27.7 1.6 collective-permute-start.12
  30.6 1.1 broadcast_select_fusion.1.below.deep_low
  31.7 1.1 broadcast_select_fusion.above.deep_high
  34.4 6.4 %collective-permute-start.14 = (bf16[5,14,4,192]{3,2,1,0:T(4,128)(2,1)}, bf16[5,14,4,192]{3,2,1,0:T(4,128)(2,1)S(1)}, u32[]{:S(2)}, u32[]{:S(2)}) collective-permute-start(bf16[5,14,4,192]{3,2,1,0:T(4,128)(2,1)} %get-tuple-element.172), channel_id=1, source_target_pairs={{0,1},{1,2},{2,3},{3,4},{4,5},{5,6},{6,7},{7,8},{8,9},{9,10},{10,1... | collective-permute-start | bytes 322568 | tf_op jit(solution)/shard_map/ppermute | solution.py:433
  40.8 1.3 collective-permute-start.15
  42.2 2.2 %copy-done.5 = bf16[2,192,6144]{2,1,0:T(8,128)(2,1)} copy-done((bf16[2,192,6144]{2,1,0:T(8,128)(2,1)}, bf16[2,192,6144]{2,1,0:T(8,128)(2,1)S(1)}, u32[]{:S(2)}) %copy-start.5) | copy-done | bytes 4718616
  44.4 2.3 %copy-done.6 = bf16[2,192,6144]{2,1,0:T(8,128)(2,1)S(1)} copy-done((bf16[2,192,6144]{2,1,0:T(8,128)(2,1)S(1)}, bf16[2,192,6144]{2,1,0:T(8,128)(2,1)}, u32[]{:S(2)}) %copy-start.6) | copy-done | bytes 4718616
  46.8 1.4 solve_layer.11
  48.2 96.0 %conditional.23 = ((f32[4,192]{1,0:T(4,128)S(1)}, bf16[16,4,192]{2,1,0:T(4,128)(2,1)S(1)})) conditional(s32[]{:T(128)} %convert_element_type.42, (f32[4,192]{1,0:T(4,128)S(1)}, bf16[16,4,192]{2,1,0:T(4,128)(2,1)S(1)}) %tuple.105, (bf16[2,192,6144]{2,1,0:T(8,128)(2,1)}, bf16[16,4,192]{2,1,0:T(4,128)(2,1)S(1)}, f32[4,192]{1,0:T(4,128)S(1)}, ...), branch_computations={%region_20.0_spmd, %region_21.0_spmd} | conditional | flops 9437184 | bytes 4921432 | solution.py:490
  48.2 91.1 %collective-permute-start.7 = (bf16[16,4,192]{2,1,0:T(4,128)(2,1)S(1)}, bf16[16,4,192]{2,1,0:T(4,128)(2,1)S(1)}, u32[]{:S(2)}, u32[]{:S(2)}) collective-permute-start(bf16[16,4,192]{2,1,0:T(4,128)(2,1)S(1)} %get-tuple-element.141), channel_id=1, source_target_pairs={{0,97},{1,96},{2,99},{3,98},{4,101},{5,100},{6,103},{7,102},{8,105... | collective-permute-start | bytes 73736 | tf_op jit(solution)/shard_map/cond/branch_1_fun/ppermute | solution.py:470
  139.3 2.3 %hold.10.matrix = bf16[2,192,6144]{2,1,0:T(8,128)(2,1)S(1)} custom-call(bf16[2,192,6144]{2,1,0:T(8,128)(2,1)} %get-tuple-element.140.matrix), custom_call_target="tpu_custom_call" | custom-call | tf_op jit(solution)/shard_map/cond/branch_1_fun/hold/pallas_call | solution.py:93
  142.7 1.4 solve_layer.9
  144.2 10.8 %conditional.24 = (bf16[16,4,192]{2,1,0:T(4,128)(2,1)S(1)}) conditional(s32[]{:T(128)} %convert_element_type.52, bf16[16,4,192]{2,1,0:T(4,128)(2,1)S(1)} %get-tuple-element.189, bf16[16,4,192]{2,1,0:T(4,128)(2,1)S(1)} %get-tuple-element.189), branch_computations={%region_22.23_spmd, %region_23.24_spmd} | conditional | bytes 98312 | solution.py:455
  144.3 10.7 %all_to_all.39 = bf16[16,4,192]{2,1,0:T(4,128)(2,1)S(1)} all-to-all(bf16[16,4,192]{2,1,0:T(4,128)(2,1)S(1)} %copy.55), channel_id=1, replica_groups={{0,2,4,6,8,10,12,14,16,18,20,22,24,26,28,30},{1,3,5,7,9,11,13,15,17,19,..., dimensions={0} | all-to-all | bytes 49152 | tf_op jit(solution)/shard_map/cond/branch_1_fun/all_to_all | solution.py:457
  155.0 1.0 copy-done.10
  156.0 12.1 %smooth.1 = f32[2,2,8,64,192]{4,3,2,1,0:T(8,128)S(1)} custom-call(f32[4]{0:T(128)S(1)} %add_convert_fusion.inside, f32[2,2,8,64,192]{4,3,2,1,0:T(8,128)S(1)} %copy-done.2, f32[8,64,192]{2,1,0:T(8,128)S(1)} %copy-done.8, bf16[5,14,4,192]{3,2,1,0:T(4,128)(2,1)S(1)} %collective-permute-done.14.row_low, ...), custom_call_target="tpu_custom_call" | custom-call | flops 117964800 | bytes 4718592 | tf_op jit(solution)/shard_map/smooth/pallas_call | solution.py:321
  168.1 9.1 %conditional.25 = (f32[2,2,8,64,192]{4,3,2,1,0:T(8,128)}) conditional(s32[]{:T(128)} %convert_element_type.40, (f32[2,2,8,64,192]{4,3,2,1,0:T(8,128)S(1)}, f32[4,192]{1,0:T(4,128)S(1)}) %tuple.107, (bf16[2,192,6144]{2,1,0:T(8,128)(2,1)}, bf16[16,4,192]{2,1,0:T(4,128)(2,1)S(1)}, f32[2,2,8,64,192]{4,3,2,1,0:T(8,128)S(1)}, ...), branch_computations={%region_24.25_spmd, %region_25.26_spmd} | conditional | bytes 196696 | solution.py:520
  168.2 2.9 %collective-permute-start.8 = (bf16[16,4,192]{2,1,0:T(4,128)(2,1)S(1)}, bf16[16,4,192]{2,1,0:T(4,128)(2,1)S(1)}, u32[]{:S(2)}, u32[]{:S(2)}) collective-permute-start(bf16[16,4,192]{2,1,0:T(4,128)(2,1)S(1)} %get-tuple-element.149), channel_id=1, source_target_pairs={{0,32},{1,33},{2,34},{3,35},{4,36},{5,37},{6,38},{7,39},{8,40},{9,... | collective-permute-start | bytes 73736 | tf_op jit(solution)/shard_map/cond/branch_1_fun/ppermute | solution.py:470
  171.1 4.3 %collective-permute-done.9.other = bf16[16,4,192]{2,1,0:T(4,128)(2,1)S(1)} collective-permute-done((bf16[16,4,192]{2,1,0:T(4,128)(2,1)S(1)}, bf16[16,4,192]{2,1,0:T(4,128)(2,1)S(1)}, u32[]{:S(2)}, u32[]{:S(2)}) %collective-permute-start.9) | collective-permute-done | bytes 24608 | tf_op jit(solution)/shard_map/cond/branch_1_fun/ppermute | solution.py:470
  175.5 1.7 lift.3
  (52 shorter events, 6.8 us)
Async XLA Ops:
  0.0 1.6 copy-start
  1.6 1.0 copy-start.7
  3.5 26.4 %collective-permute-start.11 = (bf16[5,3,64,192]{3,2,1,0:T(8,128)(2,1)S(1)}, bf16[5,3,64,192]{3,2,1,0:T(8,128)(2,1)}, u32[]{:S(2)}, u32[]{:S(2)}) collective-permute-start(bf16[5,3,64,192]{3,2,1,0:T(8,128)(2,1)S(1)} %get-tuple-element.170), channel_id=1, source_target_pairs={{0,32},{64,96},{96,128},{128,160},{160,192},{192,224},{1,33},{65,9... | collective-permute-start | bytes 1105928 | tf_op jit(solution)/shard_map/ppermute | solution.py:500
  5.4 25.2 %collective-permute-start.10 = (bf16[5,3,64,192]{3,2,1,0:T(8,128)(2,1)S(1)}, bf16[5,3,64,192]{3,2,1,0:T(8,128)(2,1)}, u32[]{:S(2)}, u32[]{:S(2)}) collective-permute-start(bf16[5,3,64,192]{3,2,1,0:T(8,128)(2,1)S(1)} %get-tuple-element.170), channel_id=1, source_target_pairs={{32,64},{33,65},{34,66},{35,67},{36,68},{37,69},{38,70},{39,71},{4... | collective-permute-start | bytes 1105928 | tf_op jit(solution)/shard_map/ppermute | solution.py:500
  6.9 1.6 copy-start.1
  8.9 5.0 %collective-permute-start.16 = (f32[4,192]{1,0:T(4,128)S(1)}, f32[4,192]{1,0:T(4,128)S(1)}, u32[]{:S(2)}, u32[]{:S(2)}) collective-permute-start(f32[4,192]{1,0:T(4,128)S(1)} %get-tuple-element.175), channel_id=1, source_target_pairs={{32,0},{64,32},{96,64},{128,96},{160,128},{192,160},{224,192},{33,... | collective-permute-start | bytes 9224 | tf_op jit(solution)/shard_map/ppermute | solution.py:442
  16.7 7.2 %collective-permute-start.18 = (bf16[16,4,192]{2,1,0:T(4,128)(2,1)S(1)}, bf16[16,4,192]{2,1,0:T(4,128)(2,1)S(1)}, u32[]{:S(2)}, u32[]{:S(2)}) collective-permute-start(bf16[16,4,192]{2,1,0:T(4,128)(2,1)S(1)} %get-tuple-element.212), channel_id=1, source_target_pairs={{32,65},{33,64},{34,67},{35,66},{36,69},{37,68},{38,71},{39,70},{4... | collective-permute-start | bytes 73736 | tf_op jit(solution)/shard_map/ppermute | solution.py:477
  17.4 6.5 %collective-permute-start.17 = (bf16[16,4,192]{2,1,0:T(4,128)(2,1)S(1)}, bf16[16,4,192]{2,1,0:T(4,128)(2,1)S(1)}, u32[]{:S(2)}, u32[]{:S(2)}) collective-permute-start(bf16[16,4,192]{2,1,0:T(4,128)(2,1)S(1)} %get-tuple-element.212), channel_id=1, source_target_pairs={{32,64},{33,65},{34,66},{35,67},{36,68},{37,69},{38,70},{39,71},{4... | collective-permute-start | bytes 73736 | tf_op jit(solution)/shard_map/ppermute | solution.py:477
  18.0 13.7 %collective-permute-start.13 = (bf16[5,3,64,192]{3,2,1,0:T(8,128)(2,1)}, bf16[5,3,64,192]{3,2,1,0:T(8,128)(2,1)}, u32[]{:S(2)}, u32[]{:S(2)}) collective-permute-start(bf16[5,3,64,192]{3,2,1,0:T(8,128)(2,1)} %get-tuple-element.171), channel_id=1, source_target_pairs={{32,0},{96,64},{128,96},{160,128},{192,160},{224,192},{33,1},{97,6... | collective-permute-start | bytes 1105928 | tf_op jit(solution)/shard_map/ppermute | solution.py:500
  21.7 2.2 %copy-start.3 = (bf16[2,192,6144]{2,1,0:T(8,128)(2,1)}, bf16[2,192,6144]{2,1,0:T(8,128)(2,1)S(1)}, u32[]{:S(2)}) copy-start(bf16[2,192,6144]{2,1,0:T(8,128)(2,1)S(1)} %hold.13.matrix) | copy-start | bytes 14155780
  23.9 2.3 %copy-start.4 = (bf16[2,192,6144]{2,1,0:T(8,128)(2,1)S(1)}, bf16[2,192,6144]{2,1,0:T(8,128)(2,1)}, u32[]{:S(2)}) copy-start(bf16[2,192,6144]{2,1,0:T(8,128)(2,1)} %copy-done.3) | copy-start | bytes 14155780
  27.6 5.2 %copy-start.2 = (f32[2,2,8,64,192]{4,3,2,1,0:T(8,128)S(1)}, f32[2,2,8,64,192]{4,3,2,1,0:T(8,128)}, u32[]{:S(2)}) copy-start(f32[2,2,8,64,192]{4,3,2,1,0:T(8,128)} %residual.7) | copy-start | bytes 4718596
  27.6 5.2 %copy-start.8 = (f32[8,64,192]{2,1,0:T(8,128)S(1)}, f32[8,64,192]{2,1,0:T(8,128)}, u32[]{:S(2)}) copy-start(f32[8,64,192]{2,1,0:T(8,128)} %wavenumber.5) | copy-start | bytes 1179652
  27.7 4.1 %collective-permute-start.12 = (bf16[5,3,64,192]{3,2,1,0:T(8,128)(2,1)}, bf16[5,3,64,192]{3,2,1,0:T(8,128)(2,1)}, u32[]{:S(2)}, u32[]{:S(2)}) collective-permute-start(bf16[5,3,64,192]{3,2,1,0:T(8,128)(2,1)} %get-tuple-element.171), channel_id=1, source_target_pairs={{64,32},{65,33},{66,34},{67,35},{68,36},{69,37},{70,38},{71,39},{7... | collective-permute-start | bytes 1105928 | tf_op jit(solution)/shard_map/ppermute | solution.py:500
  29.3 15.2 %collective-permute-start.20 = (bf16[16,4,192]{2,1,0:T(4,128)(2,1)S(1)}, bf16[16,4,192]{2,1,0:T(4,128)(2,1)S(1)}, u32[]{:S(2)}, u32[]{:S(2)}) collective-permute-start(bf16[16,4,192]{2,1,0:T(4,128)(2,1)S(1)} %get-tuple-element.215), channel_id=1, source_target_pairs={{96,129},{97,128},{98,131},{99,130},{100,133},{101,132},{102,135},... | collective-permute-start | bytes 73736 | tf_op jit(solution)/shard_map/ppermute | solution.py:477
  29.9 14.5 %collective-permute-start.19 = (bf16[16,4,192]{2,1,0:T(4,128)(2,1)S(1)}, bf16[16,4,192]{2,1,0:T(4,128)(2,1)S(1)}, u32[]{:S(2)}, u32[]{:S(2)}) collective-permute-start(bf16[16,4,192]{2,1,0:T(4,128)(2,1)S(1)} %get-tuple-element.215), channel_id=1, source_target_pairs={{96,128},{97,129},{98,130},{99,131},{100,132},{101,133},{102,134},... | collective-permute-start | bytes 73736 | tf_op jit(solution)/shard_map/ppermute | solution.py:477
  33.7 0.8 copy-start.9
  34.4 120.6 %collective-permute-start.14 = (bf16[5,14,4,192]{3,2,1,0:T(4,128)(2,1)}, bf16[5,14,4,192]{3,2,1,0:T(4,128)(2,1)S(1)}, u32[]{:S(2)}, u32[]{:S(2)}) collective-permute-start(bf16[5,14,4,192]{3,2,1,0:T(4,128)(2,1)} %get-tuple-element.172), channel_id=1, source_target_pairs={{0,1},{1,2},{2,3},{3,4},{4,5},{5,6},{6,7},{7,8},{8,9},{9,10},{10,1... | collective-permute-start | bytes 322568 | tf_op jit(solution)/shard_map/ppermute | solution.py:433
  40.8 114.2 %collective-permute-start.15 = (bf16[5,14,4,192]{3,2,1,0:T(4,128)(2,1)}, bf16[5,14,4,192]{3,2,1,0:T(4,128)(2,1)S(1)}, u32[]{:S(2)}, u32[]{:S(2)}) collective-permute-start(bf16[5,14,4,192]{3,2,1,0:T(4,128)(2,1)} %get-tuple-element.173), channel_id=1, source_target_pairs={{1,0},{2,1},{3,2},{4,3},{5,4},{6,5},{7,6},{8,7},{9,8},{10,9},{11,1... | collective-permute-start | bytes 322568 | tf_op jit(solution)/shard_map/ppermute | solution.py:433
  42.2 2.2 %copy-start.5 = (bf16[2,192,6144]{2,1,0:T(8,128)(2,1)}, bf16[2,192,6144]{2,1,0:T(8,128)(2,1)S(1)}, u32[]{:S(2)}) copy-start(bf16[2,192,6144]{2,1,0:T(8,128)(2,1)S(1)} %hold.12.matrix) | copy-start | bytes 14155780
  44.4 2.3 %copy-start.6 = (bf16[2,192,6144]{2,1,0:T(8,128)(2,1)S(1)}, bf16[2,192,6144]{2,1,0:T(8,128)(2,1)}, u32[]{:S(2)}) copy-start(bf16[2,192,6144]{2,1,0:T(8,128)(2,1)} %copy-done.5) | copy-start | bytes 14155780
  48.2 93.5 %collective-permute-start.7 = (bf16[16,4,192]{2,1,0:T(4,128)(2,1)S(1)}, bf16[16,4,192]{2,1,0:T(4,128)(2,1)S(1)}, u32[]{:S(2)}, u32[]{:S(2)}) collective-permute-start(bf16[16,4,192]{2,1,0:T(4,128)(2,1)S(1)} %get-tuple-element.141), channel_id=1, source_target_pairs={{0,97},{1,96},{2,99},{3,98},{4,101},{5,100},{6,103},{7,102},{8,105... | collective-permute-start | bytes 73736 | tf_op jit(solution)/shard_map/cond/branch_1_fun/ppermute | solution.py:470
  139.3 3.3 %collective-permute-start.6 = (bf16[16,4,192]{2,1,0:T(4,128)(2,1)S(1)}, bf16[16,4,192]{2,1,0:T(4,128)(2,1)S(1)}, u32[]{:S(2)}, u32[]{:S(2)}) collective-permute-start(bf16[16,4,192]{2,1,0:T(4,128)(2,1)S(1)} %get-tuple-element.141), channel_id=1, source_target_pairs={{0,96},{1,97},{2,98},{3,99},{4,100},{5,101},{6,102},{7,103},{8,104... | collective-permute-start | bytes 73736 | tf_op jit(solution)/shard_map/cond/branch_1_fun/ppermute | solution.py:470
  155.0 1.0 copy-start.10
  168.1 7.3 %collective-permute-start.9 = (bf16[16,4,192]{2,1,0:T(4,128)(2,1)S(1)}, bf16[16,4,192]{2,1,0:T(4,128)(2,1)S(1)}, u32[]{:S(2)}, u32[]{:S(2)}) collective-permute-start(bf16[16,4,192]{2,1,0:T(4,128)(2,1)S(1)} %get-tuple-element.149), channel_id=1, source_target_pairs={{0,33},{1,32},{2,35},{3,34},{4,37},{5,36},{6,39},{7,38},{8,41},{9,... | collective-permute-start | bytes 73736 | tf_op jit(solution)/shard_map/cond/branch_1_fun/ppermute | solution.py:470
  168.2 7.2 %collective-permute-start.8 = (bf16[16,4,192]{2,1,0:T(4,128)(2,1)S(1)}, bf16[16,4,192]{2,1,0:T(4,128)(2,1)S(1)}, u32[]{:S(2)}, u32[]{:S(2)}) collective-permute-start(bf16[16,4,192]{2,1,0:T(4,128)(2,1)S(1)} %get-tuple-element.149), channel_id=1, source_target_pairs={{0,32},{1,33},{2,34},{3,35},{4,36},{5,37},{6,38},{7,39},{8,40},{9,... | collective-permute-start | bytes 73736 | tf_op jit(solution)/shard_map/cond/branch_1_fun/ppermute | solution.py:470

commit v10 on v9

--- a/solution.py
+++ b/solution.py
@@ -101,53 +101,59 @@
     )(matrix)
 
 
-def ordered(vector, same, other, first_end):
-    columns, _, cells = same.shape
-    for column in range(columns):
-        own, far = same[column], other[column]
+def ordered(vector, pairs):
+    first_end = lax.axis_index("row") % 2 == 0
+    for column, (own, far) in enumerate(pairs):
+        cells = own.shape[-1]
         at = 2 * column * cells
         vector[:, at : at + cells] = jnp.where(first_end, own, far)
         vector[:, at + cells : at + 2 * cells] = jnp.where(first_end, far, own)
 
 
+def halves(both):
+    lines = both.shape[1] // 2
+    return [(both[column, :lines], both[column, lines:]) for column in range(both.shape[0])]
+
+
 def combined(by_re, by_im):
     shots = by_re.shape[0] // 2
     return jnp.concatenate([by_re[:shots] - by_im[shots:], by_re[shots:] + by_im[:shots]], axis=0)
 
 
-def hand_on(solved, next_rhs, spread):
-    out = (next_rhs[...] + coupling * solved).astype(bf16)
-    for column in range(spread.shape[0]):
-        spread[column] = out
+def handed_on(solved, next_rhs):
+    return (next_rhs[...] + coupling * solved).astype(bf16)
 
 
 def times(part, rows):
     return lax.dot_general(part, rows, (((1,), (1,)), ((), ())), preferred_element_type=f32)
 
 
-def first_kernel(matrix, gathered, next_rhs, kept, spread, held, vector, arrived):
+def first_kernel(matrix, gathered, next_rhs, kept, block, held, vector, arrived):
     devices, _, cells = gathered.shape
     pieces = arrived.shape[0]
     across = matrix.shape[2] // pieces
     columns = [slice(piece * across, (piece + 1) * across) for piece in range(pieces)]
-    copies = [
-        pltpu.make_async_copy(matrix.at[:, :, columns[piece]], held.at[:, :, columns[piece]], arrived.at[piece])
-        for piece in range(pieces)
-    ]
-    for copy in copies:
-        copy.start()
-    for device in range(devices):
-        vector[:, device * cells : (device + 1) * cells] = gathered[device]
-    by = [None, None]
-    for piece in range(pieces):
-        part = vector[:, columns[piece]]
-        copies[piece].wait()
-        for side in range(2):
-            product = times(part, held[side, :, columns[piece]])
-            by[side] = product if by[side] is None else by[side] + product
-    solved = combined(by[0], by[1])
-    kept[...] = solved
-    hand_on(solved, next_rhs, spread)
+
+    @pl.when(lax.axis_index("layer") == 0)
+    def _():
+        copies = [
+            pltpu.make_async_copy(matrix.at[:, :, columns[piece]], held.at[:, :, columns[piece]], arrived.at[piece])
+            for piece in range(pieces)
+        ]
+        for copy in copies:
+            copy.start()
+        for device in range(devices):
+            vector[:, device * cells : (device + 1) * cells] = gathered[device]
+        by = [None, None]
+        for piece in range(pieces):
+            part = vector[:, columns[piece]]
+            copies[piece].wait()
+            for side in range(2):
+                product = times(part, held[side, :, columns[piece]])
+                by[side] = product if by[side] is None else by[side] + product
+        solved = combined(by[0], by[1])
+        kept[...] = solved
+        block[...] = handed_on(solved, next_rhs)
 
 
 def solve_first(matrix, gathered, next_rhs):
@@ -157,7 +163,7 @@
         first_kernel,
         out_shape=(
             jax.ShapeDtypeStruct((lines, cells), f32),
-            jax.ShapeDtypeStruct((devices // 2, lines, cells), bf16),
+            jax.ShapeDtypeStruct((lines, cells), bf16),
         ),
         in_specs=[pl.BlockSpec(memory_space=pltpu.HBM)] + [pl.BlockSpec(memory_space=VMEM)] * 2,
         scratch_shapes=[
@@ -171,28 +177,54 @@
     )(matrix, gathered, next_rhs)
 
 
-def layer_kernel(step, matrix, same, other, next_rhs, kept_before, kept, spread, vector):
-    ordered(vector, same, other, lax.axis_index("row") % 2 == 0)
+def pair_up_kernel(near, far, spread):
+    lines = near.shape[0]
+    for column in range(spread.shape[0]):
+        spread[column, :lines] = near[...]
+        spread[column, lines:] = far[...]
+
+
+def pair_up(near, far, columns):
+    lines, cells = near.shape
+    return pl.pallas_call(
+        pair_up_kernel,
+        out_shape=jax.ShapeDtypeStruct((columns, 2 * lines, cells), bf16),
+        compiler_params=limit(2),
+        name="pair_up",
+    )(near, far)
+
+
+def odd_kernel(matrix, both, next_rhs, product, spread, vector):
+    ordered(vector, halves(both))
     full = vector[...]
     solved = combined(times(full, matrix[0]), times(full, matrix[1]))
-    kept[...] = jnp.where(lax.axis_index("layer") == step, solved, kept_before[...])
-    hand_on(solved, next_rhs, spread)
-
-
-def solve_layer(step, matrix, same, other, next_rhs, kept):
-    columns, lines, cells = same.shape
-    return pl.pallas_call(
-        functools.partial(layer_kernel, step),
-        out_shape=(
-            jax.ShapeDtypeStruct((lines, cells), f32),
-            jax.ShapeDtypeStruct((columns, lines, cells), bf16),
-        ),
-        in_specs=[pl.BlockSpec(memory_space=VMEM)] * 5,
+    product[...] = solved
+    block = handed_on(solved, next_rhs)
+    for column in range(spread.shape[0]):
+        spread[column] = block
+
+
+def even_kernel(matrix, same, other, next_rhs, product, block, vector):
+    ordered(vector, [(same[column], other[column]) for column in range(same.shape[0])])
+    full = vector[...]
+    solved = combined(times(full, matrix[0]), times(full, matrix[1]))
+    product[...] = solved
+    block[...] = handed_on(solved, next_rhs)
+
+
+def solve_layer(step, matrix, blocks, next_rhs):
+    lines, cells = next_rhs.shape
+    columns = blocks[0].shape[0]
+    out = (columns, lines, cells) if step % 2 else (lines, cells)
+    return pl.pallas_call(
+        odd_kernel if step % 2 else even_kernel,
+        out_shape=(jax.ShapeDtypeStruct((lines, cells), f32), jax.ShapeDtypeStruct(out, bf16)),
+        in_specs=[pl.BlockSpec(memory_space=VMEM)] * (2 + len(blocks)),
         scratch_shapes=[pltpu.VMEM((lines, 2 * columns * cells), bf16)],
         compiler_params=limit(3),
         cost_estimate=pl.CostEstimate(flops=4 * matrix.size, bytes_accessed=2 * matrix.size, transcendentals=0),
         name="solve_layer",
-    )(matrix, same, other, next_rhs, kept)
+    )(matrix, *blocks, next_rhs)
 
 
 def smooth_kernel(inside, residual, wavenumber, row_low, row_high, deep_low, deep_high, smoothed, gain, source, first, second):
@@ -352,12 +384,12 @@
     lifted(smoothed, coarse[...], out, fine, wide, left)
 
 
-def last_kernel(step, smoothed, kept_before, matrix, same, other, out, fine, wide, left, vector, coarse):
+def last_kernel(step, smoothed, kept_before, matrix, both, out, fine, wide, left, vector, coarse):
     coarse[...] = kept_before[...]
 
     @pl.when(lax.axis_index("layer") == step)
     def _():
-        ordered(vector, same, other, lax.axis_index("row") % 2 == 0)
+        ordered(vector, halves(both))
         full = vector[...]
         coarse[...] = combined(times(full, matrix[0]), times(full, matrix[1]))
 
@@ -447,53 +479,73 @@
         lambda blocks: blocks,
         spread,
     )
-    kept, spread = solve_first(matrix, gathered, next_rhs)
-
-    ends = [[2 * column + end for column in range(devices // 2)] for end in range(2)]
-
-    def gather(step, spread):
-        return lax.cond(
-            layer == step,
-            lambda blocks: lax.all_to_all(blocks, "row", 0, 0, axis_index_groups=ends, tiled=True),
-            lambda blocks: blocks,
-            spread,
-        )
-
-    def swap(step, half):
+    kept, block = solve_first(matrix, gathered, next_rhs)
+
+    columns = devices // 2
+    ends = [[2 * column + end for column in range(columns)] for end in range(2)]
+
+    def gather(blocks):
+        return lax.all_to_all(blocks, "row", 0, 0, axis_index_groups=ends, tiled=True)
+
+    def hop(step, sent, way):
         found = []
         for flip in (1, 0):
-            way = [
-                (i * devices + j, (i ^ (step - 1) ^ step) * devices + (j ^ flip))
-                for i in range(layers)
-                for j in range(devices)
-            ]
-            found.append(lax.ppermute(half, ("layer", "row"), way))
-        return found
-
-    def send(step, half):
-        found = []
-        for flip in (1, 0):
-            way = [((step - 1) * devices + j, step * devices + (j ^ flip)) for j in range(devices)]
-            found.append(lax.ppermute(half, ("layer", "row"), way))
-        return found
-
-    def solve(step, other, same, kept):
-        held = hold(step, matrix)
-        return solve_layer(step, held, same, other, next_rhs, kept)
+            found.append(lax.ppermute(sent, ("layer", "row"), way(step, flip)))
+        return found[1], found[0]
+
+    def swapped(step, flip):
+        return [
+            (i * devices + j, (i ^ (step - 1) ^ step) * devices + (j ^ flip))
+            for i in range(layers)
+            for j in range(devices)
+        ]
+
+    def straight(step, flip):
+        return [((step - 1) * devices + j, step * devices + (j ^ flip)) for j in range(devices)]
+
+    def held(step):
+        return hold(step, matrix)
+
+    def solve(step, own, blocks):
+        return tuple(solve_layer(step, own, blocks, next_rhs))
+
+    def to_odd(step, block):
+        near, far = hop(step, block, swapped)
+        return gather(pair_up(near, far, columns))
+
+    def odd_step(step, kept, block):
+        own = held(step)
+        return solve(step, own, [to_odd(step, block)])
+
+    def even_step(step, kept, half, block):
+        own = held(step)
+        return solve(step, own, hop(step, half, swapped))
 
     open_hops = (2, layers // 2)
     for step in range(1, layers - 1):
-        half = gather(step - 1, spread)
-        if step in open_hops:
-            kept, spread = solve(step, *send(step, half), kept)
-            continue
-        kept, spread = lax.cond(
-            (layer == step - 1) | (layer == step),
-            lambda half, kept, step=step: tuple(solve(step, *swap(step, half), kept)),
-            lambda half, kept: (kept, half),
-            half,
-            kept,
-        )
+        takes_part = (layer == step - 1) | (layer == step)
+        if step % 2:
+            product, spread = lax.cond(
+                takes_part,
+                functools.partial(odd_step, step),
+                lambda kept, block: (kept, jnp.broadcast_to(block[None], (columns, *block.shape))),
+                kept,
+                block,
+            )
+        else:
+            half = lax.cond(layer == step - 1, gather, lambda blocks: blocks, spread)
+            if step in open_hops:
+                product, block = solve(step, held(step), hop(step, half, straight))
+            else:
+                product, block = lax.cond(
+                    takes_part,
+                    functools.partial(even_step, step),
+                    lambda kept, half, block: (kept, block),
+                    kept,
+                    half,
+                    block,
+                )
+        kept = jnp.where(layer == step, product, kept)
 
     def planes_of(first, last, pairs):
         back = [(high, low) for low, high in pairs]
@@ -510,15 +562,14 @@
     smoothed = smooth(inside, residual, wavenumber, row_low, row_high, below, above)
 
     step = layers - 1
-    half = gather(step - 1, spread)
-
-    def finish(half, smoothed, kept):
-        other, same = swap(step, half)
-        held = hold(step, matrix)
-        return lift(smoothed, kept, step, held, same, other)
+
+    def finish(block, smoothed, kept):
+        own = held(step)
+        both = to_odd(step, block)
+        return lift(smoothed, kept, step, own, both)
 
     return lax.cond(
-        layer >= step - 1, finish, lambda half, smoothed, kept: lift(smoothed, kept), half, smoothed, kept
+        layer >= step - 1, finish, lambda block, smoothed, kept: lift(smoothed, kept), block, smoothed, kept
     )
 
 

time: 178 us -> 211 us (1.19)
  the two profiles are of different devices: /device:TPU:96 before, /device:TPU:224 now
where the time goes in v10:
time: 211 us
  starting transfers between devices  151 us (72%)
  Pallas kernels  22.3 us (11%)
  waiting for transfers between devices  19.2 us (9%)
  local copies, waits for them, and re-layouts  15.4 us (7%)
  other arithmetic  2.32 us (1%)
    ppermute x8, starting transfers between devices, hop(): found.append(lax.ppermute(sent, ('layer', 'row'), way(step, flip)))  122 us
    pallas_call x1, Pallas kernels, smooth(): pl.pallas_call(smooth_kernel, out_shape=jax.ShapeDtypeStruct(residual.sha...  12.1 us
    unnamed x14, local copies, waits for them, and re-layouts  10.7 us
    all_to_all x1, starting transfers between devices, gather(): lax.all_to_all(blocks, 'row', 0, 0, axis_index_groups=ends, tiled=True)  7.64 us
    ppermute x8, waiting for transfers between devices, hop(): found.append(lax.ppermute(sent, ('layer', 'row'), way(step, flip)))  5.87 us
    ppermute x1, waiting for transfers between devices, both_ways(): lax.ppermute(low_block, axis, [(b, a) for a, b in up])  5.57 us
    all_to_all x1, waiting for transfers between devices, gather(): lax.all_to_all(blocks, 'row', 0, 0, axis_index_groups=ends, tiled=True)  5.35 us
    ppermute x2, starting transfers between devices, planes_of(): lax.ppermute(first, 'layer', back)  5.1 us
  transfers between devices with their start and end apart: 16, of which 7 were waited for; matrix products, arithmetic and copies ran while one was open for 1% of the time, Pallas kernels for 3%

profile of v10, /device:TPU:224, one launch (start us, length us, event | category | flops | bytes accessed | tf_op | source)
XLA Modules:
  0.0 210.6 jit_solution(10766535098460875624)
XLA Ops:
  0.0 1.6 copy-done
  2.0 2.4 %collective-permute-start.16 = (f32[4,192]{1,0:T(4,128)S(1)}, f32[4,192]{1,0:T(4,128)S(1)}, u32[]{:S(2)}, u32[]{:S(2)}) collective-permute-start(f32[4,192]{1,0:T(4,128)S(1)} %get-tuple-element.138), channel_id=1, source_target_pairs={{32,0},{64,32},{96,64},{128,96},{160,128},{192,160},{224,192},{33,... | collective-permute-start | bytes 9224 | tf_op jit(solution)/shard_map/ppermute | solution.py:474
  4.4 1.3 collective-permute-done.16.next_rhs
  7.2 2.2 %copy-done.4 = bf16[2,192,6144]{2,1,0:T(8,128)(2,1)} copy-done((bf16[2,192,6144]{2,1,0:T(8,128)(2,1)}, bf16[2,192,6144]{2,1,0:T(8,128)(2,1)S(1)}, u32[]{:S(2)}) %copy-start.4) | copy-done | bytes 4718616
  9.3 2.3 %copy-done.5 = bf16[2,192,6144]{2,1,0:T(8,128)(2,1)S(1)} copy-done((bf16[2,192,6144]{2,1,0:T(8,128)(2,1)S(1)}, bf16[2,192,6144]{2,1,0:T(8,128)(2,1)}, u32[]{:S(2)}) %copy-start.5) | copy-done | bytes 4718616
  11.7 1.4 solve_layer.10
  15.6 1.9 collective-permute-start.11
  17.5 1.4 collective-permute-start.10
  19.0 3.6 %collective-permute-start.13 = (bf16[5,3,64,192]{3,2,1,0:T(8,128)(2,1)S(1)}, bf16[5,3,64,192]{3,2,1,0:T(8,128)(2,1)}, u32[]{:S(2)}, u32[]{:S(2)}) collective-permute-start(bf16[5,3,64,192]{3,2,1,0:T(8,128)(2,1)S(1)} %get-tuple-element.134), channel_id=1, source_target_pairs={{32,0},{96,64},{128,96},{160,128},{192,160},{224,192},{33,1},{97,6... | collective-permute-start | bytes 1105928 | tf_op jit(solution)/shard_map/ppermute | solution.py:552
  22.6 2.2 %copy-done.2 = bf16[2,192,6144]{2,1,0:T(8,128)(2,1)} copy-done((bf16[2,192,6144]{2,1,0:T(8,128)(2,1)}, bf16[2,192,6144]{2,1,0:T(8,128)(2,1)S(1)}, u32[]{:S(2)}) %copy-start.2) | copy-done | bytes 4718616
  24.8 2.3 %copy-done.3 = bf16[2,192,6144]{2,1,0:T(8,128)(2,1)S(1)} copy-done((bf16[2,192,6144]{2,1,0:T(8,128)(2,1)S(1)}, bf16[2,192,6144]{2,1,0:T(8,128)(2,1)}, u32[]{:S(2)}) %copy-start.3) | copy-done | bytes 4718616
  27.2 1.4 solve_layer.11
  28.6 122.4 %conditional.16 = ((f32[4,192]{1,0:T(4,128)S(1)}, bf16[4,192]{1,0:T(4,128)(2,1)S(1)})) conditional(s32[]{:T(128)} %convert_element_type.32, (f32[4,192]{1,0:T(4,128)S(1)}, bf16[4,192]{1,0:T(4,128)(2,1)S(1)}) %tuple.80, (bf16[2,192,6144]{2,1,0:T(8,128)(2,1)}, bf16[16,4,192]{2,1,0:T(4,128)(2,1)S(1)}, f32[4,192]{1,0:T(4,128)S(1)}) %tuple.115), branch_computations={%region_14.15_spmd, %region_15.16_spmd} | conditional | flops 9437184 | bytes 4915288 | solution.py:540
  28.6 117.2 %collective-permute-start.7 = (bf16[16,4,192]{2,1,0:T(4,128)(2,1)S(1)}, bf16[16,4,192]{2,1,0:T(4,128)(2,1)S(1)}, u32[]{:S(2)}, u32[]{:S(2)}) collective-permute-start(bf16[16,4,192]{2,1,0:T(4,128)(2,1)S(1)} %get-tuple-element.105), channel_id=1, source_target_pairs={{0,97},{1,96},{2,99},{3,98},{4,101},{5,100},{6,103},{7,102},{8,105... | collective-permute-start | bytes 73736 | tf_op jit(solution)/shard_map/cond/branch_1_fun/ppermute | solution.py:493
  145.8 2.3 %hold.10.matrix = bf16[2,192,6144]{2,1,0:T(8,128)(2,1)S(1)} custom-call(bf16[2,192,6144]{2,1,0:T(8,128)(2,1)} %get-tuple-element.104.matrix), custom_call_target="tpu_custom_call" | custom-call | tf_op jit(solution)/shard_map/cond/branch_1_fun/hold/pallas_call | solution.py:93
  148.4 1.2 collective-permute-done.6.same
  149.5 1.4 solve_layer.9
  151.0 1.5 collective-permute-start.12
  152.5 1.1 broadcast_select_fusion.1.below.deep_low
  154.9 4.7 %collective-permute-start.14 = (bf16[5,14,4,192]{3,2,1,0:T(4,128)(2,1)S(1)}, bf16[5,14,4,192]{3,2,1,0:T(4,128)(2,1)S(1)}, u32[]{:S(2)}, u32[]{:S(2)}) collective-permute-start(bf16[5,14,4,192]{3,2,1,0:T(4,128)(2,1)S(1)} %get-tuple-element.135), channel_id=1, source_target_pairs={{0,1},{1,2},{2,3},{3,4},{4,5},{5,6},{6,7},{7,8},{8,9},{9,10},{10,1... | collective-permute-start | bytes 322568 | tf_op jit(solution)/shard_map/ppermute | solution.py:465
  159.5 5.1 %collective-permute-start.15 = (bf16[5,14,4,192]{3,2,1,0:T(4,128)(2,1)S(1)}, bf16[5,14,4,192]{3,2,1,0:T(4,128)(2,1)S(1)}, u32[]{:S(2)}, u32[]{:S(2)}) collective-permute-start(bf16[5,14,4,192]{3,2,1,0:T(4,128)(2,1)S(1)} %get-tuple-element.136), channel_id=1, source_target_pairs={{1,0},{2,1},{3,2},{4,3},{5,4},{6,5},{7,6},{8,7},{9,8},{10,9},{11,1... | collective-permute-start | bytes 322568 | tf_op jit(solution)/shard_map/ppermute | solution.py:465
  164.6 1.1 collective-permute-done.14.row_low
  165.8 5.6 %collective-permute-done.15.row_high = bf16[5,14,4,192]{3,2,1,0:T(4,128)(2,1)S(1)} collective-permute-done((bf16[5,14,4,192]{3,2,1,0:T(4,128)(2,1)S(1)}, bf16[5,14,4,192]{3,2,1,0:T(4,128)(2,1)S(1)}, u32[]{:S(2)}, u32[]{:S(2)}) %collective-permute-start.15) | collective-permute-done | bytes 107552 | tf_op jit(solution)/shard_map/ppermute | solution.py:465
  171.3 12.1 %smooth.1 = f32[2,2,8,64,192]{4,3,2,1,0:T(8,128)S(1)} custom-call(f32[4]{0:T(128)S(1)} %add_convert_fusion.inside, f32[2,2,8,64,192]{4,3,2,1,0:T(8,128)S(1)} %copy-done.1, f32[8,64,192]{2,1,0:T(8,128)S(1)} %copy-done.14, bf16[5,14,4,192]{3,2,1,0:T(4,128)(2,1)S(1)} %collective-permute-done.14.row_low, ...), custom_call_target="tpu_custom_call" | custom-call | flops 117964800 | bytes 4718592 | tf_op jit(solution)/shard_map/smooth/pallas_call | solution.py:353
  183.4 27.0 %conditional.17 = (f32[2,2,8,64,192]{4,3,2,1,0:T(8,128)}) conditional(s32[]{:T(128)} %convert_element_type.30, (f32[2,2,8,64,192]{4,3,2,1,0:T(8,128)S(1)}, f32[4,192]{1,0:T(4,128)S(1)}) %tuple.82, (bf16[2,192,6144]{2,1,0:T(8,128)(2,1)}, bf16[4,192]{1,0:T(4,128)(2,1)S(1)}, f32[2,2,8,64,192]{4,3,2,1,0:T(8,128)S(1)}, f32[4,192]{1,0:T(4,128)S(1)}) %tuple.116), branch_computations={%region_16.17_spmd, %region_17.18_spmd} | conditional | bytes 50524392 | solution.py:571
  183.6 2.4 %collective-permute-start.8 = (bf16[4,192]{1,0:T(4,128)(2,1)S(1)}, bf16[4,192]{1,0:T(4,128)(2,1)S(1)}, u32[]{:S(2)}, u32[]{:S(2)}) collective-permute-start(bf16[4,192]{1,0:T(4,128)(2,1)S(1)} %get-tuple-element.112), channel_id=1, source_target_pairs={{0,32},{1,33},{2,34},{3,35},{4,36},{5,37},{6,38},{7,39},{8,40},{9,... | collective-permute-start | bytes 4616 | tf_op jit(solution)/shard_map/cond/branch_1_fun/ppermute | solution.py:493
  185.9 4.5 %collective-permute-done.9.far = bf16[4,192]{1,0:T(4,128)(2,1)S(1)} collective-permute-done((bf16[4,192]{1,0:T(4,128)(2,1)S(1)}, bf16[4,192]{1,0:T(4,128)(2,1)S(1)}, u32[]{:S(2)}, u32[]{:S(2)}) %collective-permute-start.9) | collective-permute-done | bytes 1568 | tf_op jit(solution)/shard_map/cond/branch_1_fun/ppermute | solution.py:493
  191.1 7.6 %all-to-all-start.7 = ((bf16[16,8,192]{2,1,0:T(8,128)(2,1)}), bf16[16,8,192]{2,1,0:T(8,128)(2,1)S(1)}, u32[]{:S(2)}, u32[]{:S(2)}) async-start(bf16[16,8,192]{2,1,0:T(8,128)(2,1)} %pair_up.7), calls=%async_computation.7 | async-start | bytes 131072 | tf_op jit(solution)/shard_map/cond/branch_1_fun/all_to_all | solution.py:488
  198.8 2.3 %copy-done.12 = bf16[2,192,6144]{2,1,0:T(8,128)(2,1)} copy-done((bf16[2,192,6144]{2,1,0:T(8,128)(2,1)}, bf16[2,192,6144]{2,1,0:T(8,128)(2,1)S(1)}, u32[]{:S(2)}) %copy-start.12) | copy-done | bytes 4718616 | tf_op jit(solution)/shard_map/cond
  201.1 5.3 %all-to-all-done.7.both = bf16[16,8,192]{2,1,0:T(8,128)(2,1)S(1)} async-done(((bf16[16,8,192]{2,1,0:T(8,128)(2,1)}), bf16[16,8,192]{2,1,0:T(8,128)(2,1)S(1)}, u32[]{:S(2)}, u32[]{:S(2)}) %all-to-all-start.7) | async-done | bytes 49184 | tf_op jit(solution)/shard_map/cond/branch_1_fun/all_to_all | solution.py:488
  206.4 2.3 %copy-done.13 = bf16[2,192,6144]{2,1,0:T(8,128)(2,1)S(1)} copy-done((bf16[2,192,6144]{2,1,0:T(8,128)(2,1)S(1)}, bf16[2,192,6144]{2,1,0:T(8,128)(2,1)}, u32[]{:S(2)}) %copy-start.13) | copy-done | bytes 4718616 | tf_op jit(solution)/shard_map/cond
  208.8 1.7 lift.3
  (58 shorter events, 6.8 us)
Async XLA Ops:
  0.0 1.6 copy-start
  2.0 3.7 %collective-permute-start.16 = (f32[4,192]{1,0:T(4,128)S(1)}, f32[4,192]{1,0:T(4,128)S(1)}, u32[]{:S(2)}, u32[]{:S(2)}) collective-permute-start(f32[4,192]{1,0:T(4,128)S(1)} %get-tuple-element.138), channel_id=1, source_target_pairs={{32,0},{64,32},{96,64},{128,96},{160,128},{192,160},{224,192},{33,... | collective-permute-start | bytes 9224 | tf_op jit(solution)/shard_map/ppermute | solution.py:474
  5.8 3.5 %collective-permute-start.18 = (bf16[16,4,192]{2,1,0:T(4,128)(2,1)S(1)}, bf16[16,4,192]{2,1,0:T(4,128)(2,1)S(1)}, u32[]{:S(2)}, u32[]{:S(2)}) collective-permute-start(bf16[16,4,192]{2,1,0:T(4,128)(2,1)S(1)} %get-tuple-element.174), channel_id=1, source_target_pairs={{32,65},{33,64},{34,67},{35,66},{36,69},{37,68},{38,71},{39,70},{4... | collective-permute-start | bytes 73736 | tf_op jit(solution)/shard_map/ppermute | solution.py:493
  6.5 2.9 %collective-permute-start.17 = (bf16[16,4,192]{2,1,0:T(4,128)(2,1)S(1)}, bf16[16,4,192]{2,1,0:T(4,128)(2,1)S(1)}, u32[]{:S(2)}, u32[]{:S(2)}) collective-permute-start(bf16[16,4,192]{2,1,0:T(4,128)(2,1)S(1)} %get-tuple-element.174), channel_id=1, source_target_pairs={{32,64},{33,65},{34,66},{35,67},{36,68},{37,69},{38,70},{39,71},{4... | collective-permute-start | bytes 73736 | tf_op jit(solution)/shard_map/ppermute | solution.py:493
  7.2 2.2 %copy-start.4 = (bf16[2,192,6144]{2,1,0:T(8,128)(2,1)}, bf16[2,192,6144]{2,1,0:T(8,128)(2,1)S(1)}, u32[]{:S(2)}) copy-start(bf16[2,192,6144]{2,1,0:T(8,128)(2,1)S(1)} %hold.13.matrix) | copy-start | bytes 14155780
  9.3 2.3 %copy-start.5 = (bf16[2,192,6144]{2,1,0:T(8,128)(2,1)S(1)}, bf16[2,192,6144]{2,1,0:T(8,128)(2,1)}, u32[]{:S(2)}) copy-start(bf16[2,192,6144]{2,1,0:T(8,128)(2,1)} %copy-done.4) | copy-start | bytes 14155780
  13.1 1.6 copy-start.1
  13.1 1.7 copy-start.14
  13.1 11.7 %collective-permute-start.20 = (bf16[16,4,192]{2,1,0:T(4,128)(2,1)S(1)}, bf16[16,4,192]{2,1,0:T(4,128)(2,1)S(1)}, u32[]{:S(2)}, u32[]{:S(2)}) collective-permute-start(bf16[16,4,192]{2,1,0:T(4,128)(2,1)S(1)} %get-tuple-element.176), channel_id=1, source_target_pairs={{96,129},{97,128},{98,131},{99,130},{100,133},{101,132},{102,135},... | collective-permute-start | bytes 73736 | tf_op jit(solution)/shard_map/ppermute | solution.py:493
  13.9 10.9 %collective-permute-start.19 = (bf16[16,4,192]{2,1,0:T(4,128)(2,1)S(1)}, bf16[16,4,192]{2,1,0:T(4,128)(2,1)S(1)}, u32[]{:S(2)}, u32[]{:S(2)}) collective-permute-start(bf16[16,4,192]{2,1,0:T(4,128)(2,1)S(1)} %get-tuple-element.176), channel_id=1, source_target_pairs={{96,128},{97,129},{98,130},{99,131},{100,132},{101,133},{102,134},... | collective-permute-start | bytes 73736 | tf_op jit(solution)/shard_map/ppermute | solution.py:493
  15.6 136.9 %collective-permute-start.11 = (bf16[5,3,64,192]{3,2,1,0:T(8,128)(2,1)}, bf16[5,3,64,192]{3,2,1,0:T(8,128)(2,1)}, u32[]{:S(2)}, u32[]{:S(2)}) collective-permute-start(bf16[5,3,64,192]{3,2,1,0:T(8,128)(2,1)} %get-tuple-element.133), channel_id=1, source_target_pairs={{0,32},{64,96},{96,128},{128,160},{160,192},{192,224},{1,33},{65,9... | collective-permute-start | bytes 1105928 | tf_op jit(solution)/shard_map/ppermute | solution.py:552
  17.5 135.0 %collective-permute-start.10 = (bf16[5,3,64,192]{3,2,1,0:T(8,128)(2,1)}, bf16[5,3,64,192]{3,2,1,0:T(8,128)(2,1)}, u32[]{:S(2)}, u32[]{:S(2)}) collective-permute-start(bf16[5,3,64,192]{3,2,1,0:T(8,128)(2,1)} %get-tuple-element.133), channel_id=1, source_target_pairs={{32,64},{33,65},{34,66},{35,67},{36,68},{37,69},{38,70},{39,71},{4... | collective-permute-start | bytes 1105928 | tf_op jit(solution)/shard_map/ppermute | solution.py:552
  19.0 134.7 %collective-permute-start.13 = (bf16[5,3,64,192]{3,2,1,0:T(8,128)(2,1)S(1)}, bf16[5,3,64,192]{3,2,1,0:T(8,128)(2,1)}, u32[]{:S(2)}, u32[]{:S(2)}) collective-permute-start(bf16[5,3,64,192]{3,2,1,0:T(8,128)(2,1)S(1)} %get-tuple-element.134), channel_id=1, source_target_pairs={{32,0},{96,64},{128,96},{160,128},{192,160},{224,192},{33,1},{97,6... | collective-permute-start | bytes 1105928 | tf_op jit(solution)/shard_map/ppermute | solution.py:552
  22.6 2.2 %copy-start.2 = (bf16[2,192,6144]{2,1,0:T(8,128)(2,1)}, bf16[2,192,6144]{2,1,0:T(8,128)(2,1)S(1)}, u32[]{:S(2)}) copy-start(bf16[2,192,6144]{2,1,0:T(8,128)(2,1)S(1)} %hold.12.matrix) | copy-start | bytes 14155780
  24.8 2.3 %copy-start.3 = (bf16[2,192,6144]{2,1,0:T(8,128)(2,1)S(1)}, bf16[2,192,6144]{2,1,0:T(8,128)(2,1)}, u32[]{:S(2)}) copy-start(bf16[2,192,6144]{2,1,0:T(8,128)(2,1)} %copy-done.2) | copy-start | bytes 14155780
  28.6 119.7 %collective-permute-start.7 = (bf16[16,4,192]{2,1,0:T(4,128)(2,1)S(1)}, bf16[16,4,192]{2,1,0:T(4,128)(2,1)S(1)}, u32[]{:S(2)}, u32[]{:S(2)}) collective-permute-start(bf16[16,4,192]{2,1,0:T(4,128)(2,1)S(1)} %get-tuple-element.105), channel_id=1, source_target_pairs={{0,97},{1,96},{2,99},{3,98},{4,101},{5,100},{6,103},{7,102},{8,105... | collective-permute-start | bytes 73736 | tf_op jit(solution)/shard_map/cond/branch_1_fun/ppermute | solution.py:493
  145.8 3.7 %collective-permute-start.6 = (bf16[16,4,192]{2,1,0:T(4,128)(2,1)S(1)}, bf16[16,4,192]{2,1,0:T(4,128)(2,1)S(1)}, u32[]{:S(2)}, u32[]{:S(2)}) collective-permute-start(bf16[16,4,192]{2,1,0:T(4,128)(2,1)S(1)} %get-tuple-element.105), channel_id=1, source_target_pairs={{0,96},{1,97},{2,98},{3,99},{4,100},{5,101},{6,102},{7,103},{8,104... | collective-permute-start | bytes 73736 | tf_op jit(solution)/shard_map/cond/branch_1_fun/ppermute | solution.py:493
  151.0 2.7 %collective-permute-start.12 = (bf16[5,3,64,192]{3,2,1,0:T(8,128)(2,1)S(1)}, bf16[5,3,64,192]{3,2,1,0:T(8,128)(2,1)}, u32[]{:S(2)}, u32[]{:S(2)}) collective-permute-start(bf16[5,3,64,192]{3,2,1,0:T(8,128)(2,1)S(1)} %get-tuple-element.134), channel_id=1, source_target_pairs={{64,32},{65,33},{66,34},{67,35},{68,36},{69,37},{70,38},{71,39},{7... | collective-permute-start | bytes 1105928 | tf_op jit(solution)/shard_map/ppermute | solution.py:552
  154.9 10.9 %collective-permute-start.14 = (bf16[5,14,4,192]{3,2,1,0:T(4,128)(2,1)S(1)}, bf16[5,14,4,192]{3,2,1,0:T(4,128)(2,1)S(1)}, u32[]{:S(2)}, u32[]{:S(2)}) collective-permute-start(bf16[5,14,4,192]{3,2,1,0:T(4,128)(2,1)S(1)} %get-tuple-element.135), channel_id=1, source_target_pairs={{0,1},{1,2},{2,3},{3,4},{4,5},{5,6},{6,7},{7,8},{8,9},{9,10},{10,1... | collective-permute-start | bytes 322568 | tf_op jit(solution)/shard_map/ppermute | solution.py:465
  159.5 11.8 %collective-permute-start.15 = (bf16[5,14,4,192]{3,2,1,0:T(4,128)(2,1)S(1)}, bf16[5,14,4,192]{3,2,1,0:T(4,128)(2,1)S(1)}, u32[]{:S(2)}, u32[]{:S(2)}) collective-permute-start(bf16[5,14,4,192]{3,2,1,0:T(4,128)(2,1)S(1)} %get-tuple-element.136), channel_id=1, source_target_pairs={{1,0},{2,1},{3,2},{4,3},{5,4},{6,5},{7,6},{8,7},{9,8},{10,9},{11,1... | collective-permute-start | bytes 322568 | tf_op jit(solution)/shard_map/ppermute | solution.py:465
  183.4 7.0 %copy-start.15 = (f32[2,2,8,64,192]{4,3,2,1,0:T(8,128)}, f32[2,2,8,64,192]{4,3,2,1,0:T(8,128)S(1)}, u32[]{:S(2)}) copy-start(f32[2,2,8,64,192]{4,3,2,1,0:T(8,128)S(1)} %get-tuple-element.109.smoothed) | copy-start | bytes 4718596 | tf_op jit(solution)/shard_map/cond
  183.5 7.0 %collective-permute-start.9 = (bf16[4,192]{1,0:T(4,128)(2,1)S(1)}, bf16[4,192]{1,0:T(4,128)(2,1)S(1)}, u32[]{:S(2)}, u32[]{:S(2)}) collective-permute-start(bf16[4,192]{1,0:T(4,128)(2,1)S(1)} %get-tuple-element.112), channel_id=1, source_target_pairs={{0,33},{1,32},{2,35},{3,34},{4,37},{5,36},{6,39},{7,38},{8,41},{9,... | collective-permute-start | bytes 4616 | tf_op jit(solution)/shard_map/cond/branch_1_fun/ppermute | solution.py:493
  183.6 6.9 %collective-permute-start.8 = (bf16[4,192]{1,0:T(4,128)(2,1)S(1)}, bf16[4,192]{1,0:T(4,128)(2,1)S(1)}, u32[]{:S(2)}, u32[]{:S(2)}) collective-permute-start(bf16[4,192]{1,0:T(4,128)(2,1)S(1)} %get-tuple-element.112), channel_id=1, source_target_pairs={{0,32},{1,33},{2,34},{3,35},{4,36},{5,37},{6,38},{7,39},{8,40},{9,... | collective-permute-start | bytes 4616 | tf_op jit(solution)/shard_map/cond/branch_1_fun/ppermute | solution.py:493
  191.1 15.3 %all-to-all-start.7 = ((bf16[16,8,192]{2,1,0:T(8,128)(2,1)}), bf16[16,8,192]{2,1,0:T(8,128)(2,1)S(1)}, u32[]{:S(2)}, u32[]{:S(2)}) async-start(bf16[16,8,192]{2,1,0:T(8,128)(2,1)} %pair_up.7), calls=%async_computation.7 | async-start | bytes 131072 | tf_op jit(solution)/shard_map/cond/branch_1_fun/all_to_all | solution.py:488
  198.8 7.7 %copy-start.16 = (f32[2,2,8,64,192]{4,3,2,1,0:T(8,128)S(1)}, f32[2,2,8,64,192]{4,3,2,1,0:T(8,128)}, u32[]{:S(2)}) copy-start(f32[2,2,8,64,192]{4,3,2,1,0:T(8,128)} %copy-done.15) | copy-start | bytes 4718596 | tf_op jit(solution)/shard_map/cond
  198.8 2.3 %copy-start.12 = (bf16[2,192,6144]{2,1,0:T(8,128)(2,1)}, bf16[2,192,6144]{2,1,0:T(8,128)(2,1)S(1)}, u32[]{:S(2)}) copy-start(bf16[2,192,6144]{2,1,0:T(8,128)(2,1)S(1)} %hold.11.matrix) | copy-start | bytes 14155780 | tf_op jit(solution)/shard_map/cond
  206.4 2.3 %copy-start.13 = (bf16[2,192,6144]{2,1,0:T(8,128)(2,1)S(1)}, bf16[2,192,6144]{2,1,0:T(8,128)(2,1)}, u32[]{:S(2)}) copy-start(bf16[2,192,6144]{2,1,0:T(8,128)(2,1)} %copy-done.12) | copy-start | bytes 14155780 | tf_op jit(solution)/shard_map/cond

commit v11 on v10

--- a/solution.py
+++ b/solution.py
@@ -47,19 +47,25 @@
     return total
 
 
-def restrict_kernel(residual, rhs, spread):
+def restrict_kernel(residual, rhs, spread, brick, arrived):
     shots, _, depth, height, width = residual.shape
     strips, across = height // QY, width // PX
-    sums = []
-    for strip in range(strips):
-        for part in range(2):
-            for shot in range(shots):
-                total = residual[shot, part, 0, strip * QY : (strip + 1) * QY, :]
-                for plane in range(1, depth):
-                    total = total + residual[shot, part, plane, strip * QY : (strip + 1) * QY, :]
-                sums.append(jnp.sum(total, axis=0, keepdims=True))
+    lines = 2 * shots
+    blocks = [(shot, part) for part in range(2) for shot in range(shots)]
+    copies = [
+        pltpu.make_async_copy(residual.at[block], brick.at[at], arrived.at[at]) for at, block in enumerate(blocks)
+    ]
+    for copy in copies:
+        copy.start()
+    sums = [None] * (strips * lines)
+    for at in range(lines):
+        copies[at].wait()
+        for strip in range(strips):
+            total = brick[at, 0, strip * QY : (strip + 1) * QY, :]
+            for plane in range(1, depth):
+                total = total + brick[at, plane, strip * QY : (strip + 1) * QY, :]
+            sums[strip * lines + at] = jnp.sum(total, axis=0, keepdims=True)
     means = exact_dot(jnp.concatenate(sums, axis=0), membership(width, across), 0) * (1.0 / (depth * QY * PX))
-    lines = 2 * shots
     for strip in range(strips):
         rhs[:, strip * across : (strip + 1) * across] = means[strip * lines : (strip + 1) * lines, :]
     vector = rhs[...].astype(bf16)
@@ -68,7 +74,7 @@
 
 
 def restrict(residual, devices):
-    shots, _, _, height, width = residual.shape
+    shots, _, depth, height, width = residual.shape
     cells = (height // QY) * (width // PX)
     return pl.pallas_call(
         restrict_kernel,
@@ -76,9 +82,14 @@
             jax.ShapeDtypeStruct((2 * shots, cells), f32),
             jax.ShapeDtypeStruct((devices, 2 * shots, cells), bf16),
         ),
+        in_specs=[pl.BlockSpec(memory_space=pltpu.HBM)],
+        scratch_shapes=[
+            pltpu.VMEM((2 * shots, depth, height, width), f32),
+            pltpu.SemaphoreType.DMA((2 * shots,)),
+        ],
         compiler_params=limit(8),
         name="restrict",
-    )(residual)
+    )(pltpu.with_memory_space_constraint(residual, pltpu.HBM))
 
 
 def hold_kernel(step, matrix, held, arrived):
@@ -384,16 +395,11 @@
     lifted(smoothed, coarse[...], out, fine, wide, left)
 
 
-def last_kernel(step, smoothed, kept_before, matrix, both, out, fine, wide, left, vector, coarse):
-    coarse[...] = kept_before[...]
-
-    @pl.when(lax.axis_index("layer") == step)
-    def _():
-        ordered(vector, halves(both))
-        full = vector[...]
-        coarse[...] = combined(times(full, matrix[0]), times(full, matrix[1]))
-
-    lifted(smoothed, coarse[...], out, fine, wide, left)
+def last_kernel(step, smoothed, kept, matrix, both, out, fine, wide, left, vector):
+    ordered(vector, halves(both))
+    full = vector[...]
+    solved = combined(times(full, matrix[0]), times(full, matrix[1]))
+    lifted(smoothed, jnp.where(lax.axis_index("layer") == step, solved, kept[...]), out, fine, wide, left)
 
 
 def lift(smoothed, kept, step=None, *operands):
@@ -408,7 +414,7 @@
     if operands:
         columns = operands[1].shape[0]
         kernel = functools.partial(last_kernel, step)
-        scratch += [pltpu.VMEM((lines, 2 * columns * cells), bf16), pltpu.VMEM((lines, cells), f32)]
+        scratch += [pltpu.VMEM((lines, 2 * columns * cells), bf16)]
     return pl.pallas_call(
         kernel,
         out_shape=pltpu.HBM(smoothed.shape, f32),

time: 211 us -> 213 us (level)
  Pallas kernels: 22.3 us -> 25.2 us
    unnamed x14 -> x12, local copies, waits for them, and re-layouts: 10.7 us -> 9.08 us
where the time goes in v11:
time: 213 us; the launch traced here: 212 us
  starting transfers between devices  151 us (71%)
  Pallas kernels  25.2 us (12%)
  waiting for transfers between devices  19.2 us (9%)
  local copies, waits for them, and re-layouts  13.7 us (6%)
  other arithmetic  2.32 us (1%)
    ppermute x8, starting transfers between devices, hop(): found.append(lax.ppermute(sent, ('layer', 'row'), way(step, flip)))  122 us
    pallas_call x1, Pallas kernels, smooth(): pl.pallas_call(smooth_kernel, out_shape=jax.ShapeDtypeStruct(residual.sha...  12.1 us
    unnamed x12, local copies, waits for them, and re-layouts  9.08 us
    all_to_all x1, starting transfers between devices, gather(): lax.all_to_all(blocks, 'row', 0, 0, axis_index_groups=ends, tiled=True)  7.64 us
    ppermute x8, waiting for transfers between devices, hop(): found.append(lax.ppermute(sent, ('layer', 'row'), way(step, flip)))  5.87 us
    ppermute x1, waiting for transfers between devices, both_ways(): lax.ppermute(low_block, axis, [(b, a) for a, b in up])  5.57 us
    all_to_all x1, waiting for transfers between devices, gather(): lax.all_to_all(blocks, 'row', 0, 0, axis_index_groups=ends, tiled=True)  5.35 us
    ppermute x2, starting transfers between devices, planes_of(): lax.ppermute(first, 'layer', back)  5.1 us
  transfers between devices with their start and end apart: 16, of which 7 were waited for; matrix products, arithmetic and copies ran while one was open for 1% of the time, Pallas kernels for 3%

profile of v11, /device:TPU:224, one launch (start us, length us, event | category | flops | bytes accessed | tf_op | source)
XLA Modules:
  0.0 211.9 jit_solution(5762015429744032574)
XLA Ops:
  0.0 1.8 restrict.1
  1.8 2.4 %collective-permute-start.16 = (f32[4,192]{1,0:T(4,128)S(1)}, f32[4,192]{1,0:T(4,128)S(1)}, u32[]{:S(2)}, u32[]{:S(2)}) collective-permute-start(f32[4,192]{1,0:T(4,128)S(1)} %get-tuple-element.138), channel_id=1, source_target_pairs={{32,0},{64,32},{96,64},{128,96},{160,128},{192,160},{224,192},{33,... | collective-permute-start | bytes 9224 | tf_op jit(solution)/shard_map/ppermute | solution.py:480
  4.2 1.3 collective-permute-done.16.next_rhs
  7.0 2.1 %copy-done.3 = bf16[2,192,6144]{2,1,0:T(8,128)(2,1)} copy-done((bf16[2,192,6144]{2,1,0:T(8,128)(2,1)}, bf16[2,192,6144]{2,1,0:T(8,128)(2,1)S(1)}, u32[]{:S(2)}) %copy-start.3) | copy-done | bytes 4718616
  9.2 2.3 %copy-done.4 = bf16[2,192,6144]{2,1,0:T(8,128)(2,1)S(1)} copy-done((bf16[2,192,6144]{2,1,0:T(8,128)(2,1)S(1)}, bf16[2,192,6144]{2,1,0:T(8,128)(2,1)}, u32[]{:S(2)}) %copy-start.4) | copy-done | bytes 4718616
  11.5 1.4 solve_layer.10
  15.5 1.9 collective-permute-start.11
  17.4 1.4 collective-permute-start.10
  18.8 3.6 %collective-permute-start.13 = (bf16[5,3,64,192]{3,2,1,0:T(8,128)(2,1)S(1)}, bf16[5,3,64,192]{3,2,1,0:T(8,128)(2,1)}, u32[]{:S(2)}, u32[]{:S(2)}) collective-permute-start(bf16[5,3,64,192]{3,2,1,0:T(8,128)(2,1)S(1)} %get-tuple-element.134), channel_id=1, source_target_pairs={{32,0},{96,64},{128,96},{160,128},{192,160},{224,192},{33,1},{97,6... | collective-permute-start | bytes 1105928 | tf_op jit(solution)/shard_map/ppermute | solution.py:558
  22.5 2.1 %copy-done.1 = bf16[2,192,6144]{2,1,0:T(8,128)(2,1)} copy-done((bf16[2,192,6144]{2,1,0:T(8,128)(2,1)}, bf16[2,192,6144]{2,1,0:T(8,128)(2,1)S(1)}, u32[]{:S(2)}) %copy-start.1) | copy-done | bytes 4718616
  24.7 2.3 %copy-done.2 = bf16[2,192,6144]{2,1,0:T(8,128)(2,1)S(1)} copy-done((bf16[2,192,6144]{2,1,0:T(8,128)(2,1)S(1)}, bf16[2,192,6144]{2,1,0:T(8,128)(2,1)}, u32[]{:S(2)}) %copy-start.2) | copy-done | bytes 4718616
  27.0 1.4 solve_layer.11
  28.5 122.3 %conditional.16 = ((f32[4,192]{1,0:T(4,128)S(1)}, bf16[4,192]{1,0:T(4,128)(2,1)S(1)})) conditional(s32[]{:T(128)} %convert_element_type.32, (f32[4,192]{1,0:T(4,128)S(1)}, bf16[4,192]{1,0:T(4,128)(2,1)S(1)}) %tuple.80, (bf16[2,192,6144]{2,1,0:T(8,128)(2,1)}, bf16[16,4,192]{2,1,0:T(4,128)(2,1)S(1)}, f32[4,192]{1,0:T(4,128)S(1)}) %tuple.115), branch_computations={%region_14.15_spmd, %region_15.16_spmd} | conditional | flops 9437184 | bytes 4915288 | solution.py:546
  28.5 117.2 %collective-permute-start.7 = (bf16[16,4,192]{2,1,0:T(4,128)(2,1)S(1)}, bf16[16,4,192]{2,1,0:T(4,128)(2,1)S(1)}, u32[]{:S(2)}, u32[]{:S(2)}) collective-permute-start(bf16[16,4,192]{2,1,0:T(4,128)(2,1)S(1)} %get-tuple-element.105), channel_id=1, source_target_pairs={{0,97},{1,96},{2,99},{3,98},{4,101},{5,100},{6,103},{7,102},{8,105... | collective-permute-start | bytes 73736 | tf_op jit(solution)/shard_map/cond/branch_1_fun/ppermute | solution.py:499
  145.7 2.3 %hold.10.matrix = bf16[2,192,6144]{2,1,0:T(8,128)(2,1)S(1)} custom-call(bf16[2,192,6144]{2,1,0:T(8,128)(2,1)} %get-tuple-element.104.matrix), custom_call_target="tpu_custom_call" | custom-call | tf_op jit(solution)/shard_map/cond/branch_1_fun/hold/pallas_call | solution.py:104
  148.2 1.2 collective-permute-done.6.same
  149.4 1.4 solve_layer.9
  150.8 1.5 collective-permute-start.12
  152.4 1.1 broadcast_select_fusion.1.below.deep_low
  154.7 4.7 %collective-permute-start.14 = (bf16[5,14,4,192]{3,2,1,0:T(4,128)(2,1)S(1)}, bf16[5,14,4,192]{3,2,1,0:T(4,128)(2,1)S(1)}, u32[]{:S(2)}, u32[]{:S(2)}) collective-permute-start(bf16[5,14,4,192]{3,2,1,0:T(4,128)(2,1)S(1)} %get-tuple-element.135), channel_id=1, source_target_pairs={{0,1},{1,2},{2,3},{3,4},{4,5},{5,6},{6,7},{7,8},{8,9},{9,10},{10,1... | collective-permute-start | bytes 322568 | tf_op jit(solution)/shard_map/ppermute | solution.py:471
  159.4 5.1 %collective-permute-start.15 = (bf16[5,14,4,192]{3,2,1,0:T(4,128)(2,1)S(1)}, bf16[5,14,4,192]{3,2,1,0:T(4,128)(2,1)S(1)}, u32[]{:S(2)}, u32[]{:S(2)}) collective-permute-start(bf16[5,14,4,192]{3,2,1,0:T(4,128)(2,1)S(1)} %get-tuple-element.136), channel_id=1, source_target_pairs={{1,0},{2,1},{3,2},{4,3},{5,4},{6,5},{7,6},{8,7},{9,8},{10,9},{11,1... | collective-permute-start | bytes 322568 | tf_op jit(solution)/shard_map/ppermute | solution.py:471
  164.5 1.1 collective-permute-done.14.row_low
  165.6 5.6 %collective-permute-done.15.row_high = bf16[5,14,4,192]{3,2,1,0:T(4,128)(2,1)S(1)} collective-permute-done((bf16[5,14,4,192]{3,2,1,0:T(4,128)(2,1)S(1)}, bf16[5,14,4,192]{3,2,1,0:T(4,128)(2,1)S(1)}, u32[]{:S(2)}, u32[]{:S(2)}) %collective-permute-start.15) | collective-permute-done | bytes 107552 | tf_op jit(solution)/shard_map/ppermute | solution.py:471
  171.2 12.1 %smooth.1 = f32[2,2,8,64,192]{4,3,2,1,0:T(8,128)S(1)} custom-call(f32[4]{0:T(128)S(1)} %add_convert_fusion.inside, f32[2,2,8,64,192]{4,3,2,1,0:T(8,128)S(1)} %copy-done, f32[8,64,192]{2,1,0:T(8,128)S(1)} %copy-done.13, bf16[5,14,4,192]{3,2,1,0:T(4,128)(2,1)S(1)} %collective-permute-done.14.row_low, ...), custom_call_target="tpu_custom_call" | custom-call | flops 117964800 | bytes 4718592 | tf_op jit(solution)/shard_map/smooth/pallas_call | solution.py:364
  183.2 28.5 %conditional.17 = (f32[2,2,8,64,192]{4,3,2,1,0:T(8,128)}) conditional(s32[]{:T(128)} %convert_element_type.30, (f32[2,2,8,64,192]{4,3,2,1,0:T(8,128)S(1)}, f32[4,192]{1,0:T(4,128)S(1)}) %tuple.82, (bf16[2,192,6144]{2,1,0:T(8,128)(2,1)}, bf16[4,192]{1,0:T(4,128)(2,1)S(1)}, f32[2,2,8,64,192]{4,3,2,1,0:T(8,128)S(1)}, f32[4,192]{1,0:T(4,128)S(1)}) %tuple.116), branch_computations={%region_16.17_spmd, %region_17.18_spmd} | conditional | bytes 50524392 | solution.py:577
  183.4 2.4 %collective-permute-start.8 = (bf16[4,192]{1,0:T(4,128)(2,1)S(1)}, bf16[4,192]{1,0:T(4,128)(2,1)S(1)}, u32[]{:S(2)}, u32[]{:S(2)}) collective-permute-start(bf16[4,192]{1,0:T(4,128)(2,1)S(1)} %get-tuple-element.112), channel_id=1, source_target_pairs={{0,32},{1,33},{2,34},{3,35},{4,36},{5,37},{6,38},{7,39},{8,40},{9,... | collective-permute-start | bytes 4616 | tf_op jit(solution)/shard_map/cond/branch_1_fun/ppermute | solution.py:499
  185.8 4.5 %collective-permute-done.9.far = bf16[4,192]{1,0:T(4,128)(2,1)S(1)} collective-permute-done((bf16[4,192]{1,0:T(4,128)(2,1)S(1)}, bf16[4,192]{1,0:T(4,128)(2,1)S(1)}, u32[]{:S(2)}, u32[]{:S(2)}) %collective-permute-start.9) | collective-permute-done | bytes 1568 | tf_op jit(solution)/shard_map/cond/branch_1_fun/ppermute | solution.py:499
  190.9 7.6 %all-to-all-start.7 = ((bf16[16,8,192]{2,1,0:T(8,128)(2,1)}), bf16[16,8,192]{2,1,0:T(8,128)(2,1)S(1)}, u32[]{:S(2)}, u32[]{:S(2)}) async-start(bf16[16,8,192]{2,1,0:T(8,128)(2,1)} %pair_up.7), calls=%async_computation.7 | async-start | bytes 131072 | tf_op jit(solution)/shard_map/cond/branch_1_fun/all_to_all | solution.py:494
  198.6 2.3 %copy-done.11 = bf16[2,192,6144]{2,1,0:T(8,128)(2,1)} copy-done((bf16[2,192,6144]{2,1,0:T(8,128)(2,1)}, bf16[2,192,6144]{2,1,0:T(8,128)(2,1)S(1)}, u32[]{:S(2)}) %copy-start.11) | copy-done | bytes 4718616 | tf_op jit(solution)/shard_map/cond
  200.9 5.3 %all-to-all-done.7.both = bf16[16,8,192]{2,1,0:T(8,128)(2,1)S(1)} async-done(((bf16[16,8,192]{2,1,0:T(8,128)(2,1)}), bf16[16,8,192]{2,1,0:T(8,128)(2,1)S(1)}, u32[]{:S(2)}, u32[]{:S(2)}) %all-to-all-start.7) | async-done | bytes 49184 | tf_op jit(solution)/shard_map/cond/branch_1_fun/all_to_all | solution.py:494
  206.2 2.3 %copy-done.12 = bf16[2,192,6144]{2,1,0:T(8,128)(2,1)S(1)} copy-done((bf16[2,192,6144]{2,1,0:T(8,128)(2,1)S(1)}, bf16[2,192,6144]{2,1,0:T(8,128)(2,1)}, u32[]{:S(2)}) %copy-start.12) | copy-done | bytes 4718616 | tf_op jit(solution)/shard_map/cond
  208.6 3.2 %lift.3 = f32[2,2,8,64,192]{4,3,2,1,0:T(8,128)} custom-call(f32[2,2,8,64,192]{4,3,2,1,0:T(8,128)S(1)} %copy-done.15, f32[4,192]{1,0:T(4,128)S(1)} %get-tuple-element.110.kept, bf16[2,192,6144]{2,1,0:T(8,128)(2,1)S(1)} %copy-done.12, bf16[16,8,192]{2,1,0:T(8,128)(2,1)S(1)} %all-to-all-done.7.both), custom_call_target="tpu_custom_call" | custom-call | tf_op jit(solution)/shard_map/cond/branch_1_fun/lift/pallas_call | solution.py:418
  (56 shorter events, 6.4 us)
Async XLA Ops:
  1.8 3.7 %collective-permute-start.16 = (f32[4,192]{1,0:T(4,128)S(1)}, f32[4,192]{1,0:T(4,128)S(1)}, u32[]{:S(2)}, u32[]{:S(2)}) collective-permute-start(f32[4,192]{1,0:T(4,128)S(1)} %get-tuple-element.138), channel_id=1, source_target_pairs={{32,0},{64,32},{96,64},{128,96},{160,128},{192,160},{224,192},{33,... | collective-permute-start | bytes 9224 | tf_op jit(solution)/shard_map/ppermute | solution.py:480
  5.6 3.5 %collective-permute-start.18 = (bf16[16,4,192]{2,1,0:T(4,128)(2,1)S(1)}, bf16[16,4,192]{2,1,0:T(4,128)(2,1)S(1)}, u32[]{:S(2)}, u32[]{:S(2)}) collective-permute-start(bf16[16,4,192]{2,1,0:T(4,128)(2,1)S(1)} %get-tuple-element.174), channel_id=1, source_target_pairs={{32,65},{33,64},{34,67},{35,66},{36,69},{37,68},{38,71},{39,70},{4... | collective-permute-start | bytes 73736 | tf_op jit(solution)/shard_map/ppermute | solution.py:499
  6.3 2.9 %collective-permute-start.17 = (bf16[16,4,192]{2,1,0:T(4,128)(2,1)S(1)}, bf16[16,4,192]{2,1,0:T(4,128)(2,1)S(1)}, u32[]{:S(2)}, u32[]{:S(2)}) collective-permute-start(bf16[16,4,192]{2,1,0:T(4,128)(2,1)S(1)} %get-tuple-element.174), channel_id=1, source_target_pairs={{32,64},{33,65},{34,66},{35,67},{36,68},{37,69},{38,70},{39,71},{4... | collective-permute-start | bytes 73736 | tf_op jit(solution)/shard_map/ppermute | solution.py:499
  7.0 2.2 %copy-start.3 = (bf16[2,192,6144]{2,1,0:T(8,128)(2,1)}, bf16[2,192,6144]{2,1,0:T(8,128)(2,1)S(1)}, u32[]{:S(2)}) copy-start(bf16[2,192,6144]{2,1,0:T(8,128)(2,1)S(1)} %hold.13.matrix) | copy-start | bytes 14155780
  9.2 2.3 %copy-start.4 = (bf16[2,192,6144]{2,1,0:T(8,128)(2,1)S(1)}, bf16[2,192,6144]{2,1,0:T(8,128)(2,1)}, u32[]{:S(2)}) copy-start(bf16[2,192,6144]{2,1,0:T(8,128)(2,1)} %copy-done.3) | copy-start | bytes 14155780
  12.9 1.6 copy-start
  12.9 1.7 copy-start.13
  13.0 11.6 %collective-permute-start.20 = (bf16[16,4,192]{2,1,0:T(4,128)(2,1)S(1)}, bf16[16,4,192]{2,1,0:T(4,128)(2,1)S(1)}, u32[]{:S(2)}, u32[]{:S(2)}) collective-permute-start(bf16[16,4,192]{2,1,0:T(4,128)(2,1)S(1)} %get-tuple-element.176), channel_id=1, source_target_pairs={{96,129},{97,128},{98,131},{99,130},{100,133},{101,132},{102,135},... | collective-permute-start | bytes 73736 | tf_op jit(solution)/shard_map/ppermute | solution.py:499
  13.8 10.8 %collective-permute-start.19 = (bf16[16,4,192]{2,1,0:T(4,128)(2,1)S(1)}, bf16[16,4,192]{2,1,0:T(4,128)(2,1)S(1)}, u32[]{:S(2)}, u32[]{:S(2)}) collective-permute-start(bf16[16,4,192]{2,1,0:T(4,128)(2,1)S(1)} %get-tuple-element.176), channel_id=1, source_target_pairs={{96,128},{97,129},{98,130},{99,131},{100,132},{101,133},{102,134},... | collective-permute-start | bytes 73736 | tf_op jit(solution)/shard_map/ppermute | solution.py:499
  15.5 136.9 %collective-permute-start.11 = (bf16[5,3,64,192]{3,2,1,0:T(8,128)(2,1)}, bf16[5,3,64,192]{3,2,1,0:T(8,128)(2,1)}, u32[]{:S(2)}, u32[]{:S(2)}) collective-permute-start(bf16[5,3,64,192]{3,2,1,0:T(8,128)(2,1)} %get-tuple-element.133), channel_id=1, source_target_pairs={{0,32},{64,96},{96,128},{128,160},{160,192},{192,224},{1,33},{65,9... | collective-permute-start | bytes 1105928 | tf_op jit(solution)/shard_map/ppermute | solution.py:558
  17.4 135.0 %collective-permute-start.10 = (bf16[5,3,64,192]{3,2,1,0:T(8,128)(2,1)}, bf16[5,3,64,192]{3,2,1,0:T(8,128)(2,1)}, u32[]{:S(2)}, u32[]{:S(2)}) collective-permute-start(bf16[5,3,64,192]{3,2,1,0:T(8,128)(2,1)} %get-tuple-element.133), channel_id=1, source_target_pairs={{32,64},{33,65},{34,66},{35,67},{36,68},{37,69},{38,70},{39,71},{4... | collective-permute-start | bytes 1105928 | tf_op jit(solution)/shard_map/ppermute | solution.py:558
  18.8 134.6 %collective-permute-start.13 = (bf16[5,3,64,192]{3,2,1,0:T(8,128)(2,1)S(1)}, bf16[5,3,64,192]{3,2,1,0:T(8,128)(2,1)}, u32[]{:S(2)}, u32[]{:S(2)}) collective-permute-start(bf16[5,3,64,192]{3,2,1,0:T(8,128)(2,1)S(1)} %get-tuple-element.134), channel_id=1, source_target_pairs={{32,0},{96,64},{128,96},{160,128},{192,160},{224,192},{33,1},{97,6... | collective-permute-start | bytes 1105928 | tf_op jit(solution)/shard_map/ppermute | solution.py:558
  22.5 2.2 %copy-start.1 = (bf16[2,192,6144]{2,1,0:T(8,128)(2,1)}, bf16[2,192,6144]{2,1,0:T(8,128)(2,1)S(1)}, u32[]{:S(2)}) copy-start(bf16[2,192,6144]{2,1,0:T(8,128)(2,1)S(1)} %hold.12.matrix) | copy-start | bytes 14155780
  24.7 2.3 %copy-start.2 = (bf16[2,192,6144]{2,1,0:T(8,128)(2,1)S(1)}, bf16[2,192,6144]{2,1,0:T(8,128)(2,1)}, u32[]{:S(2)}) copy-start(bf16[2,192,6144]{2,1,0:T(8,128)(2,1)} %copy-done.1) | copy-start | bytes 14155780
  28.5 119.7 %collective-permute-start.7 = (bf16[16,4,192]{2,1,0:T(4,128)(2,1)S(1)}, bf16[16,4,192]{2,1,0:T(4,128)(2,1)S(1)}, u32[]{:S(2)}, u32[]{:S(2)}) collective-permute-start(bf16[16,4,192]{2,1,0:T(4,128)(2,1)S(1)} %get-tuple-element.105), channel_id=1, source_target_pairs={{0,97},{1,96},{2,99},{3,98},{4,101},{5,100},{6,103},{7,102},{8,105... | collective-permute-start | bytes 73736 | tf_op jit(solution)/shard_map/cond/branch_1_fun/ppermute | solution.py:499
  145.7 3.7 %collective-permute-start.6 = (bf16[16,4,192]{2,1,0:T(4,128)(2,1)S(1)}, bf16[16,4,192]{2,1,0:T(4,128)(2,1)S(1)}, u32[]{:S(2)}, u32[]{:S(2)}) collective-permute-start(bf16[16,4,192]{2,1,0:T(4,128)(2,1)S(1)} %get-tuple-element.105), channel_id=1, source_target_pairs={{0,96},{1,97},{2,98},{3,99},{4,100},{5,101},{6,102},{7,103},{8,104... | collective-permute-start | bytes 73736 | tf_op jit(solution)/shard_map/cond/branch_1_fun/ppermute | solution.py:499
  150.8 2.7 %collective-permute-start.12 = (bf16[5,3,64,192]{3,2,1,0:T(8,128)(2,1)S(1)}, bf16[5,3,64,192]{3,2,1,0:T(8,128)(2,1)}, u32[]{:S(2)}, u32[]{:S(2)}) collective-permute-start(bf16[5,3,64,192]{3,2,1,0:T(8,128)(2,1)S(1)} %get-tuple-element.134), channel_id=1, source_target_pairs={{64,32},{65,33},{66,34},{67,35},{68,36},{69,37},{70,38},{71,39},{7... | collective-permute-start | bytes 1105928 | tf_op jit(solution)/shard_map/ppermute | solution.py:558
  154.7 10.9 %collective-permute-start.14 = (bf16[5,14,4,192]{3,2,1,0:T(4,128)(2,1)S(1)}, bf16[5,14,4,192]{3,2,1,0:T(4,128)(2,1)S(1)}, u32[]{:S(2)}, u32[]{:S(2)}) collective-permute-start(bf16[5,14,4,192]{3,2,1,0:T(4,128)(2,1)S(1)} %get-tuple-element.135), channel_id=1, source_target_pairs={{0,1},{1,2},{2,3},{3,4},{4,5},{5,6},{6,7},{7,8},{8,9},{9,10},{10,1... | collective-permute-start | bytes 322568 | tf_op jit(solution)/shard_map/ppermute | solution.py:471
  159.4 11.8 %collective-permute-start.15 = (bf16[5,14,4,192]{3,2,1,0:T(4,128)(2,1)S(1)}, bf16[5,14,4,192]{3,2,1,0:T(4,128)(2,1)S(1)}, u32[]{:S(2)}, u32[]{:S(2)}) collective-permute-start(bf16[5,14,4,192]{3,2,1,0:T(4,128)(2,1)S(1)} %get-tuple-element.136), channel_id=1, source_target_pairs={{1,0},{2,1},{3,2},{4,3},{5,4},{6,5},{7,6},{8,7},{9,8},{10,9},{11,1... | collective-permute-start | bytes 322568 | tf_op jit(solution)/shard_map/ppermute | solution.py:471
  183.3 7.0 %copy-start.14 = (f32[2,2,8,64,192]{4,3,2,1,0:T(8,128)}, f32[2,2,8,64,192]{4,3,2,1,0:T(8,128)S(1)}, u32[]{:S(2)}) copy-start(f32[2,2,8,64,192]{4,3,2,1,0:T(8,128)S(1)} %get-tuple-element.109.smoothed) | copy-start | bytes 4718596 | tf_op jit(solution)/shard_map/cond
  183.3 7.0 %collective-permute-start.9 = (bf16[4,192]{1,0:T(4,128)(2,1)S(1)}, bf16[4,192]{1,0:T(4,128)(2,1)S(1)}, u32[]{:S(2)}, u32[]{:S(2)}) collective-permute-start(bf16[4,192]{1,0:T(4,128)(2,1)S(1)} %get-tuple-element.112), channel_id=1, source_target_pairs={{0,33},{1,32},{2,35},{3,34},{4,37},{5,36},{6,39},{7,38},{8,41},{9,... | collective-permute-start | bytes 4616 | tf_op jit(solution)/shard_map/cond/branch_1_fun/ppermute | solution.py:499
  183.4 6.9 %collective-permute-start.8 = (bf16[4,192]{1,0:T(4,128)(2,1)S(1)}, bf16[4,192]{1,0:T(4,128)(2,1)S(1)}, u32[]{:S(2)}, u32[]{:S(2)}) collective-permute-start(bf16[4,192]{1,0:T(4,128)(2,1)S(1)} %get-tuple-element.112), channel_id=1, source_target_pairs={{0,32},{1,33},{2,34},{3,35},{4,36},{5,37},{6,38},{7,39},{8,40},{9,... | collective-permute-start | bytes 4616 | tf_op jit(solution)/shard_map/cond/branch_1_fun/ppermute | solution.py:499
  190.9 15.3 %all-to-all-start.7 = ((bf16[16,8,192]{2,1,0:T(8,128)(2,1)}), bf16[16,8,192]{2,1,0:T(8,128)(2,1)S(1)}, u32[]{:S(2)}, u32[]{:S(2)}) async-start(bf16[16,8,192]{2,1,0:T(8,128)(2,1)} %pair_up.7), calls=%async_computation.7 | async-start | bytes 131072 | tf_op jit(solution)/shard_map/cond/branch_1_fun/all_to_all | solution.py:494
  198.6 7.7 %copy-start.15 = (f32[2,2,8,64,192]{4,3,2,1,0:T(8,128)S(1)}, f32[2,2,8,64,192]{4,3,2,1,0:T(8,128)}, u32[]{:S(2)}) copy-start(f32[2,2,8,64,192]{4,3,2,1,0:T(8,128)} %copy-done.14) | copy-start | bytes 4718596 | tf_op jit(solution)/shard_map/cond
  198.6 2.3 %copy-start.11 = (bf16[2,192,6144]{2,1,0:T(8,128)(2,1)}, bf16[2,192,6144]{2,1,0:T(8,128)(2,1)S(1)}, u32[]{:S(2)}) copy-start(bf16[2,192,6144]{2,1,0:T(8,128)(2,1)S(1)} %hold.11.matrix) | copy-start | bytes 14155780 | tf_op jit(solution)/shard_map/cond
  206.2 2.3 %copy-start.12 = (bf16[2,192,6144]{2,1,0:T(8,128)(2,1)S(1)}, bf16[2,192,6144]{2,1,0:T(8,128)(2,1)}, u32[]{:S(2)}) copy-start(bf16[2,192,6144]{2,1,0:T(8,128)(2,1)} %copy-done.11) | copy-start | bytes 14155780 | tf_op jit(solution)/shard_map/cond

commit v12 on v10

--- a/solution.py
+++ b/solution.py
@@ -471,7 +471,7 @@
     inside = jnp.stack([layer > 0, layer < layers - 1, row > 0, row < devices - 1]).astype(f32)
 
     rhs, spread = restrict(residual, devices)
-    next_rhs = lax.ppermute(rhs, "layer", [(i + 1, i) for i in range(layers - 1)])
+    flipped = lax.ppermute(rhs, "layer", [(i, i ^ 1) for i in range(layers)])
     matrix = pltpu.with_memory_space_constraint(inverse[:, 0], pltpu.HBM)
     gathered = lax.cond(
         layer == 0,
@@ -479,6 +479,13 @@
         lambda blocks: blocks,
         spread,
     )
+    above_rhs = lax.cond(
+        layer == 0,
+        lambda rhs: rhs,
+        lambda rhs: lax.ppermute(rhs, "layer", [(i + 1, i) for i in range(1, layers - 1, 2)]),
+        rhs,
+    )
+    next_rhs = jnp.where((layer & 1) == 0, flipped, above_rhs)
     kept, block = solve_first(matrix, gathered, next_rhs)
 
     columns = devices // 2

time: 211 us -> 211 us (level)
  transfers between devices with their start and end apart: 16 -> 17, of which waited for: 7 -> 7; matrix products, arithmetic and copies ran while one was open for 1% -> 1% of each run, Pallas kernels for 3% -> 3%
where the time goes in v12:
time: 211 us
  starting transfers between devices  150 us (71%)
  Pallas kernels  22.9 us (11%)
  waiting for transfers between devices  19.4 us (9%)
  local copies, waits for them, and re-layouts  15.3 us (7%)
  other arithmetic  2.33 us (1%)
    ppermute x8, starting transfers between devices, hop(): found.append(lax.ppermute(sent, ('layer', 'row'), way(step, flip)))  121 us
    pallas_call x1, Pallas kernels, smooth(): pl.pallas_call(smooth_kernel, out_shape=jax.ShapeDtypeStruct(residual.sha...  12.1 us
    unnamed x14, local copies, waits for them, and re-layouts  10.7 us
    all_to_all x1, starting transfers between devices, gather(): lax.all_to_all(blocks, 'row', 0, 0, axis_index_groups=ends, tiled=True)  7.64 us
    ppermute x8, waiting for transfers between devices, hop(): found.append(lax.ppermute(sent, ('layer', 'row'), way(step, flip)))  5.87 us
    ppermute x1, waiting for transfers between devices, both_ways(): lax.ppermute(low_block, axis, [(b, a) for a, b in up])  5.57 us
    all_to_all x1, waiting for transfers between devices, gather(): lax.all_to_all(blocks, 'row', 0, 0, axis_index_groups=ends, tiled=True)  5.35 us
    ppermute x2, starting transfers between devices, planes_of(): lax.ppermute(first, 'layer', back)  5.11 us
  transfers between devices with their start and end apart: 17, of which 7 were waited for; matrix products, arithmetic and copies ran while one was open for 1% of the time, Pallas kernels for 3%

profile of v12, /device:TPU:224, one launch (start us, length us, event | category | flops | bytes accessed | tf_op | source)
XLA Modules:
  0.0 210.5 jit_solution(15011034234652133051)
XLA Ops:
  0.0 1.6 copy-done
  2.6 4.5 %conditional.11 = (f32[4,192]{1,0:T(4,128)S(1)}) conditional(s32[]{:T(128)} %convert_element_type.39, f32[4,192]{1,0:T(4,128)} %get-tuple-element.143, f32[4,192]{1,0:T(4,128)} %get-tuple-element.143), branch_computations={%region_2.0_spmd, %region_3.0_spmd} | conditional | bytes 12336 | solution.py:482
  2.6 3.0 %collective-permute-start = (f32[4,192]{1,0:T(4,128)}, f32[4,192]{1,0:T(4,128)S(1)}, u32[]{:S(2)}, u32[]{:S(2)}) collective-permute-start(f32[4,192]{1,0:T(4,128)} %param.2), channel_id=1, source_target_pairs={{64,32},{128,96},{192,160},{65,33},{129,97},{193,161},{66,34},{130... | collective-permute-start | bytes 9224 | tf_op jit(solution)/shard_map/cond/branch_0_fun/ppermute | solution.py:485
  5.6 1.5 collective-permute-done
  8.6 2.1 %copy-done.4 = bf16[2,192,6144]{2,1,0:T(8,128)(2,1)} copy-done((bf16[2,192,6144]{2,1,0:T(8,128)(2,1)}, bf16[2,192,6144]{2,1,0:T(8,128)(2,1)S(1)}, u32[]{:S(2)}) %copy-start.4) | copy-done | bytes 4718616
  10.8 2.3 %copy-done.5 = bf16[2,192,6144]{2,1,0:T(8,128)(2,1)S(1)} copy-done((bf16[2,192,6144]{2,1,0:T(8,128)(2,1)S(1)}, bf16[2,192,6144]{2,1,0:T(8,128)(2,1)}, u32[]{:S(2)}) %copy-start.5) | copy-done | bytes 4718616
  13.1 1.4 solve_layer.10
  17.1 1.9 collective-permute-start.12
  19.0 1.4 collective-permute-start.11
  20.4 3.6 %collective-permute-start.14 = (bf16[5,3,64,192]{3,2,1,0:T(8,128)(2,1)S(1)}, bf16[5,3,64,192]{3,2,1,0:T(8,128)(2,1)}, u32[]{:S(2)}, u32[]{:S(2)}) collective-permute-start(bf16[5,3,64,192]{3,2,1,0:T(8,128)(2,1)S(1)} %get-tuple-element.139), channel_id=1, source_target_pairs={{32,0},{96,64},{128,96},{160,128},{192,160},{224,192},{33,1},{97,6... | collective-permute-start | bytes 1105928 | tf_op jit(solution)/shard_map/ppermute | solution.py:559
  24.1 2.1 %copy-done.2 = bf16[2,192,6144]{2,1,0:T(8,128)(2,1)} copy-done((bf16[2,192,6144]{2,1,0:T(8,128)(2,1)}, bf16[2,192,6144]{2,1,0:T(8,128)(2,1)S(1)}, u32[]{:S(2)}) %copy-start.2) | copy-done | bytes 4718616
  26.3 2.3 %copy-done.3 = bf16[2,192,6144]{2,1,0:T(8,128)(2,1)S(1)} copy-done((bf16[2,192,6144]{2,1,0:T(8,128)(2,1)S(1)}, bf16[2,192,6144]{2,1,0:T(8,128)(2,1)}, u32[]{:S(2)}) %copy-start.3) | copy-done | bytes 4718616
  28.6 1.4 solve_layer.11
  30.1 120.8 %conditional.18 = ((f32[4,192]{1,0:T(4,128)S(1)}, bf16[4,192]{1,0:T(4,128)(2,1)S(1)})) conditional(s32[]{:T(128)} %convert_element_type.33, (f32[4,192]{1,0:T(4,128)S(1)}, bf16[4,192]{1,0:T(4,128)(2,1)S(1)}) %tuple.86, (bf16[2,192,6144]{2,1,0:T(8,128)(2,1)}, bf16[16,4,192]{2,1,0:T(4,128)(2,1)S(1)}, f32[4,192]{1,0:T(4,128)S(1)}) %tuple.123), branch_computations={%region_16.17_spmd, %region_17.18_spmd} | conditional | flops 9437184 | bytes 4915288 | solution.py:547
  30.1 115.7 %collective-permute-start.8 = (bf16[16,4,192]{2,1,0:T(4,128)(2,1)S(1)}, bf16[16,4,192]{2,1,0:T(4,128)(2,1)S(1)}, u32[]{:S(2)}, u32[]{:S(2)}) collective-permute-start(bf16[16,4,192]{2,1,0:T(4,128)(2,1)S(1)} %get-tuple-element.110), channel_id=1, source_target_pairs={{0,97},{1,96},{2,99},{3,98},{4,101},{5,100},{6,103},{7,102},{8,105... | collective-permute-start | bytes 73736 | tf_op jit(solution)/shard_map/cond/branch_1_fun/ppermute | solution.py:500
  145.8 2.3 %hold.10.matrix = bf16[2,192,6144]{2,1,0:T(8,128)(2,1)S(1)} custom-call(bf16[2,192,6144]{2,1,0:T(8,128)(2,1)} %get-tuple-element.109.matrix), custom_call_target="tpu_custom_call" | custom-call | tf_op jit(solution)/shard_map/cond/branch_1_fun/hold/pallas_call | solution.py:93
  148.3 1.2 collective-permute-done.7.same
  149.5 1.4 solve_layer.9
  150.9 1.5 collective-permute-start.13
  154.8 4.7 %collective-permute-start.15 = (bf16[5,14,4,192]{3,2,1,0:T(4,128)(2,1)S(1)}, bf16[5,14,4,192]{3,2,1,0:T(4,128)(2,1)S(1)}, u32[]{:S(2)}, u32[]{:S(2)}) collective-permute-start(bf16[5,14,4,192]{3,2,1,0:T(4,128)(2,1)S(1)} %get-tuple-element.140), channel_id=1, source_target_pairs={{0,1},{1,2},{2,3},{3,4},{4,5},{5,6},{6,7},{7,8},{8,9},{9,10},{10,1... | collective-permute-start | bytes 322568 | tf_op jit(solution)/shard_map/ppermute | solution.py:465
  159.5 5.1 %collective-permute-start.16 = (bf16[5,14,4,192]{3,2,1,0:T(4,128)(2,1)S(1)}, bf16[5,14,4,192]{3,2,1,0:T(4,128)(2,1)S(1)}, u32[]{:S(2)}, u32[]{:S(2)}) collective-permute-start(bf16[5,14,4,192]{3,2,1,0:T(4,128)(2,1)S(1)} %get-tuple-element.141), channel_id=1, source_target_pairs={{1,0},{2,1},{3,2},{4,3},{5,4},{6,5},{7,6},{8,7},{9,8},{10,9},{11,1... | collective-permute-start | bytes 322568 | tf_op jit(solution)/shard_map/ppermute | solution.py:465
  164.6 1.1 collective-permute-done.15.row_low
  165.7 5.6 %collective-permute-done.16.row_high = bf16[5,14,4,192]{3,2,1,0:T(4,128)(2,1)S(1)} collective-permute-done((bf16[5,14,4,192]{3,2,1,0:T(4,128)(2,1)S(1)}, bf16[5,14,4,192]{3,2,1,0:T(4,128)(2,1)S(1)}, u32[]{:S(2)}, u32[]{:S(2)}) %collective-permute-start.16) | collective-permute-done | bytes 107552 | tf_op jit(solution)/shard_map/ppermute | solution.py:465
  171.3 12.1 %smooth.1 = f32[2,2,8,64,192]{4,3,2,1,0:T(8,128)S(1)} custom-call(f32[4]{0:T(128)S(1)} %add_convert_fusion.inside, f32[2,2,8,64,192]{4,3,2,1,0:T(8,128)S(1)} %copy-done.1, f32[8,64,192]{2,1,0:T(8,128)S(1)} %copy-done.14, bf16[5,14,4,192]{3,2,1,0:T(4,128)(2,1)S(1)} %collective-permute-done.15.row_low, ...), custom_call_target="tpu_custom_call" | custom-call | flops 117964800 | bytes 4718592 | tf_op jit(solution)/shard_map/smooth/pallas_call | solution.py:353
  183.4 27.0 %conditional.19 = (f32[2,2,8,64,192]{4,3,2,1,0:T(8,128)}) conditional(s32[]{:T(128)} %convert_element_type.31, (f32[2,2,8,64,192]{4,3,2,1,0:T(8,128)S(1)}, f32[4,192]{1,0:T(4,128)S(1)}) %tuple.88, (bf16[2,192,6144]{2,1,0:T(8,128)(2,1)}, bf16[4,192]{1,0:T(4,128)(2,1)S(1)}, f32[2,2,8,64,192]{4,3,2,1,0:T(8,128)S(1)}, f32[4,192]{1,0:T(4,128)S(1)}) %tuple.124), branch_computations={%region_18.19_spmd, %region_19.20_spmd} | conditional | bytes 50524392 | solution.py:578
  183.5 2.4 %collective-permute-start.9 = (bf16[4,192]{1,0:T(4,128)(2,1)S(1)}, bf16[4,192]{1,0:T(4,128)(2,1)S(1)}, u32[]{:S(2)}, u32[]{:S(2)}) collective-permute-start(bf16[4,192]{1,0:T(4,128)(2,1)S(1)} %get-tuple-element.117), channel_id=1, source_target_pairs={{0,32},{1,33},{2,34},{3,35},{4,36},{5,37},{6,38},{7,39},{8,40},{9,... | collective-permute-start | bytes 4616 | tf_op jit(solution)/shard_map/cond/branch_1_fun/ppermute | solution.py:500
  185.9 4.5 %collective-permute-done.10.far = bf16[4,192]{1,0:T(4,128)(2,1)S(1)} collective-permute-done((bf16[4,192]{1,0:T(4,128)(2,1)S(1)}, bf16[4,192]{1,0:T(4,128)(2,1)S(1)}, u32[]{:S(2)}, u32[]{:S(2)}) %collective-permute-start.10) | collective-permute-done | bytes 1568 | tf_op jit(solution)/shard_map/cond/branch_1_fun/ppermute | solution.py:500
  191.0 7.6 %all-to-all-start.7 = ((bf16[16,8,192]{2,1,0:T(8,128)(2,1)}), bf16[16,8,192]{2,1,0:T(8,128)(2,1)S(1)}, u32[]{:S(2)}, u32[]{:S(2)}) async-start(bf16[16,8,192]{2,1,0:T(8,128)(2,1)} %pair_up.7), calls=%async_computation.7 | async-start | bytes 131072 | tf_op jit(solution)/shard_map/cond/branch_1_fun/all_to_all | solution.py:495
  198.7 2.3 %copy-done.12 = bf16[2,192,6144]{2,1,0:T(8,128)(2,1)} copy-done((bf16[2,192,6144]{2,1,0:T(8,128)(2,1)}, bf16[2,192,6144]{2,1,0:T(8,128)(2,1)S(1)}, u32[]{:S(2)}) %copy-start.12) | copy-done | bytes 4718616 | tf_op jit(solution)/shard_map/cond
  201.0 5.3 %all-to-all-done.7.both = bf16[16,8,192]{2,1,0:T(8,128)(2,1)S(1)} async-done(((bf16[16,8,192]{2,1,0:T(8,128)(2,1)}), bf16[16,8,192]{2,1,0:T(8,128)(2,1)S(1)}, u32[]{:S(2)}, u32[]{:S(2)}) %all-to-all-start.7) | async-done | bytes 49184 | tf_op jit(solution)/shard_map/cond/branch_1_fun/all_to_all | solution.py:495
  206.4 2.3 %copy-done.13 = bf16[2,192,6144]{2,1,0:T(8,128)(2,1)S(1)} copy-done((bf16[2,192,6144]{2,1,0:T(8,128)(2,1)S(1)}, bf16[2,192,6144]{2,1,0:T(8,128)(2,1)}, u32[]{:S(2)}) %copy-start.13) | copy-done | bytes 4718616 | tf_op jit(solution)/shard_map/cond
  208.7 1.7 lift.3
  (62 shorter events, 8.4 us)
Async XLA Ops:
  0.0 1.6 copy-start
  2.6 4.5 %collective-permute-start.17 = (f32[4,192]{1,0:T(4,128)}, f32[4,192]{1,0:T(4,128)S(1)}, u32[]{:S(2)}, u32[]{:S(2)}) collective-permute-start(f32[4,192]{1,0:T(4,128)} %get-tuple-element.143), channel_id=1, source_target_pairs={{0,32},{32,0},{64,96},{96,64},{128,160},{160,128},{192,224},{224,1... | collective-permute-start | bytes 9224 | tf_op jit(solution)/shard_map/ppermute | solution.py:474
  2.6 4.5 %collective-permute-start = (f32[4,192]{1,0:T(4,128)}, f32[4,192]{1,0:T(4,128)S(1)}, u32[]{:S(2)}, u32[]{:S(2)}) collective-permute-start(f32[4,192]{1,0:T(4,128)} %param.2), channel_id=1, source_target_pairs={{64,32},{128,96},{192,160},{65,33},{129,97},{193,161},{66,34},{130... | collective-permute-start | bytes 9224 | tf_op jit(solution)/shard_map/cond/branch_0_fun/ppermute | solution.py:485
  7.3 3.5 %collective-permute-start.19 = (bf16[16,4,192]{2,1,0:T(4,128)(2,1)S(1)}, bf16[16,4,192]{2,1,0:T(4,128)(2,1)S(1)}, u32[]{:S(2)}, u32[]{:S(2)}) collective-permute-start(bf16[16,4,192]{2,1,0:T(4,128)(2,1)S(1)} %get-tuple-element.180), channel_id=1, source_target_pairs={{32,65},{33,64},{34,67},{35,66},{36,69},{37,68},{38,71},{39,70},{4... | collective-permute-start | bytes 73736 | tf_op jit(solution)/shard_map/ppermute | solution.py:500
  7.9 2.9 %collective-permute-start.18 = (bf16[16,4,192]{2,1,0:T(4,128)(2,1)S(1)}, bf16[16,4,192]{2,1,0:T(4,128)(2,1)S(1)}, u32[]{:S(2)}, u32[]{:S(2)}) collective-permute-start(bf16[16,4,192]{2,1,0:T(4,128)(2,1)S(1)} %get-tuple-element.180), channel_id=1, source_target_pairs={{32,64},{33,65},{34,66},{35,67},{36,68},{37,69},{38,70},{39,71},{4... | collective-permute-start | bytes 73736 | tf_op jit(solution)/shard_map/ppermute | solution.py:500
  8.6 2.2 %copy-start.4 = (bf16[2,192,6144]{2,1,0:T(8,128)(2,1)}, bf16[2,192,6144]{2,1,0:T(8,128)(2,1)S(1)}, u32[]{:S(2)}) copy-start(bf16[2,192,6144]{2,1,0:T(8,128)(2,1)S(1)} %hold.13.matrix) | copy-start | bytes 14155780
  10.8 2.3 %copy-start.5 = (bf16[2,192,6144]{2,1,0:T(8,128)(2,1)S(1)}, bf16[2,192,6144]{2,1,0:T(8,128)(2,1)}, u32[]{:S(2)}) copy-start(bf16[2,192,6144]{2,1,0:T(8,128)(2,1)} %copy-done.4) | copy-start | bytes 14155780
  14.5 1.6 copy-start.1
  14.5 1.7 copy-start.14
  14.6 11.7 %collective-permute-start.21 = (bf16[16,4,192]{2,1,0:T(4,128)(2,1)S(1)}, bf16[16,4,192]{2,1,0:T(4,128)(2,1)S(1)}, u32[]{:S(2)}, u32[]{:S(2)}) collective-permute-start(bf16[16,4,192]{2,1,0:T(4,128)(2,1)S(1)} %get-tuple-element.182), channel_id=1, source_target_pairs={{96,129},{97,128},{98,131},{99,130},{100,133},{101,132},{102,135},... | collective-permute-start | bytes 73736 | tf_op jit(solution)/shard_map/ppermute | solution.py:500
  15.4 10.9 %collective-permute-start.20 = (bf16[16,4,192]{2,1,0:T(4,128)(2,1)S(1)}, bf16[16,4,192]{2,1,0:T(4,128)(2,1)S(1)}, u32[]{:S(2)}, u32[]{:S(2)}) collective-permute-start(bf16[16,4,192]{2,1,0:T(4,128)(2,1)S(1)} %get-tuple-element.182), channel_id=1, source_target_pairs={{96,128},{97,129},{98,130},{99,131},{100,132},{101,133},{102,134},... | collective-permute-start | bytes 73736 | tf_op jit(solution)/shard_map/ppermute | solution.py:500
  17.1 135.4 %collective-permute-start.12 = (bf16[5,3,64,192]{3,2,1,0:T(8,128)(2,1)}, bf16[5,3,64,192]{3,2,1,0:T(8,128)(2,1)}, u32[]{:S(2)}, u32[]{:S(2)}) collective-permute-start(bf16[5,3,64,192]{3,2,1,0:T(8,128)(2,1)} %get-tuple-element.138), channel_id=1, source_target_pairs={{0,32},{64,96},{96,128},{128,160},{160,192},{192,224},{1,33},{65,9... | collective-permute-start | bytes 1105928 | tf_op jit(solution)/shard_map/ppermute | solution.py:559
  19.0 133.5 %collective-permute-start.11 = (bf16[5,3,64,192]{3,2,1,0:T(8,128)(2,1)}, bf16[5,3,64,192]{3,2,1,0:T(8,128)(2,1)}, u32[]{:S(2)}, u32[]{:S(2)}) collective-permute-start(bf16[5,3,64,192]{3,2,1,0:T(8,128)(2,1)} %get-tuple-element.138), channel_id=1, source_target_pairs={{32,64},{33,65},{34,66},{35,67},{36,68},{37,69},{38,70},{39,71},{4... | collective-permute-start | bytes 1105928 | tf_op jit(solution)/shard_map/ppermute | solution.py:559
  20.4 133.1 %collective-permute-start.14 = (bf16[5,3,64,192]{3,2,1,0:T(8,128)(2,1)S(1)}, bf16[5,3,64,192]{3,2,1,0:T(8,128)(2,1)}, u32[]{:S(2)}, u32[]{:S(2)}) collective-permute-start(bf16[5,3,64,192]{3,2,1,0:T(8,128)(2,1)S(1)} %get-tuple-element.139), channel_id=1, source_target_pairs={{32,0},{96,64},{128,96},{160,128},{192,160},{224,192},{33,1},{97,6... | collective-permute-start | bytes 1105928 | tf_op jit(solution)/shard_map/ppermute | solution.py:559
  24.1 2.2 %copy-start.2 = (bf16[2,192,6144]{2,1,0:T(8,128)(2,1)}, bf16[2,192,6144]{2,1,0:T(8,128)(2,1)S(1)}, u32[]{:S(2)}) copy-start(bf16[2,192,6144]{2,1,0:T(8,128)(2,1)S(1)} %hold.12.matrix) | copy-start | bytes 14155780
  26.3 2.3 %copy-start.3 = (bf16[2,192,6144]{2,1,0:T(8,128)(2,1)S(1)}, bf16[2,192,6144]{2,1,0:T(8,128)(2,1)}, u32[]{:S(2)}) copy-start(bf16[2,192,6144]{2,1,0:T(8,128)(2,1)} %copy-done.2) | copy-start | bytes 14155780
  30.1 118.2 %collective-permute-start.8 = (bf16[16,4,192]{2,1,0:T(4,128)(2,1)S(1)}, bf16[16,4,192]{2,1,0:T(4,128)(2,1)S(1)}, u32[]{:S(2)}, u32[]{:S(2)}) collective-permute-start(bf16[16,4,192]{2,1,0:T(4,128)(2,1)S(1)} %get-tuple-element.110), channel_id=1, source_target_pairs={{0,97},{1,96},{2,99},{3,98},{4,101},{5,100},{6,103},{7,102},{8,105... | collective-permute-start | bytes 73736 | tf_op jit(solution)/shard_map/cond/branch_1_fun/ppermute | solution.py:500
  145.8 3.7 %collective-permute-start.7 = (bf16[16,4,192]{2,1,0:T(4,128)(2,1)S(1)}, bf16[16,4,192]{2,1,0:T(4,128)(2,1)S(1)}, u32[]{:S(2)}, u32[]{:S(2)}) collective-permute-start(bf16[16,4,192]{2,1,0:T(4,128)(2,1)S(1)} %get-tuple-element.110), channel_id=1, source_target_pairs={{0,96},{1,97},{2,98},{3,99},{4,100},{5,101},{6,102},{7,103},{8,104... | collective-permute-start | bytes 73736 | tf_op jit(solution)/shard_map/cond/branch_1_fun/ppermute | solution.py:500
  150.9 2.7 %collective-permute-start.13 = (bf16[5,3,64,192]{3,2,1,0:T(8,128)(2,1)S(1)}, bf16[5,3,64,192]{3,2,1,0:T(8,128)(2,1)}, u32[]{:S(2)}, u32[]{:S(2)}) collective-permute-start(bf16[5,3,64,192]{3,2,1,0:T(8,128)(2,1)S(1)} %get-tuple-element.139), channel_id=1, source_target_pairs={{64,32},{65,33},{66,34},{67,35},{68,36},{69,37},{70,38},{71,39},{7... | collective-permute-start | bytes 1105928 | tf_op jit(solution)/shard_map/ppermute | solution.py:559
  154.8 10.9 %collective-permute-start.15 = (bf16[5,14,4,192]{3,2,1,0:T(4,128)(2,1)S(1)}, bf16[5,14,4,192]{3,2,1,0:T(4,128)(2,1)S(1)}, u32[]{:S(2)}, u32[]{:S(2)}) collective-permute-start(bf16[5,14,4,192]{3,2,1,0:T(4,128)(2,1)S(1)} %get-tuple-element.140), channel_id=1, source_target_pairs={{0,1},{1,2},{2,3},{3,4},{4,5},{5,6},{6,7},{7,8},{8,9},{9,10},{10,1... | collective-permute-start | bytes 322568 | tf_op jit(solution)/shard_map/ppermute | solution.py:465
  159.5 11.8 %collective-permute-start.16 = (bf16[5,14,4,192]{3,2,1,0:T(4,128)(2,1)S(1)}, bf16[5,14,4,192]{3,2,1,0:T(4,128)(2,1)S(1)}, u32[]{:S(2)}, u32[]{:S(2)}) collective-permute-start(bf16[5,14,4,192]{3,2,1,0:T(4,128)(2,1)S(1)} %get-tuple-element.141), channel_id=1, source_target_pairs={{1,0},{2,1},{3,2},{4,3},{5,4},{6,5},{7,6},{8,7},{9,8},{10,9},{11,1... | collective-permute-start | bytes 322568 | tf_op jit(solution)/shard_map/ppermute | solution.py:465
  183.4 7.0 %copy-start.15 = (f32[2,2,8,64,192]{4,3,2,1,0:T(8,128)}, f32[2,2,8,64,192]{4,3,2,1,0:T(8,128)S(1)}, u32[]{:S(2)}) copy-start(f32[2,2,8,64,192]{4,3,2,1,0:T(8,128)S(1)} %get-tuple-element.114.smoothed) | copy-start | bytes 4718596 | tf_op jit(solution)/shard_map/cond
  183.4 7.0 %collective-permute-start.10 = (bf16[4,192]{1,0:T(4,128)(2,1)S(1)}, bf16[4,192]{1,0:T(4,128)(2,1)S(1)}, u32[]{:S(2)}, u32[]{:S(2)}) collective-permute-start(bf16[4,192]{1,0:T(4,128)(2,1)S(1)} %get-tuple-element.117), channel_id=1, source_target_pairs={{0,33},{1,32},{2,35},{3,34},{4,37},{5,36},{6,39},{7,38},{8,41},{9,... | collective-permute-start | bytes 4616 | tf_op jit(solution)/shard_map/cond/branch_1_fun/ppermute | solution.py:500
  183.5 6.9 %collective-permute-start.9 = (bf16[4,192]{1,0:T(4,128)(2,1)S(1)}, bf16[4,192]{1,0:T(4,128)(2,1)S(1)}, u32[]{:S(2)}, u32[]{:S(2)}) collective-permute-start(bf16[4,192]{1,0:T(4,128)(2,1)S(1)} %get-tuple-element.117), channel_id=1, source_target_pairs={{0,32},{1,33},{2,34},{3,35},{4,36},{5,37},{6,38},{7,39},{8,40},{9,... | collective-permute-start | bytes 4616 | tf_op jit(solution)/shard_map/cond/branch_1_fun/ppermute | solution.py:500
  191.0 15.3 %all-to-all-start.7 = ((bf16[16,8,192]{2,1,0:T(8,128)(2,1)}), bf16[16,8,192]{2,1,0:T(8,128)(2,1)S(1)}, u32[]{:S(2)}, u32[]{:S(2)}) async-start(bf16[16,8,192]{2,1,0:T(8,128)(2,1)} %pair_up.7), calls=%async_computation.7 | async-start | bytes 131072 | tf_op jit(solution)/shard_map/cond/branch_1_fun/all_to_all | solution.py:495
  198.7 7.7 %copy-start.16 = (f32[2,2,8,64,192]{4,3,2,1,0:T(8,128)S(1)}, f32[2,2,8,64,192]{4,3,2,1,0:T(8,128)}, u32[]{:S(2)}) copy-start(f32[2,2,8,64,192]{4,3,2,1,0:T(8,128)} %copy-done.15) | copy-start | bytes 4718596 | tf_op jit(solution)/shard_map/cond
  198.7 2.3 %copy-start.12 = (bf16[2,192,6144]{2,1,0:T(8,128)(2,1)}, bf16[2,192,6144]{2,1,0:T(8,128)(2,1)S(1)}, u32[]{:S(2)}) copy-start(bf16[2,192,6144]{2,1,0:T(8,128)(2,1)S(1)} %hold.11.matrix) | copy-start | bytes 14155780 | tf_op jit(solution)/shard_map/cond
  206.4 2.3 %copy-start.13 = (bf16[2,192,6144]{2,1,0:T(8,128)(2,1)S(1)}, bf16[2,192,6144]{2,1,0:T(8,128)(2,1)}, u32[]{:S(2)}) copy-start(bf16[2,192,6144]{2,1,0:T(8,128)(2,1)} %copy-done.12) | copy-start | bytes 14155780 | tf_op jit(solution)/shard_map/cond
